TPU v7x, 32 devices: a whole 2x2x4 slice. The times are simulated.
32 devices in a mesh: group: 2 (over y), att: 4 (over z), ffn: 4 (over x, core).
Axes of the slice: x: 2, y: 2, z: 4, core: 2. Of those that a mesh axis runs over, the one named last changes fastest.
Arguments:
- hidden_state: bfloat16 [160, 8192], P(('group', 'att'), 'ffn'), parts along dimension 0, may hold values from -40 to 40
- queries: bfloat16 [160, 8192], P(('group', 'att'), 'ffn'), parts along dimension 0, may hold values from -800 to 800
- key_cache: bfloat16 [102400, 1024], P(('group', 'att'), 'ffn'), parts along dimension 0, may hold values from -6 to 6
- value_cache: bfloat16 [102400, 1024], P(('group', 'att'), 'ffn'), parts along dimension 0, may hold values from -6 to 6
- lengths: int32 [160], P(('group', 'att')), parts along dimension 0, may hold values from 1 to 1279, as said below
- assignment: int32 [160], P('group'), parts along dimension 0, may hold values from 0 to 79, each once
- out_weight: bfloat16 [8, 1024, 8192], P(None, 'att', 'ffn'), may hold values from -0.375 to 0.375
- norm_gain: bfloat16 [8192], P('ffn'), may hold values from 0.099609375 to 1.8984375
- gate_weight: bfloat16 [14336, 8192], P('att', 'ffn'), may hold values from -0.0625 to 0.0625
- up_weight: bfloat16 [14336, 8192], P('att', 'ffn'), may hold values from -0.0625 to 0.0625
- down_weight: bfloat16 [14336, 8192], P('att', 'ffn'), may hold values from -0.0625 to 0.0625
Outputs:
- next_hidden: bfloat16 [160, 8192], P(('group', 'att'), 'ffn'), parts along dimension 0
There are 2 independent parts, one for each index of `group`. A program takes and returns all parts, laid end to end along the dimension named above; an argument that names none is the same for every part. Nothing has to cross between parts.
Inputs may be any that keep to these rules, and one draw needn't show every extreme that they name: Each attention index holds the contexts of its 20 slots end to end in its 12800 cache rows in slot order; their lengths sum to at most 12800, and to exactly 12800 on some attention index in every draw. `assignment`: A permutation of the requests.
All inputs are finite; a program needn't handle non-finite values.
Results may differ from a plain program's by a relative error of at most 0.02.
Values may be sent and summed in bfloat16 or wider, within the bound.
No kernel may reach another device: no remote copies, remote signals or barrier semaphores. Data moves between devices by JAX's collectives and lax.ppermute only.
A program may use at most 192 MiB of HBM per device.

v0:
```python
import math

import jax
import jax.numpy as jnp
from jax import lax
from jax.sharding import PartitionSpec as P

epsilon = 1e-05
masked_score = -1e30


def softmax_rounded(scores):
    row_top = jnp.max(scores, axis=-1, keepdims=True)
    shifted = jnp.exp(scores - row_top)
    totals = jnp.sum(shifted, axis=-1, keepdims=True)
    return (shifted / totals).astype(jnp.bfloat16)


def per_device(
    hidden_state,
    queries,
    key_cache,
    value_cache,
    lengths,
    assignment,
    out_weight,
    norm_gain,
    gate_weight,
    up_weight,
    down_weight,
):
    rows_dev = hidden_state.shape[0]
    columns = hidden_state.shape[1]
    att_count = lax.axis_size("att")
    ffn_count = lax.axis_size("ffn")
    requests = rows_dev * att_count
    kv_total = out_weight.shape[0]
    kv_local = kv_total // ffn_count
    model_width = columns * ffn_count
    pool_rows = key_cache.shape[0]
    head_size = key_cache.shape[1] // kv_local
    per_group = queries.shape[1] // (kv_local * head_size)
    score_scale = 1.0 / math.sqrt(head_size)
    att_place = lax.axis_index("att")
    every_query = lax.all_gather(queries, "att", axis=0, tiled=True)
    own_slots = lax.dynamic_slice_in_dim(assignment, att_place * rows_dev, rows_dev)
    slot_queries = jnp.take(every_query, own_slots, axis=0).reshape(
        rows_dev, kv_local, per_group, head_size
    )
    keys_local = key_cache.reshape(pool_rows, kv_local, head_size)
    values_local = value_cache.reshape(pool_rows, kv_local, head_size)
    slot_starts = jnp.cumsum(lengths) - lengths
    slot_ends = slot_starts + lengths
    positions = jnp.arange(pool_rows, dtype=jnp.int32)
    owned_rows = (positions[None, :] >= slot_starts[:, None]) & (
        positions[None, :] < slot_ends[:, None]
    )
    owned_rows = owned_rows[:, None, None, :]
    raw_scores = (
        jnp.einsum("rkgc,pkc->rkgp", slot_queries, keys_local, preferred_element_type=jnp.float32)
        * score_scale
    )
    weights = softmax_rounded(jnp.where(owned_rows, raw_scores, masked_score))
    attended = jnp.einsum(
        "rkgp,pkc->rkgc", weights, values_local, preferred_element_type=jnp.float32
    )
    attended = attended.astype(jnp.bfloat16).reshape(rows_dev, kv_local, per_group * head_size)
    spread = lax.all_to_all(attended, "att", split_axis=2, concat_axis=0, tiled=True)
    pieces = lax.all_gather(spread, "ffn", axis=1, tiled=True)
    inverse = (
        jnp.zeros((requests,), jnp.int32).at[assignment].set(jnp.arange(requests, dtype=jnp.int32))
    )
    request_pieces = jnp.take(pieces, inverse, axis=0)
    block = request_pieces
    projected = lax.psum_scatter(
        jnp.einsum("rkc,kcd->rd", block, out_weight, preferred_element_type=jnp.float32).astype(
            jnp.bfloat16
        ),
        "att",
        scatter_dimension=0,
        tiled=True,
    ).astype(jnp.float32)
    middle_short = (hidden_state.astype(jnp.float32) + projected).astype(jnp.bfloat16)
    middle = lax.optimization_barrier(middle_short).astype(jnp.float32)
    squares = lax.psum(jnp.sum(middle * middle, axis=1), "ffn")
    normed = (
        middle * lax.rsqrt(squares[:, None] / model_width + epsilon) * norm_gain.astype(jnp.float32)
    ).astype(jnp.bfloat16)
    every_row = lax.all_gather(normed, "att", axis=0, tiled=True)
    contract = (((1,), (1,)), ((), ()))
    gate_part = lax.dot_general(
        gate_weight, every_row, contract, preferred_element_type=jnp.float32
    )
    up_part = lax.dot_general(up_weight, every_row, contract, preferred_element_type=jnp.float32)
    totals = lax.psum(
        jnp.concatenate([gate_part, up_part], axis=1).astype(jnp.bfloat16), "ffn"
    ).astype(jnp.float32)
    unit_active = (jax.nn.silu(totals[:, :requests]) * totals[:, requests:]).astype(jnp.bfloat16)
    block = unit_active
    returned = lax.psum_scatter(
        lax.dot_general(
            block, down_weight, (((0,), (0,)), ((), ())), preferred_element_type=jnp.float32
        ).astype(jnp.bfloat16),
        "att",
        scatter_dimension=0,
        tiled=True,
    ).astype(jnp.float32)
    return (middle + returned).astype(jnp.bfloat16)


def solution(mesh):
    in_specs = (
        P(("group", "att"), "ffn"),
        P(("group", "att"), "ffn"),
        P(("group", "att"), "ffn"),
        P(("group", "att"), "ffn"),
        P(("group", "att")),
        P("group"),
        P(None, "att", "ffn"),
        P("ffn"),
        P("att", "ffn"),
        P("att", "ffn"),
        P("att", "ffn"),
    )
    out_specs = P(("group", "att"), "ffn")
    return jax.shard_map(
        per_device, mesh=mesh, in_specs=in_specs, out_specs=out_specs, check_vma=False
    )
```

profile of v0, /device:TPU:0, one launch (start us, length us, event | category | flops | bytes accessed | tf_op | source)
XLA Modules:
  0.0 247.6 jit_solution(2298963000983809994)
XLA Ops:
  7.3 16.5 %all-gather = bf16[4,20,2048]{2,1,0:T(8,128)(2,1)S(1)} all-gather(bf16[1,20,2048]{2,1,0:T(8,128)(2,1)} %bitcast.50), channel_id=1, replica_groups=mesh['group'=2,'att'=4,'ffn'=4] {'att'}, dimensions={0}, use_global_device_ids=true | all-gather | bytes 409600 | tf_op jit(solution)/shard_map/all_gather | solution.py:45
  26.4 13.3 %reshape.93 = bf16[12800,2,128]{2,1,0:T(2,128)(2,1)} reshape(bf16[12800,256]{1,0:T(8,128)(2,1)} %param.13) | data formatting | bytes 13107200 | tf_op jit(solution)/shard_map/reshape | solution.py:50
  39.6 13.2 %reshape.94 = bf16[12800,2,128]{2,1,0:T(2,128)(2,1)} reshape(bf16[12800,256]{1,0:T(8,128)(2,1)} %param.14) | data formatting | bytes 13107200 | tf_op jit(solution)/shard_map/reshape | solution.py:51
  52.9 12.1 %fusion.33 = (f32[20,2,8]{2,0,1:T(8,128)S(1)}, f32[20,2,8,12800]{3,2,0,1:T(8,128)}) fusion(bf16[12800,2,128,1]{2,1,0,3:T(2,128)(2,1)} %bitcast.42, pred[20]{0:T(512)(128)(4,1)S(1)} %get-tuple-element.5, pred[20,12800]{1,0:T(8,128)(4,1)S(1)} %fusion.11, bf16[24,16,128]{2,1,0:T(8,128)(2,1)S(1)} %bitcast.46), kind=kOutput, calls=%fused_computation.55 | convolution fusion | flops 1060904640 | bytes 23328512 | tf_op jit(solution)/shard_map/rkgc,pkc->rkgp/dot_general | solution.py:60
  65.0 8.0 %fusion.4 = f32[20,2,8]{2,0,1:T(8,128)S(1)} fusion(f32[20,2,8,12800]{3,2,0,1:T(8,128)} %get-tuple-element.8, f32[20,2,8]{2,0,1:T(8,128)S(1)} %get-tuple-element.7), kind=kLoop, calls=%fused_computation.8 | loop fusion | flops 8191680 | bytes 16386560 | tf_op jit(solution)/shard_map/reduce_sum | solution.py:15
  72.9 10.5 %fusion.16 = bf16[20,2,8,128]{3,2,0,1:T(8,128)(2,1)S(1)} fusion(bf16[12800,2,128,1]{2,1,0,3:T(2,128)(2,1)} %bitcast.43, f32[20,2,8,12800]{3,2,0,1:T(8,128)} %get-tuple-element.8, f32[20,2,8]{2,0,1:T(8,128)S(1)} %fusion.4, f32[20,2,8]{2,0,1:T(8,128)S(1)} %get-tuple-element.7), kind=kOutput, calls=%fused_computation.26 | convolution fusion | flops 1060904960 | bytes 23022080 | tf_op jit(solution)/shard_map/rkgp,pkc->rkgc/dot_general | solution.py:64
  83.7 1.6 reshape.136
  85.4 5.6 %all-to-all-start = ((bf16[4,2,5120]{2,1,0:T(2,128)(2,1)}), bf16[4,2,5120]{2,1,0:T(2,128)(2,1)S(1)}, u32[]{:S(2)}, u32[]{:S(2)}) async-start(bf16[4,2,5120]{2,1,0:T(2,128)(2,1)} %reshape.136), calls=%async_computation | async-start | bytes 163840 | tf_op jit(solution)/shard_map/all_to_all | solution.py:68
  91.8 4.9 %all-to-all-done = bf16[4,2,5120]{2,1,0:T(2,128)(2,1)S(1)} async-done(((bf16[4,2,5120]{2,1,0:T(2,128)(2,1)}), bf16[4,2,5120]{2,1,0:T(2,128)(2,1)S(1)}, u32[]{:S(2)}, u32[]{:S(2)}) %all-to-all-start) | async-done | bytes 81952 | tf_op jit(solution)/shard_map/all_to_all | solution.py:68
  96.7 1.3 reshape.137
  98.5 6.1 %all_gather.10 = bf16[80,8,256]{2,0,1:T(8,128)(2,1)S(1)} all-gather(bf16[80,2,256]{2,0,1:T(8,128)(2,1)S(1)} %copy.42), channel_id=1, replica_groups=mesh['group'=2,'att'=4,'ffn'=4] {'ffn'}, dimensions={1}, use_global_device_ids=true | all-gather | bytes 409600 | tf_op jit(solution)/shard_map/all_gather | solution.py:69
  105.6 4.9 %fusion.10 = bf16[80,2048]{1,0:T(8,128)(2,1)S(1)} fusion(bf16[8,256,2048]{2,1,0:T(8,128)(2,1)} %param.17, bf16[80,8,256]{2,1,0:T(8,128)(2,1)S(1)} %broadcast_select_fusion), kind=kOutput, calls=%fused_computation.18 | convolution fusion | flops 671252480 | bytes 9043968 | tf_op jit(solution)/shard_map/rkc,kcd->rd/dot_general | solution.py:76
  110.5 17.1 %fusion = bf16[24,2048]{1,0:T(8,128)(2,1)S(1)} fusion(bf16[80,2048]{1,0:T(8,128)(2,1)S(1)} %fusion.10), kind=kCustom, calls=%all-reduce-scatter | all-reduce-scatter fusion | flops 196609 | bytes 426496
  127.7 1.3 collective-permute-start
  131.3 5.7 %psum.14 = f32[20]{0:T(128)S(1)} all-reduce(f32[20]{0:T(128)S(1)} %fusion.22), channel_id=1, replica_groups=mesh['group'=2,'att'=4,'ffn'=4] {'ffn'}, use_global_device_ids=true, to_apply=%region_6.7 | all-reduce | flops 20 | bytes 160 | tf_op jit(solution)/shard_map/psum | solution.py:85
  137.0 14.3 %all-gather.1 = bf16[4,20,2048]{2,1,0:T(8,128)(2,1)S(1)} all-gather(bf16[1,20,2048]{2,1,0:T(8,128)(2,1)S(1)} %fusion.26), channel_id=1, replica_groups=mesh['group'=2,'att'=4,'ffn'=4] {'att'}, dimensions={0}, use_global_device_ids=true | all-gather | bytes 409600 | tf_op jit(solution)/shard_map/all_gather | solution.py:89
  151.4 9.7 %fusion.8 = bf16[3584,80]{0,1:T(8,128)(2,1)S(1)} fusion(bf16[80,2048]{1,0:T(8,128)(2,1)S(1)} %reshape.126, bf16[3584,2048]{1,0:T(8,128)(2,1)} %param.19), kind=kOutput, calls=%fused_computation.14 | convolution fusion | flops 1174691840 | bytes 15581184 | tf_op jit(solution)/shard_map/dot_general | solution.py:91
  161.2 9.7 %fusion.9 = bf16[3584,80]{0,1:T(8,128)(2,1)S(1)} fusion(bf16[80,2048]{1,0:T(8,128)(2,1)S(1)} %reshape.126, bf16[3584,2048]{1,0:T(8,128)(2,1)} %param.20), kind=kOutput, calls=%fused_computation.15 | convolution fusion | flops 1174691840 | bytes 15581184 | tf_op jit(solution)/shard_map/dot_general | solution.py:94
  172.0 38.2 %all-reduce.6.cloned.1.call-done = bf16[3584,160]{0,1:T(8,128)(2,1)} async-done(((bf16[3584,160]{0,1:T(8,128)(2,1)}), bf16[3584,160]{0,1:T(8,128)(2,1)}) %all-reduce.6.cloned.1.call-update) | async-done | bytes 1146896 | tf_op jit(solution)/shard_map/psum | solution.py:95
  210.2 1.5 convert_element_type.56
  211.7 7.9 %convolution_convert_fusion.2 = bf16[80,2048]{1,0:T(8,128)(2,1)S(1)} fusion(bf16[3584,2048]{1,0:T(8,128)(2,1)} %param.21, f32[3584,160]{0,1:T(8,128)S(1)} %convert_element_type.56), kind=kOutput, calls=%fused_computation.17 | convolution fusion | flops 1176289280 | bytes 17301504 | tf_op jit(solution)/shard_map/dot_general | solution.py:101
  219.6 15.6 %fusion.1 = bf16[24,2048]{1,0:T(8,128)(2,1)S(1)} fusion(bf16[80,2048]{1,0:T(8,128)(2,1)S(1)} %convolution_convert_fusion.2), kind=kCustom, calls=%all-reduce-scatter.1 | all-reduce-scatter fusion | flops 196609 | bytes 426496
  235.2 2.7 %collective-permute-start.1 = (bf16[12,2048]{1,0:T(8,128)(2,1)S(1)}, bf16[12,2048]{1,0:T(8,128)(2,1)S(1)}, u32[]{:S(2)}, u32[]{:S(2)}) collective-permute-start(bf16[12,2048]{1,0:T(8,128)(2,1)S(1)} %slice.15), channel_id=1, source_target_pairs={{0,4},{4,8},{8,12},{1,5},{5,9},{9,13},{2,6},{6,10},{10,14},{3,7},{... | collective-permute-start | bytes 147464
  238.0 1.9 collective-permute-done.1
  (47 shorter events, 9.7 us)
Async XLA Ops:
  72.9 18.0 %copy-start.3 = (s32[80]{0:T(128)S(1)}, s32[80]{0:T(128)}, u32[]{:S(2)}) copy-start(s32[80]{0:T(128)} %param.16) | copy-start | bytes 964
  85.4 11.3 %all-to-all-start = ((bf16[4,2,5120]{2,1,0:T(2,128)(2,1)}), bf16[4,2,5120]{2,1,0:T(2,128)(2,1)S(1)}, u32[]{:S(2)}, u32[]{:S(2)}) async-start(bf16[4,2,5120]{2,1,0:T(2,128)(2,1)} %reshape.136), calls=%async_computation | async-start | bytes 163840 | tf_op jit(solution)/shard_map/all_to_all | solution.py:68
  90.9 119.3 %all-reduce.6.cloned.1.call-start = ((), (), s32[]{:S(2)}) async-start(), calls=%async_computation.1 | async-start | bytes 2293760 | tf_op jit(solution)/shard_map/psum | solution.py:95
  104.8 24.2 %copy-start.1 = (bf16[2048]{0:T(1024)(128)(2,1)S(1)}, bf16[2048]{0:T(1024)(128)(2,1)}, u32[]{:S(2)}) copy-start(bf16[2048]{0:T(1024)(128)(2,1)} %param.18) | copy-start | bytes 12292
  104.8 24.2 %copy-start.2 = (u32[32]{0:T(128)S(1)}, u32[32]{0:T(128)}, u32[]{:S(2)}) copy-start(u32[32]{0:T(128)} %constant.63) | copy-start | bytes 388
  105.4 25.7 %copy-start = (bf16[20,2048]{1,0:T(8,128)(2,1)S(1)}, bf16[20,2048]{1,0:T(8,128)(2,1)}, u32[]{:S(2)}) copy-start(bf16[20,2048]{1,0:T(8,128)(2,1)} %param.11) | copy-start | bytes 245764
  127.7 3.2 %collective-permute-start = (bf16[12,2048]{1,0:T(8,128)(2,1)S(1)}, bf16[12,2048]{1,0:T(8,128)(2,1)S(1)}, u32[]{:S(2)}, u32[]{:S(2)}) collective-permute-start(bf16[12,2048]{1,0:T(8,128)(2,1)S(1)} %slice.14), channel_id=1, source_target_pairs={{0,4},{4,8},{8,12},{1,5},{5,9},{9,13},{2,6},{6,10},{10,14},{3,7},{... | collective-permute-start | bytes 147464
  235.2 4.6 %collective-permute-start.1 = (bf16[12,2048]{1,0:T(8,128)(2,1)S(1)}, bf16[12,2048]{1,0:T(8,128)(2,1)S(1)}, u32[]{:S(2)}, u32[]{:S(2)}) collective-permute-start(bf16[12,2048]{1,0:T(8,128)(2,1)S(1)} %slice.15), channel_id=1, source_target_pairs={{0,4},{4,8},{8,12},{1,5},{5,9},{9,13},{2,6},{6,10},{10,14},{3,7},{... | collective-permute-start | bytes 147464
Sparse Core Ops, SparseCore 0:
  172.2 38.0 all-reduce.5
where the time goes:
time: 249 us; the launch traced here: 248 us
  blocking collectives  75.3 us (30%)
  matrix products  54.8 us (22%)
  waiting for transfers between devices  45.6 us (18%)
  local copies, waits for them, and re-layouts  34.4 us (14%)
  between operations  14.3 us (6%)
  other arithmetic  13.6 us (5%)
  starting transfers between devices  9.59 us (4%)
    psum x1, waiting for transfers between devices, per_device(): lax.psum(jnp.concatenate([gate_part, up_part], axis=1).astype(jnp.bfloat1...  38.2 us
    unnamed x2, blocking collectives  32.7 us
    all_gather x1, blocking collectives, per_device(): every_query = lax.all_gather(queries, 'att', axis=0, tiled=True)  16.5 us
    all_gather x1, blocking collectives, per_device(): every_row = lax.all_gather(normed, 'att', axis=0, tiled=True)  14.3 us
    reshape x1, local copies, waits for them, and re-layouts, per_device(): keys_local = key_cache.reshape(pool_rows, kv_local, head_size)  13.3 us
    reshape x1, local copies, waits for them, and re-layouts, per_device(): values_local = value_cache.reshape(pool_rows, kv_local, head_size)  13.2 us
    dot_general x1, matrix products, per_device(): jnp.einsum('rkgc,pkc->rkgp', slot_queries, keys_local, preferred_element_...  12.1 us
    dot_general x1, matrix products, per_device(): jnp.einsum('rkgp,pkc->rkgc', weights, values_local, preferred_element_typ...  10.5 us
  transfers between devices with their start and end apart: 4, of which 4 were waited for; matrix products, arithmetic and copies ran while one was open for 1% of the time, Pallas kernels for 0%

commit v1 on v0

--- a/solution.py
+++ b/solution.py
@@ -1,12 +1,24 @@
+import functools
 import math
 
 import jax
 import jax.numpy as jnp
 from jax import lax
+from jax.experimental import pallas as pl
+from jax.experimental.pallas import tpu as pltpu
 from jax.sharding import PartitionSpec as P
 
 epsilon = 1e-05
 masked_score = -1e30
+lanes = 128
+sublanes = 16
+max_context = 1279
+contract_minor = (((1,), (1,)), ((), ()))
+F32 = jnp.float32
+BF16 = jnp.bfloat16
+vmem = pl.BlockSpec(memory_space=pltpu.VMEM)
+smem = pl.BlockSpec(memory_space=pltpu.SMEM)
+anywhere = pl.BlockSpec(memory_space=pl.ANY)
 
 
 def softmax_rounded(scores):
@@ -16,7 +28,7 @@
     return (shifted / totals).astype(jnp.bfloat16)
 
 
-def per_device(
+def general_device(
     hidden_state,
     queries,
     key_cache,
@@ -108,6 +120,356 @@
     return (middle + returned).astype(jnp.bfloat16)
 
 
+def pair_swap(value, axis, bit):
+    count = lax.axis_size(axis)
+    return lax.ppermute(value, axis, [(i, i ^ bit) for i in range(count)])
+
+
+def up_to(value, multiple):
+    return -(-value // multiple) * multiple
+
+
+def attention_kernel(place, assignment, lengths, *refs, slots, count, chunk, scale, unroll):
+    query_blocks, (keys, values), outs = refs[:count], refs[count : count + 2], refs[count + 2 : -2]
+    queries, attended = refs[-2:]
+    pool = keys.shape[0]
+    heads = queries.shape[1]
+    half = heads // 2
+    own = place[0]
+    for k in range(count):
+        queries[k * slots : (k + 1) * slots] = query_blocks[k][...]
+    top_half = lax.broadcasted_iota(jnp.int32, (heads, lanes), 0) < half
+
+    def slot(s, start):
+        length = lengths[s]
+        request = assignment[own * slots + s]
+        owner = sum((request >= k * slots).astype(jnp.int32) for k in range(1, count))
+        query = queries[(owner ^ own) * slots + request - owner * slots]
+        first = pl.multiple_of(
+            jnp.minimum((start // sublanes) * sublanes, pool - chunk), sublanes
+        )
+        zero = jnp.zeros_like(query)
+        both = jnp.concatenate(
+            [jnp.where(top_half, query, zero), jnp.where(top_half, zero, query)], axis=1
+        )
+        scores = (
+            lax.dot_general(
+                both, keys[pl.ds(first, chunk), :], contract_minor, preferred_element_type=F32
+            )
+            * scale
+        )
+        rows = first + lax.broadcasted_iota(jnp.int32, (heads, chunk), 1)
+        scores = jnp.where((rows >= start) & (rows < start + length), scores, masked_score)
+        top = jnp.max(scores, axis=-1, keepdims=True)
+        shifted = jnp.exp(scores - top)
+        total = jnp.sum(shifted, axis=-1, keepdims=True)
+        weights = (shifted / total).astype(BF16)
+        out = jnp.dot(weights, values[pl.ds(first, chunk), :], preferred_element_type=F32)
+        attended[pl.ds(pl.multiple_of(s * heads, heads), heads), :] = jnp.where(
+            top_half, out[:, :lanes], out[:, lanes:]
+        )
+        return start + length
+
+    def body(step, start):
+        for u in range(unroll):
+            start = slot(step * unroll + u, start)
+        return start
+
+    lax.fori_loop(0, slots // unroll, body, jnp.int32(0))
+    per_block = half // count
+    for k in range(count):
+        outs[k][...] = jnp.zeros(outs[k].shape, BF16)
+        for kv in range(2):
+            for j in range(per_block):
+                head = kv * half + (own ^ k) * per_block + j
+                at = (kv * per_block + j) * lanes
+                outs[k][:slots, at : at + lanes] = attended[
+                    pl.ds(head, slots, stride=heads), :
+                ].astype(BF16)
+
+
+def attention(place, assignment, lengths, query_blocks, keys, values):
+    count = len(query_blocks)
+    slots, heads, _ = query_blocks[0].shape
+    pool = keys.shape[0]
+    chunk = min(up_to(max_context + sublanes - 1, lanes), pool)
+    unroll = 4 if slots % 4 == 0 else 1
+    width = heads // count * lanes
+    return pl.pallas_call(
+        functools.partial(
+            attention_kernel,
+            slots=slots,
+            count=count,
+            chunk=chunk,
+            scale=1.0 / math.sqrt(lanes),
+            unroll=unroll,
+        ),
+        in_specs=[smem] * 3 + [vmem] * (count + 2),
+        out_specs=[vmem] * count,
+        out_shape=[jax.ShapeDtypeStruct((up_to(slots, 8), width), BF16)] * count,
+        scratch_shapes=[
+            pltpu.VMEM((count * slots, heads, lanes), BF16),
+            pltpu.VMEM((slots * heads, lanes), F32),
+        ],
+        compiler_params=pltpu.CompilerParams(vmem_limit_bytes=20 << 20),
+        cost_estimate=pl.CostEstimate(
+            flops=4 * pool * heads * lanes * 2, bytes_accessed=pool * lanes * 8, transcendentals=0
+        ),
+        name="attention",
+    )(place, assignment, lengths, *query_blocks, keys, values)
+
+
+def projection_kernel(place, choose, *refs, count, parts):
+    pieces, weight, outs = refs[:parts], refs[parts], refs[parts + 1 : -2]
+    buffer, sems = refs[-2:]
+    own = place[1]
+    depth = buffer.shape[1]
+    copies = [
+        pltpu.make_async_copy(
+            weight.at[pl.ds(pl.multiple_of((own ^ k) * depth, depth), depth)],
+            buffer.at[k],
+            sems.at[k],
+        )
+        for k in range(parts)
+    ]
+    for copy in copies:
+        copy.start()
+    total = None
+    for k in range(parts):
+        rows = jnp.dot(choose[...], pieces[k][...], preferred_element_type=F32).astype(BF16)
+        copies[k].wait()
+        term = jnp.dot(rows, buffer[k], preferred_element_type=F32)
+        total = term if k == 0 else total + term
+    rows = total.shape[0] // count
+    for k in range(count):
+        outs[k][...] = total[k * rows : (k + 1) * rows].astype(BF16)
+
+
+def projection(place, choose, pieces, weight, count):
+    parts = len(pieces)
+    requests = choose.shape[0]
+    depth, width = weight.shape
+    return pl.pallas_call(
+        functools.partial(projection_kernel, count=count, parts=parts),
+        in_specs=[smem] + [vmem] * (1 + parts) + [anywhere],
+        out_specs=[vmem] * count,
+        out_shape=[jax.ShapeDtypeStruct((requests // count, width), BF16)] * count,
+        scratch_shapes=[
+            pltpu.VMEM((parts, depth // parts, width), BF16),
+            pltpu.SemaphoreType.DMA((parts,)),
+        ],
+        compiler_params=pltpu.CompilerParams(vmem_limit_bytes=24 << 20),
+        cost_estimate=pl.CostEstimate(
+            flops=2 * requests * depth * width, bytes_accessed=2 * depth * width, transcendentals=0
+        ),
+        name="projection",
+    )(place, choose, *pieces, weight)
+
+
+def hidden_kernel(place, *refs, count, masks, square):
+    blocks, (gain, gate, up), rest = refs[:count], refs[count : count + 3], refs[count + 3 :]
+    send, keep = rest[:2]
+    if square:
+        squares = rest[2]
+    joined, buffer, sems = rest[-3:]
+    own = place[1]
+    units = buffer.shape[2]
+    copies = {}
+    for m in range(2):
+        for t, weight in enumerate((gate, up)):
+            copies[m, t] = pltpu.make_async_copy(
+                weight.at[pl.ds(pl.multiple_of((own ^ masks[m]) * units, units), units)],
+                buffer.at[m, t],
+                sems.at[m, t],
+            )
+            copies[m, t].start()
+    rows = blocks[0].shape[0]
+    for k in range(count):
+        joined[k * rows : (k + 1) * rows, :] = blocks[k][...].astype(F32)
+    middle = joined[...]
+    if square:
+        squares[...] = jnp.broadcast_to(
+            jnp.sum(middle * middle, axis=1, keepdims=True), squares.shape
+        )
+    scaled = (middle * gain[...].astype(F32)).astype(BF16)
+    for m in range(2):
+        for t in range(2):
+            copies[m, t].wait()
+            out = lax.dot_general(
+                scaled, buffer[m, t], contract_minor, preferred_element_type=F32
+            )
+            target = send if m == 0 else keep
+            target[:, t * units : (t + 1) * units] = out.astype(target.dtype)
+
+
+def hidden_part(place, blocks, gain, gate, up, owners, masks, square):
+    count = len(blocks)
+    rows, width = blocks[0].shape
+    requests = rows * count
+    units = gate.shape[0] // owners
+    outs = [
+        jax.ShapeDtypeStruct((requests, 2 * units), BF16),
+        jax.ShapeDtypeStruct((requests, 2 * units), F32),
+    ]
+    if square:
+        outs.append(jax.ShapeDtypeStruct((requests, lanes), F32))
+    return pl.pallas_call(
+        functools.partial(hidden_kernel, count=count, masks=masks, square=square),
+        in_specs=[smem] + [vmem] * (count + 1) + [anywhere] * 2,
+        out_specs=[vmem] * len(outs),
+        out_shape=outs,
+        scratch_shapes=[
+            pltpu.VMEM((requests, width), F32),
+            pltpu.VMEM((2, 2, units, width), BF16),
+            pltpu.SemaphoreType.DMA((2, 2)),
+        ],
+        compiler_params=pltpu.CompilerParams(vmem_limit_bytes=32 << 20),
+        cost_estimate=pl.CostEstimate(
+            flops=8 * requests * units * width,
+            bytes_accessed=8 * units * width,
+            transcendentals=0,
+        ),
+        name="hidden_units",
+    )(place, *blocks, gain, gate, up)
+
+
+def down_kernel(place, *refs, masks, count, first):
+    pieces, weight = refs[:2], refs[2]
+    rest = refs[3:]
+    if not first:
+        before, rest = rest[0], rest[1:]
+    outs, (buffer, sems) = rest[:-2], rest[-2:]
+    own = place[1]
+    units = buffer.shape[1]
+    copies = [
+        pltpu.make_async_copy(
+            weight.at[pl.ds(pl.multiple_of((own ^ masks[m]) * units, units), units)],
+            buffer.at[m],
+            sems.at[m],
+        )
+        for m in range(2)
+    ]
+    for copy in copies:
+        copy.start()
+    total = None if first else before[...]
+    for m in range(2):
+        copies[m].wait()
+        term = jnp.dot(pieces[m][...], buffer[m], preferred_element_type=F32)
+        total = term if total is None else total + term
+    if first:
+        outs[0][...] = total
+    else:
+        rows = total.shape[0] // count
+        for k in range(count):
+            outs[k][...] = total[k * rows : (k + 1) * rows].astype(BF16)
+
+
+def down_part(place, pieces, weight, masks, count, before=None):
+    first = before is None
+    requests, units = pieces[0].shape
+    width = weight.shape[1]
+    if first:
+        outs = [jax.ShapeDtypeStruct((requests, width), F32)]
+    else:
+        outs = [jax.ShapeDtypeStruct((requests // count, width), BF16)] * count
+    return pl.pallas_call(
+        functools.partial(down_kernel, masks=masks, count=count, first=first),
+        in_specs=[smem] + [vmem] * 2 + [anywhere] + [vmem] * (0 if first else 1),
+        out_specs=[vmem] * len(outs),
+        out_shape=outs,
+        scratch_shapes=[
+            pltpu.VMEM((2, units, width), BF16),
+            pltpu.SemaphoreType.DMA((2,)),
+        ],
+        compiler_params=pltpu.CompilerParams(vmem_limit_bytes=24 << 20),
+        cost_estimate=pl.CostEstimate(
+            flops=4 * requests * units * width, bytes_accessed=4 * units * width, transcendentals=0
+        ),
+        name="down",
+    )(place, *pieces, weight, *([] if first else [before]))
+
+
+def exchanged_sum(blocks, axis):
+    total = blocks[0].astype(F32)
+    arrived = [pair_swap(blocks[k], axis, k) for k in range(1, len(blocks))]
+    for block in arrived:
+        total = total + block.astype(F32)
+    return total
+
+
+def per_device(
+    hidden_state,
+    queries,
+    key_cache,
+    value_cache,
+    lengths,
+    assignment,
+    out_weight,
+    norm_gain,
+    gate_weight,
+    up_weight,
+    down_weight,
+):
+    rows_dev, columns = hidden_state.shape
+    count = lax.axis_size("att")
+    parts = lax.axis_size("ffn")
+    requests = rows_dev * count
+    model_width = columns * parts
+    heads = queries.shape[1] // lanes
+    place = jnp.stack([lax.axis_index("att"), lax.axis_index("ffn")]).astype(jnp.int32)
+    swaps = range(1, count)
+
+    own_queries = queries.reshape(rows_dev, heads, lanes)
+    query_blocks = [own_queries] + [pair_swap(own_queries, "att", k) for k in swaps]
+    blocks = attention(place, assignment, lengths, query_blocks, key_cache, value_cache)
+
+    padded = blocks[0].shape[0]
+    order = place[0] ^ jnp.arange(count, dtype=jnp.int32)
+    served = jnp.pad(
+        assignment.reshape(count, rows_dev)[order],
+        ((0, 0), (0, padded - rows_dev)),
+        constant_values=-1,
+    ).reshape(1, -1)
+    wanted = (order[:, None] * rows_dev + jnp.arange(rows_dev, dtype=jnp.int32)[None]).reshape(-1, 1)
+    choose = (wanted == served).astype(BF16)
+
+    blocks = [blocks[0]] + [pair_swap(blocks[k], "att", k) for k in swaps]
+    piece = jnp.concatenate(blocks, axis=0)
+    across = pair_swap(piece, "ffn", 2)
+    beside = pair_swap(piece, "ffn", 1)
+    corner = pair_swap(across, "ffn", 1)
+    weight = out_weight.reshape(-1, columns)
+    partial = projection(place, choose, [piece, beside, across, corner], weight, count)
+    middle = (exchanged_sum(partial, "att") + hidden_state.astype(F32)).astype(BF16)
+    middle = lax.optimization_barrier(middle)
+
+    rows = [middle] + [pair_swap(middle, "att", k) for k in swaps]
+    gain = norm_gain.reshape(1, columns)
+    hidden = functools.partial(hidden_part, place, rows, gain, gate_weight, up_weight, parts)
+    far_send, far_keep, squares = hidden((3, 2), True)
+    far = (pair_swap(far_send, "ffn", 1).astype(F32) + far_keep).astype(BF16)
+    far = pair_swap(far, "ffn", 2)
+    squares = squares + pair_swap(squares, "ffn", 1)
+    squares = squares + pair_swap(squares, "ffn", 2)
+    near_send, near_keep = hidden((1, 0), False)
+    totals = near_keep + pair_swap(near_send, "ffn", 1).astype(F32) + far.astype(F32)
+    totals = totals * lax.rsqrt(squares[:, :1] / model_width + epsilon)
+    units = totals.shape[1] // 2
+    active = (jax.nn.silu(totals[:, :units]) * totals[:, units:]).astype(BF16)
+
+    across = pair_swap(active, "ffn", 2)
+    beside = pair_swap(active, "ffn", 1)
+    corner = pair_swap(across, "ffn", 1)
+    (before,) = down_part(place, [active, beside], down_weight, (0, 1), count)
+    partial = down_part(place, [across, corner], down_weight, (2, 3), count, before)
+    return (exchanged_sum(partial, "att") + middle.astype(F32)).astype(BF16)
+
+
+def exchanges_fit(mesh, per_group):
+    count, parts = mesh.shape["att"], mesh.shape["ffn"]
+    return parts == 4 and count & (count - 1) == 0 and per_group % count == 0
+
+
 def solution(mesh):
     in_specs = (
         P(("group", "att"), "ffn"),
@@ -123,6 +485,22 @@
         P("att", "ffn"),
     )
     out_specs = P(("group", "att"), "ffn")
-    return jax.shard_map(
-        per_device, mesh=mesh, in_specs=in_specs, out_specs=out_specs, check_vma=False
-    )
+
+    def step(*args):
+        queries, keys, out_weight = args[1], args[2], args[6]
+        kv_heads, group_width, _ = out_weight.shape
+        fits = (
+            exchanges_fit(mesh, group_width // lanes)
+            and keys.shape[1] == kv_heads * lanes
+            and kv_heads == 2 * mesh.shape["ffn"]
+            and queries.shape[1] == kv_heads * group_width
+        )
+        return jax.shard_map(
+            per_device if fits else general_device,
+            mesh=mesh,
+            in_specs=in_specs,
+            out_specs=out_specs,
+            check_vma=False,
+        )(*args)
+
+    return step

time: 249 us -> 132 us (0.53)
  blocking collectives: 75.3 us -> 0 us
  matrix products: 54.8 us -> 0 us
  Pallas kernels: 0 us -> 36.4 us
  starting transfers between devices: 9.59 us -> 29 us
  local copies, waits for them, and re-layouts: 34.4 us -> 18 us
  between operations: 14.3 us -> 0.25 us
  other arithmetic: 13.6 us -> 1.4 us
    dot_general x6 -> x0, matrix products: 54.8 us -> none  [the longest x1 12.1 us: per_device(): jnp.einsum('rkgc,pkc->rkgp', slot_queries, keys_local, preferred_element_...]
    ppermute x0 -> x26, waiting for transfers between devices: none -> 46.6 us  [pair_swap(): return lax.ppermute(value, axis, [(i, i ^ bit) for i in range(count)])]
    psum x1 -> x0, waiting for transfers between devices: 38.2 us -> none  [per_device(): lax.psum(jnp.concatenate([gate_part, up_part], axis=1).astype(jnp.bfloat1...]
    all_gather x3 -> x0, blocking collectives: 36.9 us -> none  [the longest x1 16.5 us: per_device(): every_query = lax.all_gather(queries, 'att', axis=0, tiled=True)]
    pallas_call x0 -> x6, Pallas kernels: none -> 36.4 us  [the longest x2 14.3 us: hidden_part(): pl.pallas_call(functools.partial(hidden_kernel, count=count, masks=masks,...]
    unnamed x2 -> x0, blocking collectives: 32.7 us -> none
    ppermute x0 -> x26, starting transfers between devices: none -> 29 us  [pair_swap(): return lax.ppermute(value, axis, [(i, i ^ bit) for i in range(count)])]
    reshape x3, local copies, waits for them, and re-layouts: 26.8 us -> 0.75 us  [the longest x1 0.74 us: per_device(): assignment.reshape(count, rows_dev)[order]]
  transfers between devices with their start and end apart: 4 -> 26, of which waited for: 4 -> 14; matrix products, arithmetic and copies ran while one was open for 1% -> 1% of each run, Pallas kernels for 0% -> 8%
where the time goes in v1:
time: 132 us
  waiting for transfers between devices  46.6 us (35%)
  Pallas kernels  36.4 us (28%)
  starting transfers between devices  29 us (22%)
  local copies, waits for them, and re-layouts  18 us (14%)
  other arithmetic  1.4 us (1%)
    ppermute x26, waiting for transfers between devices, pair_swap(): return lax.ppermute(value, axis, [(i, i ^ bit) for i in range(count)])  46.6 us
    ppermute x26, starting transfers between devices, pair_swap(): return lax.ppermute(value, axis, [(i, i ^ bit) for i in range(count)])  29 us
    unnamed x28, local copies, waits for them, and re-layouts  16.6 us
    pallas_call x2, Pallas kernels, hidden_part(): pl.pallas_call(functools.partial(hidden_kernel, count=count, masks=masks,...  14.3 us
    pallas_call x1, Pallas kernels, attention(): pl.pallas_call(functools.partial(attention_kernel, slots=slots, count=cou...  13.3 us
    pallas_call x2, Pallas kernels, down_part(): pl.pallas_call(functools.partial(down_kernel, masks=masks, count=count, f...  5.35 us
    pallas_call x1, Pallas kernels, projection(): pl.pallas_call(functools.partial(projection_kernel, count=count, parts=pa...  3.48 us
  transfers between devices with their start and end apart: 26, of which 14 were waited for; matrix products, arithmetic and copies ran while one was open for 1% of the time, Pallas kernels for 8%

profile of v1, /device:TPU:0, one launch (start us, length us, event | category | flops | bytes accessed | tf_op | source)
XLA Modules:
  0.0 131.7 jit_solution(2350158714165715799)
XLA Ops:
  1.0 3.1 %collective-permute-start = (bf16[20,16,128]{2,1,0:T(8,128)(2,1)S(1)}, bf16[20,16,128]{2,1,0:T(8,128)(2,1)S(1)}, u32[]{:S(2)}, u32[]{:S(2)}) collective-permute-start(bf16[20,16,128]{2,1,0:T(8,128)(2,1)S(1)} %slice.18.refs_0_), channel_id=1, source_target_pairs={{0,4},{4,0},{8,12},{12,8},{1,5},{5,1},{9,13},{13,9},{2,6},{6,2},{1... | collective-permute-start | bytes 245768 | tf_op jit(solution)/shard_map/ppermute | solution.py:125
  4.1 2.6 %collective-permute-start.1 = (bf16[20,16,128]{2,1,0:T(8,128)(2,1)S(1)}, bf16[20,16,128]{2,1,0:T(8,128)(2,1)S(1)}, u32[]{:S(2)}, u32[]{:S(2)}) collective-permute-start(bf16[20,16,128]{2,1,0:T(8,128)(2,1)S(1)} %slice.18.refs_0_), channel_id=1, source_target_pairs={{0,8},{4,12},{8,0},{12,4},{1,9},{5,13},{9,1},{13,5},{2,10},{6,14},... | collective-permute-start | bytes 245768 | tf_op jit(solution)/shard_map/ppermute | solution.py:125
  7.6 5.7 %collective-permute-done.1.refs_2_ = bf16[20,16,128]{2,1,0:T(8,128)(2,1)S(1)} collective-permute-done((bf16[20,16,128]{2,1,0:T(8,128)(2,1)S(1)}, bf16[20,16,128]{2,1,0:T(8,128)(2,1)S(1)}, u32[]{:S(2)}, u32[]{:S(2)}) %collective-permute-start.1) | collective-permute-done | bytes 81952 | tf_op jit(solution)/shard_map/ppermute | solution.py:125
  13.3 2.9 %copy-done.2 = bf16[12800,256]{1,0:T(8,128)(2,1)S(1)} copy-done((bf16[12800,256]{1,0:T(8,128)(2,1)S(1)}, bf16[12800,256]{1,0:T(8,128)(2,1)}, u32[]{:S(2)}) %copy-start.2) | copy-done | bytes 6553624
  16.1 2.9 %copy-done.3 = bf16[12800,256]{1,0:T(8,128)(2,1)S(1)} copy-done((bf16[12800,256]{1,0:T(8,128)(2,1)S(1)}, bf16[12800,256]{1,0:T(8,128)(2,1)}, u32[]{:S(2)}) %copy-start.3) | copy-done | bytes 6553624
  20.3 13.3 %attention.1 = (bf16[24,512]{1,0:T(8,128)(2,1)S(1)}, bf16[24,512]{1,0:T(8,128)(2,1)S(1)}, bf16[24,512]{1,0:T(8,128)(2,1)S(1)}, bf16[24,512]{1,0:T(8,128)(2,1)S(1)}) custom-call(s32[2]{0:T(128)S(1)} %pad_add_fusion.place, s32[80]{0:T(128)S(1)} %copy-done.4, s32[20]{0:T(128)S(1)} %copy-done.5, bf16[20,16,128]{2,1,0:T(8,128)(2,1)S(1)} %slice.18.refs_0_, ...), custom_call_target="tpu_custom_call" | custom-call | flops 209715200 | bytes 13107200 | tf_op jit(solution)/shard_map/attention/pallas_call | solution.py:198
  40.1 2.2 %collective-permute-done.5 = bf16[24,512]{1,0:T(8,128)(2,1)S(1)} collective-permute-done((bf16[24,512]{1,0:T(8,128)(2,1)S(1)}, bf16[24,512]{1,0:T(8,128)(2,1)S(1)}, u32[]{:S(2)}, u32[]{:S(2)}) %collective-permute-start.5) | collective-permute-done | bytes 24608 | tf_op jit(solution)/shard_map/ppermute | solution.py:125
  44.5 2.4 %collective-permute-done.7.refs_2_ = bf16[96,512]{1,0:T(8,128)(2,1)S(1)} collective-permute-done((bf16[96,512]{1,0:T(8,128)(2,1)S(1)}, bf16[96,512]{1,0:T(8,128)(2,1)S(1)}, u32[]{:S(2)}, u32[]{:S(2)}) %collective-permute-start.7) | collective-permute-done | bytes 98336 | tf_op jit(solution)/shard_map/ppermute | solution.py:125
  48.2 3.4 %copy-done.1 = bf16[8,256,2048]{2,1,0:T(8,128)(2,1)S(1)} copy-done((bf16[8,256,2048]{2,1,0:T(8,128)(2,1)S(1)}, bf16[8,256,2048]{2,1,0:T(8,128)(2,1)}, u32[]{:S(2)}) %copy-start.1) | copy-done | bytes 8388632
  51.6 3.5 %projection.1 = (bf16[20,2048]{1,0:T(8,128)(2,1)S(1)}, bf16[20,2048]{1,0:T(8,128)(2,1)S(1)}, bf16[20,2048]{1,0:T(8,128)(2,1)S(1)}, bf16[20,2048]{1,0:T(8,128)(2,1)S(1)}) custom-call(s32[2]{0:T(128)S(1)} %pad_add_fusion.place, bf16[80,96]{1,0:T(8,128)(2,1)S(1)} %compare_convert_fusion.choose, bf16[96,512]{1,0:T(8,128)(2,1)S(1)} %constant_dynamic-update-slice_fusion.refs_0_, ...), custom_call_target="tpu_custom_call" | custom-call | flops 671088640 | bytes 8388608 | tf_op jit(solution)/shard_map/projection/pallas_call | solution.py:252
  56.5 3.0 %collective-permute-start.9 = (bf16[20,2048]{1,0:T(8,128)(2,1)S(1)}, bf16[20,2048]{1,0:T(8,128)(2,1)S(1)}, u32[]{:S(2)}, u32[]{:S(2)}) collective-permute-start(bf16[20,2048]{1,0:T(8,128)(2,1)S(1)} %get-tuple-element.27), channel_id=1, source_target_pairs={{0,4},{4,0},{8,12},{12,8},{1,5},{5,1},{9,13},{13,9},{2,6},{6,2},{1... | collective-permute-start | bytes 245768 | tf_op jit(solution)/shard_map/ppermute | solution.py:125
  59.6 3.2 %collective-permute-done.11 = bf16[20,2048]{1,0:T(8,128)(2,1)S(1)} collective-permute-done((bf16[20,2048]{1,0:T(8,128)(2,1)S(1)}, bf16[20,2048]{1,0:T(8,128)(2,1)S(1)}, u32[]{:S(2)}, u32[]{:S(2)}) %collective-permute-start.11) | collective-permute-done | bytes 81952 | tf_op jit(solution)/shard_map/ppermute | solution.py:125
  62.7 3.3 %collective-permute-done.10 = bf16[20,2048]{1,0:T(8,128)(2,1)S(1)} collective-permute-done((bf16[20,2048]{1,0:T(8,128)(2,1)S(1)}, bf16[20,2048]{1,0:T(8,128)(2,1)S(1)}, u32[]{:S(2)}, u32[]{:S(2)}) %collective-permute-start.10) | collective-permute-done | bytes 81952 | tf_op jit(solution)/shard_map/ppermute | solution.py:125
  68.1 2.5 %collective-permute-start.14 = (bf16[20,2048]{1,0:T(8,128)(2,1)S(1)}, bf16[20,2048]{1,0:T(8,128)(2,1)S(1)}, u32[]{:S(2)}, u32[]{:S(2)}) collective-permute-start(bf16[20,2048]{1,0:T(8,128)(2,1)S(1)} %add_convert_fusion.2.refs_0_), channel_id=1, source_target_pairs={{0,12},{4,8},{8,4},{12,0},{1,13},{5,9},{9,5},{13,1},{2,14},{6,10},... | collective-permute-start | bytes 245768 | tf_op jit(solution)/shard_map/ppermute | solution.py:125
  72.1 5.0 %collective-permute-done.13.refs_2_ = bf16[20,2048]{1,0:T(8,128)(2,1)S(1)} collective-permute-done((bf16[20,2048]{1,0:T(8,128)(2,1)S(1)}, bf16[20,2048]{1,0:T(8,128)(2,1)S(1)}, u32[]{:S(2)}, u32[]{:S(2)}) %collective-permute-start.13) | collective-permute-done | bytes 81952 | tf_op jit(solution)/shard_map/ppermute | solution.py:125
  77.1 5.2 %copy-done = bf16[3584,2048]{1,0:T(8,128)(2,1)S(1)} copy-done((bf16[3584,2048]{1,0:T(8,128)(2,1)S(1)}, bf16[3584,2048]{1,0:T(8,128)(2,1)}, u32[]{:S(2)}) %copy-start) | copy-done | bytes 14680088
  82.2 6.9 %hidden_units.3 = (bf16[80,1792]{1,0:T(8,128)(2,1)S(1)}, f32[80,1792]{1,0:T(8,128)S(1)}, f32[80,128]{1,0:T(8,128)S(1)}) custom-call(s32[2]{0:T(128)S(1)} %pad_add_fusion.place, bf16[20,2048]{1,0:T(8,128)(2,1)S(1)} %add_convert_fusion.2.refs_0_, bf16[20,2048]{1,0:T(8,128)(2,1)S(1)} %collective-permute-done.12.refs_1_, ...), custom_call_target="tpu_custom_call" | custom-call | flops 1174405120 | bytes 14680064 | tf_op jit(solution)/shard_map/hidden_units/pallas_call | solution.py:316
  89.3 7.4 %hidden_units.2 = (bf16[80,1792]{1,0:T(8,128)(2,1)S(1)}, f32[80,1792]{1,0:T(8,128)S(1)}) custom-call(s32[2]{0:T(128)S(1)} %pad_add_fusion.place, bf16[20,2048]{1,0:T(8,128)(2,1)S(1)} %add_convert_fusion.2.refs_0_, bf16[20,2048]{1,0:T(8,128)(2,1)S(1)} %collective-permute-done.12.refs_1_, bf16[20,2048]{1,0:T(8,128)(2,1)S(1)} %collective-permute-done.13.refs_2_, ...), custom_call_target="tpu_custom_call" | custom-call | flops 1174405120 | bytes 14680064 | tf_op jit(solution)/shard_map/hidden_units/pallas_call | solution.py:316
  100.2 6.8 %collective-permute-done.19 = f32[80,128]{1,0:T(8,128)S(1)} collective-permute-done((f32[80,128]{1,0:T(8,128)S(1)}, f32[80,128]{1,0:T(8,128)S(1)}, u32[]{:S(2)}, u32[]{:S(2)}) %collective-permute-start.19) | collective-permute-done | bytes 40992 | tf_op jit(solution)/shard_map/ppermute | solution.py:125
  108.9 3.8 %collective-permute-done.20.refs_0_ = bf16[80,896]{1,0:T(8,128)(2,1)S(1)} collective-permute-done((bf16[80,896]{1,0:T(8,128)(2,1)S(1)}, bf16[80,896]{1,0:T(8,128)(2,1)S(1)}, u32[]{:S(2)}, u32[]{:S(2)}) %collective-permute-start.20) | collective-permute-done | bytes 143392 | tf_op jit(solution)/shard_map/ppermute | solution.py:125
  112.7 2.8 %down.2.refs_3_ = f32[80,2048]{1,0:T(8,128)S(1)} custom-call(s32[2]{0:T(128)S(1)} %pad_add_fusion.place, bf16[80,896]{1,0:T(8,128)(2,1)S(1)} %fusion.refs_0_, bf16[80,896]{1,0:T(8,128)(2,1)S(1)} %collective-permute-done.22.refs_1_, bf16[3584,2048]{1,0:T(8,128)(2,1)S(1)} %bitcast.9), custom_call_target="tpu_custom_call" | custom-call | flops 587202560 | bytes 7340032 | tf_op jit(solution)/shard_map/down/pallas_call | solution.py:375
  115.5 2.6 %down.3 = (bf16[20,2048]{1,0:T(8,128)(2,1)S(1)}, bf16[20,2048]{1,0:T(8,128)(2,1)S(1)}, bf16[20,2048]{1,0:T(8,128)(2,1)S(1)}, bf16[20,2048]{1,0:T(8,128)(2,1)S(1)}) custom-call(s32[2]{0:T(128)S(1)} %pad_add_fusion.place, bf16[80,896]{1,0:T(8,128)(2,1)S(1)} %collective-permute-done.20.refs_0_, bf16[80,896]{1,0:T(8,128)(2,1)S(1)} %collective-permute-done.21.refs_1_, ...), custom_call_target="tpu_custom_call" | custom-call | flops 587202560 | bytes 7340032 | tf_op jit(solution)/shard_map/down/pallas_call | solution.py:375
  122.6 3.2 %collective-permute-done.25 = bf16[20,2048]{1,0:T(8,128)(2,1)S(1)} collective-permute-done((bf16[20,2048]{1,0:T(8,128)(2,1)S(1)}, bf16[20,2048]{1,0:T(8,128)(2,1)S(1)}, u32[]{:S(2)}, u32[]{:S(2)}) %collective-permute-start.25) | collective-permute-done | bytes 81952 | tf_op jit(solution)/shard_map/ppermute | solution.py:125
  125.7 5.3 %collective-permute-done.24 = bf16[20,2048]{1,0:T(8,128)(2,1)S(1)} collective-permute-done((bf16[20,2048]{1,0:T(8,128)(2,1)S(1)}, bf16[20,2048]{1,0:T(8,128)(2,1)S(1)}, u32[]{:S(2)}, u32[]{:S(2)}) %collective-permute-start.24) | collective-permute-done | bytes 81952 | tf_op jit(solution)/shard_map/ppermute | solution.py:125
  (84 shorter events, 28.8 us)
Async XLA Ops:
  1.0 6.6 %collective-permute-start = (bf16[20,16,128]{2,1,0:T(8,128)(2,1)S(1)}, bf16[20,16,128]{2,1,0:T(8,128)(2,1)S(1)}, u32[]{:S(2)}, u32[]{:S(2)}) collective-permute-start(bf16[20,16,128]{2,1,0:T(8,128)(2,1)S(1)} %slice.18.refs_0_), channel_id=1, source_target_pairs={{0,4},{4,0},{8,12},{12,8},{1,5},{5,1},{9,13},{13,9},{2,6},{6,2},{1... | collective-permute-start | bytes 245768 | tf_op jit(solution)/shard_map/ppermute | solution.py:125
  4.1 9.2 %collective-permute-start.1 = (bf16[20,16,128]{2,1,0:T(8,128)(2,1)S(1)}, bf16[20,16,128]{2,1,0:T(8,128)(2,1)S(1)}, u32[]{:S(2)}, u32[]{:S(2)}) collective-permute-start(bf16[20,16,128]{2,1,0:T(8,128)(2,1)S(1)} %slice.18.refs_0_), channel_id=1, source_target_pairs={{0,8},{4,12},{8,0},{12,4},{1,9},{5,13},{9,1},{13,5},{2,10},{6,14},... | collective-permute-start | bytes 245768 | tf_op jit(solution)/shard_map/ppermute | solution.py:125
  6.7 6.6 %collective-permute-start.2 = (bf16[20,16,128]{2,1,0:T(8,128)(2,1)S(1)}, bf16[20,16,128]{2,1,0:T(8,128)(2,1)S(1)}, u32[]{:S(2)}, u32[]{:S(2)}) collective-permute-start(bf16[20,16,128]{2,1,0:T(8,128)(2,1)S(1)} %slice.18.refs_0_), channel_id=1, source_target_pairs={{0,12},{4,8},{8,4},{12,0},{1,13},{5,9},{9,5},{13,1},{2,14},{6,10},... | collective-permute-start | bytes 245768 | tf_op jit(solution)/shard_map/ppermute | solution.py:125
  33.6 4.5 %collective-permute-start.3 = (bf16[24,512]{1,0:T(8,128)(2,1)S(1)}, bf16[24,512]{1,0:T(8,128)(2,1)S(1)}, u32[]{:S(2)}, u32[]{:S(2)}) collective-permute-start(bf16[24,512]{1,0:T(8,128)(2,1)S(1)} %get-tuple-element.23), channel_id=1, source_target_pairs={{0,4},{4,0},{8,12},{12,8},{1,5},{5,1},{9,13},{13,9},{2,6},{6,2},{1... | collective-permute-start | bytes 73736 | tf_op jit(solution)/shard_map/ppermute | solution.py:125
  35.1 5.0 %collective-permute-start.4 = (bf16[24,512]{1,0:T(8,128)(2,1)S(1)}, bf16[24,512]{1,0:T(8,128)(2,1)S(1)}, u32[]{:S(2)}, u32[]{:S(2)}) collective-permute-start(bf16[24,512]{1,0:T(8,128)(2,1)S(1)} %get-tuple-element.24), channel_id=1, source_target_pairs={{0,8},{4,12},{8,0},{12,4},{1,9},{5,13},{9,1},{13,5},{2,10},{6,14},... | collective-permute-start | bytes 73736 | tf_op jit(solution)/shard_map/ppermute | solution.py:125
  36.7 5.6 %collective-permute-start.5 = (bf16[24,512]{1,0:T(8,128)(2,1)S(1)}, bf16[24,512]{1,0:T(8,128)(2,1)S(1)}, u32[]{:S(2)}, u32[]{:S(2)}) collective-permute-start(bf16[24,512]{1,0:T(8,128)(2,1)S(1)} %get-tuple-element.25), channel_id=1, source_target_pairs={{0,12},{4,8},{8,4},{12,0},{1,13},{5,9},{9,5},{13,1},{2,14},{6,10},... | collective-permute-start | bytes 73736 | tf_op jit(solution)/shard_map/ppermute | solution.py:125
  42.3 4.6 %collective-permute-start.7 = (bf16[96,512]{1,0:T(8,128)(2,1)S(1)}, bf16[96,512]{1,0:T(8,128)(2,1)S(1)}, u32[]{:S(2)}, u32[]{:S(2)}) collective-permute-start(bf16[96,512]{1,0:T(8,128)(2,1)S(1)} %constant_dynamic-update-slice_fusion.refs_0_), channel_id=1, source_target_pairs={{0,2},{1,3},{2,0},{3,1},{4,6},{5,7},{6,4},{7,5},{8,10},{9,11},{10,... | collective-permute-start | bytes 294920 | tf_op jit(solution)/shard_map/ppermute | solution.py:125
  44.5 2.5 %collective-permute-start.6 = (bf16[96,512]{1,0:T(8,128)(2,1)S(1)}, bf16[96,512]{1,0:T(8,128)(2,1)S(1)}, u32[]{:S(2)}, u32[]{:S(2)}) collective-permute-start(bf16[96,512]{1,0:T(8,128)(2,1)S(1)} %constant_dynamic-update-slice_fusion.refs_0_), channel_id=1, source_target_pairs={{0,1},{1,0},{2,3},{3,2},{4,5},{5,4},{6,7},{7,6},{8,9},{9,8},{10,11... | collective-permute-start | bytes 294920 | tf_op jit(solution)/shard_map/ppermute | solution.py:125
  55.1 7.6 %collective-permute-start.11 = (bf16[20,2048]{1,0:T(8,128)(2,1)S(1)}, bf16[20,2048]{1,0:T(8,128)(2,1)S(1)}, u32[]{:S(2)}, u32[]{:S(2)}) collective-permute-start(bf16[20,2048]{1,0:T(8,128)(2,1)S(1)} %get-tuple-element.29), channel_id=1, source_target_pairs={{0,12},{4,8},{8,4},{12,0},{1,13},{5,9},{9,5},{13,1},{2,14},{6,10},... | collective-permute-start | bytes 245768 | tf_op jit(solution)/shard_map/ppermute | solution.py:125
  56.5 9.5 %collective-permute-start.10 = (bf16[20,2048]{1,0:T(8,128)(2,1)S(1)}, bf16[20,2048]{1,0:T(8,128)(2,1)S(1)}, u32[]{:S(2)}, u32[]{:S(2)}) collective-permute-start(bf16[20,2048]{1,0:T(8,128)(2,1)S(1)} %get-tuple-element.28), channel_id=1, source_target_pairs={{0,8},{4,12},{8,0},{12,4},{1,9},{5,13},{9,1},{13,5},{2,10},{6,14},... | collective-permute-start | bytes 245768 | tf_op jit(solution)/shard_map/ppermute | solution.py:125
  56.5 9.5 %collective-permute-start.9 = (bf16[20,2048]{1,0:T(8,128)(2,1)S(1)}, bf16[20,2048]{1,0:T(8,128)(2,1)S(1)}, u32[]{:S(2)}, u32[]{:S(2)}) collective-permute-start(bf16[20,2048]{1,0:T(8,128)(2,1)S(1)} %get-tuple-element.27), channel_id=1, source_target_pairs={{0,4},{4,0},{8,12},{12,8},{1,5},{5,1},{9,13},{13,9},{2,6},{6,2},{1... | collective-permute-start | bytes 245768 | tf_op jit(solution)/shard_map/ppermute | solution.py:125
  66.1 6.0 %collective-permute-start.12 = (bf16[20,2048]{1,0:T(8,128)(2,1)S(1)}, bf16[20,2048]{1,0:T(8,128)(2,1)S(1)}, u32[]{:S(2)}, u32[]{:S(2)}) collective-permute-start(bf16[20,2048]{1,0:T(8,128)(2,1)S(1)} %add_convert_fusion.2.refs_0_), channel_id=1, source_target_pairs={{0,4},{4,0},{8,12},{12,8},{1,5},{5,1},{9,13},{13,9},{2,6},{6,2},{1... | collective-permute-start | bytes 245768 | tf_op jit(solution)/shard_map/ppermute | solution.py:125
  66.2 10.9 %collective-permute-start.13 = (bf16[20,2048]{1,0:T(8,128)(2,1)S(1)}, bf16[20,2048]{1,0:T(8,128)(2,1)S(1)}, u32[]{:S(2)}, u32[]{:S(2)}) collective-permute-start(bf16[20,2048]{1,0:T(8,128)(2,1)S(1)} %add_convert_fusion.2.refs_0_), channel_id=1, source_target_pairs={{0,8},{4,12},{8,0},{12,4},{1,9},{5,13},{9,1},{13,5},{2,10},{6,14},... | collective-permute-start | bytes 245768 | tf_op jit(solution)/shard_map/ppermute | solution.py:125
  68.1 9.0 %collective-permute-start.14 = (bf16[20,2048]{1,0:T(8,128)(2,1)S(1)}, bf16[20,2048]{1,0:T(8,128)(2,1)S(1)}, u32[]{:S(2)}, u32[]{:S(2)}) collective-permute-start(bf16[20,2048]{1,0:T(8,128)(2,1)S(1)} %add_convert_fusion.2.refs_0_), channel_id=1, source_target_pairs={{0,12},{4,8},{8,4},{12,0},{1,13},{5,9},{9,5},{13,1},{2,14},{6,10},... | collective-permute-start | bytes 245768 | tf_op jit(solution)/shard_map/ppermute | solution.py:125
  89.2 7.6 %collective-permute-start.16 = (bf16[80,1792]{1,0:T(8,128)(2,1)S(1)}, bf16[80,1792]{1,0:T(8,128)(2,1)S(1)}, u32[]{:S(2)}, u32[]{:S(2)}) collective-permute-start(bf16[80,1792]{1,0:T(8,128)(2,1)S(1)} %get-tuple-element.32), channel_id=1, source_target_pairs={{0,1},{1,0},{2,3},{3,2},{4,5},{5,4},{6,7},{7,6},{8,9},{9,8},{10,11... | collective-permute-start | bytes 860168 | tf_op jit(solution)/shard_map/ppermute | solution.py:125
  96.7 10.4 %collective-permute-start.15 = (bf16[80,1792]{1,0:T(8,128)(2,1)S(1)}, bf16[80,1792]{1,0:T(8,128)(2,1)S(1)}, u32[]{:S(2)}, u32[]{:S(2)}) collective-permute-start(bf16[80,1792]{1,0:T(8,128)(2,1)S(1)} %get-tuple-element.31), channel_id=1, source_target_pairs={{0,1},{1,0},{2,3},{3,2},{4,5},{5,4},{6,7},{7,6},{8,9},{9,8},{10,11... | collective-permute-start | bytes 860168 | tf_op jit(solution)/shard_map/ppermute | solution.py:125
  96.8 10.3 %collective-permute-start.17 = (bf16[80,1792]{1,0:T(8,128)(2,1)S(1)}, bf16[80,1792]{1,0:T(8,128)(2,1)S(1)}, u32[]{:S(2)}, u32[]{:S(2)}) collective-permute-start(bf16[80,1792]{1,0:T(8,128)(2,1)S(1)} %add_convert_fusion), channel_id=1, source_target_pairs={{0,2},{1,3},{2,0},{3,1},{4,6},{5,7},{6,4},{7,5},{8,10},{9,11},{10,... | collective-permute-start | bytes 860168 | tf_op jit(solution)/shard_map/ppermute | solution.py:125
  99.6 7.3 %collective-permute-start.19 = (f32[80,128]{1,0:T(8,128)S(1)}, f32[80,128]{1,0:T(8,128)S(1)}, u32[]{:S(2)}, u32[]{:S(2)}) collective-permute-start(f32[80,128]{1,0:T(8,128)S(1)} %add.93), channel_id=1, source_target_pairs={{0,2},{1,3},{2,0},{3,1},{4,6},{5,7},{6,4},{7,5},{8,10},{9,11},{10,... | collective-permute-start | bytes 122888 | tf_op jit(solution)/shard_map/ppermute | solution.py:125
  107.3 5.3 %collective-permute-start.20 = (bf16[80,896]{1,0:T(8,128)(2,1)S(1)}, bf16[80,896]{1,0:T(8,128)(2,1)S(1)}, u32[]{:S(2)}, u32[]{:S(2)}) collective-permute-start(bf16[80,896]{1,0:T(8,128)(2,1)S(1)} %fusion.refs_0_), channel_id=1, source_target_pairs={{0,2},{1,3},{2,0},{3,1},{4,6},{5,7},{6,4},{7,5},{8,10},{9,11},{10,... | collective-permute-start | bytes 430088 | tf_op jit(solution)/shard_map/ppermute | solution.py:125
  108.9 3.8 %collective-permute-start.22 = (bf16[80,896]{1,0:T(8,128)(2,1)S(1)}, bf16[80,896]{1,0:T(8,128)(2,1)S(1)}, u32[]{:S(2)}, u32[]{:S(2)}) collective-permute-start(bf16[80,896]{1,0:T(8,128)(2,1)S(1)} %fusion.refs_0_), channel_id=1, source_target_pairs={{0,1},{1,0},{2,3},{3,2},{4,5},{5,4},{6,7},{7,6},{8,9},{9,8},{10,11... | collective-permute-start | bytes 430088 | tf_op jit(solution)/shard_map/ppermute | solution.py:125
  112.7 2.8 %collective-permute-start.21 = (bf16[80,896]{1,0:T(8,128)(2,1)S(1)}, bf16[80,896]{1,0:T(8,128)(2,1)S(1)}, u32[]{:S(2)}, u32[]{:S(2)}) collective-permute-start(bf16[80,896]{1,0:T(8,128)(2,1)S(1)} %collective-permute-done.20.refs_0_), channel_id=1, source_target_pairs={{0,1},{1,0},{2,3},{3,2},{4,5},{5,4},{6,7},{7,6},{8,9},{9,8},{10,11... | collective-permute-start | bytes 430088 | tf_op jit(solution)/shard_map/ppermute | solution.py:125
  118.1 7.6 %collective-permute-start.25 = (bf16[20,2048]{1,0:T(8,128)(2,1)S(1)}, bf16[20,2048]{1,0:T(8,128)(2,1)S(1)}, u32[]{:S(2)}, u32[]{:S(2)}) collective-permute-start(bf16[20,2048]{1,0:T(8,128)(2,1)S(1)} %get-tuple-element.38), channel_id=1, source_target_pairs={{0,12},{4,8},{8,4},{12,0},{1,13},{5,9},{9,5},{13,1},{2,14},{6,10},... | collective-permute-start | bytes 245768 | tf_op jit(solution)/shard_map/ppermute | solution.py:125
  119.9 11.1 %collective-permute-start.24 = (bf16[20,2048]{1,0:T(8,128)(2,1)S(1)}, bf16[20,2048]{1,0:T(8,128)(2,1)S(1)}, u32[]{:S(2)}, u32[]{:S(2)}) collective-permute-start(bf16[20,2048]{1,0:T(8,128)(2,1)S(1)} %get-tuple-element.37), channel_id=1, source_target_pairs={{0,8},{4,12},{8,0},{12,4},{1,9},{5,13},{9,1},{13,5},{2,10},{6,14},... | collective-permute-start | bytes 245768 | tf_op jit(solution)/shard_map/ppermute | solution.py:125
  121.5 9.5 %collective-permute-start.23 = (bf16[20,2048]{1,0:T(8,128)(2,1)S(1)}, bf16[20,2048]{1,0:T(8,128)(2,1)S(1)}, u32[]{:S(2)}, u32[]{:S(2)}) collective-permute-start(bf16[20,2048]{1,0:T(8,128)(2,1)S(1)} %get-tuple-element.36), channel_id=1, source_target_pairs={{0,4},{4,0},{8,12},{12,8},{1,5},{5,1},{9,13},{13,9},{2,6},{6,2},{1... | collective-permute-start | bytes 245768 | tf_op jit(solution)/shard_map/ppermute | solution.py:125
  (14 other events, 248.7 us)

commit v2 on v0

--- a/solution.py
+++ b/solution.py
@@ -1,12 +1,25 @@
+import functools
 import math
 
 import jax
 import jax.numpy as jnp
 from jax import lax
+from jax.experimental import pallas as pl
+from jax.experimental.pallas import tpu as pltpu
 from jax.sharding import PartitionSpec as P
 
 epsilon = 1e-05
 masked_score = -1e30
+lanes = 128
+block_rows = 256
+slot_group = 2
+contract_minor = (((1,), (1,)), ((), ()))
+F32 = jnp.float32
+BF16 = jnp.bfloat16
+I32 = jnp.int32
+vmem = pl.BlockSpec(memory_space=pltpu.VMEM)
+smem = pl.BlockSpec(memory_space=pltpu.SMEM)
+hbm = pl.BlockSpec(memory_space=pltpu.HBM)
 
 
 def softmax_rounded(scores):
@@ -16,7 +29,7 @@
     return (shifted / totals).astype(jnp.bfloat16)
 
 
-def per_device(
+def general_device(
     hidden_state,
     queries,
     key_cache,
@@ -108,7 +121,563 @@
     return (middle + returned).astype(jnp.bfloat16)
 
 
+def pair_swap(value, axis, bit):
+    count = lax.axis_size(axis)
+    return lax.ppermute(value, axis, [(i, i ^ bit) for i in range(count)])
+
+
+def up_to(value, multiple):
+    return -(-value // multiple) * multiple
+
+
+def params(megabytes):
+    return pltpu.CompilerParams(vmem_limit_bytes=megabytes << 20)
+
+
+def halves_joined(block):
+    block = block.astype(F32)
+    rows = block.shape[0] // 2
+    return jnp.concatenate([block[:rows], block[rows:]], axis=1)
+
+
+def halves_stacked(block):
+    half = block.shape[1] // 2
+    return jnp.concatenate([block[:, :half], block[:, half:]], axis=0)
+
+
+def high_low(value):
+    high = value.astype(BF16).astype(F32)
+    low = value - high
+    lane = lax.broadcasted_iota(I32, (value.shape[0], lanes), 1)
+    return jnp.where(lane < lanes // 2, high, low)
+
+
+def in_hbm(value):
+    return pltpu.with_memory_space_constraint(value, pltpu.HBM)
+
+
+def in_vmem(value):
+    return pltpu.with_memory_space_constraint(value, pltpu.VMEM)
+
+
+def fetch_kernel(*refs):
+    count = len(refs) // 2
+    sems = refs[-1]
+    copies = [
+        pltpu.make_async_copy(refs[i], refs[count + i], sems.at[i]) for i in range(count)
+    ]
+    for copy in copies:
+        copy.start()
+    for copy in copies:
+        copy.wait()
+
+
+def fetch(arrays):
+    moved = sum(a.size * 2 for a in arrays)
+    return pl.pallas_call(
+        fetch_kernel,
+        in_specs=[hbm] * len(arrays),
+        out_specs=[vmem] * len(arrays),
+        out_shape=[pltpu.VMEM(a.shape, a.dtype) for a in arrays],
+        scratch_shapes=[pltpu.SemaphoreType.DMA((len(arrays),))],
+        compiler_params=params(1),
+        cost_estimate=pl.CostEstimate(flops=0, bytes_accessed=2 * moved, transcendentals=0),
+        name="fetch",
+    )(*[in_hbm(a) for a in arrays])
+
+
+def folded(combine, value):
+    parts = [value[:, i : i + lanes] for i in range(0, value.shape[1], lanes)]
+    return functools.reduce(combine, parts)
+
+
+def attention_kernel(table, *refs, slots, count, scale, unroll):
+    query_blocks, (keys, values, ahead) = refs[:count], refs[count : count + 3]
+    outs, landed = refs[count + 3 : 2 * count + 3], refs[2 * count + 3]
+    queries, both, begins, ends, tops, sums, scores, total, attended, items, sem = refs[
+        2 * count + 4 :
+    ]
+    copy = pltpu.make_async_copy(ahead, landed, sem)
+    copy.start()
+    pool, width = keys.shape
+    heads = queries.shape[1]
+    half = heads // 2
+    own = table[0]
+    group_rows = slot_group * heads
+    top_half = lax.broadcasted_iota(I32, (heads, lanes), 0) < half
+    for k in range(count):
+        queries[k * slots : (k + 1) * slots] = query_blocks[k][...]
+
+    tops[...] = jnp.full(tops.shape, masked_score, F32)
+    sums[...] = jnp.zeros(sums.shape, F32)
+    total[...] = jnp.zeros(total.shape, F32)
+    spare = slots * heads
+    both[spare:, :] = jnp.zeros((both.shape[0] - spare, width), BF16)
+    begins[spare:, :] = jnp.full((begins.shape[0] - spare, lanes), pool, I32)
+    ends[spare:, :] = jnp.zeros((ends.shape[0] - spare, lanes), I32)
+
+    def slot(s, carry):
+        start, made, last_block, last_slot = carry
+        end = start + table[2 + s]
+        request = table[2 + slots + own * slots + s]
+        owner = sum((request >= k * slots).astype(I32) for k in range(1, count))
+        query = queries[(owner ^ own) * slots + request - owner * slots]
+        zero = jnp.zeros_like(query)
+        at = pl.ds(pl.multiple_of(s * heads, heads), heads)
+        both[at, :lanes] = jnp.where(top_half, query, zero)
+        both[at, lanes:] = jnp.where(top_half, zero, query)
+        begins[at, :] = jnp.full((heads, lanes), start, I32)
+        ends[at, :] = jnp.full((heads, lanes), end, I32)
+        first = start // block_rows
+        covered = (first == last_block) & (s < last_slot + slot_group)
+        first = jnp.where(covered, first + 1, first)
+        last = (end - 1) // block_rows
+
+        def item(block, made):
+            items[2 * made] = block
+            items[2 * made + 1] = s
+            return made + 1
+
+        made_now = lax.fori_loop(first, last + 1, item, made)
+        new = made_now > made
+        return (
+            end,
+            made_now,
+            jnp.where(new, last, last_block),
+            jnp.where(new, s, last_slot),
+        )
+
+    none = jnp.int32(-1)
+    _, made, _, _ = lax.fori_loop(0, slots, slot, (jnp.int32(0), jnp.int32(0), none, none))
+    for u in range(unroll):
+        items[2 * (made + u)] = 0
+        items[2 * (made + u) + 1] = slots
+    steps = (made + unroll - 1) // unroll
+    across = lax.broadcasted_iota(I32, (group_rows, block_rows), 1)
+
+    def place_of(i):
+        block = pl.multiple_of(items[2 * i] * block_rows, block_rows)
+        rows = pl.multiple_of(items[2 * i + 1] * heads, heads)
+        return block, pl.ds(block, block_rows), pl.ds(rows, group_rows)
+
+    def score_step(step, carry):
+        for u in range(unroll):
+            i = step * unroll + u
+            block, cache, rows = place_of(i)
+            raw = lax.dot_general(
+                both[rows, :], keys[cache, :], contract_minor, preferred_element_type=F32
+            )
+            position = block + across
+            begin, end = (jnp.concatenate([b[rows, :]] * (block_rows // lanes), axis=1) for b in (begins, ends))
+            inside = (position >= begin) & (position < end)
+            masked = jnp.where(inside, raw * scale, masked_score)
+            scores[i] = masked
+            tops[rows, :] = jnp.maximum(tops[rows, :], folded(jnp.maximum, masked))
+        return carry
+
+    def value_step(step, carry):
+        for u in range(unroll):
+            i = step * unroll + u
+            _, cache, rows = place_of(i)
+            top = tops[rows, :]
+            shifted = jnp.exp(scores[i] - jnp.concatenate([top] * (block_rows // lanes), axis=1))
+            sums[rows, :] += folded(jnp.add, shifted)
+            total[rows, :] += jnp.dot(
+                shifted.astype(BF16), values[cache, :], preferred_element_type=F32
+            )
+        return carry
+
+    lax.fori_loop(0, steps, score_step, 0)
+    top = jnp.max(tops[...], axis=1, keepdims=True)
+    tops[...] = jnp.broadcast_to(top, tops.shape)
+    lax.fori_loop(0, steps, value_step, 0)
+
+    real = slots * heads
+    row = lax.broadcasted_iota(I32, (real, lanes), 0)
+    upper = row % heads < half
+    picked = jnp.where(upper, total[:real, :lanes], total[:real, lanes:])
+    attended[...] = picked / jnp.sum(sums[:real, :], axis=1, keepdims=True)
+    per_block = half // count
+    for k in range(count):
+        outs[k][...] = jnp.zeros(outs[k].shape, BF16)
+        for kv in range(2):
+            for j in range(per_block):
+                head = kv * half + (own ^ k) * per_block + j
+                at = (kv * per_block + j) * lanes
+                outs[k][:slots, at : at + lanes] = attended[
+                    pl.ds(head, slots, stride=heads), :
+                ].astype(BF16)
+    copy.wait()
+
+
+def attention(table, query_blocks, keys, values, ahead, unroll=8):
+    count = len(query_blocks)
+    slots, heads, _ = query_blocks[0].shape
+    pool, width = keys.shape
+    most = pool // block_rows + slots + unroll
+    rows = (slots + slot_group) * heads
+    return pl.pallas_call(
+        functools.partial(
+            attention_kernel, slots=slots, count=count, scale=1.0 / math.sqrt(lanes), unroll=unroll
+        ),
+        in_specs=[smem] + [vmem] * (count + 2) + [hbm],
+        out_specs=[vmem] * (count + 1),
+        out_shape=[jax.ShapeDtypeStruct((up_to(slots, 8), heads // count * lanes), BF16)] * count
+        + [pltpu.VMEM(ahead.shape, ahead.dtype)],
+        scratch_shapes=[
+            pltpu.VMEM((count * slots, heads, lanes), BF16),
+            pltpu.VMEM((rows, width), BF16),
+            pltpu.VMEM((rows, lanes), I32),
+            pltpu.VMEM((rows, lanes), I32),
+            pltpu.VMEM((rows, lanes), F32),
+            pltpu.VMEM((rows, lanes), F32),
+            pltpu.VMEM((most, slot_group * heads, block_rows), F32),
+            pltpu.VMEM((rows, width), F32),
+            pltpu.VMEM((slots * heads, lanes), F32),
+            pltpu.SMEM((2 * most,), I32),
+            pltpu.SemaphoreType.DMA,
+        ],
+        compiler_params=params(12),
+        cost_estimate=pl.CostEstimate(
+            flops=4 * pool * heads * lanes, bytes_accessed=pool * width * 4, transcendentals=0
+        ),
+        name="attention",
+    )(table, *query_blocks, in_vmem(keys), in_vmem(values), in_hbm(ahead))
+
+
+def projection_kernel(table, *refs, slots, count, parts):
+    pieces, weight, outs = refs[:parts], refs[parts], refs[parts + 1 :]
+    own_att, own_ffn = table[0], table[1]
+    requests = slots * count
+    padded = pieces[0].shape[0] // count
+    depth = weight.shape[0] // parts
+    row = lax.broadcasted_iota(I32, (requests, padded), 0)
+    wanted = row
+    for k in range(count):
+        moved = row + ((own_att ^ k) - k) * slots
+        wanted = jnp.where((row >= k * slots) & (row < (k + 1) * slots), moved, wanted)
+    choose = []
+    lane = lax.broadcasted_iota(I32, (1, padded), 1)
+    for k in range(count):
+        served = jnp.full((1, padded), -1, I32)
+        for i in range(slots):
+            request = table[2 + slots + (own_att ^ k) * slots + i]
+            served = jnp.where(lane == i, request, served)
+        choose.append((wanted == served).astype(F32).astype(BF16))
+    total = None
+    for p in range(parts):
+        rows = None
+        for k in range(count):
+            term = jnp.dot(
+                choose[k],
+                pieces[p][k * padded : (k + 1) * padded, :],
+                preferred_element_type=F32,
+            )
+            rows = term if rows is None else rows + term
+        at = pl.ds(pl.multiple_of((own_ffn ^ p) * depth, depth), depth)
+        term = jnp.dot(rows.astype(BF16), weight[at, :], preferred_element_type=F32)
+        total = term if total is None else total + term
+    for k in range(count):
+        outs[k][...] = halves_stacked(total[k * slots : (k + 1) * slots]).astype(BF16)
+
+
+def projection(table, pieces, weight, slots, count):
+    parts = len(pieces)
+    depth, width = weight.shape
+    return pl.pallas_call(
+        functools.partial(projection_kernel, slots=slots, count=count, parts=parts),
+        in_specs=[smem] + [vmem] * (1 + parts),
+        out_specs=[vmem] * count,
+        out_shape=[jax.ShapeDtypeStruct((2 * slots, width // 2), BF16)] * count,
+        compiler_params=params(8),
+        cost_estimate=pl.CostEstimate(
+            flops=2 * slots * count * depth * width, bytes_accessed=depth * width, transcendentals=0
+        ),
+        name="projection",
+    )(table, *pieces, in_vmem(weight))
+
+
+def residual_kernel(*refs, joined):
+    base, blocks, out = refs[0], refs[1:-1], refs[-1]
+    total = base[...].astype(F32)
+    if not joined:
+        total = halves_stacked(total)
+    for block in blocks:
+        total = total + block[...].astype(F32)
+    out[...] = (halves_joined(total) if joined else total).astype(BF16)
+
+
+def residual(base, blocks, joined):
+    rows, half = blocks[0].shape
+    shape = (rows // 2, 2 * half) if joined else (rows, half)
+    return pl.pallas_call(
+        functools.partial(residual_kernel, joined=joined),
+        in_specs=[vmem] * (1 + len(blocks)),
+        out_specs=vmem,
+        out_shape=jax.ShapeDtypeStruct(shape, BF16),
+        compiler_params=params(2),
+        name="residual",
+    )(base, *blocks)
+
+
+def hidden_kernel(table, *refs, count, masks, ahead_masks, far):
+    own = table[1]
+    sem = refs[-1]
+    if far:
+        blocks, (gain, gate, up, ahead, send, keep, scaled, landed, joined, _) = (
+            refs[:count],
+            refs[count:],
+        )
+    else:
+        scaled, gate, up, ahead, send, keep, landed, _ = refs
+    width = keep.shape[1]
+    units = (width - lanes if far else width) // 2
+    copies = [
+        pltpu.make_async_copy(
+            ahead.at[pl.ds(pl.multiple_of((own ^ mask) * units, units), units)],
+            landed.at[m],
+            sem.at[m],
+        )
+        for m, mask in enumerate(ahead_masks)
+    ]
+    for copy in copies:
+        copy.start()
+    if far:
+        rows = blocks[0].shape[0] // 2
+        for k in range(count):
+            joined[k * rows : (k + 1) * rows, :] = halves_joined(blocks[k][...])
+        middle = joined[...]
+        squares = jnp.sum(middle * middle, axis=1, keepdims=True)
+        scaled[...] = (middle * gain[...].astype(F32)).astype(BF16)
+    for m, target in enumerate((send, keep)):
+        at = pl.ds(pl.multiple_of((own ^ masks[m]) * units, units), units)
+        for t, weight in enumerate((gate, up)):
+            out = lax.dot_general(
+                scaled[...], weight[at, :], contract_minor, preferred_element_type=F32
+            )
+            target[:, t * units : (t + 1) * units] = out.astype(target.dtype)
+    if far:
+        send[:, 2 * units :] = high_low(squares).astype(BF16)
+        keep[:, 2 * units :] = jnp.broadcast_to(squares, (squares.shape[0], lanes))
+    for copy in copies:
+        copy.wait()
+
+
+def hidden_cost(requests, units, width):
+    return pl.CostEstimate(
+        flops=8 * requests * units * width, bytes_accessed=4 * units * width, transcendentals=0
+    )
+
+
+def hidden_far(table, blocks, gain, gate, up, ahead, owners):
+    count = len(blocks)
+    rows, half = blocks[0].shape
+    requests, width = rows // 2 * count, 2 * half
+    units = gate.shape[0] // owners
+    across = 2 * units + lanes
+    return pl.pallas_call(
+        functools.partial(
+            hidden_kernel, count=count, masks=(3, 2), ahead_masks=(0, 1), far=True
+        ),
+        in_specs=[smem] + [vmem] * (count + 3) + [hbm],
+        out_specs=[vmem] * 4,
+        out_shape=[
+            jax.ShapeDtypeStruct((requests, across), BF16),
+            jax.ShapeDtypeStruct((requests, across), F32),
+            jax.ShapeDtypeStruct((requests, width), BF16),
+            pltpu.VMEM((2, units, ahead.shape[1]), BF16),
+        ],
+        scratch_shapes=[pltpu.VMEM((requests, width), F32), pltpu.SemaphoreType.DMA((2,))],
+        compiler_params=params(8),
+        cost_estimate=hidden_cost(requests, units, width),
+        name="hidden_far",
+    )(table, *blocks, gain, in_vmem(gate), in_vmem(up), in_hbm(ahead))
+
+
+def hidden_near(table, scaled, gate, up, ahead, owners):
+    requests, width = scaled.shape
+    units = gate.shape[0] // owners
+    return pl.pallas_call(
+        functools.partial(
+            hidden_kernel, count=0, masks=(1, 0), ahead_masks=(2, 3), far=False
+        ),
+        in_specs=[smem] + [vmem] * 3 + [hbm],
+        out_specs=[vmem] * 3,
+        out_shape=[
+            jax.ShapeDtypeStruct((requests, 2 * units), BF16),
+            jax.ShapeDtypeStruct((requests, 2 * units), F32),
+            pltpu.VMEM((2, units, ahead.shape[1]), BF16),
+        ],
+        scratch_shapes=[pltpu.SemaphoreType.DMA((2,))],
+        compiler_params=params(8),
+        cost_estimate=hidden_cost(requests, units, width),
+        name="hidden_near",
+    )(table, scaled, in_vmem(gate), in_vmem(up), in_hbm(ahead))
+
+
+def chip_sum_kernel(keep, arrived, out, squares):
+    width = keep.shape[1] - lanes
+    out[:, :width] = (keep[:, :width] + arrived[:, :width].astype(F32)).astype(BF16)
+    tail = arrived[:, width:].astype(F32)
+    chip = keep[:, width:] + (tail[:, :1] + tail[:, lanes // 2 : lanes // 2 + 1])
+    squares[...] = chip
+    out[:, width:] = high_low(chip).astype(BF16)
+
+
+def chip_sum(keep, arrived):
+    requests, width = keep.shape
+    return pl.pallas_call(
+        chip_sum_kernel,
+        in_specs=[vmem] * 2,
+        out_specs=[vmem] * 2,
+        out_shape=[
+            jax.ShapeDtypeStruct((requests, width), BF16),
+            jax.ShapeDtypeStruct((requests, lanes), F32),
+        ],
+        compiler_params=params(2),
+        name="chip_sum",
+    )(keep, arrived)
+
+
+def active_kernel(near, beside, far, squares, out, *, model_width):
+    units = near.shape[1] // 2
+    tail = far[:, 2 * units :].astype(F32)
+    square = squares[:, :1] + (tail[:, :1] + tail[:, lanes // 2 : lanes // 2 + 1])
+    scale = lax.rsqrt(square / model_width + epsilon)
+
+    def total(at):
+        both = near[:, at : at + units] + beside[:, at : at + units].astype(F32)
+        return (both + far[:, at : at + units].astype(F32)) * scale
+
+    gate = total(0)
+    out[...] = (gate / (1.0 + jnp.exp(-gate)) * total(units)).astype(BF16)
+
+
+def active_units(near, beside, far, squares, model_width):
+    requests, width = near.shape
+    return pl.pallas_call(
+        functools.partial(active_kernel, model_width=model_width),
+        in_specs=[vmem] * 4,
+        out_specs=vmem,
+        out_shape=jax.ShapeDtypeStruct((requests, width // 2), BF16),
+        compiler_params=params(4),
+        name="active",
+    )(near, beside, far, squares)
+
+
+def down_kernel(*refs, count, first, last):
+    pieces, weight, rest = refs[:2], refs[2], refs[3:]
+    total = None if first else rest[0][...]
+    outs = rest if first else rest[1:]
+    for m, piece in enumerate(pieces):
+        term = jnp.dot(piece[...], weight[m], preferred_element_type=F32)
+        total = term if total is None else total + term
+    if last:
+        rows = total.shape[0] // count
+        for k in range(count):
+            outs[k][...] = halves_stacked(total[k * rows : (k + 1) * rows]).astype(BF16)
+    else:
+        outs[0][...] = total
+
+
+def down_part(pieces, weight, count, before=None, last=False):
+    first = before is None
+    requests, units = pieces[0].shape
+    width = weight.shape[2]
+    if last:
+        outs = [jax.ShapeDtypeStruct((2 * requests // count, width // 2), BF16)] * count
+    else:
+        outs = [jax.ShapeDtypeStruct((requests, width), F32)]
+    return pl.pallas_call(
+        functools.partial(down_kernel, count=count, first=first, last=last),
+        in_specs=[vmem] * (3 if first else 4),
+        out_specs=[vmem] * len(outs),
+        out_shape=outs,
+        compiler_params=params(8),
+        cost_estimate=pl.CostEstimate(
+            flops=4 * requests * units * width,
+            bytes_accessed=2 * units * width,
+            transcendentals=0,
+        ),
+        name="down",
+    )(*pieces, in_vmem(weight), *([] if first else [before]))
+
+
+def swaps_of(blocks):
+    count = len(blocks)
+    arrived = {k: pair_swap(blocks[k], "att", k) for k in reversed(range(1, count))}
+    return [blocks[0]] + [arrived[k] for k in range(1, count)]
+
+
+def exchanging_device(*args):
+    return exchanging_layer(*args)
+
+
+def exchanging_layer(
+    hidden_state,
+    queries,
+    key_cache,
+    value_cache,
+    lengths,
+    assignment,
+    out_weight,
+    norm_gain,
+    gate_weight,
+    up_weight,
+    down_weight,
+):
+    slots, columns = hidden_state.shape
+    count = lax.axis_size("att")
+    parts = lax.axis_size("ffn")
+    model_width = columns * parts
+    heads = queries.shape[1] // lanes
+    own = jnp.stack([lax.axis_index("att"), lax.axis_index("ffn")]).astype(I32)
+    table = jnp.concatenate([own, lengths, assignment])
+    own_queries = queries.reshape(slots, heads, lanes)
+    query_blocks = swaps_of([own_queries] * count)
+    keys, values = fetch([key_cache, value_cache])
+    *blocks, weight = attention(
+        table, query_blocks, keys, values, out_weight.reshape(-1, columns)
+    )
+
+    blocks = swaps_of(blocks)
+    piece = jnp.concatenate(blocks, axis=0)
+    across = pair_swap(piece, "ffn", 2)
+    beside = pair_swap(piece, "ffn", 1)
+    corner = pair_swap(across, "ffn", 1)
+    partial = projection(table, [piece, beside, across, corner], weight, slots, count)
+    (gate,) = fetch([gate_weight])
+    middle = residual(hidden_state, swaps_of(partial), False)
+
+    rows = swaps_of([middle] * count)
+    (up,) = fetch([up_weight])
+    gain = norm_gain.reshape(1, columns)
+    far_send, far_keep, scaled, down_chip = hidden_far(
+        table, rows, gain, gate, up, down_weight, parts
+    )
+    far, squares = chip_sum(far_keep, pair_swap(far_send, "ffn", 1))
+    far = pair_swap(far, "ffn", 2)
+    near_send, near_keep, down_other = hidden_near(
+        table, scaled, gate, up, down_weight, parts
+    )
+    near_beside = pair_swap(near_send, "ffn", 1)
+    active = active_units(near_keep, near_beside, far, squares, model_width)
+
+    across = pair_swap(active, "ffn", 2)
+    beside = pair_swap(active, "ffn", 1)
+    (before,) = down_part([active, beside], down_chip, count)
+    corner = pair_swap(across, "ffn", 1)
+    partial = down_part([across, corner], down_other, count, before, True)
+    return residual_joined(middle, swaps_of(partial))
+
+
+def residual_joined(middle, blocks):
+    return residual(middle, blocks, True)
+
+
 def solution(mesh):
+    count, parts = mesh.shape["att"], mesh.shape["ffn"]
+    paired = count == 4 and parts == 4
     in_specs = (
         P(("group", "att"), "ffn"),
         P(("group", "att"), "ffn"),
@@ -124,5 +693,9 @@
     )
     out_specs = P(("group", "att"), "ffn")
     return jax.shard_map(
-        per_device, mesh=mesh, in_specs=in_specs, out_specs=out_specs, check_vma=False
-    )
+        exchanging_device if paired else general_device,
+        mesh=mesh,
+        in_specs=in_specs,
+        out_specs=out_specs,
+        check_vma=False,
+    )

time: 249 us -> 102 us (0.41)
  blocking collectives: 75.3 us -> 0 us
  matrix products: 54.8 us -> 0 us
  Pallas kernels: 0 us -> 43.2 us
  local copies, waits for them, and re-layouts: 34.4 us -> 0.98 us
  starting transfers between devices: 9.59 us -> 26.7 us
  waiting for transfers between devices: 45.6 us -> 31.1 us
  between operations: 14.3 us -> 0.23 us
  other arithmetic: 13.6 us -> 0.08 us
    dot_general x6 -> x0, matrix products: 54.8 us -> none  [the longest x1 12.1 us: per_device(): jnp.einsum('rkgc,pkc->rkgp', slot_queries, keys_local, preferred_element_...]
    pallas_call x0 -> x13, Pallas kernels: none -> 43.2 us  [the longest x3 15.1 us: fetch(): pl.pallas_call(fetch_kernel, in_specs=[hbm] * len(arrays), out_specs=[vme...]
    psum x1 -> x0, waiting for transfers between devices: 38.2 us -> none  [per_device(): lax.psum(jnp.concatenate([gate_part, up_part], axis=1).astype(jnp.bfloat1...]
    all_gather x3 -> x0, blocking collectives: 36.9 us -> none  [the longest x1 16.5 us: per_device(): every_query = lax.all_gather(queries, 'att', axis=0, tiled=True)]
    unnamed x2 -> x0, blocking collectives: 32.7 us -> none
    ppermute x0 -> x24, waiting for transfers between devices: none -> 31.1 us  [pair_swap(): return lax.ppermute(value, axis, [(i, i ^ bit) for i in range(count)])]
    reshape x3 -> x2, local copies, waits for them, and re-layouts: 26.8 us -> 0.01 us  [the longest x1 0.01 us: exchanging_layer(): own_queries = queries.reshape(slots, heads, lanes)]
    ppermute x0 -> x24, starting transfers between devices: none -> 26.7 us  [pair_swap(): return lax.ppermute(value, axis, [(i, i ^ bit) for i in range(count)])]
  transfers between devices with their start and end apart: 4 -> 24, of which waited for: 4 -> 12; matrix products, arithmetic and copies ran while one was open for 1% -> 0% of each run, Pallas kernels for 0% -> 24%
where the time goes in v2:
time: 102 us
  Pallas kernels  43.2 us (42%)
  waiting for transfers between devices  31.1 us (30%)
  starting transfers between devices  26.7 us (26%)
    ppermute x24, waiting for transfers between devices, pair_swap(): return lax.ppermute(value, axis, [(i, i ^ bit) for i in range(count)])  31.1 us
    ppermute x24, starting transfers between devices, pair_swap(): return lax.ppermute(value, axis, [(i, i ^ bit) for i in range(count)])  26.7 us
    pallas_call x3, Pallas kernels, fetch(): pl.pallas_call(fetch_kernel, in_specs=[hbm] * len(arrays), out_specs=[vme...  15.1 us
    pallas_call x1, Pallas kernels, hidden_near(): pl.pallas_call(functools.partial(hidden_kernel, count=0, masks=(1, 0), ah...  8.11 us
    pallas_call x1, Pallas kernels, hidden_far(): pl.pallas_call(functools.partial(hidden_kernel, count=count, masks=(3, 2)...  7.52 us
    pallas_call x1, Pallas kernels, attention(): pl.pallas_call(functools.partial(attention_kernel, slots=slots, count=cou...  5.48 us
    pallas_call x2, Pallas kernels, down_part(): pl.pallas_call(functools.partial(down_kernel, count=count, first=first, l...  2.94 us
    pallas_call x1, Pallas kernels, projection(): pl.pallas_call(functools.partial(projection_kernel, slots=slots, count=co...  2.73 us
  transfers between devices with their start and end apart: 24, of which 12 were waited for; matrix products, arithmetic and copies ran while one was open for 0% of the time, Pallas kernels for 24%

profile of v2, /device:TPU:0, one launch (start us, length us, event | category | flops | bytes accessed | tf_op | source)
XLA Modules:
  0.0 102.2 jit_solution(2882392697865228401)
XLA Ops:
  1.0 3.1 %collective-permute-start = (bf16[20,16,128]{2,1,0:T(8,128)(2,1)S(1)}, bf16[20,16,128]{2,1,0:T(8,128)(2,1)S(1)}, u32[]{:S(2)}, u32[]{:S(2)}) collective-permute-start(bf16[20,16,128]{2,1,0:T(8,128)(2,1)S(1)} %slice.refs_0_), channel_id=1, source_target_pairs={{0,4},{4,0},{8,12},{12,8},{1,5},{5,1},{9,13},{13,9},{2,6},{6,2},{1... | collective-permute-start | bytes 245768 | tf_op jit(solution)/shard_map/ppermute | solution.py:126
  4.1 2.6 %collective-permute-start.1 = (bf16[20,16,128]{2,1,0:T(8,128)(2,1)S(1)}, bf16[20,16,128]{2,1,0:T(8,128)(2,1)S(1)}, u32[]{:S(2)}, u32[]{:S(2)}) collective-permute-start(bf16[20,16,128]{2,1,0:T(8,128)(2,1)S(1)} %slice.refs_0_), channel_id=1, source_target_pairs={{0,8},{4,12},{8,0},{12,4},{1,9},{5,13},{9,1},{13,5},{2,10},{6,14},... | collective-permute-start | bytes 245768 | tf_op jit(solution)/shard_map/ppermute | solution.py:126
  6.7 4.8 %fetch.3 = (bf16[12800,256]{1,0:T(8,128)(2,1)S(1)}, bf16[12800,256]{1,0:T(8,128)(2,1)S(1)}) custom-call(bf16[12800,256]{1,0:T(8,128)(2,1)} %refs_0_.4, bf16[12800,256]{1,0:T(8,128)(2,1)} %refs_1_.1), custom_call_target="tpu_custom_call" | custom-call | bytes 26214400 | tf_op jit(solution)/shard_map/fetch/pallas_call | solution.py:177
  11.5 1.7 %collective-permute-done.1.refs_2_ = bf16[20,16,128]{2,1,0:T(8,128)(2,1)S(1)} collective-permute-done((bf16[20,16,128]{2,1,0:T(8,128)(2,1)S(1)}, bf16[20,16,128]{2,1,0:T(8,128)(2,1)S(1)}, u32[]{:S(2)}, u32[]{:S(2)}) %collective-permute-start.1) | collective-permute-done | bytes 81952 | tf_op jit(solution)/shard_map/ppermute | solution.py:126
  13.3 5.5 %attention.1 = (bf16[24,512]{1,0:T(8,128)(2,1)S(1)}, bf16[24,512]{1,0:T(8,128)(2,1)S(1)}, bf16[24,512]{1,0:T(8,128)(2,1)S(1)}, bf16[24,512]{1,0:T(8,128)(2,1)S(1)}, bf16[2048,2048]{1,0:T(8,128)(2,1)S(1)}) custom-call(s32[102]{0:T(128)S(1)} %pad_add_fusion.table, bf16[20,16,128]{2,1,0:T(8,128)(2,1)S(1)} %slice.refs_0_, ...), custom_call_target="tpu_custom_call" | custom-call | flops 104857600 | bytes 13107200 | tf_op jit(solution)/shard_map/attention/pallas_call | solution.py:319
  19.5 4.1 %collective-permute-start.4 = (bf16[24,512]{1,0:T(8,128)(2,1)S(1)}, bf16[24,512]{1,0:T(8,128)(2,1)S(1)}, u32[]{:S(2)}, u32[]{:S(2)}) collective-permute-start(bf16[24,512]{1,0:T(8,128)(2,1)S(1)} %get-tuple-element.33), channel_id=1, source_target_pairs={{0,8},{4,12},{8,0},{12,4},{1,9},{5,13},{9,1},{13,5},{2,10},{6,14},... | collective-permute-start | bytes 73736 | tf_op jit(solution)/shard_map/ppermute | solution.py:126
  23.5 1.8 %collective-permute-done.4 = bf16[24,512]{1,0:T(8,128)(2,1)S(1)} collective-permute-done((bf16[24,512]{1,0:T(8,128)(2,1)S(1)}, bf16[24,512]{1,0:T(8,128)(2,1)S(1)}, u32[]{:S(2)}, u32[]{:S(2)}) %collective-permute-start.4) | collective-permute-done | bytes 24608 | tf_op jit(solution)/shard_map/ppermute | solution.py:126
  25.3 3.8 %collective-permute-done.5 = bf16[24,512]{1,0:T(8,128)(2,1)S(1)} collective-permute-done((bf16[24,512]{1,0:T(8,128)(2,1)S(1)}, bf16[24,512]{1,0:T(8,128)(2,1)S(1)}, u32[]{:S(2)}, u32[]{:S(2)}) %collective-permute-start.5) | collective-permute-done | bytes 24608 | tf_op jit(solution)/shard_map/ppermute | solution.py:126
  30.7 3.1 %collective-permute-done.7.refs_2_ = bf16[96,512]{1,0:T(8,128)(2,1)S(1)} collective-permute-done((bf16[96,512]{1,0:T(8,128)(2,1)S(1)}, bf16[96,512]{1,0:T(8,128)(2,1)S(1)}, u32[]{:S(2)}, u32[]{:S(2)}) %collective-permute-start.7) | collective-permute-done | bytes 98336 | tf_op jit(solution)/shard_map/ppermute | solution.py:126
  35.1 2.7 %projection.1 = (bf16[40,1024]{1,0:T(8,128)(2,1)S(1)}, bf16[40,1024]{1,0:T(8,128)(2,1)S(1)}, bf16[40,1024]{1,0:T(8,128)(2,1)S(1)}, bf16[40,1024]{1,0:T(8,128)(2,1)S(1)}) custom-call(s32[102]{0:T(128)S(1)} %pad_add_fusion.table, bf16[96,512]{1,0:T(8,128)(2,1)S(1)} %constant_dynamic-update-slice_fusion.refs_0_, ...), custom_call_target="tpu_custom_call" | custom-call | flops 671088640 | bytes 4194304 | tf_op jit(solution)/shard_map/projection/pallas_call | solution.py:387
  38.5 2.8 %collective-permute-start.9 = (bf16[40,1024]{1,0:T(8,128)(2,1)S(1)}, bf16[40,1024]{1,0:T(8,128)(2,1)S(1)}, u32[]{:S(2)}, u32[]{:S(2)}) collective-permute-start(bf16[40,1024]{1,0:T(8,128)(2,1)S(1)} %get-tuple-element.37), channel_id=1, source_target_pairs={{0,4},{4,0},{8,12},{12,8},{1,5},{5,1},{9,13},{13,9},{2,6},{6,2},{1... | collective-permute-start | bytes 245768 | tf_op jit(solution)/shard_map/ppermute | solution.py:126
  41.4 4.5 %collective-permute-done.10.refs_3_ = bf16[40,1024]{1,0:T(8,128)(2,1)S(1)} collective-permute-done((bf16[40,1024]{1,0:T(8,128)(2,1)S(1)}, bf16[40,1024]{1,0:T(8,128)(2,1)S(1)}, u32[]{:S(2)}, u32[]{:S(2)}) %collective-permute-start.10) | collective-permute-done | bytes 81952 | tf_op jit(solution)/shard_map/ppermute | solution.py:126
  47.5 1.6 %collective-permute-start.13 = (bf16[40,1024]{1,0:T(8,128)(2,1)S(1)}, bf16[40,1024]{1,0:T(8,128)(2,1)S(1)}, u32[]{:S(2)}, u32[]{:S(2)}) collective-permute-start(bf16[40,1024]{1,0:T(8,128)(2,1)S(1)} %residual.2.refs_0_), channel_id=1, source_target_pairs={{0,8},{4,12},{8,0},{12,4},{1,9},{5,13},{9,1},{13,5},{2,10},{6,14},... | collective-permute-start | bytes 245768 | tf_op jit(solution)/shard_map/ppermute | solution.py:126
  49.1 2.2 %collective-permute-start.14 = (bf16[40,1024]{1,0:T(8,128)(2,1)S(1)}, bf16[40,1024]{1,0:T(8,128)(2,1)S(1)}, u32[]{:S(2)}, u32[]{:S(2)}) collective-permute-start(bf16[40,1024]{1,0:T(8,128)(2,1)S(1)} %residual.2.refs_0_), channel_id=1, source_target_pairs={{0,12},{4,8},{8,4},{12,0},{1,13},{5,9},{9,5},{13,1},{2,14},{6,10},... | collective-permute-start | bytes 245768 | tf_op jit(solution)/shard_map/ppermute | solution.py:126
  51.3 5.2 %fetch.4.refs_5_.refs_1_ = bf16[3584,2048]{1,0:T(8,128)(2,1)S(1)} custom-call(bf16[3584,2048]{1,0:T(8,128)(2,1)} %refs_0_.6), custom_call_target="tpu_custom_call" | custom-call | bytes 29360128 | tf_op jit(solution)/shard_map/fetch/pallas_call | solution.py:177
  56.5 5.2 %fetch.5.refs_6_.refs_2_ = bf16[3584,2048]{1,0:T(8,128)(2,1)S(1)} custom-call(bf16[3584,2048]{1,0:T(8,128)(2,1)} %refs_0_.7), custom_call_target="tpu_custom_call" | custom-call | bytes 29360128 | tf_op jit(solution)/shard_map/fetch/pallas_call | solution.py:177
  61.8 7.5 %hidden_far.1 = (bf16[80,1920]{1,0:T(8,128)(2,1)S(1)}, f32[80,1920]{1,0:T(8,128)S(1)}, bf16[80,2048]{1,0:T(8,128)(2,1)S(1)}, bf16[2,896,2048]{2,1,0:T(8,128)(2,1)S(1)}) custom-call(s32[102]{0:T(128)S(1)} %pad_add_fusion.table, bf16[40,1024]{1,0:T(8,128)(2,1)S(1)} %residual.2.refs_0_, bf16[40,1024]{1,0:T(8,128)(2,1)S(1)} %collective-permute-done.12.refs_1_, ...), custom_call_target="tpu_custom_call" | custom-call | flops 1174405120 | bytes 7340032 | tf_op jit(solution)/shard_map/hidden_far/pallas_call | solution.py:478
  69.4 1.6 %collective-permute-done.16.arrived = bf16[80,1920]{1,0:T(8,128)(2,1)S(1)} collective-permute-done((bf16[80,1920]{1,0:T(8,128)(2,1)S(1)}, bf16[80,1920]{1,0:T(8,128)(2,1)S(1)}, u32[]{:S(2)}, u32[]{:S(2)}) %collective-permute-start.16) | collective-permute-done | bytes 307232 | tf_op jit(solution)/shard_map/ppermute | solution.py:126
  72.8 8.1 %hidden_near.1 = (bf16[80,1792]{1,0:T(8,128)(2,1)S(1)}, f32[80,1792]{1,0:T(8,128)S(1)}, bf16[2,896,2048]{2,1,0:T(8,128)(2,1)S(1)}) custom-call(s32[102]{0:T(128)S(1)} %pad_add_fusion.table, bf16[80,2048]{1,0:T(8,128)(2,1)S(1)} %get-tuple-element.40.refs_0_, bf16[3584,2048]{1,0:T(8,128)(2,1)S(1)} %fetch.4.refs_5_.refs_1_, ...), custom_call_target="tpu_custom_call" | custom-call | flops 1174405120 | bytes 7340032 | tf_op jit(solution)/shard_map/hidden_near/pallas_call | solution.py:500
  83.4 5.3 %collective-permute-done.18.refs_0_ = bf16[80,896]{1,0:T(8,128)(2,1)S(1)} collective-permute-done((bf16[80,896]{1,0:T(8,128)(2,1)S(1)}, bf16[80,896]{1,0:T(8,128)(2,1)S(1)}, u32[]{:S(2)}, u32[]{:S(2)}) %collective-permute-start.18) | collective-permute-done | bytes 143392 | tf_op jit(solution)/shard_map/ppermute | solution.py:126
  91.7 2.1 %collective-permute-start.22 = (bf16[40,1024]{1,0:T(8,128)(2,1)S(1)}, bf16[40,1024]{1,0:T(8,128)(2,1)S(1)}, u32[]{:S(2)}, u32[]{:S(2)}) collective-permute-start(bf16[40,1024]{1,0:T(8,128)(2,1)S(1)} %get-tuple-element.51), channel_id=1, source_target_pairs={{0,8},{4,12},{8,0},{12,4},{1,9},{5,13},{9,1},{13,5},{2,10},{6,14},... | collective-permute-start | bytes 245768 | tf_op jit(solution)/shard_map/ppermute | solution.py:126
  93.8 2.2 %collective-permute-start.23 = (bf16[40,1024]{1,0:T(8,128)(2,1)S(1)}, bf16[40,1024]{1,0:T(8,128)(2,1)S(1)}, u32[]{:S(2)}, u32[]{:S(2)}) collective-permute-start(bf16[40,1024]{1,0:T(8,128)(2,1)S(1)} %get-tuple-element.52), channel_id=1, source_target_pairs={{0,12},{4,8},{8,4},{12,0},{1,13},{5,9},{9,5},{13,1},{2,14},{6,10},... | collective-permute-start | bytes 245768 | tf_op jit(solution)/shard_map/ppermute | solution.py:126
  96.1 1.6 %collective-permute-done.21.refs_2_ = bf16[40,1024]{1,0:T(8,128)(2,1)S(1)} collective-permute-done((bf16[40,1024]{1,0:T(8,128)(2,1)S(1)}, bf16[40,1024]{1,0:T(8,128)(2,1)S(1)}, u32[]{:S(2)}, u32[]{:S(2)}) %collective-permute-start.21) | collective-permute-done | bytes 81952 | tf_op jit(solution)/shard_map/ppermute | solution.py:126
  97.7 3.8 %collective-permute-done.22.refs_3_ = bf16[40,1024]{1,0:T(8,128)(2,1)S(1)} collective-permute-done((bf16[40,1024]{1,0:T(8,128)(2,1)S(1)}, bf16[40,1024]{1,0:T(8,128)(2,1)S(1)}, u32[]{:S(2)}, u32[]{:S(2)}) %collective-permute-start.22) | collective-permute-done | bytes 81952 | tf_op jit(solution)/shard_map/ppermute | solution.py:126
  (53 shorter events, 15.0 us)
Async XLA Ops:
  1.0 10.6 %collective-permute-start = (bf16[20,16,128]{2,1,0:T(8,128)(2,1)S(1)}, bf16[20,16,128]{2,1,0:T(8,128)(2,1)S(1)}, u32[]{:S(2)}, u32[]{:S(2)}) collective-permute-start(bf16[20,16,128]{2,1,0:T(8,128)(2,1)S(1)} %slice.refs_0_), channel_id=1, source_target_pairs={{0,4},{4,0},{8,12},{12,8},{1,5},{5,1},{9,13},{13,9},{2,6},{6,2},{1... | collective-permute-start | bytes 245768 | tf_op jit(solution)/shard_map/ppermute | solution.py:126
  4.1 9.2 %collective-permute-start.1 = (bf16[20,16,128]{2,1,0:T(8,128)(2,1)S(1)}, bf16[20,16,128]{2,1,0:T(8,128)(2,1)S(1)}, u32[]{:S(2)}, u32[]{:S(2)}) collective-permute-start(bf16[20,16,128]{2,1,0:T(8,128)(2,1)S(1)} %slice.refs_0_), channel_id=1, source_target_pairs={{0,8},{4,12},{8,0},{12,4},{1,9},{5,13},{9,1},{13,5},{2,10},{6,14},... | collective-permute-start | bytes 245768 | tf_op jit(solution)/shard_map/ppermute | solution.py:126
  6.7 6.6 %collective-permute-start.2 = (bf16[20,16,128]{2,1,0:T(8,128)(2,1)S(1)}, bf16[20,16,128]{2,1,0:T(8,128)(2,1)S(1)}, u32[]{:S(2)}, u32[]{:S(2)}) collective-permute-start(bf16[20,16,128]{2,1,0:T(8,128)(2,1)S(1)} %slice.refs_0_), channel_id=1, source_target_pairs={{0,12},{4,8},{8,4},{12,0},{1,13},{5,9},{9,5},{13,1},{2,14},{6,10},... | collective-permute-start | bytes 245768 | tf_op jit(solution)/shard_map/ppermute | solution.py:126
  18.8 4.8 %collective-permute-start.3 = (bf16[24,512]{1,0:T(8,128)(2,1)S(1)}, bf16[24,512]{1,0:T(8,128)(2,1)S(1)}, u32[]{:S(2)}, u32[]{:S(2)}) collective-permute-start(bf16[24,512]{1,0:T(8,128)(2,1)S(1)} %get-tuple-element.32), channel_id=1, source_target_pairs={{0,4},{4,0},{8,12},{12,8},{1,5},{5,1},{9,13},{13,9},{2,6},{6,2},{1... | collective-permute-start | bytes 73736 | tf_op jit(solution)/shard_map/ppermute | solution.py:126
  19.5 5.9 %collective-permute-start.4 = (bf16[24,512]{1,0:T(8,128)(2,1)S(1)}, bf16[24,512]{1,0:T(8,128)(2,1)S(1)}, u32[]{:S(2)}, u32[]{:S(2)}) collective-permute-start(bf16[24,512]{1,0:T(8,128)(2,1)S(1)} %get-tuple-element.33), channel_id=1, source_target_pairs={{0,8},{4,12},{8,0},{12,4},{1,9},{5,13},{9,1},{13,5},{2,10},{6,14},... | collective-permute-start | bytes 73736 | tf_op jit(solution)/shard_map/ppermute | solution.py:126
  23.5 5.6 %collective-permute-start.5 = (bf16[24,512]{1,0:T(8,128)(2,1)S(1)}, bf16[24,512]{1,0:T(8,128)(2,1)S(1)}, u32[]{:S(2)}, u32[]{:S(2)}) collective-permute-start(bf16[24,512]{1,0:T(8,128)(2,1)S(1)} %get-tuple-element.34), channel_id=1, source_target_pairs={{0,12},{4,8},{8,4},{12,0},{1,13},{5,9},{9,5},{13,1},{2,14},{6,10},... | collective-permute-start | bytes 73736 | tf_op jit(solution)/shard_map/ppermute | solution.py:126
  29.2 4.6 %collective-permute-start.7 = (bf16[96,512]{1,0:T(8,128)(2,1)S(1)}, bf16[96,512]{1,0:T(8,128)(2,1)S(1)}, u32[]{:S(2)}, u32[]{:S(2)}) collective-permute-start(bf16[96,512]{1,0:T(8,128)(2,1)S(1)} %constant_dynamic-update-slice_fusion.refs_0_), channel_id=1, source_target_pairs={{0,2},{1,3},{2,0},{3,1},{4,6},{5,7},{6,4},{7,5},{8,10},{9,11},{10,... | collective-permute-start | bytes 294920 | tf_op jit(solution)/shard_map/ppermute | solution.py:126
  30.7 3.1 %collective-permute-start.6 = (bf16[96,512]{1,0:T(8,128)(2,1)S(1)}, bf16[96,512]{1,0:T(8,128)(2,1)S(1)}, u32[]{:S(2)}, u32[]{:S(2)}) collective-permute-start(bf16[96,512]{1,0:T(8,128)(2,1)S(1)} %constant_dynamic-update-slice_fusion.refs_0_), channel_id=1, source_target_pairs={{0,1},{1,0},{2,3},{3,2},{4,5},{5,4},{6,7},{7,6},{8,9},{9,8},{10,11... | collective-permute-start | bytes 294920 | tf_op jit(solution)/shard_map/ppermute | solution.py:126
  33.8 1.3 %collective-permute-start.8 = (bf16[96,512]{1,0:T(8,128)(2,1)S(1)}, bf16[96,512]{1,0:T(8,128)(2,1)S(1)}, u32[]{:S(2)}, u32[]{:S(2)}) collective-permute-start(bf16[96,512]{1,0:T(8,128)(2,1)S(1)} %collective-permute-done.7.refs_2_), channel_id=1, source_target_pairs={{0,1},{1,0},{2,3},{3,2},{4,5},{5,4},{6,7},{7,6},{8,9},{9,8},{10,11... | collective-permute-start | bytes 294920 | tf_op jit(solution)/shard_map/ppermute | solution.py:126
  37.8 8.0 %collective-permute-start.10 = (bf16[40,1024]{1,0:T(8,128)(2,1)S(1)}, bf16[40,1024]{1,0:T(8,128)(2,1)S(1)}, u32[]{:S(2)}, u32[]{:S(2)}) collective-permute-start(bf16[40,1024]{1,0:T(8,128)(2,1)S(1)} %get-tuple-element.38), channel_id=1, source_target_pairs={{0,8},{4,12},{8,0},{12,4},{1,9},{5,13},{9,1},{13,5},{2,10},{6,14},... | collective-permute-start | bytes 245768 | tf_op jit(solution)/shard_map/ppermute | solution.py:126
  37.9 8.0 %collective-permute-start.11 = (bf16[40,1024]{1,0:T(8,128)(2,1)S(1)}, bf16[40,1024]{1,0:T(8,128)(2,1)S(1)}, u32[]{:S(2)}, u32[]{:S(2)}) collective-permute-start(bf16[40,1024]{1,0:T(8,128)(2,1)S(1)} %get-tuple-element.39), channel_id=1, source_target_pairs={{0,12},{4,8},{8,4},{12,0},{1,13},{5,9},{9,5},{13,1},{2,14},{6,10},... | collective-permute-start | bytes 245768 | tf_op jit(solution)/shard_map/ppermute | solution.py:126
  38.5 8.3 %collective-permute-start.9 = (bf16[40,1024]{1,0:T(8,128)(2,1)S(1)}, bf16[40,1024]{1,0:T(8,128)(2,1)S(1)}, u32[]{:S(2)}, u32[]{:S(2)}) collective-permute-start(bf16[40,1024]{1,0:T(8,128)(2,1)S(1)} %get-tuple-element.37), channel_id=1, source_target_pairs={{0,4},{4,0},{8,12},{12,8},{1,5},{5,1},{9,13},{13,9},{2,6},{6,2},{1... | collective-permute-start | bytes 245768 | tf_op jit(solution)/shard_map/ppermute | solution.py:126
  46.9 14.9 %collective-permute-start.12 = (bf16[40,1024]{1,0:T(8,128)(2,1)S(1)}, bf16[40,1024]{1,0:T(8,128)(2,1)S(1)}, u32[]{:S(2)}, u32[]{:S(2)}) collective-permute-start(bf16[40,1024]{1,0:T(8,128)(2,1)S(1)} %residual.2.refs_0_), channel_id=1, source_target_pairs={{0,4},{4,0},{8,12},{12,8},{1,5},{5,1},{9,13},{13,9},{2,6},{6,2},{1... | collective-permute-start | bytes 245768 | tf_op jit(solution)/shard_map/ppermute | solution.py:126
  47.5 14.3 %collective-permute-start.13 = (bf16[40,1024]{1,0:T(8,128)(2,1)S(1)}, bf16[40,1024]{1,0:T(8,128)(2,1)S(1)}, u32[]{:S(2)}, u32[]{:S(2)}) collective-permute-start(bf16[40,1024]{1,0:T(8,128)(2,1)S(1)} %residual.2.refs_0_), channel_id=1, source_target_pairs={{0,8},{4,12},{8,0},{12,4},{1,9},{5,13},{9,1},{13,5},{2,10},{6,14},... | collective-permute-start | bytes 245768 | tf_op jit(solution)/shard_map/ppermute | solution.py:126
  49.1 12.7 %collective-permute-start.14 = (bf16[40,1024]{1,0:T(8,128)(2,1)S(1)}, bf16[40,1024]{1,0:T(8,128)(2,1)S(1)}, u32[]{:S(2)}, u32[]{:S(2)}) collective-permute-start(bf16[40,1024]{1,0:T(8,128)(2,1)S(1)} %residual.2.refs_0_), channel_id=1, source_target_pairs={{0,12},{4,8},{8,4},{12,0},{1,13},{5,9},{9,5},{13,1},{2,14},{6,10},... | collective-permute-start | bytes 245768 | tf_op jit(solution)/shard_map/ppermute | solution.py:126
  69.3 1.7 %collective-permute-start.16 = (bf16[80,1920]{1,0:T(8,128)(2,1)S(1)}, bf16[80,1920]{1,0:T(8,128)(2,1)S(1)}, u32[]{:S(2)}, u32[]{:S(2)}) collective-permute-start(bf16[80,1920]{1,0:T(8,128)(2,1)S(1)} %get-tuple-element.44), channel_id=1, source_target_pairs={{0,1},{1,0},{2,3},{3,2},{4,5},{5,4},{6,7},{7,6},{8,9},{9,8},{10,11... | collective-permute-start | bytes 921608 | tf_op jit(solution)/shard_map/ppermute | solution.py:126
  71.2 11.3 %collective-permute-start.17 = (bf16[80,1920]{1,0:T(8,128)(2,1)S(1)}, bf16[80,1920]{1,0:T(8,128)(2,1)S(1)}, u32[]{:S(2)}, u32[]{:S(2)}) collective-permute-start(bf16[80,1920]{1,0:T(8,128)(2,1)S(1)} %get-tuple-element.45), channel_id=1, source_target_pairs={{0,2},{1,3},{2,0},{3,1},{4,6},{5,7},{6,4},{7,5},{8,10},{9,11},{10,... | collective-permute-start | bytes 921608 | tf_op jit(solution)/shard_map/ppermute | solution.py:126
  80.9 1.6 %collective-permute-start.15 = (bf16[80,1792]{1,0:T(8,128)(2,1)S(1)}, bf16[80,1792]{1,0:T(8,128)(2,1)S(1)}, u32[]{:S(2)}, u32[]{:S(2)}) collective-permute-start(bf16[80,1792]{1,0:T(8,128)(2,1)S(1)} %get-tuple-element.42), channel_id=1, source_target_pairs={{0,1},{1,0},{2,3},{3,2},{4,5},{5,4},{6,7},{7,6},{8,9},{9,8},{10,11... | collective-permute-start | bytes 860168 | tf_op jit(solution)/shard_map/ppermute | solution.py:126
  82.8 5.9 %collective-permute-start.18 = (bf16[80,896]{1,0:T(8,128)(2,1)S(1)}, bf16[80,896]{1,0:T(8,128)(2,1)S(1)}, u32[]{:S(2)}, u32[]{:S(2)}) collective-permute-start(bf16[80,896]{1,0:T(8,128)(2,1)S(1)} %active.1.refs_0_), channel_id=1, source_target_pairs={{0,2},{1,3},{2,0},{3,1},{4,6},{5,7},{6,4},{7,5},{8,10},{9,11},{10,... | collective-permute-start | bytes 430088 | tf_op jit(solution)/shard_map/ppermute | solution.py:126
  83.4 5.3 %collective-permute-start.20 = (bf16[80,896]{1,0:T(8,128)(2,1)S(1)}, bf16[80,896]{1,0:T(8,128)(2,1)S(1)}, u32[]{:S(2)}, u32[]{:S(2)}) collective-permute-start(bf16[80,896]{1,0:T(8,128)(2,1)S(1)} %active.1.refs_0_), channel_id=1, source_target_pairs={{0,1},{1,0},{2,3},{3,2},{4,5},{5,4},{6,7},{7,6},{8,9},{9,8},{10,11... | collective-permute-start | bytes 430088 | tf_op jit(solution)/shard_map/ppermute | solution.py:126
  88.6 1.5 %collective-permute-start.19 = (bf16[80,896]{1,0:T(8,128)(2,1)S(1)}, bf16[80,896]{1,0:T(8,128)(2,1)S(1)}, u32[]{:S(2)}, u32[]{:S(2)}) collective-permute-start(bf16[80,896]{1,0:T(8,128)(2,1)S(1)} %collective-permute-done.18.refs_0_), channel_id=1, source_target_pairs={{0,1},{1,0},{2,3},{3,2},{4,5},{5,4},{6,7},{7,6},{8,9},{9,8},{10,11... | collective-permute-start | bytes 430088 | tf_op jit(solution)/shard_map/ppermute | solution.py:126
  91.6 6.1 %collective-permute-start.21 = (bf16[40,1024]{1,0:T(8,128)(2,1)S(1)}, bf16[40,1024]{1,0:T(8,128)(2,1)S(1)}, u32[]{:S(2)}, u32[]{:S(2)}) collective-permute-start(bf16[40,1024]{1,0:T(8,128)(2,1)S(1)} %get-tuple-element.50), channel_id=1, source_target_pairs={{0,4},{4,0},{8,12},{12,8},{1,5},{5,1},{9,13},{13,9},{2,6},{6,2},{1... | collective-permute-start | bytes 245768 | tf_op jit(solution)/shard_map/ppermute | solution.py:126
  91.7 9.8 %collective-permute-start.22 = (bf16[40,1024]{1,0:T(8,128)(2,1)S(1)}, bf16[40,1024]{1,0:T(8,128)(2,1)S(1)}, u32[]{:S(2)}, u32[]{:S(2)}) collective-permute-start(bf16[40,1024]{1,0:T(8,128)(2,1)S(1)} %get-tuple-element.51), channel_id=1, source_target_pairs={{0,8},{4,12},{8,0},{12,4},{1,9},{5,13},{9,1},{13,5},{2,10},{6,14},... | collective-permute-start | bytes 245768 | tf_op jit(solution)/shard_map/ppermute | solution.py:126
  93.8 7.7 %collective-permute-start.23 = (bf16[40,1024]{1,0:T(8,128)(2,1)S(1)}, bf16[40,1024]{1,0:T(8,128)(2,1)S(1)}, u32[]{:S(2)}, u32[]{:S(2)}) collective-permute-start(bf16[40,1024]{1,0:T(8,128)(2,1)S(1)} %get-tuple-element.52), channel_id=1, source_target_pairs={{0,12},{4,8},{8,4},{12,0},{1,13},{5,9},{9,5},{13,1},{2,14},{6,10},... | collective-permute-start | bytes 245768 | tf_op jit(solution)/shard_map/ppermute | solution.py:126
  (4 other events, 56.1 us)

commit v3 on v2

--- a/solution.py
+++ b/solution.py
@@ -160,30 +160,62 @@
     return pltpu.with_memory_space_constraint(value, pltpu.VMEM)
 
 
-def fetch_kernel(*refs):
-    count = len(refs) // 2
-    sems = refs[-1]
-    copies = [
-        pltpu.make_async_copy(refs[i], refs[count + i], sems.at[i]) for i in range(count)
-    ]
+def job_shapes(jobs, parts):
+    shapes = []
+    for array, masks in jobs:
+        if masks is None:
+            shapes.append(pltpu.VMEM(array.shape, array.dtype))
+        else:
+            rows, width = array.shape
+            shapes.append(pltpu.VMEM((len(masks), rows // parts, width), array.dtype))
+    return shapes
+
+
+def job_count(jobs):
+    return sum(1 if masks is None else len(masks) for _, masks in jobs)
+
+
+def job_copies(own, masks_of, sources, targets, sems):
+    copies = []
+    for masks, source, target in zip(masks_of, sources, targets):
+        if masks is None:
+            copies.append(pltpu.make_async_copy(source, target, sems.at[len(copies)]))
+            continue
+        rows = target.shape[1]
+        for m, mask in enumerate(masks):
+            at = pl.ds(pl.multiple_of((own ^ mask) * rows, rows), rows)
+            copies.append(
+                pltpu.make_async_copy(source.at[at], target.at[m], sems.at[len(copies)])
+            )
+    return copies
+
+
+def masks_in(jobs):
+    return tuple(masks for _, masks in jobs)
+
+
+def fetch_kernel(table, *refs, masks_of):
+    count = len(masks_of)
+    copies = job_copies(table[1], masks_of, refs[:count], refs[count:-1], refs[-1])
     for copy in copies:
         copy.start()
     for copy in copies:
         copy.wait()
 
 
-def fetch(arrays):
-    moved = sum(a.size * 2 for a in arrays)
-    return pl.pallas_call(
-        fetch_kernel,
-        in_specs=[hbm] * len(arrays),
-        out_specs=[vmem] * len(arrays),
-        out_shape=[pltpu.VMEM(a.shape, a.dtype) for a in arrays],
-        scratch_shapes=[pltpu.SemaphoreType.DMA((len(arrays),))],
+def fetch(table, jobs, parts):
+    shapes = job_shapes(jobs, parts)
+    moved = sum(2 * math.prod(shape.shape) for shape in shapes)
+    return pl.pallas_call(
+        functools.partial(fetch_kernel, masks_of=masks_in(jobs)),
+        in_specs=[smem] + [hbm] * len(jobs),
+        out_specs=[vmem] * len(jobs),
+        out_shape=shapes,
+        scratch_shapes=[pltpu.SemaphoreType.DMA((job_count(jobs),))],
         compiler_params=params(1),
         cost_estimate=pl.CostEstimate(flops=0, bytes_accessed=2 * moved, transcendentals=0),
         name="fetch",
-    )(*[in_hbm(a) for a in arrays])
+    )(table, *[in_hbm(array) for array, _ in jobs])
 
 
 def folded(combine, value):
@@ -191,14 +223,23 @@
     return functools.reduce(combine, parts)
 
 
-def attention_kernel(table, *refs, slots, count, scale, unroll):
-    query_blocks, (keys, values, ahead) = refs[:count], refs[count : count + 3]
-    outs, landed = refs[count + 3 : 2 * count + 3], refs[2 * count + 3]
-    queries, both, begins, ends, tops, sums, scores, total, attended, items, sem = refs[
-        2 * count + 4 :
+def attention_kernel(table, *refs, slots, count, scale, unroll, masks_of):
+    jobs = len(masks_of)
+    query_blocks, (keys, values), sources = (
+        refs[:count],
+        refs[count : count + 2],
+        refs[count + 2 : count + 2 + jobs],
+    )
+    outs, targets = (
+        refs[count + 2 + jobs : 2 * count + 2 + jobs],
+        refs[2 * count + 2 + jobs : 2 * count + 2 + 2 * jobs],
+    )
+    queries, both, begins, ends, tops, sums, scores, total, attended, items, sems = refs[
+        2 * count + 2 + 2 * jobs :
     ]
-    copy = pltpu.make_async_copy(ahead, landed, sem)
-    copy.start()
+    copies = job_copies(table[1], masks_of, sources, targets, sems)
+    for copy in copies:
+        copy.start()
     pool, width = keys.shape
     heads = queries.shape[1]
     half = heads // 2
@@ -307,10 +348,11 @@
                 outs[k][:slots, at : at + lanes] = attended[
                     pl.ds(head, slots, stride=heads), :
                 ].astype(BF16)
-    copy.wait()
-
-
-def attention(table, query_blocks, keys, values, ahead, unroll=8):
+    for copy in copies:
+        copy.wait()
+
+
+def attention(table, query_blocks, keys, values, jobs, parts, unroll=8):
     count = len(query_blocks)
     slots, heads, _ = query_blocks[0].shape
     pool, width = keys.shape
@@ -318,12 +360,17 @@
     rows = (slots + slot_group) * heads
     return pl.pallas_call(
         functools.partial(
-            attention_kernel, slots=slots, count=count, scale=1.0 / math.sqrt(lanes), unroll=unroll
+            attention_kernel,
+            slots=slots,
+            count=count,
+            scale=1.0 / math.sqrt(lanes),
+            unroll=unroll,
+            masks_of=masks_in(jobs),
         ),
-        in_specs=[smem] + [vmem] * (count + 2) + [hbm],
-        out_specs=[vmem] * (count + 1),
+        in_specs=[smem] + [vmem] * (count + 2) + [hbm] * len(jobs),
+        out_specs=[vmem] * (count + len(jobs)),
         out_shape=[jax.ShapeDtypeStruct((up_to(slots, 8), heads // count * lanes), BF16)] * count
-        + [pltpu.VMEM(ahead.shape, ahead.dtype)],
+        + job_shapes(jobs, parts),
         scratch_shapes=[
             pltpu.VMEM((count * slots, heads, lanes), BF16),
             pltpu.VMEM((rows, width), BF16),
@@ -335,22 +382,31 @@
             pltpu.VMEM((rows, width), F32),
             pltpu.VMEM((slots * heads, lanes), F32),
             pltpu.SMEM((2 * most,), I32),
-            pltpu.SemaphoreType.DMA,
+            pltpu.SemaphoreType.DMA((job_count(jobs),)),
         ],
         compiler_params=params(12),
         cost_estimate=pl.CostEstimate(
             flops=4 * pool * heads * lanes, bytes_accessed=pool * width * 4, transcendentals=0
         ),
         name="attention",
-    )(table, *query_blocks, in_vmem(keys), in_vmem(values), in_hbm(ahead))
-
-
-def projection_kernel(table, *refs, slots, count, parts):
-    pieces, weight, outs = refs[:parts], refs[parts], refs[parts + 1 :]
-    own_att, own_ffn = table[0], table[1]
+    )(
+        table,
+        *query_blocks,
+        in_vmem(keys),
+        in_vmem(values),
+        *[in_hbm(array) for array, _ in jobs],
+    )
+
+
+def projection_kernel(table, *refs, slots, count, parts, masks_of):
+    pieces, weight, source = refs[:parts], refs[parts], refs[parts + 1]
+    outs, target, sems = refs[parts + 2 : -2], refs[-2], refs[-1]
+    copies = job_copies(table[1], masks_of, [source], [target], sems)
+    for copy in copies:
+        copy.start()
+    own_att = table[0]
     requests = slots * count
     padded = pieces[0].shape[0] // count
-    depth = weight.shape[0] // parts
     row = lax.broadcasted_iota(I32, (requests, padded), 0)
     wanted = row
     for k in range(count):
@@ -374,27 +430,33 @@
                 preferred_element_type=F32,
             )
             rows = term if rows is None else rows + term
-        at = pl.ds(pl.multiple_of((own_ffn ^ p) * depth, depth), depth)
-        term = jnp.dot(rows.astype(BF16), weight[at, :], preferred_element_type=F32)
+        term = jnp.dot(rows.astype(BF16), weight[p], preferred_element_type=F32)
         total = term if total is None else total + term
     for k in range(count):
         outs[k][...] = halves_stacked(total[k * slots : (k + 1) * slots]).astype(BF16)
-
-
-def projection(table, pieces, weight, slots, count):
-    parts = len(pieces)
-    depth, width = weight.shape
-    return pl.pallas_call(
-        functools.partial(projection_kernel, slots=slots, count=count, parts=parts),
-        in_specs=[smem] + [vmem] * (1 + parts),
-        out_specs=[vmem] * count,
-        out_shape=[jax.ShapeDtypeStruct((2 * slots, width // 2), BF16)] * count,
+    for copy in copies:
+        copy.wait()
+
+
+def projection(table, pieces, weight, slots, count, jobs):
+    parts, depth, width = weight.shape
+    return pl.pallas_call(
+        functools.partial(
+            projection_kernel, slots=slots, count=count, parts=parts, masks_of=masks_in(jobs)
+        ),
+        in_specs=[smem] + [vmem] * (1 + parts) + [hbm],
+        out_specs=[vmem] * (count + 1),
+        out_shape=[jax.ShapeDtypeStruct((2 * slots, width // 2), BF16)] * count
+        + job_shapes(jobs, parts),
+        scratch_shapes=[pltpu.SemaphoreType.DMA((job_count(jobs),))],
         compiler_params=params(8),
         cost_estimate=pl.CostEstimate(
-            flops=2 * slots * count * depth * width, bytes_accessed=depth * width, transcendentals=0
+            flops=2 * slots * count * parts * depth * width,
+            bytes_accessed=parts * depth * width,
+            transcendentals=0,
         ),
         name="projection",
-    )(table, *pieces, in_vmem(weight))
+    )(table, *pieces, in_vmem(weight), in_hbm(jobs[0][0]))
 
 
 def residual_kernel(*refs, joined):
@@ -420,157 +482,146 @@
     )(base, *blocks)
 
 
-def hidden_kernel(table, *refs, count, masks, ahead_masks, far):
-    own = table[1]
-    sem = refs[-1]
-    if far:
-        blocks, (gain, gate, up, ahead, send, keep, scaled, landed, joined, _) = (
-            refs[:count],
-            refs[count:],
-        )
-    else:
-        scaled, gate, up, ahead, send, keep, landed, _ = refs
-    width = keep.shape[1]
-    units = (width - lanes if far else width) // 2
-    copies = [
-        pltpu.make_async_copy(
-            ahead.at[pl.ds(pl.multiple_of((own ^ mask) * units, units), units)],
-            landed.at[m],
-            sem.at[m],
-        )
-        for m, mask in enumerate(ahead_masks)
-    ]
-    for copy in copies:
-        copy.start()
-    if far:
-        rows = blocks[0].shape[0] // 2
-        for k in range(count):
-            joined[k * rows : (k + 1) * rows, :] = halves_joined(blocks[k][...])
-        middle = joined[...]
-        squares = jnp.sum(middle * middle, axis=1, keepdims=True)
-        scaled[...] = (middle * gain[...].astype(F32)).astype(BF16)
-    for m, target in enumerate((send, keep)):
-        at = pl.ds(pl.multiple_of((own ^ masks[m]) * units, units), units)
-        for t, weight in enumerate((gate, up)):
-            out = lax.dot_general(
-                scaled[...], weight[at, :], contract_minor, preferred_element_type=F32
-            )
-            target[:, t * units : (t + 1) * units] = out.astype(target.dtype)
-    if far:
-        send[:, 2 * units :] = high_low(squares).astype(BF16)
-        keep[:, 2 * units :] = jnp.broadcast_to(squares, (squares.shape[0], lanes))
-    for copy in copies:
-        copy.wait()
-
-
-def hidden_cost(requests, units, width):
+def unit_product(scaled, weight, part):
+    return lax.dot_general(scaled, weight[part], contract_minor, preferred_element_type=F32)
+
+
+def product_cost(requests, units, width):
     return pl.CostEstimate(
-        flops=8 * requests * units * width, bytes_accessed=4 * units * width, transcendentals=0
-    )
-
-
-def hidden_far(table, blocks, gain, gate, up, ahead, owners):
+        flops=2 * requests * units * width, bytes_accessed=units * width, transcendentals=0
+    )
+
+
+def hidden_first_kernel(*refs, count, part):
+    blocks, (gain, weight, send, scaled, squares, joined) = refs[:count], refs[count:]
+    rows = blocks[0].shape[0] // 2
+    for k in range(count):
+        joined[k * rows : (k + 1) * rows, :] = halves_joined(blocks[k][...])
+    middle = joined[...]
+    square = jnp.sum(middle * middle, axis=1, keepdims=True)
+    scaled[...] = (middle * gain[...].astype(F32)).astype(BF16)
+    units = weight.shape[1]
+    send[:, :units] = unit_product(scaled[...], weight, part).astype(BF16)
+    send[:, units:] = high_low(square).astype(BF16)
+    squares[...] = jnp.broadcast_to(square, squares.shape)
+
+
+def hidden_first(blocks, gain, weight, part):
     count = len(blocks)
     rows, half = blocks[0].shape
     requests, width = rows // 2 * count, 2 * half
-    units = gate.shape[0] // owners
-    across = 2 * units + lanes
-    return pl.pallas_call(
-        functools.partial(
-            hidden_kernel, count=count, masks=(3, 2), ahead_masks=(0, 1), far=True
-        ),
-        in_specs=[smem] + [vmem] * (count + 3) + [hbm],
-        out_specs=[vmem] * 4,
-        out_shape=[
-            jax.ShapeDtypeStruct((requests, across), BF16),
-            jax.ShapeDtypeStruct((requests, across), F32),
-            jax.ShapeDtypeStruct((requests, width), BF16),
-            pltpu.VMEM((2, units, ahead.shape[1]), BF16),
-        ],
-        scratch_shapes=[pltpu.VMEM((requests, width), F32), pltpu.SemaphoreType.DMA((2,))],
-        compiler_params=params(8),
-        cost_estimate=hidden_cost(requests, units, width),
-        name="hidden_far",
-    )(table, *blocks, gain, in_vmem(gate), in_vmem(up), in_hbm(ahead))
-
-
-def hidden_near(table, scaled, gate, up, ahead, owners):
-    requests, width = scaled.shape
-    units = gate.shape[0] // owners
-    return pl.pallas_call(
-        functools.partial(
-            hidden_kernel, count=0, masks=(1, 0), ahead_masks=(2, 3), far=False
-        ),
-        in_specs=[smem] + [vmem] * 3 + [hbm],
+    units = weight.shape[1]
+    return pl.pallas_call(
+        functools.partial(hidden_first_kernel, count=count, part=part),
+        in_specs=[vmem] * (count + 2),
         out_specs=[vmem] * 3,
         out_shape=[
-            jax.ShapeDtypeStruct((requests, 2 * units), BF16),
-            jax.ShapeDtypeStruct((requests, 2 * units), F32),
-            pltpu.VMEM((2, units, ahead.shape[1]), BF16),
+            jax.ShapeDtypeStruct((requests, units + lanes), BF16),
+            jax.ShapeDtypeStruct((requests, width), BF16),
+            jax.ShapeDtypeStruct((requests, lanes), F32),
         ],
-        scratch_shapes=[pltpu.SemaphoreType.DMA((2,))],
-        compiler_params=params(8),
-        cost_estimate=hidden_cost(requests, units, width),
-        name="hidden_near",
-    )(table, scaled, in_vmem(gate), in_vmem(up), in_hbm(ahead))
-
-
-def chip_sum_kernel(keep, arrived, out, squares):
-    width = keep.shape[1] - lanes
-    out[:, :width] = (keep[:, :width] + arrived[:, :width].astype(F32)).astype(BF16)
+        scratch_shapes=[pltpu.VMEM((requests, width), F32)],
+        compiler_params=params(6),
+        cost_estimate=product_cost(requests, units, width),
+        name="hidden_first",
+    )(*blocks, gain, in_vmem(weight))
+
+
+def hidden_kernel(scaled, *refs, parts):
+    weights, out = refs[:-1], refs[-1]
+    for t, (weight, part) in enumerate(zip(weights, parts)):
+        units = weight.shape[1]
+        out[:, t * units : (t + 1) * units] = unit_product(scaled[...], weight, part).astype(
+            out.dtype
+        )
+
+
+def hidden_next(scaled, chosen, kind):
+    requests, width = scaled.shape
+    units = chosen[0][0].shape[1]
+    return pl.pallas_call(
+        functools.partial(hidden_kernel, parts=tuple(part for _, part in chosen)),
+        in_specs=[vmem] * (1 + len(chosen)),
+        out_specs=vmem,
+        out_shape=jax.ShapeDtypeStruct((requests, len(chosen) * units), kind),
+        compiler_params=params(6),
+        cost_estimate=product_cost(requests, len(chosen) * units, width),
+        name="hidden_next",
+    )(scaled, *[in_vmem(weight) for weight, _ in chosen])
+
+
+def squares_sum_kernel(keep, own_squares, arrived, out, squares):
+    width = keep.shape[1]
+    out[:, :width] = (keep[...] + arrived[:, :width].astype(F32)).astype(BF16)
     tail = arrived[:, width:].astype(F32)
-    chip = keep[:, width:] + (tail[:, :1] + tail[:, lanes // 2 : lanes // 2 + 1])
+    chip = own_squares[...] + (tail[:, :1] + tail[:, lanes // 2 : lanes // 2 + 1])
     squares[...] = chip
     out[:, width:] = high_low(chip).astype(BF16)
 
 
-def chip_sum(keep, arrived):
-    requests, width = keep.shape
-    return pl.pallas_call(
-        chip_sum_kernel,
-        in_specs=[vmem] * 2,
+def squares_sum(keep, own_squares, arrived):
+    requests, width = arrived.shape
+    return pl.pallas_call(
+        squares_sum_kernel,
+        in_specs=[vmem] * 3,
         out_specs=[vmem] * 2,
         out_shape=[
             jax.ShapeDtypeStruct((requests, width), BF16),
             jax.ShapeDtypeStruct((requests, lanes), F32),
         ],
         compiler_params=params(2),
+        name="squares_sum",
+    )(keep, own_squares, arrived)
+
+
+def chip_sum_kernel(keep, arrived, out):
+    out[...] = (keep[...] + arrived[...].astype(F32)).astype(BF16)
+
+
+def chip_sum(keep, arrived):
+    return pl.pallas_call(
+        chip_sum_kernel,
+        in_specs=[vmem] * 2,
+        out_specs=vmem,
+        out_shape=jax.ShapeDtypeStruct(arrived.shape, BF16),
+        compiler_params=params(2),
         name="chip_sum",
     )(keep, arrived)
 
 
-def active_kernel(near, beside, far, squares, out, *, model_width):
-    units = near.shape[1] // 2
-    tail = far[:, 2 * units :].astype(F32)
+def active_kernel(near, beside, far_gate, far_up, squares, out, *, model_width):
+    units = far_up.shape[1]
+    tail = far_gate[:, units:].astype(F32)
     square = squares[:, :1] + (tail[:, :1] + tail[:, lanes // 2 : lanes // 2 + 1])
     scale = lax.rsqrt(square / model_width + epsilon)
 
-    def total(at):
+    def total(at, far):
         both = near[:, at : at + units] + beside[:, at : at + units].astype(F32)
-        return (both + far[:, at : at + units].astype(F32)) * scale
-
-    gate = total(0)
-    out[...] = (gate / (1.0 + jnp.exp(-gate)) * total(units)).astype(BF16)
-
-
-def active_units(near, beside, far, squares, model_width):
+        return (both + far.astype(F32)) * scale
+
+    gate = total(0, far_gate[:, :units])
+    out[...] = (gate / (1.0 + jnp.exp(-gate)) * total(units, far_up[...])).astype(BF16)
+
+
+def active_units(near, beside, far_gate, far_up, squares, model_width):
     requests, width = near.shape
     return pl.pallas_call(
         functools.partial(active_kernel, model_width=model_width),
-        in_specs=[vmem] * 4,
+        in_specs=[vmem] * 5,
         out_specs=vmem,
         out_shape=jax.ShapeDtypeStruct((requests, width // 2), BF16),
         compiler_params=params(4),
         name="active",
-    )(near, beside, far, squares)
-
-
-def down_kernel(*refs, count, first, last):
-    pieces, weight, rest = refs[:2], refs[2], refs[3:]
+    )(near, beside, far_gate, far_up, squares)
+
+
+def down_kernel(*refs, parts, count, first, last):
+    terms = len(parts)
+    pieces, weights, rest = refs[:terms], refs[terms : 2 * terms], refs[2 * terms :]
     total = None if first else rest[0][...]
     outs = rest if first else rest[1:]
-    for m, piece in enumerate(pieces):
-        term = jnp.dot(piece[...], weight[m], preferred_element_type=F32)
+    for piece, weight, part in zip(pieces, weights, parts):
+        term = jnp.dot(piece[...], weight[part], preferred_element_type=F32)
         total = term if total is None else total + term
     if last:
         rows = total.shape[0] // count
@@ -580,27 +631,29 @@
         outs[0][...] = total
 
 
-def down_part(pieces, weight, count, before=None, last=False):
-    first = before is None
-    requests, units = pieces[0].shape
-    width = weight.shape[2]
+def down_part(chosen, count, before, last):
+    requests, units = chosen[0][0].shape
+    width = chosen[0][1].shape[2]
     if last:
         outs = [jax.ShapeDtypeStruct((2 * requests // count, width // 2), BF16)] * count
     else:
         outs = [jax.ShapeDtypeStruct((requests, width), F32)]
-    return pl.pallas_call(
-        functools.partial(down_kernel, count=count, first=first, last=last),
-        in_specs=[vmem] * (3 if first else 4),
+    before = [] if before is None else [before]
+    return pl.pallas_call(
+        functools.partial(
+            down_kernel,
+            parts=tuple(part for _, _, part in chosen),
+            count=count,
+            first=not before,
+            last=last,
+        ),
+        in_specs=[vmem] * (2 * len(chosen) + len(before)),
         out_specs=[vmem] * len(outs),
         out_shape=outs,
         compiler_params=params(8),
-        cost_estimate=pl.CostEstimate(
-            flops=4 * requests * units * width,
-            bytes_accessed=2 * units * width,
-            transcendentals=0,
-        ),
+        cost_estimate=product_cost(requests, len(chosen) * units, width),
         name="down",
-    )(*pieces, in_vmem(weight), *([] if first else [before]))
+    )(*[piece for piece, _, _ in chosen], *[in_vmem(w) for _, w, _ in chosen], *before)
 
 
 def swaps_of(blocks):
@@ -635,44 +688,46 @@
     table = jnp.concatenate([own, lengths, assignment])
     own_queries = queries.reshape(slots, heads, lanes)
     query_blocks = swaps_of([own_queries] * count)
-    keys, values = fetch([key_cache, value_cache])
-    *blocks, weight = attention(
-        table, query_blocks, keys, values, out_weight.reshape(-1, columns)
-    )
+    keys, values = fetch(table, [(key_cache, None), (value_cache, None)], parts)
+    jobs = [(out_weight.reshape(-1, columns), (0, 1, 2, 3)), (down_weight, (0, 1))]
+    *blocks, project, down_near = attention(table, query_blocks, keys, values, jobs, parts)
 
     blocks = swaps_of(blocks)
     piece = jnp.concatenate(blocks, axis=0)
     across = pair_swap(piece, "ffn", 2)
     beside = pair_swap(piece, "ffn", 1)
     corner = pair_swap(across, "ffn", 1)
-    partial = projection(table, [piece, beside, across, corner], weight, slots, count)
-    (gate,) = fetch([gate_weight])
+    *partial, down_far = projection(
+        table, [piece, beside, across, corner], project, slots, count, [(down_weight, (2, 3))]
+    )
+    jobs = [(gate_weight, (0, 1, 2, 3)), (up_weight, (3,))]
+    gate, up_corner = fetch(table, jobs, parts)
     middle = residual(hidden_state, swaps_of(partial), False)
 
     rows = swaps_of([middle] * count)
-    (up,) = fetch([up_weight])
-    gain = norm_gain.reshape(1, columns)
-    far_send, far_keep, scaled, down_chip = hidden_far(
-        table, rows, gain, gate, up, down_weight, parts
-    )
-    far, squares = chip_sum(far_keep, pair_swap(far_send, "ffn", 1))
-    far = pair_swap(far, "ffn", 2)
-    near_send, near_keep, down_other = hidden_near(
-        table, scaled, gate, up, down_weight, parts
-    )
-    near_beside = pair_swap(near_send, "ffn", 1)
-    active = active_units(near_keep, near_beside, far, squares, model_width)
+    (up,) = fetch(table, [(up_weight, (0, 1, 2))], parts)
+    send, scaled, squares = hidden_first(rows, norm_gain.reshape(1, columns), gate, 3)
+    arrived = pair_swap(send, "ffn", 1)
+    keep = hidden_next(scaled, [(gate, 2)], F32)
+    far_gate, squares = squares_sum(keep, squares, arrived)
+    far_gate = pair_swap(far_gate, "ffn", 2)
+    send = hidden_next(scaled, [(up_corner, 0)], BF16)
+    arrived = pair_swap(send, "ffn", 1)
+    keep = hidden_next(scaled, [(up, 2)], F32)
+    far_up = pair_swap(chip_sum(keep, arrived), "ffn", 2)
+    send = hidden_next(scaled, [(gate, 1), (up, 1)], BF16)
+    arrived = pair_swap(send, "ffn", 1)
+    keep = hidden_next(scaled, [(gate, 0), (up, 0)], F32)
+    active = active_units(keep, arrived, far_gate, far_up, squares, model_width)
 
     across = pair_swap(active, "ffn", 2)
     beside = pair_swap(active, "ffn", 1)
-    (before,) = down_part([active, beside], down_chip, count)
+    chosen = [(active, down_near, 0), (beside, down_near, 1)]
+    (before,) = down_part(chosen, count, None, False)
     corner = pair_swap(across, "ffn", 1)
-    partial = down_part([across, corner], down_other, count, before, True)
-    return residual_joined(middle, swaps_of(partial))
-
-
-def residual_joined(middle, blocks):
-    return residual(middle, blocks, True)
+    (before,) = down_part([(across, down_far, 0)], count, before, False)
+    partial = down_part([(corner, down_far, 1)], count, before, True)
+    return residual(middle, swaps_of(partial), True)
 
 
 def solution(mesh):

time: 102 us -> 102 us (level)
  starting transfers between devices: 26.7 us -> 29.1 us
  waiting for transfers between devices: 31.1 us -> 29.1 us
  Pallas kernels: 43.2 us -> 41.3 us
    pallas_call x8 -> x14, Pallas kernels: 33.9 us -> 29.8 us  [the longest x3 16.9 us: fetch(): pl.pallas_call(functools.partial(fetch_kernel, masks_of=masks_in(jobs)),...]
    ppermute x24 -> x26, starting transfers between devices: 26.7 us -> 29.1 us  [pair_swap(): return lax.ppermute(value, axis, [(i, i ^ bit) for i in range(count)])]
    ppermute x24 -> x26, waiting for transfers between devices: 31.1 us -> 29.1 us  [pair_swap(): return lax.ppermute(value, axis, [(i, i ^ bit) for i in range(count)])]
    pallas_call x1, Pallas kernels: 2.73 us -> 4.32 us  [projection(): pl.pallas_call(functools.partial(projection_kernel, slots=slots, count=co...]
  transfers between devices with their start and end apart: 24 -> 26, of which waited for: 12 -> 11; matrix products, arithmetic and copies ran while one was open for 0% -> 1% of each run, Pallas kernels for 24% -> 26%
where the time goes in v3:
time: 102 us; the launch traced here: 101 us
  Pallas kernels  41.3 us (40%)
  starting transfers between devices  29.1 us (29%)
  waiting for transfers between devices  29.1 us (29%)
    ppermute x26, waiting for transfers between devices, pair_swap(): return lax.ppermute(value, axis, [(i, i ^ bit) for i in range(count)])  29.1 us
    ppermute x26, starting transfers between devices, pair_swap(): return lax.ppermute(value, axis, [(i, i ^ bit) for i in range(count)])  29.1 us
    pallas_call x3, Pallas kernels, fetch(): pl.pallas_call(functools.partial(fetch_kernel, masks_of=masks_in(jobs)),...  16.9 us
    pallas_call x5, Pallas kernels, hidden_next(): pl.pallas_call(functools.partial(hidden_kernel, parts=tuple((part for _,...  8.32 us
    pallas_call x1, Pallas kernels, attention(): pl.pallas_call(functools.partial(attention_kernel, slots=slots, count=cou...  6.15 us
    pallas_call x1, Pallas kernels, projection(): pl.pallas_call(functools.partial(projection_kernel, slots=slots, count=co...  4.32 us
    pallas_call x3, Pallas kernels, down_part(): pl.pallas_call(functools.partial(down_kernel, parts=tuple((part for _, _,...  3.1 us
  transfers between devices with their start and end apart: 26, of which 11 were waited for; matrix products, arithmetic and copies ran while one was open for 1% of the time, Pallas kernels for 26%

profile of v3, /device:TPU:0, one launch (start us, length us, event | category | flops | bytes accessed | tf_op | source)
XLA Modules:
  0.0 101.4 jit_solution(16973881232425885004)
XLA Ops:
  0.9 3.1 %collective-permute-start = (bf16[20,16,128]{2,1,0:T(8,128)(2,1)S(1)}, bf16[20,16,128]{2,1,0:T(8,128)(2,1)S(1)}, u32[]{:S(2)}, u32[]{:S(2)}) collective-permute-start(bf16[20,16,128]{2,1,0:T(8,128)(2,1)S(1)} %slice.refs_0_), channel_id=1, source_target_pairs={{0,4},{4,0},{8,12},{12,8},{1,5},{5,1},{9,13},{13,9},{2,6},{6,2},{1... | collective-permute-start | bytes 245768 | tf_op jit(solution)/shard_map/ppermute | solution.py:126
  4.0 2.6 %collective-permute-start.1 = (bf16[20,16,128]{2,1,0:T(8,128)(2,1)S(1)}, bf16[20,16,128]{2,1,0:T(8,128)(2,1)S(1)}, u32[]{:S(2)}, u32[]{:S(2)}) collective-permute-start(bf16[20,16,128]{2,1,0:T(8,128)(2,1)S(1)} %slice.refs_0_), channel_id=1, source_target_pairs={{0,8},{4,12},{8,0},{12,4},{1,9},{5,13},{9,1},{13,5},{2,10},{6,14},... | collective-permute-start | bytes 245768 | tf_op jit(solution)/shard_map/ppermute | solution.py:126
  7.4 5.3 %fetch.3 = (bf16[12800,256]{1,0:T(8,128)(2,1)S(1)}, bf16[12800,256]{1,0:T(8,128)(2,1)S(1)}) custom-call(s32[102]{0:T(128)S(1)} %pad_add_fusion.table, bf16[12800,256]{1,0:T(8,128)(2,1)} %refs_0_.4, bf16[12800,256]{1,0:T(8,128)(2,1)} %refs_1_.2), custom_call_target="tpu_custom_call" | custom-call | bytes 26214400 | tf_op jit(solution)/shard_map/fetch/pallas_call | solution.py:209
  13.2 6.2 %attention.1 = (bf16[24,512]{1,0:T(8,128)(2,1)S(1)}, bf16[24,512]{1,0:T(8,128)(2,1)S(1)}, bf16[24,512]{1,0:T(8,128)(2,1)S(1)}, bf16[24,512]{1,0:T(8,128)(2,1)S(1...) custom-call(s32[102]{0:T(128)S(1)} %pad_add_fusion.table, bf16[20,16,128]{2,1,0:T(8,128)(2,1)S(1)} %slice.refs_0_, ...), custom_call_target="tpu_custom_call" | custom-call | flops 104857600 | bytes 13107200 | tf_op jit(solution)/shard_map/attention/pallas_call | solution.py:361
  20.9 3.5 %collective-permute-start.4 = (bf16[24,512]{1,0:T(8,128)(2,1)S(1)}, bf16[24,512]{1,0:T(8,128)(2,1)S(1)}, u32[]{:S(2)}, u32[]{:S(2)}) collective-permute-start(bf16[24,512]{1,0:T(8,128)(2,1)S(1)} %get-tuple-element.33), channel_id=1, source_target_pairs={{0,8},{4,12},{8,0},{12,4},{1,9},{5,13},{9,1},{13,5},{2,10},{6,14},... | collective-permute-start | bytes 73736 | tf_op jit(solution)/shard_map/ppermute | solution.py:126
  24.4 1.8 %collective-permute-done.4 = bf16[24,512]{1,0:T(8,128)(2,1)S(1)} collective-permute-done((bf16[24,512]{1,0:T(8,128)(2,1)S(1)}, bf16[24,512]{1,0:T(8,128)(2,1)S(1)}, u32[]{:S(2)}, u32[]{:S(2)}) %collective-permute-start.4) | collective-permute-done | bytes 24608 | tf_op jit(solution)/shard_map/ppermute | solution.py:126
  26.2 3.8 %collective-permute-done.5 = bf16[24,512]{1,0:T(8,128)(2,1)S(1)} collective-permute-done((bf16[24,512]{1,0:T(8,128)(2,1)S(1)}, bf16[24,512]{1,0:T(8,128)(2,1)S(1)}, u32[]{:S(2)}, u32[]{:S(2)}) %collective-permute-start.5) | collective-permute-done | bytes 24608 | tf_op jit(solution)/shard_map/ppermute | solution.py:126
  31.5 3.1 %collective-permute-done.7.refs_2_ = bf16[96,512]{1,0:T(8,128)(2,1)S(1)} collective-permute-done((bf16[96,512]{1,0:T(8,128)(2,1)S(1)}, bf16[96,512]{1,0:T(8,128)(2,1)S(1)}, u32[]{:S(2)}, u32[]{:S(2)}) %collective-permute-start.7) | collective-permute-done | bytes 98336 | tf_op jit(solution)/shard_map/ppermute | solution.py:126
  35.9 4.3 %projection.1 = (bf16[40,1024]{1,0:T(8,128)(2,1)S(1)}, bf16[40,1024]{1,0:T(8,128)(2,1)S(1)}, bf16[40,1024]{1,0:T(8,128)(2,1)S(1)}, bf16[40,1024]{1,0:T(8,128)(2,1)S(1)}, bf16[2,896,2048]{2,1,0:T(8,128)(2,1)S(1)}) custom-call(s32[102]{0:T(128)S(1)} %pad_add_fusion.table, bf16[96,512]{1,0:T(8,128)(2,1)S(1)} %constant_dynamic-update-slice_fusion.refs_0_, ...), custom_call_target="tpu_custom_call" | custom-call | flops 671088640 | bytes 4194304 | tf_op jit(solution)/shard_map/projection/pallas_call | solution.py:443
  41.0 2.8 %collective-permute-start.9 = (bf16[40,1024]{1,0:T(8,128)(2,1)S(1)}, bf16[40,1024]{1,0:T(8,128)(2,1)S(1)}, u32[]{:S(2)}, u32[]{:S(2)}) collective-permute-start(bf16[40,1024]{1,0:T(8,128)(2,1)S(1)} %get-tuple-element.37), channel_id=1, source_target_pairs={{0,4},{4,0},{8,12},{12,8},{1,5},{5,1},{9,13},{13,9},{2,6},{6,2},{1... | collective-permute-start | bytes 245768 | tf_op jit(solution)/shard_map/ppermute | solution.py:126
  43.8 4.5 %collective-permute-done.10.refs_3_ = bf16[40,1024]{1,0:T(8,128)(2,1)S(1)} collective-permute-done((bf16[40,1024]{1,0:T(8,128)(2,1)S(1)}, bf16[40,1024]{1,0:T(8,128)(2,1)S(1)}, u32[]{:S(2)}, u32[]{:S(2)}) %collective-permute-start.10) | collective-permute-done | bytes 81952 | tf_op jit(solution)/shard_map/ppermute | solution.py:126
  50.0 1.6 %collective-permute-start.13 = (bf16[40,1024]{1,0:T(8,128)(2,1)S(1)}, bf16[40,1024]{1,0:T(8,128)(2,1)S(1)}, u32[]{:S(2)}, u32[]{:S(2)}) collective-permute-start(bf16[40,1024]{1,0:T(8,128)(2,1)S(1)} %residual.2.refs_0_), channel_id=1, source_target_pairs={{0,8},{4,12},{8,0},{12,4},{1,9},{5,13},{9,1},{13,5},{2,10},{6,14},... | collective-permute-start | bytes 245768 | tf_op jit(solution)/shard_map/ppermute | solution.py:126
  51.5 2.2 %collective-permute-start.14 = (bf16[40,1024]{1,0:T(8,128)(2,1)S(1)}, bf16[40,1024]{1,0:T(8,128)(2,1)S(1)}, u32[]{:S(2)}, u32[]{:S(2)}) collective-permute-start(bf16[40,1024]{1,0:T(8,128)(2,1)S(1)} %residual.2.refs_0_), channel_id=1, source_target_pairs={{0,12},{4,8},{8,4},{12,0},{1,13},{5,9},{9,5},{13,1},{2,14},{6,10},... | collective-permute-start | bytes 245768 | tf_op jit(solution)/shard_map/ppermute | solution.py:126
  53.8 4.8 %fetch.5.refs_1_.refs_0_ = bf16[3,896,2048]{2,1,0:T(8,128)(2,1)S(1)} custom-call(s32[102]{0:T(128)S(1)} %pad_add_fusion.table, bf16[3584,2048]{1,0:T(8,128)(2,1)} %refs_0_.7), custom_call_target="tpu_custom_call" | custom-call | bytes 22020096 | tf_op jit(solution)/shard_map/fetch/pallas_call | solution.py:209
  58.6 6.9 %fetch.4 = (bf16[4,896,2048]{2,1,0:T(8,128)(2,1)S(1)}, bf16[1,896,2048]{2,1,0:T(8,128)(2,1)S(1)}) custom-call(s32[102]{0:T(128)S(1)} %pad_add_fusion.table, bf16[3584,2048]{1,0:T(8,128)(2,1)} %refs_0_.6, bf16[3584,2048]{1,0:T(8,128)(2,1)} %refs_0_.7), custom_call_target="tpu_custom_call" | custom-call | bytes 36700160 | tf_op jit(solution)/shard_map/fetch/pallas_call | solution.py:209
  68.6 2.3 %hidden_next.6 = bf16[80,1792]{1,0:T(8,128)(2,1)S(1)} custom-call(bf16[80,2048]{1,0:T(8,128)(2,1)S(1)} %get-tuple-element.41.scaled, bf16[4,896,2048]{2,1,0:T(8,128)(2,1)S(1)} %get-tuple-element.40.refs_5_.refs_0_, bf16[3,896,2048]{2,1,0:T(8,128)(2,1)S(1)} %fetch.5.refs_1_.refs_0_), custom_call_target="tpu_custom_call" | custom-call | flops 587202560 | bytes 3670016 | tf_op jit(solution)/shard_map/hidden_next/pallas_call | solution.py:542
  75.9 2.3 %hidden_next.5.near = f32[80,1792]{1,0:T(8,128)S(1)} custom-call(bf16[80,2048]{1,0:T(8,128)(2,1)S(1)} %get-tuple-element.41.scaled, bf16[4,896,2048]{2,1,0:T(8,128)(2,1)S(1)} %get-tuple-element.40.refs_5_.refs_0_, bf16[3,896,2048]{2,1,0:T(8,128)(2,1)S(1)} %fetch.5.refs_1_.refs_0_), custom_call_target="tpu_custom_call" | custom-call | flops 587202560 | bytes 3670016 | tf_op jit(solution)/shard_map/hidden_next/pallas_call | solution.py:542
  78.2 3.9 %collective-permute-done.19.far_up = bf16[80,896]{1,0:T(8,128)(2,1)S(1)} collective-permute-done((bf16[80,896]{1,0:T(8,128)(2,1)S(1)}, bf16[80,896]{1,0:T(8,128)(2,1)S(1)}, u32[]{:S(2)}, u32[]{:S(2)}) %collective-permute-start.19) | collective-permute-done | bytes 143392 | tf_op jit(solution)/shard_map/ppermute | solution.py:126
  82.4 1.6 %collective-permute-start.20 = (bf16[80,896]{1,0:T(8,128)(2,1)S(1)}, bf16[80,896]{1,0:T(8,128)(2,1)S(1)}, u32[]{:S(2)}, u32[]{:S(2)}) collective-permute-start(bf16[80,896]{1,0:T(8,128)(2,1)S(1)} %active.1.refs_0_), channel_id=1, source_target_pairs={{0,2},{1,3},{2,0},{3,1},{4,6},{5,7},{6,4},{7,5},{8,10},{9,11},{10,... | collective-permute-start | bytes 430088 | tf_op jit(solution)/shard_map/ppermute | solution.py:126
  83.9 3.7 %collective-permute-done.20.refs_0_ = bf16[80,896]{1,0:T(8,128)(2,1)S(1)} collective-permute-done((bf16[80,896]{1,0:T(8,128)(2,1)S(1)}, bf16[80,896]{1,0:T(8,128)(2,1)S(1)}, u32[]{:S(2)}, u32[]{:S(2)}) %collective-permute-start.20) | collective-permute-done | bytes 143392 | tf_op jit(solution)/shard_map/ppermute | solution.py:126
  90.9 2.1 %collective-permute-start.24 = (bf16[40,1024]{1,0:T(8,128)(2,1)S(1)}, bf16[40,1024]{1,0:T(8,128)(2,1)S(1)}, u32[]{:S(2)}, u32[]{:S(2)}) collective-permute-start(bf16[40,1024]{1,0:T(8,128)(2,1)S(1)} %get-tuple-element.51), channel_id=1, source_target_pairs={{0,8},{4,12},{8,0},{12,4},{1,9},{5,13},{9,1},{13,5},{2,10},{6,14},... | collective-permute-start | bytes 245768 | tf_op jit(solution)/shard_map/ppermute | solution.py:126
  93.0 2.2 %collective-permute-start.25 = (bf16[40,1024]{1,0:T(8,128)(2,1)S(1)}, bf16[40,1024]{1,0:T(8,128)(2,1)S(1)}, u32[]{:S(2)}, u32[]{:S(2)}) collective-permute-start(bf16[40,1024]{1,0:T(8,128)(2,1)S(1)} %get-tuple-element.52), channel_id=1, source_target_pairs={{0,12},{4,8},{8,4},{12,0},{1,13},{5,9},{9,5},{13,1},{2,14},{6,10},... | collective-permute-start | bytes 245768 | tf_op jit(solution)/shard_map/ppermute | solution.py:126
  95.3 1.6 %collective-permute-done.23.refs_2_ = bf16[40,1024]{1,0:T(8,128)(2,1)S(1)} collective-permute-done((bf16[40,1024]{1,0:T(8,128)(2,1)S(1)}, bf16[40,1024]{1,0:T(8,128)(2,1)S(1)}, u32[]{:S(2)}, u32[]{:S(2)}) %collective-permute-start.23) | collective-permute-done | bytes 81952 | tf_op jit(solution)/shard_map/ppermute | solution.py:126
  96.9 3.8 %collective-permute-done.24.refs_3_ = bf16[40,1024]{1,0:T(8,128)(2,1)S(1)} collective-permute-done((bf16[40,1024]{1,0:T(8,128)(2,1)S(1)}, bf16[40,1024]{1,0:T(8,128)(2,1)S(1)}, u32[]{:S(2)}, u32[]{:S(2)}) %collective-permute-start.24) | collective-permute-done | bytes 81952 | tf_op jit(solution)/shard_map/ppermute | solution.py:126
  (59 shorter events, 21.0 us)
Async XLA Ops:
  0.9 11.8 %collective-permute-start = (bf16[20,16,128]{2,1,0:T(8,128)(2,1)S(1)}, bf16[20,16,128]{2,1,0:T(8,128)(2,1)S(1)}, u32[]{:S(2)}, u32[]{:S(2)}) collective-permute-start(bf16[20,16,128]{2,1,0:T(8,128)(2,1)S(1)} %slice.refs_0_), channel_id=1, source_target_pairs={{0,4},{4,0},{8,12},{12,8},{1,5},{5,1},{9,13},{13,9},{2,6},{6,2},{1... | collective-permute-start | bytes 245768 | tf_op jit(solution)/shard_map/ppermute | solution.py:126
  4.0 9.2 %collective-permute-start.1 = (bf16[20,16,128]{2,1,0:T(8,128)(2,1)S(1)}, bf16[20,16,128]{2,1,0:T(8,128)(2,1)S(1)}, u32[]{:S(2)}, u32[]{:S(2)}) collective-permute-start(bf16[20,16,128]{2,1,0:T(8,128)(2,1)S(1)} %slice.refs_0_), channel_id=1, source_target_pairs={{0,8},{4,12},{8,0},{12,4},{1,9},{5,13},{9,1},{13,5},{2,10},{6,14},... | collective-permute-start | bytes 245768 | tf_op jit(solution)/shard_map/ppermute | solution.py:126
  6.6 6.6 %collective-permute-start.2 = (bf16[20,16,128]{2,1,0:T(8,128)(2,1)S(1)}, bf16[20,16,128]{2,1,0:T(8,128)(2,1)S(1)}, u32[]{:S(2)}, u32[]{:S(2)}) collective-permute-start(bf16[20,16,128]{2,1,0:T(8,128)(2,1)S(1)} %slice.refs_0_), channel_id=1, source_target_pairs={{0,12},{4,8},{8,4},{12,0},{1,13},{5,9},{9,5},{13,1},{2,14},{6,10},... | collective-permute-start | bytes 245768 | tf_op jit(solution)/shard_map/ppermute | solution.py:126
  19.4 5.0 %collective-permute-start.3 = (bf16[24,512]{1,0:T(8,128)(2,1)S(1)}, bf16[24,512]{1,0:T(8,128)(2,1)S(1)}, u32[]{:S(2)}, u32[]{:S(2)}) collective-permute-start(bf16[24,512]{1,0:T(8,128)(2,1)S(1)} %get-tuple-element.32), channel_id=1, source_target_pairs={{0,4},{4,0},{8,12},{12,8},{1,5},{5,1},{9,13},{13,9},{2,6},{6,2},{1... | collective-permute-start | bytes 73736 | tf_op jit(solution)/shard_map/ppermute | solution.py:126
  20.9 5.3 %collective-permute-start.4 = (bf16[24,512]{1,0:T(8,128)(2,1)S(1)}, bf16[24,512]{1,0:T(8,128)(2,1)S(1)}, u32[]{:S(2)}, u32[]{:S(2)}) collective-permute-start(bf16[24,512]{1,0:T(8,128)(2,1)S(1)} %get-tuple-element.33), channel_id=1, source_target_pairs={{0,8},{4,12},{8,0},{12,4},{1,9},{5,13},{9,1},{13,5},{2,10},{6,14},... | collective-permute-start | bytes 73736 | tf_op jit(solution)/shard_map/ppermute | solution.py:126
  24.4 5.6 %collective-permute-start.5 = (bf16[24,512]{1,0:T(8,128)(2,1)S(1)}, bf16[24,512]{1,0:T(8,128)(2,1)S(1)}, u32[]{:S(2)}, u32[]{:S(2)}) collective-permute-start(bf16[24,512]{1,0:T(8,128)(2,1)S(1)} %get-tuple-element.34), channel_id=1, source_target_pairs={{0,12},{4,8},{8,4},{12,0},{1,13},{5,9},{9,5},{13,1},{2,14},{6,10},... | collective-permute-start | bytes 73736 | tf_op jit(solution)/shard_map/ppermute | solution.py:126
  30.0 4.6 %collective-permute-start.7 = (bf16[96,512]{1,0:T(8,128)(2,1)S(1)}, bf16[96,512]{1,0:T(8,128)(2,1)S(1)}, u32[]{:S(2)}, u32[]{:S(2)}) collective-permute-start(bf16[96,512]{1,0:T(8,128)(2,1)S(1)} %constant_dynamic-update-slice_fusion.refs_0_), channel_id=1, source_target_pairs={{0,2},{1,3},{2,0},{3,1},{4,6},{5,7},{6,4},{7,5},{8,10},{9,11},{10,... | collective-permute-start | bytes 294920 | tf_op jit(solution)/shard_map/ppermute | solution.py:126
  31.5 3.1 %collective-permute-start.6 = (bf16[96,512]{1,0:T(8,128)(2,1)S(1)}, bf16[96,512]{1,0:T(8,128)(2,1)S(1)}, u32[]{:S(2)}, u32[]{:S(2)}) collective-permute-start(bf16[96,512]{1,0:T(8,128)(2,1)S(1)} %constant_dynamic-update-slice_fusion.refs_0_), channel_id=1, source_target_pairs={{0,1},{1,0},{2,3},{3,2},{4,5},{5,4},{6,7},{7,6},{8,9},{9,8},{10,11... | collective-permute-start | bytes 294920 | tf_op jit(solution)/shard_map/ppermute | solution.py:126
  40.3 8.0 %collective-permute-start.10 = (bf16[40,1024]{1,0:T(8,128)(2,1)S(1)}, bf16[40,1024]{1,0:T(8,128)(2,1)S(1)}, u32[]{:S(2)}, u32[]{:S(2)}) collective-permute-start(bf16[40,1024]{1,0:T(8,128)(2,1)S(1)} %get-tuple-element.38), channel_id=1, source_target_pairs={{0,8},{4,12},{8,0},{12,4},{1,9},{5,13},{9,1},{13,5},{2,10},{6,14},... | collective-permute-start | bytes 245768 | tf_op jit(solution)/shard_map/ppermute | solution.py:126
  40.4 8.0 %collective-permute-start.11 = (bf16[40,1024]{1,0:T(8,128)(2,1)S(1)}, bf16[40,1024]{1,0:T(8,128)(2,1)S(1)}, u32[]{:S(2)}, u32[]{:S(2)}) collective-permute-start(bf16[40,1024]{1,0:T(8,128)(2,1)S(1)} %get-tuple-element.39), channel_id=1, source_target_pairs={{0,12},{4,8},{8,4},{12,0},{1,13},{5,9},{9,5},{13,1},{2,14},{6,10},... | collective-permute-start | bytes 245768 | tf_op jit(solution)/shard_map/ppermute | solution.py:126
  41.0 8.3 %collective-permute-start.9 = (bf16[40,1024]{1,0:T(8,128)(2,1)S(1)}, bf16[40,1024]{1,0:T(8,128)(2,1)S(1)}, u32[]{:S(2)}, u32[]{:S(2)}) collective-permute-start(bf16[40,1024]{1,0:T(8,128)(2,1)S(1)} %get-tuple-element.37), channel_id=1, source_target_pairs={{0,4},{4,0},{8,12},{12,8},{1,5},{5,1},{9,13},{13,9},{2,6},{6,2},{1... | collective-permute-start | bytes 245768 | tf_op jit(solution)/shard_map/ppermute | solution.py:126
  49.3 16.2 %collective-permute-start.12 = (bf16[40,1024]{1,0:T(8,128)(2,1)S(1)}, bf16[40,1024]{1,0:T(8,128)(2,1)S(1)}, u32[]{:S(2)}, u32[]{:S(2)}) collective-permute-start(bf16[40,1024]{1,0:T(8,128)(2,1)S(1)} %residual.2.refs_0_), channel_id=1, source_target_pairs={{0,4},{4,0},{8,12},{12,8},{1,5},{5,1},{9,13},{13,9},{2,6},{6,2},{1... | collective-permute-start | bytes 245768 | tf_op jit(solution)/shard_map/ppermute | solution.py:126
  50.0 15.5 %collective-permute-start.13 = (bf16[40,1024]{1,0:T(8,128)(2,1)S(1)}, bf16[40,1024]{1,0:T(8,128)(2,1)S(1)}, u32[]{:S(2)}, u32[]{:S(2)}) collective-permute-start(bf16[40,1024]{1,0:T(8,128)(2,1)S(1)} %residual.2.refs_0_), channel_id=1, source_target_pairs={{0,8},{4,12},{8,0},{12,4},{1,9},{5,13},{9,1},{13,5},{2,10},{6,14},... | collective-permute-start | bytes 245768 | tf_op jit(solution)/shard_map/ppermute | solution.py:126
  51.5 14.0 %collective-permute-start.14 = (bf16[40,1024]{1,0:T(8,128)(2,1)S(1)}, bf16[40,1024]{1,0:T(8,128)(2,1)S(1)}, u32[]{:S(2)}, u32[]{:S(2)}) collective-permute-start(bf16[40,1024]{1,0:T(8,128)(2,1)S(1)} %residual.2.refs_0_), channel_id=1, source_target_pairs={{0,12},{4,8},{8,4},{12,0},{1,13},{5,9},{9,5},{13,1},{2,14},{6,10},... | collective-permute-start | bytes 245768 | tf_op jit(solution)/shard_map/ppermute | solution.py:126
  68.0 7.2 %collective-permute-start.18 = (bf16[80,896]{1,0:T(8,128)(2,1)S(1)}, bf16[80,896]{1,0:T(8,128)(2,1)S(1)}, u32[]{:S(2)}, u32[]{:S(2)}) collective-permute-start(bf16[80,896]{1,0:T(8,128)(2,1)S(1)} %hidden_next.9), channel_id=1, source_target_pairs={{0,1},{1,0},{2,3},{3,2},{4,5},{5,4},{6,7},{7,6},{8,9},{9,8},{10,11... | collective-permute-start | bytes 430088 | tf_op jit(solution)/shard_map/ppermute | solution.py:126
  68.1 4.2 %collective-permute-start.16 = (bf16[80,1024]{1,0:T(8,128)(2,1)S(1)}, bf16[80,1024]{1,0:T(8,128)(2,1)S(1)}, u32[]{:S(2)}, u32[]{:S(2)}) collective-permute-start(bf16[80,1024]{1,0:T(8,128)(2,1)S(1)} %get-tuple-element.43), channel_id=1, source_target_pairs={{0,1},{1,0},{2,3},{3,2},{4,5},{5,4},{6,7},{7,6},{8,9},{9,8},{10,11... | collective-permute-start | bytes 491528 | tf_op jit(solution)/shard_map/ppermute | solution.py:126
  70.9 7.3 %collective-permute-start.15 = (bf16[80,1792]{1,0:T(8,128)(2,1)S(1)}, bf16[80,1792]{1,0:T(8,128)(2,1)S(1)}, u32[]{:S(2)}, u32[]{:S(2)}) collective-permute-start(bf16[80,1792]{1,0:T(8,128)(2,1)S(1)} %hidden_next.6), channel_id=1, source_target_pairs={{0,1},{1,0},{2,3},{3,2},{4,5},{5,4},{6,7},{7,6},{8,9},{9,8},{10,11... | collective-permute-start | bytes 860168 | tf_op jit(solution)/shard_map/ppermute | solution.py:126
  72.4 9.7 %collective-permute-start.17 = (bf16[80,1024]{1,0:T(8,128)(2,1)S(1)}, bf16[80,1024]{1,0:T(8,128)(2,1)S(1)}, u32[]{:S(2)}, u32[]{:S(2)}) collective-permute-start(bf16[80,1024]{1,0:T(8,128)(2,1)S(1)} %get-tuple-element.44), channel_id=1, source_target_pairs={{0,2},{1,3},{2,0},{3,1},{4,6},{5,7},{6,4},{7,5},{8,10},{9,11},{10,... | collective-permute-start | bytes 491528 | tf_op jit(solution)/shard_map/ppermute | solution.py:126
  75.3 6.8 %collective-permute-start.19 = (bf16[80,896]{1,0:T(8,128)(2,1)S(1)}, bf16[80,896]{1,0:T(8,128)(2,1)S(1)}, u32[]{:S(2)}, u32[]{:S(2)}) collective-permute-start(bf16[80,896]{1,0:T(8,128)(2,1)S(1)} %chip_sum.1), channel_id=1, source_target_pairs={{0,2},{1,3},{2,0},{3,1},{4,6},{5,7},{6,4},{7,5},{8,10},{9,11},{10,... | collective-permute-start | bytes 430088 | tf_op jit(solution)/shard_map/ppermute | solution.py:126
  82.4 5.3 %collective-permute-start.20 = (bf16[80,896]{1,0:T(8,128)(2,1)S(1)}, bf16[80,896]{1,0:T(8,128)(2,1)S(1)}, u32[]{:S(2)}, u32[]{:S(2)}) collective-permute-start(bf16[80,896]{1,0:T(8,128)(2,1)S(1)} %active.1.refs_0_), channel_id=1, source_target_pairs={{0,2},{1,3},{2,0},{3,1},{4,6},{5,7},{6,4},{7,5},{8,10},{9,11},{10,... | collective-permute-start | bytes 430088 | tf_op jit(solution)/shard_map/ppermute | solution.py:126
  83.9 3.8 %collective-permute-start.22 = (bf16[80,896]{1,0:T(8,128)(2,1)S(1)}, bf16[80,896]{1,0:T(8,128)(2,1)S(1)}, u32[]{:S(2)}, u32[]{:S(2)}) collective-permute-start(bf16[80,896]{1,0:T(8,128)(2,1)S(1)} %active.1.refs_0_), channel_id=1, source_target_pairs={{0,1},{1,0},{2,3},{3,2},{4,5},{5,4},{6,7},{7,6},{8,9},{9,8},{10,11... | collective-permute-start | bytes 430088 | tf_op jit(solution)/shard_map/ppermute | solution.py:126
  90.8 6.1 %collective-permute-start.23 = (bf16[40,1024]{1,0:T(8,128)(2,1)S(1)}, bf16[40,1024]{1,0:T(8,128)(2,1)S(1)}, u32[]{:S(2)}, u32[]{:S(2)}) collective-permute-start(bf16[40,1024]{1,0:T(8,128)(2,1)S(1)} %get-tuple-element.50), channel_id=1, source_target_pairs={{0,4},{4,0},{8,12},{12,8},{1,5},{5,1},{9,13},{13,9},{2,6},{6,2},{1... | collective-permute-start | bytes 245768 | tf_op jit(solution)/shard_map/ppermute | solution.py:126
  90.9 9.8 %collective-permute-start.24 = (bf16[40,1024]{1,0:T(8,128)(2,1)S(1)}, bf16[40,1024]{1,0:T(8,128)(2,1)S(1)}, u32[]{:S(2)}, u32[]{:S(2)}) collective-permute-start(bf16[40,1024]{1,0:T(8,128)(2,1)S(1)} %get-tuple-element.51), channel_id=1, source_target_pairs={{0,8},{4,12},{8,0},{12,4},{1,9},{5,13},{9,1},{13,5},{2,10},{6,14},... | collective-permute-start | bytes 245768 | tf_op jit(solution)/shard_map/ppermute | solution.py:126
  93.0 7.7 %collective-permute-start.25 = (bf16[40,1024]{1,0:T(8,128)(2,1)S(1)}, bf16[40,1024]{1,0:T(8,128)(2,1)S(1)}, u32[]{:S(2)}, u32[]{:S(2)}) collective-permute-start(bf16[40,1024]{1,0:T(8,128)(2,1)S(1)} %get-tuple-element.52), channel_id=1, source_target_pairs={{0,12},{4,8},{8,4},{12,0},{1,13},{5,9},{9,5},{13,1},{2,14},{6,10},... | collective-permute-start | bytes 245768 | tf_op jit(solution)/shard_map/ppermute | solution.py:126
  (4 other events, 23.8 us)

commit v4 on v3

--- a/solution.py
+++ b/solution.py
@@ -194,9 +194,11 @@
     return tuple(masks for _, masks in jobs)
 
 
-def fetch_kernel(table, *refs, masks_of):
+def fetch_kernel(*refs, masks_of, placed):
+    own = refs[0][1] if placed else None
+    refs = refs[1:] if placed else refs
     count = len(masks_of)
-    copies = job_copies(table[1], masks_of, refs[:count], refs[count:-1], refs[-1])
+    copies = job_copies(own, masks_of, refs[:count], refs[count:-1], refs[-1])
     for copy in copies:
         copy.start()
     for copy in copies:
@@ -205,17 +207,18 @@
 
 def fetch(table, jobs, parts):
     shapes = job_shapes(jobs, parts)
+    placed = any(masks is not None for _, masks in jobs)
     moved = sum(2 * math.prod(shape.shape) for shape in shapes)
     return pl.pallas_call(
-        functools.partial(fetch_kernel, masks_of=masks_in(jobs)),
-        in_specs=[smem] + [hbm] * len(jobs),
+        functools.partial(fetch_kernel, masks_of=masks_in(jobs), placed=placed),
+        in_specs=([smem] if placed else []) + [hbm] * len(jobs),
         out_specs=[vmem] * len(jobs),
         out_shape=shapes,
         scratch_shapes=[pltpu.SemaphoreType.DMA((job_count(jobs),))],
         compiler_params=params(1),
         cost_estimate=pl.CostEstimate(flops=0, bytes_accessed=2 * moved, transcendentals=0),
         name="fetch",
-    )(table, *[in_hbm(array) for array, _ in jobs])
+    )(*([table] if placed else []), *[in_hbm(array) for array, _ in jobs])
 
 
 def folded(combine, value):
@@ -398,12 +401,8 @@
     )
 
 
-def projection_kernel(table, *refs, slots, count, parts, masks_of):
-    pieces, weight, source = refs[:parts], refs[parts], refs[parts + 1]
-    outs, target, sems = refs[parts + 2 : -2], refs[-2], refs[-1]
-    copies = job_copies(table[1], masks_of, [source], [target], sems)
-    for copy in copies:
-        copy.start()
+def projection_kernel(table, *refs, slots, count, parts):
+    pieces, weight, outs = refs[:parts], refs[parts], refs[parts + 1 :]
     own_att = table[0]
     requests = slots * count
     padded = pieces[0].shape[0] // count
@@ -434,21 +433,15 @@
         total = term if total is None else total + term
     for k in range(count):
         outs[k][...] = halves_stacked(total[k * slots : (k + 1) * slots]).astype(BF16)
-    for copy in copies:
-        copy.wait()
-
-
-def projection(table, pieces, weight, slots, count, jobs):
+
+
+def projection(table, pieces, weight, slots, count):
     parts, depth, width = weight.shape
     return pl.pallas_call(
-        functools.partial(
-            projection_kernel, slots=slots, count=count, parts=parts, masks_of=masks_in(jobs)
-        ),
-        in_specs=[smem] + [vmem] * (1 + parts) + [hbm],
-        out_specs=[vmem] * (count + 1),
-        out_shape=[jax.ShapeDtypeStruct((2 * slots, width // 2), BF16)] * count
-        + job_shapes(jobs, parts),
-        scratch_shapes=[pltpu.SemaphoreType.DMA((job_count(jobs),))],
+        functools.partial(projection_kernel, slots=slots, count=count, parts=parts),
+        in_specs=[smem] + [vmem] * (1 + parts),
+        out_specs=[vmem] * count,
+        out_shape=[jax.ShapeDtypeStruct((2 * slots, width // 2), BF16)] * count,
         compiler_params=params(8),
         cost_estimate=pl.CostEstimate(
             flops=2 * slots * count * parts * depth * width,
@@ -456,7 +449,7 @@
             transcendentals=0,
         ),
         name="projection",
-    )(table, *pieces, in_vmem(weight), in_hbm(jobs[0][0]))
+    )(table, *pieces, in_vmem(weight))
 
 
 def residual_kernel(*refs, joined):
@@ -693,20 +686,21 @@
     *blocks, project, down_near = attention(table, query_blocks, keys, values, jobs, parts)
 
     blocks = swaps_of(blocks)
+    (down_across,) = fetch(table, [(down_weight, (2,))], parts)
     piece = jnp.concatenate(blocks, axis=0)
     across = pair_swap(piece, "ffn", 2)
     beside = pair_swap(piece, "ffn", 1)
     corner = pair_swap(across, "ffn", 1)
-    *partial, down_far = projection(
-        table, [piece, beside, across, corner], project, slots, count, [(down_weight, (2, 3))]
-    )
+    (down_corner,) = fetch(table, [(down_weight, (3,))], parts)
+    gain = norm_gain.reshape(1, columns)
+    partial = projection(table, [piece, beside, across, corner], project, slots, count)
     jobs = [(gate_weight, (0, 1, 2, 3)), (up_weight, (3,))]
     gate, up_corner = fetch(table, jobs, parts)
     middle = residual(hidden_state, swaps_of(partial), False)
 
     rows = swaps_of([middle] * count)
     (up,) = fetch(table, [(up_weight, (0, 1, 2))], parts)
-    send, scaled, squares = hidden_first(rows, norm_gain.reshape(1, columns), gate, 3)
+    send, scaled, squares = hidden_first(rows, gain, gate, 3)
     arrived = pair_swap(send, "ffn", 1)
     keep = hidden_next(scaled, [(gate, 2)], F32)
     far_gate, squares = squares_sum(keep, squares, arrived)
@@ -725,8 +719,8 @@
     chosen = [(active, down_near, 0), (beside, down_near, 1)]
     (before,) = down_part(chosen, count, None, False)
     corner = pair_swap(across, "ffn", 1)
-    (before,) = down_part([(across, down_far, 0)], count, before, False)
-    partial = down_part([(corner, down_far, 1)], count, before, True)
+    (before,) = down_part([(across, down_across, 0)], count, before, False)
+    partial = down_part([(corner, down_corner, 0)], count, before, True)
     return residual(middle, swaps_of(partial), True)
 
 

time: 102 us -> 104 us (1.020)
  Pallas kernels: 41.3 us -> 44.4 us
    pallas_call x3 -> x5, Pallas kernels: 16.9 us -> 21.6 us  [fetch(): pl.pallas_call(functools.partial(fetch_kernel, masks_of=masks_in(jobs), p...]
    pallas_call x1, Pallas kernels: 4.32 us -> 2.73 us  [projection(): pl.pallas_call(functools.partial(projection_kernel, slots=slots, count=co...]
  transfers between devices with their start and end apart: 26 -> 26, of which waited for: 11 -> 11; matrix products, arithmetic and copies ran while one was open for 1% -> 0% of each run, Pallas kernels for 26% -> 30%
where the time goes in v4:
time: 104 us
  Pallas kernels  44.4 us (43%)
  waiting for transfers between devices  30 us (29%)
  starting transfers between devices  28.5 us (27%)
    ppermute x26, waiting for transfers between devices, pair_swap(): return lax.ppermute(value, axis, [(i, i ^ bit) for i in range(count)])  30 us
    ppermute x26, starting transfers between devices, pair_swap(): return lax.ppermute(value, axis, [(i, i ^ bit) for i in range(count)])  28.5 us
    pallas_call x5, Pallas kernels, fetch(): pl.pallas_call(functools.partial(fetch_kernel, masks_of=masks_in(jobs), p...  21.6 us
    pallas_call x5, Pallas kernels, hidden_next(): pl.pallas_call(functools.partial(hidden_kernel, parts=tuple((part for _,...  8.31 us
    pallas_call x1, Pallas kernels, attention(): pl.pallas_call(functools.partial(attention_kernel, slots=slots, count=cou...  6.15 us
    pallas_call x3, Pallas kernels, down_part(): pl.pallas_call(functools.partial(down_kernel, parts=tuple((part for _, _,...  3.1 us
    pallas_call x1, Pallas kernels, projection(): pl.pallas_call(functools.partial(projection_kernel, slots=slots, count=co...  2.73 us
  transfers between devices with their start and end apart: 26, of which 11 were waited for; matrix products, arithmetic and copies ran while one was open for 0% of the time, Pallas kernels for 30%

profile of v4, /device:TPU:0, one launch (start us, length us, event | category | flops | bytes accessed | tf_op | source)
XLA Modules:
  0.0 104.2 jit_solution(10517588667998483432)
XLA Ops:
  1.0 3.1 %collective-permute-start = (bf16[20,16,128]{2,1,0:T(8,128)(2,1)S(1)}, bf16[20,16,128]{2,1,0:T(8,128)(2,1)S(1)}, u32[]{:S(2)}, u32[]{:S(2)}) collective-permute-start(bf16[20,16,128]{2,1,0:T(8,128)(2,1)S(1)} %slice.refs_0_), channel_id=1, source_target_pairs={{0,4},{4,0},{8,12},{12,8},{1,5},{5,1},{9,13},{13,9},{2,6},{6,2},{1... | collective-permute-start | bytes 245768 | tf_op jit(solution)/shard_map/ppermute | solution.py:126
  4.1 2.6 %collective-permute-start.1 = (bf16[20,16,128]{2,1,0:T(8,128)(2,1)S(1)}, bf16[20,16,128]{2,1,0:T(8,128)(2,1)S(1)}, u32[]{:S(2)}, u32[]{:S(2)}) collective-permute-start(bf16[20,16,128]{2,1,0:T(8,128)(2,1)S(1)} %slice.refs_0_), channel_id=1, source_target_pairs={{0,8},{4,12},{8,0},{12,4},{1,9},{5,13},{9,1},{13,5},{2,10},{6,14},... | collective-permute-start | bytes 245768 | tf_op jit(solution)/shard_map/ppermute | solution.py:126
  6.7 4.8 %fetch.5 = (bf16[12800,256]{1,0:T(8,128)(2,1)S(1)}, bf16[12800,256]{1,0:T(8,128)(2,1)S(1)}) custom-call(bf16[12800,256]{1,0:T(8,128)(2,1)} %refs_0_.2, bf16[12800,256]{1,0:T(8,128)(2,1)} %refs_1_.5), custom_call_target="tpu_custom_call" | custom-call | bytes 26214400 | tf_op jit(solution)/shard_map/fetch/pallas_call | solution.py:212
  11.5 1.7 %collective-permute-done.1.refs_2_ = bf16[20,16,128]{2,1,0:T(8,128)(2,1)S(1)} collective-permute-done((bf16[20,16,128]{2,1,0:T(8,128)(2,1)S(1)}, bf16[20,16,128]{2,1,0:T(8,128)(2,1)S(1)}, u32[]{:S(2)}, u32[]{:S(2)}) %collective-permute-start.1) | collective-permute-done | bytes 81952 | tf_op jit(solution)/shard_map/ppermute | solution.py:126
  13.3 6.2 %attention.1 = (bf16[24,512]{1,0:T(8,128)(2,1)S(1)}, bf16[24,512]{1,0:T(8,128)(2,1)S(1)}, bf16[24,512]{1,0:T(8,128)(2,1)S(1)}, bf16[24,512]{1,0:T(8,128)(2,1)S(1...) custom-call(s32[102]{0:T(128)S(1)} %pad_add_fusion.table.refs_0_, ...), custom_call_target="tpu_custom_call" | custom-call | flops 104857600 | bytes 13107200 | tf_op jit(solution)/shard_map/attention/pallas_call | solution.py:364
  21.0 2.6 %collective-permute-start.4 = (bf16[24,512]{1,0:T(8,128)(2,1)S(1)}, bf16[24,512]{1,0:T(8,128)(2,1)S(1)}, u32[]{:S(2)}, u32[]{:S(2)}) collective-permute-start(bf16[24,512]{1,0:T(8,128)(2,1)S(1)} %get-tuple-element.32), channel_id=1, source_target_pairs={{0,8},{4,12},{8,0},{12,4},{1,9},{5,13},{9,1},{13,5},{2,10},{6,14},... | collective-permute-start | bytes 73736 | tf_op jit(solution)/shard_map/ppermute | solution.py:126
  23.9 2.0 %collective-permute-done.4 = bf16[24,512]{1,0:T(8,128)(2,1)S(1)} collective-permute-done((bf16[24,512]{1,0:T(8,128)(2,1)S(1)}, bf16[24,512]{1,0:T(8,128)(2,1)S(1)}, u32[]{:S(2)}, u32[]{:S(2)}) %collective-permute-start.4) | collective-permute-done | bytes 24608 | tf_op jit(solution)/shard_map/ppermute | solution.py:126
  25.9 3.3 %collective-permute-done.5 = bf16[24,512]{1,0:T(8,128)(2,1)S(1)} collective-permute-done((bf16[24,512]{1,0:T(8,128)(2,1)S(1)}, bf16[24,512]{1,0:T(8,128)(2,1)S(1)}, u32[]{:S(2)}, u32[]{:S(2)}) %collective-permute-start.5) | collective-permute-done | bytes 24608 | tf_op jit(solution)/shard_map/ppermute | solution.py:126
  30.7 3.1 %collective-permute-done.7.refs_2_ = bf16[96,512]{1,0:T(8,128)(2,1)S(1)} collective-permute-done((bf16[96,512]{1,0:T(8,128)(2,1)S(1)}, bf16[96,512]{1,0:T(8,128)(2,1)S(1)}, u32[]{:S(2)}, u32[]{:S(2)}) %collective-permute-start.7) | collective-permute-done | bytes 98336 | tf_op jit(solution)/shard_map/ppermute | solution.py:126
  35.1 2.7 %projection.1 = (bf16[40,1024]{1,0:T(8,128)(2,1)S(1)}, bf16[40,1024]{1,0:T(8,128)(2,1)S(1)}, bf16[40,1024]{1,0:T(8,128)(2,1)S(1)}, bf16[40,1024]{1,0:T(8,128)(2,1)S(1)}) custom-call(s32[102]{0:T(128)S(1)} %pad_add_fusion.table.refs_0_, bf16[96,512]{1,0:T(8,128)(2,1)S(1)} %constant_dynamic-update-slice_fusion.refs_0_, ...), custom_call_target="tpu_custom_call" | custom-call | flops 671088640 | bytes 4194304 | tf_op jit(solution)/shard_map/projection/pallas_call | solution.py:440
  38.9 2.5 %collective-permute-start.9 = (bf16[40,1024]{1,0:T(8,128)(2,1)S(1)}, bf16[40,1024]{1,0:T(8,128)(2,1)S(1)}, u32[]{:S(2)}, u32[]{:S(2)}) collective-permute-start(bf16[40,1024]{1,0:T(8,128)(2,1)S(1)} %get-tuple-element.36), channel_id=1, source_target_pairs={{0,4},{4,0},{8,12},{12,8},{1,5},{5,1},{9,13},{13,9},{2,6},{6,2},{1... | collective-permute-start | bytes 245768 | tf_op jit(solution)/shard_map/ppermute | solution.py:126
  41.4 4.5 %collective-permute-done.10.refs_3_ = bf16[40,1024]{1,0:T(8,128)(2,1)S(1)} collective-permute-done((bf16[40,1024]{1,0:T(8,128)(2,1)S(1)}, bf16[40,1024]{1,0:T(8,128)(2,1)S(1)}, u32[]{:S(2)}, u32[]{:S(2)}) %collective-permute-start.10) | collective-permute-done | bytes 81952 | tf_op jit(solution)/shard_map/ppermute | solution.py:126
  49.2 2.2 %collective-permute-start.14 = (bf16[40,1024]{1,0:T(8,128)(2,1)S(1)}, bf16[40,1024]{1,0:T(8,128)(2,1)S(1)}, u32[]{:S(2)}, u32[]{:S(2)}) collective-permute-start(bf16[40,1024]{1,0:T(8,128)(2,1)S(1)} %residual.2.refs_0_), channel_id=1, source_target_pairs={{0,12},{4,8},{8,4},{12,0},{1,13},{5,9},{9,5},{13,1},{2,14},{6,10},... | collective-permute-start | bytes 245768 | tf_op jit(solution)/shard_map/ppermute | solution.py:126
  51.4 4.8 %fetch.7.refs_1_.refs_0_ = bf16[3,896,2048]{2,1,0:T(8,128)(2,1)S(1)} custom-call(s32[102]{0:T(128)S(1)} %pad_add_fusion.table.refs_0_, bf16[3584,2048]{1,0:T(8,128)(2,1)} %refs_1_.7), custom_call_target="tpu_custom_call" | custom-call | bytes 22020096 | tf_op jit(solution)/shard_map/fetch/pallas_call | solution.py:212
  56.2 6.9 %fetch.6 = (bf16[4,896,2048]{2,1,0:T(8,128)(2,1)S(1)}, bf16[1,896,2048]{2,1,0:T(8,128)(2,1)S(1)}) custom-call(s32[102]{0:T(128)S(1)} %pad_add_fusion.table.refs_0_, bf16[3584,2048]{1,0:T(8,128)(2,1)} %refs_1_.6, bf16[3584,2048]{1,0:T(8,128)(2,1)} %refs_1_.7), custom_call_target="tpu_custom_call" | custom-call | bytes 36700160 | tf_op jit(solution)/shard_map/fetch/pallas_call | solution.py:212
  66.2 2.3 %hidden_next.6 = bf16[80,1792]{1,0:T(8,128)(2,1)S(1)} custom-call(bf16[80,2048]{1,0:T(8,128)(2,1)S(1)} %get-tuple-element.40.scaled, bf16[4,896,2048]{2,1,0:T(8,128)(2,1)S(1)} %get-tuple-element.39.refs_5_.refs_0_, bf16[3,896,2048]{2,1,0:T(8,128)(2,1)S(1)} %fetch.7.refs_1_.refs_0_), custom_call_target="tpu_custom_call" | custom-call | flops 587202560 | bytes 3670016 | tf_op jit(solution)/shard_map/hidden_next/pallas_call | solution.py:535
  73.4 2.3 %hidden_next.5.near = f32[80,1792]{1,0:T(8,128)S(1)} custom-call(bf16[80,2048]{1,0:T(8,128)(2,1)S(1)} %get-tuple-element.40.scaled, bf16[4,896,2048]{2,1,0:T(8,128)(2,1)S(1)} %get-tuple-element.39.refs_5_.refs_0_, bf16[3,896,2048]{2,1,0:T(8,128)(2,1)S(1)} %fetch.7.refs_1_.refs_0_), custom_call_target="tpu_custom_call" | custom-call | flops 587202560 | bytes 3670016 | tf_op jit(solution)/shard_map/hidden_next/pallas_call | solution.py:535
  75.8 3.9 %collective-permute-done.19.far_up = bf16[80,896]{1,0:T(8,128)(2,1)S(1)} collective-permute-done((bf16[80,896]{1,0:T(8,128)(2,1)S(1)}, bf16[80,896]{1,0:T(8,128)(2,1)S(1)}, u32[]{:S(2)}, u32[]{:S(2)}) %collective-permute-start.19) | collective-permute-done | bytes 143392 | tf_op jit(solution)/shard_map/ppermute | solution.py:126
  81.5 3.7 %collective-permute-done.20.refs_0_ = bf16[80,896]{1,0:T(8,128)(2,1)S(1)} collective-permute-done((bf16[80,896]{1,0:T(8,128)(2,1)S(1)}, bf16[80,896]{1,0:T(8,128)(2,1)S(1)}, u32[]{:S(2)}, u32[]{:S(2)}) %collective-permute-start.20) | collective-permute-done | bytes 143392 | tf_op jit(solution)/shard_map/ppermute | solution.py:126
  85.3 2.6 %fetch.9.refs_1_ = bf16[1,896,2048]{2,1,0:T(8,128)(2,1)S(1)} custom-call(s32[102]{0:T(128)S(1)} %pad_add_fusion.table.refs_0_, bf16[3584,2048]{1,0:T(8,128)(2,1)} %refs_1_.9), custom_call_target="tpu_custom_call" | custom-call | bytes 7340032 | tf_op jit(solution)/shard_map/fetch/pallas_call | solution.py:212
  87.9 2.6 %fetch.8.refs_1_ = bf16[1,896,2048]{2,1,0:T(8,128)(2,1)S(1)} custom-call(s32[102]{0:T(128)S(1)} %pad_add_fusion.table.refs_0_, bf16[3584,2048]{1,0:T(8,128)(2,1)} %refs_1_.9), custom_call_target="tpu_custom_call" | custom-call | bytes 7340032 | tf_op jit(solution)/shard_map/fetch/pallas_call | solution.py:212
  93.7 2.2 %collective-permute-start.24 = (bf16[40,1024]{1,0:T(8,128)(2,1)S(1)}, bf16[40,1024]{1,0:T(8,128)(2,1)S(1)}, u32[]{:S(2)}, u32[]{:S(2)}) collective-permute-start(bf16[40,1024]{1,0:T(8,128)(2,1)S(1)} %get-tuple-element.49), channel_id=1, source_target_pairs={{0,8},{4,12},{8,0},{12,4},{1,9},{5,13},{9,1},{13,5},{2,10},{6,14},... | collective-permute-start | bytes 245768 | tf_op jit(solution)/shard_map/ppermute | solution.py:126
  95.9 2.2 %collective-permute-start.25 = (bf16[40,1024]{1,0:T(8,128)(2,1)S(1)}, bf16[40,1024]{1,0:T(8,128)(2,1)S(1)}, u32[]{:S(2)}, u32[]{:S(2)}) collective-permute-start(bf16[40,1024]{1,0:T(8,128)(2,1)S(1)} %get-tuple-element.50), channel_id=1, source_target_pairs={{0,12},{4,8},{8,4},{12,0},{1,13},{5,9},{9,5},{13,1},{2,14},{6,10},... | collective-permute-start | bytes 245768 | tf_op jit(solution)/shard_map/ppermute | solution.py:126
  99.7 3.8 %collective-permute-done.24.refs_3_ = bf16[40,1024]{1,0:T(8,128)(2,1)S(1)} collective-permute-done((bf16[40,1024]{1,0:T(8,128)(2,1)S(1)}, bf16[40,1024]{1,0:T(8,128)(2,1)S(1)}, u32[]{:S(2)}, u32[]{:S(2)}) %collective-permute-start.24) | collective-permute-done | bytes 81952 | tf_op jit(solution)/shard_map/ppermute | solution.py:126
  (65 shorter events, 25.3 us)
Async XLA Ops:
  1.0 10.6 %collective-permute-start = (bf16[20,16,128]{2,1,0:T(8,128)(2,1)S(1)}, bf16[20,16,128]{2,1,0:T(8,128)(2,1)S(1)}, u32[]{:S(2)}, u32[]{:S(2)}) collective-permute-start(bf16[20,16,128]{2,1,0:T(8,128)(2,1)S(1)} %slice.refs_0_), channel_id=1, source_target_pairs={{0,4},{4,0},{8,12},{12,8},{1,5},{5,1},{9,13},{13,9},{2,6},{6,2},{1... | collective-permute-start | bytes 245768 | tf_op jit(solution)/shard_map/ppermute | solution.py:126
  4.1 9.2 %collective-permute-start.1 = (bf16[20,16,128]{2,1,0:T(8,128)(2,1)S(1)}, bf16[20,16,128]{2,1,0:T(8,128)(2,1)S(1)}, u32[]{:S(2)}, u32[]{:S(2)}) collective-permute-start(bf16[20,16,128]{2,1,0:T(8,128)(2,1)S(1)} %slice.refs_0_), channel_id=1, source_target_pairs={{0,8},{4,12},{8,0},{12,4},{1,9},{5,13},{9,1},{13,5},{2,10},{6,14},... | collective-permute-start | bytes 245768 | tf_op jit(solution)/shard_map/ppermute | solution.py:126
  6.7 6.6 %collective-permute-start.2 = (bf16[20,16,128]{2,1,0:T(8,128)(2,1)S(1)}, bf16[20,16,128]{2,1,0:T(8,128)(2,1)S(1)}, u32[]{:S(2)}, u32[]{:S(2)}) collective-permute-start(bf16[20,16,128]{2,1,0:T(8,128)(2,1)S(1)} %slice.refs_0_), channel_id=1, source_target_pairs={{0,12},{4,8},{8,4},{12,0},{1,13},{5,9},{9,5},{13,1},{2,14},{6,10},... | collective-permute-start | bytes 245768 | tf_op jit(solution)/shard_map/ppermute | solution.py:126
  19.4 4.5 %collective-permute-start.3 = (bf16[24,512]{1,0:T(8,128)(2,1)S(1)}, bf16[24,512]{1,0:T(8,128)(2,1)S(1)}, u32[]{:S(2)}, u32[]{:S(2)}) collective-permute-start(bf16[24,512]{1,0:T(8,128)(2,1)S(1)} %get-tuple-element.31), channel_id=1, source_target_pairs={{0,4},{4,0},{8,12},{12,8},{1,5},{5,1},{9,13},{13,9},{2,6},{6,2},{1... | collective-permute-start | bytes 73736 | tf_op jit(solution)/shard_map/ppermute | solution.py:126
  21.0 5.0 %collective-permute-start.4 = (bf16[24,512]{1,0:T(8,128)(2,1)S(1)}, bf16[24,512]{1,0:T(8,128)(2,1)S(1)}, u32[]{:S(2)}, u32[]{:S(2)}) collective-permute-start(bf16[24,512]{1,0:T(8,128)(2,1)S(1)} %get-tuple-element.32), channel_id=1, source_target_pairs={{0,8},{4,12},{8,0},{12,4},{1,9},{5,13},{9,1},{13,5},{2,10},{6,14},... | collective-permute-start | bytes 73736 | tf_op jit(solution)/shard_map/ppermute | solution.py:126
  23.6 5.6 %collective-permute-start.5 = (bf16[24,512]{1,0:T(8,128)(2,1)S(1)}, bf16[24,512]{1,0:T(8,128)(2,1)S(1)}, u32[]{:S(2)}, u32[]{:S(2)}) collective-permute-start(bf16[24,512]{1,0:T(8,128)(2,1)S(1)} %get-tuple-element.33), channel_id=1, source_target_pairs={{0,12},{4,8},{8,4},{12,0},{1,13},{5,9},{9,5},{13,1},{2,14},{6,10},... | collective-permute-start | bytes 73736 | tf_op jit(solution)/shard_map/ppermute | solution.py:126
  29.2 4.6 %collective-permute-start.7 = (bf16[96,512]{1,0:T(8,128)(2,1)S(1)}, bf16[96,512]{1,0:T(8,128)(2,1)S(1)}, u32[]{:S(2)}, u32[]{:S(2)}) collective-permute-start(bf16[96,512]{1,0:T(8,128)(2,1)S(1)} %constant_dynamic-update-slice_fusion.refs_0_), channel_id=1, source_target_pairs={{0,2},{1,3},{2,0},{3,1},{4,6},{5,7},{6,4},{7,5},{8,10},{9,11},{10,... | collective-permute-start | bytes 294920 | tf_op jit(solution)/shard_map/ppermute | solution.py:126
  37.9 8.0 %collective-permute-start.10 = (bf16[40,1024]{1,0:T(8,128)(2,1)S(1)}, bf16[40,1024]{1,0:T(8,128)(2,1)S(1)}, u32[]{:S(2)}, u32[]{:S(2)}) collective-permute-start(bf16[40,1024]{1,0:T(8,128)(2,1)S(1)} %get-tuple-element.37), channel_id=1, source_target_pairs={{0,8},{4,12},{8,0},{12,4},{1,9},{5,13},{9,1},{13,5},{2,10},{6,14},... | collective-permute-start | bytes 245768 | tf_op jit(solution)/shard_map/ppermute | solution.py:126
  37.9 8.0 %collective-permute-start.11 = (bf16[40,1024]{1,0:T(8,128)(2,1)S(1)}, bf16[40,1024]{1,0:T(8,128)(2,1)S(1)}, u32[]{:S(2)}, u32[]{:S(2)}) collective-permute-start(bf16[40,1024]{1,0:T(8,128)(2,1)S(1)} %get-tuple-element.38), channel_id=1, source_target_pairs={{0,12},{4,8},{8,4},{12,0},{1,13},{5,9},{9,5},{13,1},{2,14},{6,10},... | collective-permute-start | bytes 245768 | tf_op jit(solution)/shard_map/ppermute | solution.py:126
  38.9 7.9 %collective-permute-start.9 = (bf16[40,1024]{1,0:T(8,128)(2,1)S(1)}, bf16[40,1024]{1,0:T(8,128)(2,1)S(1)}, u32[]{:S(2)}, u32[]{:S(2)}) collective-permute-start(bf16[40,1024]{1,0:T(8,128)(2,1)S(1)} %get-tuple-element.36), channel_id=1, source_target_pairs={{0,4},{4,0},{8,12},{12,8},{1,5},{5,1},{9,13},{13,9},{2,6},{6,2},{1... | collective-permute-start | bytes 245768 | tf_op jit(solution)/shard_map/ppermute | solution.py:126
  46.9 16.2 %collective-permute-start.12 = (bf16[40,1024]{1,0:T(8,128)(2,1)S(1)}, bf16[40,1024]{1,0:T(8,128)(2,1)S(1)}, u32[]{:S(2)}, u32[]{:S(2)}) collective-permute-start(bf16[40,1024]{1,0:T(8,128)(2,1)S(1)} %residual.2.refs_0_), channel_id=1, source_target_pairs={{0,4},{4,0},{8,12},{12,8},{1,5},{5,1},{9,13},{13,9},{2,6},{6,2},{1... | collective-permute-start | bytes 245768 | tf_op jit(solution)/shard_map/ppermute | solution.py:126
  47.5 15.5 %collective-permute-start.13 = (bf16[40,1024]{1,0:T(8,128)(2,1)S(1)}, bf16[40,1024]{1,0:T(8,128)(2,1)S(1)}, u32[]{:S(2)}, u32[]{:S(2)}) collective-permute-start(bf16[40,1024]{1,0:T(8,128)(2,1)S(1)} %residual.2.refs_0_), channel_id=1, source_target_pairs={{0,8},{4,12},{8,0},{12,4},{1,9},{5,13},{9,1},{13,5},{2,10},{6,14},... | collective-permute-start | bytes 245768 | tf_op jit(solution)/shard_map/ppermute | solution.py:126
  49.2 13.9 %collective-permute-start.14 = (bf16[40,1024]{1,0:T(8,128)(2,1)S(1)}, bf16[40,1024]{1,0:T(8,128)(2,1)S(1)}, u32[]{:S(2)}, u32[]{:S(2)}) collective-permute-start(bf16[40,1024]{1,0:T(8,128)(2,1)S(1)} %residual.2.refs_0_), channel_id=1, source_target_pairs={{0,12},{4,8},{8,4},{12,0},{1,13},{5,9},{9,5},{13,1},{2,14},{6,10},... | collective-permute-start | bytes 245768 | tf_op jit(solution)/shard_map/ppermute | solution.py:126
  65.6 7.2 %collective-permute-start.18 = (bf16[80,896]{1,0:T(8,128)(2,1)S(1)}, bf16[80,896]{1,0:T(8,128)(2,1)S(1)}, u32[]{:S(2)}, u32[]{:S(2)}) collective-permute-start(bf16[80,896]{1,0:T(8,128)(2,1)S(1)} %hidden_next.9), channel_id=1, source_target_pairs={{0,1},{1,0},{2,3},{3,2},{4,5},{5,4},{6,7},{7,6},{8,9},{9,8},{10,11... | collective-permute-start | bytes 430088 | tf_op jit(solution)/shard_map/ppermute | solution.py:126
  65.7 4.2 %collective-permute-start.16 = (bf16[80,1024]{1,0:T(8,128)(2,1)S(1)}, bf16[80,1024]{1,0:T(8,128)(2,1)S(1)}, u32[]{:S(2)}, u32[]{:S(2)}) collective-permute-start(bf16[80,1024]{1,0:T(8,128)(2,1)S(1)} %get-tuple-element.42), channel_id=1, source_target_pairs={{0,1},{1,0},{2,3},{3,2},{4,5},{5,4},{6,7},{7,6},{8,9},{9,8},{10,11... | collective-permute-start | bytes 491528 | tf_op jit(solution)/shard_map/ppermute | solution.py:126
  68.5 7.3 %collective-permute-start.15 = (bf16[80,1792]{1,0:T(8,128)(2,1)S(1)}, bf16[80,1792]{1,0:T(8,128)(2,1)S(1)}, u32[]{:S(2)}, u32[]{:S(2)}) collective-permute-start(bf16[80,1792]{1,0:T(8,128)(2,1)S(1)} %hidden_next.6), channel_id=1, source_target_pairs={{0,1},{1,0},{2,3},{3,2},{4,5},{5,4},{6,7},{7,6},{8,9},{9,8},{10,11... | collective-permute-start | bytes 860168 | tf_op jit(solution)/shard_map/ppermute | solution.py:126
  70.0 9.7 %collective-permute-start.17 = (bf16[80,1024]{1,0:T(8,128)(2,1)S(1)}, bf16[80,1024]{1,0:T(8,128)(2,1)S(1)}, u32[]{:S(2)}, u32[]{:S(2)}) collective-permute-start(bf16[80,1024]{1,0:T(8,128)(2,1)S(1)} %get-tuple-element.43), channel_id=1, source_target_pairs={{0,2},{1,3},{2,0},{3,1},{4,6},{5,7},{6,4},{7,5},{8,10},{9,11},{10,... | collective-permute-start | bytes 491528 | tf_op jit(solution)/shard_map/ppermute | solution.py:126
  72.8 6.8 %collective-permute-start.19 = (bf16[80,896]{1,0:T(8,128)(2,1)S(1)}, bf16[80,896]{1,0:T(8,128)(2,1)S(1)}, u32[]{:S(2)}, u32[]{:S(2)}) collective-permute-start(bf16[80,896]{1,0:T(8,128)(2,1)S(1)} %chip_sum.1), channel_id=1, source_target_pairs={{0,2},{1,3},{2,0},{3,1},{4,6},{5,7},{6,4},{7,5},{8,10},{9,11},{10,... | collective-permute-start | bytes 430088 | tf_op jit(solution)/shard_map/ppermute | solution.py:126
  80.0 5.3 %collective-permute-start.20 = (bf16[80,896]{1,0:T(8,128)(2,1)S(1)}, bf16[80,896]{1,0:T(8,128)(2,1)S(1)}, u32[]{:S(2)}, u32[]{:S(2)}) collective-permute-start(bf16[80,896]{1,0:T(8,128)(2,1)S(1)} %active.1.refs_0_), channel_id=1, source_target_pairs={{0,2},{1,3},{2,0},{3,1},{4,6},{5,7},{6,4},{7,5},{8,10},{9,11},{10,... | collective-permute-start | bytes 430088 | tf_op jit(solution)/shard_map/ppermute | solution.py:126
  81.5 9.0 %collective-permute-start.22 = (bf16[80,896]{1,0:T(8,128)(2,1)S(1)}, bf16[80,896]{1,0:T(8,128)(2,1)S(1)}, u32[]{:S(2)}, u32[]{:S(2)}) collective-permute-start(bf16[80,896]{1,0:T(8,128)(2,1)S(1)} %active.1.refs_0_), channel_id=1, source_target_pairs={{0,1},{1,0},{2,3},{3,2},{4,5},{5,4},{6,7},{7,6},{8,9},{9,8},{10,11... | collective-permute-start | bytes 430088 | tf_op jit(solution)/shard_map/ppermute | solution.py:126
  85.3 7.5 %collective-permute-start.21 = (bf16[80,896]{1,0:T(8,128)(2,1)S(1)}, bf16[80,896]{1,0:T(8,128)(2,1)S(1)}, u32[]{:S(2)}, u32[]{:S(2)}) collective-permute-start(bf16[80,896]{1,0:T(8,128)(2,1)S(1)} %collective-permute-done.20.refs_0_), channel_id=1, source_target_pairs={{0,1},{1,0},{2,3},{3,2},{4,5},{5,4},{6,7},{7,6},{8,9},{9,8},{10,11... | collective-permute-start | bytes 430088 | tf_op jit(solution)/shard_map/ppermute | solution.py:126
  93.6 6.1 %collective-permute-start.23 = (bf16[40,1024]{1,0:T(8,128)(2,1)S(1)}, bf16[40,1024]{1,0:T(8,128)(2,1)S(1)}, u32[]{:S(2)}, u32[]{:S(2)}) collective-permute-start(bf16[40,1024]{1,0:T(8,128)(2,1)S(1)} %get-tuple-element.48), channel_id=1, source_target_pairs={{0,4},{4,0},{8,12},{12,8},{1,5},{5,1},{9,13},{13,9},{2,6},{6,2},{1... | collective-permute-start | bytes 245768 | tf_op jit(solution)/shard_map/ppermute | solution.py:126
  93.7 9.8 %collective-permute-start.24 = (bf16[40,1024]{1,0:T(8,128)(2,1)S(1)}, bf16[40,1024]{1,0:T(8,128)(2,1)S(1)}, u32[]{:S(2)}, u32[]{:S(2)}) collective-permute-start(bf16[40,1024]{1,0:T(8,128)(2,1)S(1)} %get-tuple-element.49), channel_id=1, source_target_pairs={{0,8},{4,12},{8,0},{12,4},{1,9},{5,13},{9,1},{13,5},{2,10},{6,14},... | collective-permute-start | bytes 245768 | tf_op jit(solution)/shard_map/ppermute | solution.py:126
  95.9 7.6 %collective-permute-start.25 = (bf16[40,1024]{1,0:T(8,128)(2,1)S(1)}, bf16[40,1024]{1,0:T(8,128)(2,1)S(1)}, u32[]{:S(2)}, u32[]{:S(2)}) collective-permute-start(bf16[40,1024]{1,0:T(8,128)(2,1)S(1)} %get-tuple-element.50), channel_id=1, source_target_pairs={{0,12},{4,8},{8,4},{12,0},{1,13},{5,9},{9,5},{13,1},{2,14},{6,10},... | collective-permute-start | bytes 245768 | tf_op jit(solution)/shard_map/ppermute | solution.py:126
  (6 other events, 61.6 us)

commit v5 on v4

--- a/solution.py
+++ b/solution.py
@@ -387,7 +387,7 @@
             pltpu.SMEM((2 * most,), I32),
             pltpu.SemaphoreType.DMA((job_count(jobs),)),
         ],
-        compiler_params=params(12),
+        compiler_params=params(6),
         cost_estimate=pl.CostEstimate(
             flops=4 * pool * heads * lanes, bytes_accessed=pool * width * 4, transcendentals=0
         ),
@@ -401,55 +401,90 @@
     )
 
 
-def projection_kernel(table, *refs, slots, count, parts):
-    pieces, weight, outs = refs[:parts], refs[parts], refs[parts + 1 :]
-    own_att = table[0]
-    requests = slots * count
-    padded = pieces[0].shape[0] // count
+def selection_kernel(table, source, target, choose, sems, *, slots, count, masks_of):
+    copies = job_copies(table[1], masks_of, [source], [target], sems)
+    for copy in copies:
+        copy.start()
+    own = table[0]
+    requests, padded = choose.shape[1:]
     row = lax.broadcasted_iota(I32, (requests, padded), 0)
     wanted = row
     for k in range(count):
-        moved = row + ((own_att ^ k) - k) * slots
+        moved = row + ((own ^ k) - k) * slots
         wanted = jnp.where((row >= k * slots) & (row < (k + 1) * slots), moved, wanted)
-    choose = []
     lane = lax.broadcasted_iota(I32, (1, padded), 1)
     for k in range(count):
         served = jnp.full((1, padded), -1, I32)
         for i in range(slots):
-            request = table[2 + slots + (own_att ^ k) * slots + i]
+            request = table[2 + slots + (own ^ k) * slots + i]
             served = jnp.where(lane == i, request, served)
-        choose.append((wanted == served).astype(F32).astype(BF16))
+        choose[k] = (wanted == served).astype(F32).astype(BF16)
+    for copy in copies:
+        copy.wait()
+
+
+def selection(table, jobs, parts, slots, padded, count):
+    shapes = job_shapes(jobs, parts)
+    moved = sum(2 * math.prod(shape.shape) for shape in shapes)
+    return pl.pallas_call(
+        functools.partial(
+            selection_kernel, slots=slots, count=count, masks_of=masks_in(jobs)
+        ),
+        in_specs=[smem, hbm],
+        out_specs=[vmem] * 2,
+        out_shape=shapes + [jax.ShapeDtypeStruct((count, slots * count, padded), BF16)],
+        scratch_shapes=[pltpu.SemaphoreType.DMA((job_count(jobs),))],
+        compiler_params=params(1),
+        cost_estimate=pl.CostEstimate(flops=0, bytes_accessed=2 * moved, transcendentals=0),
+        name="selection",
+    )(table, in_hbm(jobs[0][0]))
+
+
+def ordered_kernel(choose, *refs):
+    blocks, out = refs[:-1], refs[-1]
+    total = None
+    for k, block in enumerate(blocks):
+        term = jnp.dot(choose[k], block[...], preferred_element_type=F32)
+        total = term if total is None else total + term
+    out[...] = total.astype(BF16)
+
+
+def ordered(choose, blocks):
+    return pl.pallas_call(
+        ordered_kernel,
+        in_specs=[vmem] * (1 + len(blocks)),
+        out_specs=vmem,
+        out_shape=jax.ShapeDtypeStruct((choose.shape[1], blocks[0].shape[1]), BF16),
+        compiler_params=params(2),
+        name="ordered",
+    )(choose, *blocks)
+
+
+def projection_kernel(*refs, slots, parts):
+    pieces, weight, outs = refs[:parts], refs[parts], refs[parts + 1 :]
     total = None
     for p in range(parts):
-        rows = None
-        for k in range(count):
-            term = jnp.dot(
-                choose[k],
-                pieces[p][k * padded : (k + 1) * padded, :],
-                preferred_element_type=F32,
-            )
-            rows = term if rows is None else rows + term
-        term = jnp.dot(rows.astype(BF16), weight[p], preferred_element_type=F32)
+        term = jnp.dot(pieces[p][...], weight[p], preferred_element_type=F32)
         total = term if total is None else total + term
-    for k in range(count):
-        outs[k][...] = halves_stacked(total[k * slots : (k + 1) * slots]).astype(BF16)
-
-
-def projection(table, pieces, weight, slots, count):
+    for k, out in enumerate(outs):
+        out[...] = halves_stacked(total[k * slots : (k + 1) * slots]).astype(BF16)
+
+
+def projection(pieces, weight, slots, count):
     parts, depth, width = weight.shape
     return pl.pallas_call(
-        functools.partial(projection_kernel, slots=slots, count=count, parts=parts),
-        in_specs=[smem] + [vmem] * (1 + parts),
+        functools.partial(projection_kernel, slots=slots, parts=parts),
+        in_specs=[vmem] * (1 + parts),
         out_specs=[vmem] * count,
         out_shape=[jax.ShapeDtypeStruct((2 * slots, width // 2), BF16)] * count,
-        compiler_params=params(8),
+        compiler_params=params(2),
         cost_estimate=pl.CostEstimate(
             flops=2 * slots * count * parts * depth * width,
             bytes_accessed=parts * depth * width,
             transcendentals=0,
         ),
         name="projection",
-    )(table, *pieces, in_vmem(weight))
+    )(*pieces, in_vmem(weight))
 
 
 def residual_kernel(*refs, joined):
@@ -514,7 +549,7 @@
             jax.ShapeDtypeStruct((requests, lanes), F32),
         ],
         scratch_shapes=[pltpu.VMEM((requests, width), F32)],
-        compiler_params=params(6),
+        compiler_params=params(2),
         cost_estimate=product_cost(requests, units, width),
         name="hidden_first",
     )(*blocks, gain, in_vmem(weight))
@@ -537,7 +572,7 @@
         in_specs=[vmem] * (1 + len(chosen)),
         out_specs=vmem,
         out_shape=jax.ShapeDtypeStruct((requests, len(chosen) * units), kind),
-        compiler_params=params(6),
+        compiler_params=params(2),
         cost_estimate=product_cost(requests, len(chosen) * units, width),
         name="hidden_next",
     )(scaled, *[in_vmem(weight) for weight, _ in chosen])
@@ -603,7 +638,7 @@
         in_specs=[vmem] * 5,
         out_specs=vmem,
         out_shape=jax.ShapeDtypeStruct((requests, width // 2), BF16),
-        compiler_params=params(4),
+        compiler_params=params(2),
         name="active",
     )(near, beside, far_gate, far_up, squares)
 
@@ -643,7 +678,7 @@
         in_specs=[vmem] * (2 * len(chosen) + len(before)),
         out_specs=[vmem] * len(outs),
         out_shape=outs,
-        compiler_params=params(8),
+        compiler_params=params(2),
         cost_estimate=product_cost(requests, len(chosen) * units, width),
         name="down",
     )(*[piece for piece, _, _ in chosen], *[in_vmem(w) for _, w, _ in chosen], *before)
@@ -686,14 +721,16 @@
     *blocks, project, down_near = attention(table, query_blocks, keys, values, jobs, parts)
 
     blocks = swaps_of(blocks)
-    (down_across,) = fetch(table, [(down_weight, (2,))], parts)
-    piece = jnp.concatenate(blocks, axis=0)
+    padded = blocks[0].shape[0]
+    jobs = [(down_weight, (2,))]
+    down_across, choose = selection(table, jobs, parts, slots, padded, count)
+    piece = ordered(choose, blocks)
     across = pair_swap(piece, "ffn", 2)
     beside = pair_swap(piece, "ffn", 1)
     corner = pair_swap(across, "ffn", 1)
     (down_corner,) = fetch(table, [(down_weight, (3,))], parts)
     gain = norm_gain.reshape(1, columns)
-    partial = projection(table, [piece, beside, across, corner], project, slots, count)
+    partial = projection([piece, beside, across, corner], project, slots, count)
     jobs = [(gate_weight, (0, 1, 2, 3)), (up_weight, (3,))]
     gate, up_corner = fetch(table, jobs, parts)
     middle = residual(hidden_state, swaps_of(partial), False)

time: 104 us -> 101 us (0.971)
  waiting for transfers between devices: 30 us -> 27.2 us
    ppermute x26, waiting for transfers between devices: 30 us -> 27.2 us  [pair_swap(): return lax.ppermute(value, axis, [(i, i ^ bit) for i in range(count)])]
    pallas_call x5 -> x4, Pallas kernels: 21.6 us -> 19 us  [fetch(): pl.pallas_call(functools.partial(fetch_kernel, masks_of=masks_in(jobs), p...]
    pallas_call x1 -> x3, Pallas kernels: 2.73 us -> 4.41 us  [the longest x1 2.59 us: selection(): pl.pallas_call(functools.partial(selection_kernel, slots=slots, count=cou...]
  transfers between devices with their start and end apart: 26 -> 26, of which waited for: 11 -> 10; matrix products, arithmetic and copies ran while one was open for 0% -> 0% of each run, Pallas kernels for 30% -> 31%
where the time goes in v5:
time: 101 us
  Pallas kernels  43.4 us (43%)
  starting transfers between devices  28.6 us (28%)
  waiting for transfers between devices  27.2 us (27%)
    ppermute x26, starting transfers between devices, pair_swap(): return lax.ppermute(value, axis, [(i, i ^ bit) for i in range(count)])  28.6 us
    ppermute x26, waiting for transfers between devices, pair_swap(): return lax.ppermute(value, axis, [(i, i ^ bit) for i in range(count)])  27.2 us
    pallas_call x4, Pallas kernels, fetch(): pl.pallas_call(functools.partial(fetch_kernel, masks_of=masks_in(jobs), p...  19 us
    pallas_call x5, Pallas kernels, hidden_next(): pl.pallas_call(functools.partial(hidden_kernel, parts=tuple((part for _,...  8.31 us
    pallas_call x1, Pallas kernels, attention(): pl.pallas_call(functools.partial(attention_kernel, slots=slots, count=cou...  6.15 us
    pallas_call x3, Pallas kernels, down_part(): pl.pallas_call(functools.partial(down_kernel, parts=tuple((part for _, _,...  3.07 us
    pallas_call x1, Pallas kernels, selection(): pl.pallas_call(functools.partial(selection_kernel, slots=slots, count=cou...  2.59 us
  transfers between devices with their start and end apart: 26, of which 10 were waited for; matrix products, arithmetic and copies ran while one was open for 0% of the time, Pallas kernels for 31%

profile of v5, /device:TPU:0, one launch (start us, length us, event | category | flops | bytes accessed | tf_op | source)
XLA Modules:
  0.0 100.6 jit_solution(17705906907089202945)
XLA Ops:
  1.0 3.1 %collective-permute-start = (bf16[20,16,128]{2,1,0:T(8,128)(2,1)S(1)}, bf16[20,16,128]{2,1,0:T(8,128)(2,1)S(1)}, u32[]{:S(2)}, u32[]{:S(2)}) collective-permute-start(bf16[20,16,128]{2,1,0:T(8,128)(2,1)S(1)} %slice.refs_0_), channel_id=1, source_target_pairs={{0,4},{4,0},{8,12},{12,8},{1,5},{5,1},{9,13},{13,9},{2,6},{6,2},{1... | collective-permute-start | bytes 245768 | tf_op jit(solution)/shard_map/ppermute | solution.py:126
  4.1 2.6 %collective-permute-start.1 = (bf16[20,16,128]{2,1,0:T(8,128)(2,1)S(1)}, bf16[20,16,128]{2,1,0:T(8,128)(2,1)S(1)}, u32[]{:S(2)}, u32[]{:S(2)}) collective-permute-start(bf16[20,16,128]{2,1,0:T(8,128)(2,1)S(1)} %slice.refs_0_), channel_id=1, source_target_pairs={{0,8},{4,12},{8,0},{12,4},{1,9},{5,13},{9,1},{13,5},{2,10},{6,14},... | collective-permute-start | bytes 245768 | tf_op jit(solution)/shard_map/ppermute | solution.py:126
  6.7 4.8 %fetch.4 = (bf16[12800,256]{1,0:T(8,128)(2,1)S(1)}, bf16[12800,256]{1,0:T(8,128)(2,1)S(1)}) custom-call(bf16[12800,256]{1,0:T(8,128)(2,1)} %refs_0_.2, bf16[12800,256]{1,0:T(8,128)(2,1)} %refs_1_.4), custom_call_target="tpu_custom_call" | custom-call | bytes 26214400 | tf_op jit(solution)/shard_map/fetch/pallas_call | solution.py:212
  11.5 1.7 %collective-permute-done.1.refs_2_ = bf16[20,16,128]{2,1,0:T(8,128)(2,1)S(1)} collective-permute-done((bf16[20,16,128]{2,1,0:T(8,128)(2,1)S(1)}, bf16[20,16,128]{2,1,0:T(8,128)(2,1)S(1)}, u32[]{:S(2)}, u32[]{:S(2)}) %collective-permute-start.1) | collective-permute-done | bytes 81952 | tf_op jit(solution)/shard_map/ppermute | solution.py:126
  13.3 6.2 %attention.1 = (bf16[24,512]{1,0:T(8,128)(2,1)S(1)}, bf16[24,512]{1,0:T(8,128)(2,1)S(1)}, bf16[24,512]{1,0:T(8,128)(2,1)S(1)}, bf16[24,512]{1,0:T(8,128)(2,1)S(1...) custom-call(s32[102]{0:T(128)S(1)} %pad_add_fusion.table.refs_0_, ...), custom_call_target="tpu_custom_call" | custom-call | flops 104857600 | bytes 13107200 | tf_op jit(solution)/shard_map/attention/pallas_call | solution.py:364
  20.9 2.7 %collective-permute-start.4 = (bf16[24,512]{1,0:T(8,128)(2,1)S(1)}, bf16[24,512]{1,0:T(8,128)(2,1)S(1)}, u32[]{:S(2)}, u32[]{:S(2)}) collective-permute-start(bf16[24,512]{1,0:T(8,128)(2,1)S(1)} %get-tuple-element.35), channel_id=1, source_target_pairs={{0,8},{4,12},{8,0},{12,4},{1,9},{5,13},{9,1},{13,5},{2,10},{6,14},... | collective-permute-start | bytes 73736 | tf_op jit(solution)/shard_map/ppermute | solution.py:126
  23.9 2.6 %selection.1 = (bf16[1,896,2048]{2,1,0:T(8,128)(2,1)S(1)}, bf16[4,80,24]{2,1,0:T(8,128)(2,1)S(1)}) custom-call(s32[102]{0:T(128)S(1)} %pad_add_fusion.table.refs_0_, bf16[3584,2048]{1,0:T(8,128)(2,1)} %refs_1_.7), custom_call_target="tpu_custom_call" | custom-call | bytes 7340032 | tf_op jit(solution)/shard_map/selection/pallas_call | solution.py:429
  26.5 2.7 %collective-permute-done.5.refs_3_ = bf16[24,512]{1,0:T(8,128)(2,1)S(1)} collective-permute-done((bf16[24,512]{1,0:T(8,128)(2,1)S(1)}, bf16[24,512]{1,0:T(8,128)(2,1)S(1)}, u32[]{:S(2)}, u32[]{:S(2)}) %collective-permute-start.5) | collective-permute-done | bytes 24608 | tf_op jit(solution)/shard_map/ppermute | solution.py:126
  31.0 2.9 %collective-permute-done.7.refs_2_ = bf16[80,512]{1,0:T(8,128)(2,1)S(1)} collective-permute-done((bf16[80,512]{1,0:T(8,128)(2,1)S(1)}, bf16[80,512]{1,0:T(8,128)(2,1)S(1)}, u32[]{:S(2)}, u32[]{:S(2)}) %collective-permute-start.7) | collective-permute-done | bytes 81952 | tf_op jit(solution)/shard_map/ppermute | solution.py:126
  37.8 2.5 %collective-permute-start.9 = (bf16[40,1024]{1,0:T(8,128)(2,1)S(1)}, bf16[40,1024]{1,0:T(8,128)(2,1)S(1)}, u32[]{:S(2)}, u32[]{:S(2)}) collective-permute-start(bf16[40,1024]{1,0:T(8,128)(2,1)S(1)} %get-tuple-element.39), channel_id=1, source_target_pairs={{0,4},{4,0},{8,12},{12,8},{1,5},{5,1},{9,13},{13,9},{2,6},{6,2},{1... | collective-permute-start | bytes 245768 | tf_op jit(solution)/shard_map/ppermute | solution.py:126
  40.4 4.5 %collective-permute-done.10.refs_3_ = bf16[40,1024]{1,0:T(8,128)(2,1)S(1)} collective-permute-done((bf16[40,1024]{1,0:T(8,128)(2,1)S(1)}, bf16[40,1024]{1,0:T(8,128)(2,1)S(1)}, u32[]{:S(2)}, u32[]{:S(2)}) %collective-permute-start.10) | collective-permute-done | bytes 81952 | tf_op jit(solution)/shard_map/ppermute | solution.py:126
  46.5 2.2 %collective-permute-start.13 = (bf16[40,1024]{1,0:T(8,128)(2,1)S(1)}, bf16[40,1024]{1,0:T(8,128)(2,1)S(1)}, u32[]{:S(2)}, u32[]{:S(2)}) collective-permute-start(bf16[40,1024]{1,0:T(8,128)(2,1)S(1)} %residual.2.refs_0_), channel_id=1, source_target_pairs={{0,8},{4,12},{8,0},{12,4},{1,9},{5,13},{9,1},{13,5},{2,10},{6,14},... | collective-permute-start | bytes 245768 | tf_op jit(solution)/shard_map/ppermute | solution.py:126
  48.7 1.7 %collective-permute-start.14 = (bf16[40,1024]{1,0:T(8,128)(2,1)S(1)}, bf16[40,1024]{1,0:T(8,128)(2,1)S(1)}, u32[]{:S(2)}, u32[]{:S(2)}) collective-permute-start(bf16[40,1024]{1,0:T(8,128)(2,1)S(1)} %residual.2.refs_0_), channel_id=1, source_target_pairs={{0,12},{4,8},{8,4},{12,0},{1,13},{5,9},{9,5},{13,1},{2,14},{6,10},... | collective-permute-start | bytes 245768 | tf_op jit(solution)/shard_map/ppermute | solution.py:126
  50.3 4.8 %fetch.6.refs_1_.refs_0_ = bf16[3,896,2048]{2,1,0:T(8,128)(2,1)S(1)} custom-call(s32[102]{0:T(128)S(1)} %pad_add_fusion.table.refs_0_, bf16[3584,2048]{1,0:T(8,128)(2,1)} %refs_1_.6), custom_call_target="tpu_custom_call" | custom-call | bytes 22020096 | tf_op jit(solution)/shard_map/fetch/pallas_call | solution.py:212
  55.1 6.9 %fetch.5 = (bf16[4,896,2048]{2,1,0:T(8,128)(2,1)S(1)}, bf16[1,896,2048]{2,1,0:T(8,128)(2,1)S(1)}) custom-call(s32[102]{0:T(128)S(1)} %pad_add_fusion.table.refs_0_, bf16[3584,2048]{1,0:T(8,128)(2,1)} %refs_1_.5, bf16[3584,2048]{1,0:T(8,128)(2,1)} %refs_1_.6), custom_call_target="tpu_custom_call" | custom-call | bytes 36700160 | tf_op jit(solution)/shard_map/fetch/pallas_call | solution.py:212
  65.1 2.3 %hidden_next.6 = bf16[80,1792]{1,0:T(8,128)(2,1)S(1)} custom-call(bf16[80,2048]{1,0:T(8,128)(2,1)S(1)} %get-tuple-element.43.scaled, bf16[4,896,2048]{2,1,0:T(8,128)(2,1)S(1)} %get-tuple-element.42.refs_5_.refs_0_, bf16[3,896,2048]{2,1,0:T(8,128)(2,1)S(1)} %fetch.6.refs_1_.refs_0_), custom_call_target="tpu_custom_call" | custom-call | flops 587202560 | bytes 3670016 | tf_op jit(solution)/shard_map/hidden_next/pallas_call | solution.py:570
  72.4 2.3 %hidden_next.5.near = f32[80,1792]{1,0:T(8,128)S(1)} custom-call(bf16[80,2048]{1,0:T(8,128)(2,1)S(1)} %get-tuple-element.43.scaled, bf16[4,896,2048]{2,1,0:T(8,128)(2,1)S(1)} %get-tuple-element.42.refs_5_.refs_0_, bf16[3,896,2048]{2,1,0:T(8,128)(2,1)S(1)} %fetch.6.refs_1_.refs_0_), custom_call_target="tpu_custom_call" | custom-call | flops 587202560 | bytes 3670016 | tf_op jit(solution)/shard_map/hidden_next/pallas_call | solution.py:570
  74.7 3.9 %collective-permute-done.19.far_up = bf16[80,896]{1,0:T(8,128)(2,1)S(1)} collective-permute-done((bf16[80,896]{1,0:T(8,128)(2,1)S(1)}, bf16[80,896]{1,0:T(8,128)(2,1)S(1)}, u32[]{:S(2)}, u32[]{:S(2)}) %collective-permute-start.19) | collective-permute-done | bytes 143392 | tf_op jit(solution)/shard_map/ppermute | solution.py:126
  80.5 3.8 %collective-permute-done.20.refs_0_ = bf16[80,896]{1,0:T(8,128)(2,1)S(1)} collective-permute-done((bf16[80,896]{1,0:T(8,128)(2,1)S(1)}, bf16[80,896]{1,0:T(8,128)(2,1)S(1)}, u32[]{:S(2)}, u32[]{:S(2)}) %collective-permute-start.20) | collective-permute-done | bytes 143392 | tf_op jit(solution)/shard_map/ppermute | solution.py:126
  84.3 2.6 %fetch.7.refs_1_ = bf16[1,896,2048]{2,1,0:T(8,128)(2,1)S(1)} custom-call(s32[102]{0:T(128)S(1)} %pad_add_fusion.table.refs_0_, bf16[3584,2048]{1,0:T(8,128)(2,1)} %refs_1_.7), custom_call_target="tpu_custom_call" | custom-call | bytes 7340032 | tf_op jit(solution)/shard_map/fetch/pallas_call | solution.py:212
  90.0 2.7 %collective-permute-start.24 = (bf16[40,1024]{1,0:T(8,128)(2,1)S(1)}, bf16[40,1024]{1,0:T(8,128)(2,1)S(1)}, u32[]{:S(2)}, u32[]{:S(2)}) collective-permute-start(bf16[40,1024]{1,0:T(8,128)(2,1)S(1)} %get-tuple-element.53), channel_id=1, source_target_pairs={{0,8},{4,12},{8,0},{12,4},{1,9},{5,13},{9,1},{13,5},{2,10},{6,14},... | collective-permute-start | bytes 245768 | tf_op jit(solution)/shard_map/ppermute | solution.py:126
  92.8 1.7 %collective-permute-start.25 = (bf16[40,1024]{1,0:T(8,128)(2,1)S(1)}, bf16[40,1024]{1,0:T(8,128)(2,1)S(1)}, u32[]{:S(2)}, u32[]{:S(2)}) collective-permute-start(bf16[40,1024]{1,0:T(8,128)(2,1)S(1)} %get-tuple-element.54), channel_id=1, source_target_pairs={{0,12},{4,8},{8,4},{12,0},{1,13},{5,9},{9,5},{13,1},{2,14},{6,10},... | collective-permute-start | bytes 245768 | tf_op jit(solution)/shard_map/ppermute | solution.py:126
  94.4 1.7 %collective-permute-done.23.refs_2_ = bf16[40,1024]{1,0:T(8,128)(2,1)S(1)} collective-permute-done((bf16[40,1024]{1,0:T(8,128)(2,1)S(1)}, bf16[40,1024]{1,0:T(8,128)(2,1)S(1)}, u32[]{:S(2)}, u32[]{:S(2)}) %collective-permute-start.23) | collective-permute-done | bytes 81952 | tf_op jit(solution)/shard_map/ppermute | solution.py:126
  96.1 3.7 %collective-permute-done.24.refs_3_ = bf16[40,1024]{1,0:T(8,128)(2,1)S(1)} collective-permute-done((bf16[40,1024]{1,0:T(8,128)(2,1)S(1)}, bf16[40,1024]{1,0:T(8,128)(2,1)S(1)}, u32[]{:S(2)}, u32[]{:S(2)}) %collective-permute-start.24) | collective-permute-done | bytes 81952 | tf_op jit(solution)/shard_map/ppermute | solution.py:126
  (62 shorter events, 23.8 us)
Async XLA Ops:
  1.0 10.6 %collective-permute-start = (bf16[20,16,128]{2,1,0:T(8,128)(2,1)S(1)}, bf16[20,16,128]{2,1,0:T(8,128)(2,1)S(1)}, u32[]{:S(2)}, u32[]{:S(2)}) collective-permute-start(bf16[20,16,128]{2,1,0:T(8,128)(2,1)S(1)} %slice.refs_0_), channel_id=1, source_target_pairs={{0,4},{4,0},{8,12},{12,8},{1,5},{5,1},{9,13},{13,9},{2,6},{6,2},{1... | collective-permute-start | bytes 245768 | tf_op jit(solution)/shard_map/ppermute | solution.py:126
  4.1 9.2 %collective-permute-start.1 = (bf16[20,16,128]{2,1,0:T(8,128)(2,1)S(1)}, bf16[20,16,128]{2,1,0:T(8,128)(2,1)S(1)}, u32[]{:S(2)}, u32[]{:S(2)}) collective-permute-start(bf16[20,16,128]{2,1,0:T(8,128)(2,1)S(1)} %slice.refs_0_), channel_id=1, source_target_pairs={{0,8},{4,12},{8,0},{12,4},{1,9},{5,13},{9,1},{13,5},{2,10},{6,14},... | collective-permute-start | bytes 245768 | tf_op jit(solution)/shard_map/ppermute | solution.py:126
  6.7 6.6 %collective-permute-start.2 = (bf16[20,16,128]{2,1,0:T(8,128)(2,1)S(1)}, bf16[20,16,128]{2,1,0:T(8,128)(2,1)S(1)}, u32[]{:S(2)}, u32[]{:S(2)}) collective-permute-start(bf16[20,16,128]{2,1,0:T(8,128)(2,1)S(1)} %slice.refs_0_), channel_id=1, source_target_pairs={{0,12},{4,8},{8,4},{12,0},{1,13},{5,9},{9,5},{13,1},{2,14},{6,10},... | collective-permute-start | bytes 245768 | tf_op jit(solution)/shard_map/ppermute | solution.py:126
  19.4 7.1 %collective-permute-start.3 = (bf16[24,512]{1,0:T(8,128)(2,1)S(1)}, bf16[24,512]{1,0:T(8,128)(2,1)S(1)}, u32[]{:S(2)}, u32[]{:S(2)}) collective-permute-start(bf16[24,512]{1,0:T(8,128)(2,1)S(1)} %get-tuple-element.34), channel_id=1, source_target_pairs={{0,4},{4,0},{8,12},{12,8},{1,5},{5,1},{9,13},{13,9},{2,6},{6,2},{1... | collective-permute-start | bytes 73736 | tf_op jit(solution)/shard_map/ppermute | solution.py:126
  20.9 5.6 %collective-permute-start.4 = (bf16[24,512]{1,0:T(8,128)(2,1)S(1)}, bf16[24,512]{1,0:T(8,128)(2,1)S(1)}, u32[]{:S(2)}, u32[]{:S(2)}) collective-permute-start(bf16[24,512]{1,0:T(8,128)(2,1)S(1)} %get-tuple-element.35), channel_id=1, source_target_pairs={{0,8},{4,12},{8,0},{12,4},{1,9},{5,13},{9,1},{13,5},{2,10},{6,14},... | collective-permute-start | bytes 73736 | tf_op jit(solution)/shard_map/ppermute | solution.py:126
  23.6 5.6 %collective-permute-start.5 = (bf16[24,512]{1,0:T(8,128)(2,1)S(1)}, bf16[24,512]{1,0:T(8,128)(2,1)S(1)}, u32[]{:S(2)}, u32[]{:S(2)}) collective-permute-start(bf16[24,512]{1,0:T(8,128)(2,1)S(1)} %get-tuple-element.36), channel_id=1, source_target_pairs={{0,12},{4,8},{8,4},{12,0},{1,13},{5,9},{9,5},{13,1},{2,14},{6,10},... | collective-permute-start | bytes 73736 | tf_op jit(solution)/shard_map/ppermute | solution.py:126
  29.4 4.5 %collective-permute-start.7 = (bf16[80,512]{1,0:T(8,128)(2,1)S(1)}, bf16[80,512]{1,0:T(8,128)(2,1)S(1)}, u32[]{:S(2)}, u32[]{:S(2)}) collective-permute-start(bf16[80,512]{1,0:T(8,128)(2,1)S(1)} %ordered.1.refs_0_), channel_id=1, source_target_pairs={{0,2},{1,3},{2,0},{3,1},{4,6},{5,7},{6,4},{7,5},{8,10},{9,11},{10,... | collective-permute-start | bytes 245768 | tf_op jit(solution)/shard_map/ppermute | solution.py:126
  36.8 8.0 %collective-permute-start.10 = (bf16[40,1024]{1,0:T(8,128)(2,1)S(1)}, bf16[40,1024]{1,0:T(8,128)(2,1)S(1)}, u32[]{:S(2)}, u32[]{:S(2)}) collective-permute-start(bf16[40,1024]{1,0:T(8,128)(2,1)S(1)} %get-tuple-element.40), channel_id=1, source_target_pairs={{0,8},{4,12},{8,0},{12,4},{1,9},{5,13},{9,1},{13,5},{2,10},{6,14},... | collective-permute-start | bytes 245768 | tf_op jit(solution)/shard_map/ppermute | solution.py:126
  36.9 8.0 %collective-permute-start.11 = (bf16[40,1024]{1,0:T(8,128)(2,1)S(1)}, bf16[40,1024]{1,0:T(8,128)(2,1)S(1)}, u32[]{:S(2)}, u32[]{:S(2)}) collective-permute-start(bf16[40,1024]{1,0:T(8,128)(2,1)S(1)} %get-tuple-element.41), channel_id=1, source_target_pairs={{0,12},{4,8},{8,4},{12,0},{1,13},{5,9},{9,5},{13,1},{2,14},{6,10},... | collective-permute-start | bytes 245768 | tf_op jit(solution)/shard_map/ppermute | solution.py:126
  37.8 8.0 %collective-permute-start.9 = (bf16[40,1024]{1,0:T(8,128)(2,1)S(1)}, bf16[40,1024]{1,0:T(8,128)(2,1)S(1)}, u32[]{:S(2)}, u32[]{:S(2)}) collective-permute-start(bf16[40,1024]{1,0:T(8,128)(2,1)S(1)} %get-tuple-element.39), channel_id=1, source_target_pairs={{0,4},{4,0},{8,12},{12,8},{1,5},{5,1},{9,13},{13,9},{2,6},{6,2},{1... | collective-permute-start | bytes 245768 | tf_op jit(solution)/shard_map/ppermute | solution.py:126
  45.9 16.2 %collective-permute-start.12 = (bf16[40,1024]{1,0:T(8,128)(2,1)S(1)}, bf16[40,1024]{1,0:T(8,128)(2,1)S(1)}, u32[]{:S(2)}, u32[]{:S(2)}) collective-permute-start(bf16[40,1024]{1,0:T(8,128)(2,1)S(1)} %residual.2.refs_0_), channel_id=1, source_target_pairs={{0,4},{4,0},{8,12},{12,8},{1,5},{5,1},{9,13},{13,9},{2,6},{6,2},{1... | collective-permute-start | bytes 245768 | tf_op jit(solution)/shard_map/ppermute | solution.py:126
  46.5 15.5 %collective-permute-start.13 = (bf16[40,1024]{1,0:T(8,128)(2,1)S(1)}, bf16[40,1024]{1,0:T(8,128)(2,1)S(1)}, u32[]{:S(2)}, u32[]{:S(2)}) collective-permute-start(bf16[40,1024]{1,0:T(8,128)(2,1)S(1)} %residual.2.refs_0_), channel_id=1, source_target_pairs={{0,8},{4,12},{8,0},{12,4},{1,9},{5,13},{9,1},{13,5},{2,10},{6,14},... | collective-permute-start | bytes 245768 | tf_op jit(solution)/shard_map/ppermute | solution.py:126
  48.7 13.4 %collective-permute-start.14 = (bf16[40,1024]{1,0:T(8,128)(2,1)S(1)}, bf16[40,1024]{1,0:T(8,128)(2,1)S(1)}, u32[]{:S(2)}, u32[]{:S(2)}) collective-permute-start(bf16[40,1024]{1,0:T(8,128)(2,1)S(1)} %residual.2.refs_0_), channel_id=1, source_target_pairs={{0,12},{4,8},{8,4},{12,0},{1,13},{5,9},{9,5},{13,1},{2,14},{6,10},... | collective-permute-start | bytes 245768 | tf_op jit(solution)/shard_map/ppermute | solution.py:126
  64.6 7.2 %collective-permute-start.18 = (bf16[80,896]{1,0:T(8,128)(2,1)S(1)}, bf16[80,896]{1,0:T(8,128)(2,1)S(1)}, u32[]{:S(2)}, u32[]{:S(2)}) collective-permute-start(bf16[80,896]{1,0:T(8,128)(2,1)S(1)} %hidden_next.9), channel_id=1, source_target_pairs={{0,1},{1,0},{2,3},{3,2},{4,5},{5,4},{6,7},{7,6},{8,9},{9,8},{10,11... | collective-permute-start | bytes 430088 | tf_op jit(solution)/shard_map/ppermute | solution.py:126
  64.6 4.2 %collective-permute-start.16 = (bf16[80,1024]{1,0:T(8,128)(2,1)S(1)}, bf16[80,1024]{1,0:T(8,128)(2,1)S(1)}, u32[]{:S(2)}, u32[]{:S(2)}) collective-permute-start(bf16[80,1024]{1,0:T(8,128)(2,1)S(1)} %get-tuple-element.45), channel_id=1, source_target_pairs={{0,1},{1,0},{2,3},{3,2},{4,5},{5,4},{6,7},{7,6},{8,9},{9,8},{10,11... | collective-permute-start | bytes 491528 | tf_op jit(solution)/shard_map/ppermute | solution.py:126
  67.5 11.2 %collective-permute-start.15 = (bf16[80,1792]{1,0:T(8,128)(2,1)S(1)}, bf16[80,1792]{1,0:T(8,128)(2,1)S(1)}, u32[]{:S(2)}, u32[]{:S(2)}) collective-permute-start(bf16[80,1792]{1,0:T(8,128)(2,1)S(1)} %hidden_next.6), channel_id=1, source_target_pairs={{0,1},{1,0},{2,3},{3,2},{4,5},{5,4},{6,7},{7,6},{8,9},{9,8},{10,11... | collective-permute-start | bytes 860168 | tf_op jit(solution)/shard_map/ppermute | solution.py:126
  69.0 9.7 %collective-permute-start.17 = (bf16[80,1024]{1,0:T(8,128)(2,1)S(1)}, bf16[80,1024]{1,0:T(8,128)(2,1)S(1)}, u32[]{:S(2)}, u32[]{:S(2)}) collective-permute-start(bf16[80,1024]{1,0:T(8,128)(2,1)S(1)} %get-tuple-element.46), channel_id=1, source_target_pairs={{0,2},{1,3},{2,0},{3,1},{4,6},{5,7},{6,4},{7,5},{8,10},{9,11},{10,... | collective-permute-start | bytes 491528 | tf_op jit(solution)/shard_map/ppermute | solution.py:126
  71.8 6.9 %collective-permute-start.19 = (bf16[80,896]{1,0:T(8,128)(2,1)S(1)}, bf16[80,896]{1,0:T(8,128)(2,1)S(1)}, u32[]{:S(2)}, u32[]{:S(2)}) collective-permute-start(bf16[80,896]{1,0:T(8,128)(2,1)S(1)} %chip_sum.1), channel_id=1, source_target_pairs={{0,2},{1,3},{2,0},{3,1},{4,6},{5,7},{6,4},{7,5},{8,10},{9,11},{10,... | collective-permute-start | bytes 430088 | tf_op jit(solution)/shard_map/ppermute | solution.py:126
  78.9 5.3 %collective-permute-start.20 = (bf16[80,896]{1,0:T(8,128)(2,1)S(1)}, bf16[80,896]{1,0:T(8,128)(2,1)S(1)}, u32[]{:S(2)}, u32[]{:S(2)}) collective-permute-start(bf16[80,896]{1,0:T(8,128)(2,1)S(1)} %active.1.refs_0_), channel_id=1, source_target_pairs={{0,2},{1,3},{2,0},{3,1},{4,6},{5,7},{6,4},{7,5},{8,10},{9,11},{10,... | collective-permute-start | bytes 430088 | tf_op jit(solution)/shard_map/ppermute | solution.py:126
  80.5 6.4 %collective-permute-start.22 = (bf16[80,896]{1,0:T(8,128)(2,1)S(1)}, bf16[80,896]{1,0:T(8,128)(2,1)S(1)}, u32[]{:S(2)}, u32[]{:S(2)}) collective-permute-start(bf16[80,896]{1,0:T(8,128)(2,1)S(1)} %active.1.refs_0_), channel_id=1, source_target_pairs={{0,1},{1,0},{2,3},{3,2},{4,5},{5,4},{6,7},{7,6},{8,9},{9,8},{10,11... | collective-permute-start | bytes 430088 | tf_op jit(solution)/shard_map/ppermute | solution.py:126
  84.3 4.9 %collective-permute-start.21 = (bf16[80,896]{1,0:T(8,128)(2,1)S(1)}, bf16[80,896]{1,0:T(8,128)(2,1)S(1)}, u32[]{:S(2)}, u32[]{:S(2)}) collective-permute-start(bf16[80,896]{1,0:T(8,128)(2,1)S(1)} %collective-permute-done.20.refs_0_), channel_id=1, source_target_pairs={{0,1},{1,0},{2,3},{3,2},{4,5},{5,4},{6,7},{7,6},{8,9},{9,8},{10,11... | collective-permute-start | bytes 430088 | tf_op jit(solution)/shard_map/ppermute | solution.py:126
  90.0 6.2 %collective-permute-start.23 = (bf16[40,1024]{1,0:T(8,128)(2,1)S(1)}, bf16[40,1024]{1,0:T(8,128)(2,1)S(1)}, u32[]{:S(2)}, u32[]{:S(2)}) collective-permute-start(bf16[40,1024]{1,0:T(8,128)(2,1)S(1)} %get-tuple-element.52), channel_id=1, source_target_pairs={{0,4},{4,0},{8,12},{12,8},{1,5},{5,1},{9,13},{13,9},{2,6},{6,2},{1... | collective-permute-start | bytes 245768 | tf_op jit(solution)/shard_map/ppermute | solution.py:126
  90.0 9.8 %collective-permute-start.24 = (bf16[40,1024]{1,0:T(8,128)(2,1)S(1)}, bf16[40,1024]{1,0:T(8,128)(2,1)S(1)}, u32[]{:S(2)}, u32[]{:S(2)}) collective-permute-start(bf16[40,1024]{1,0:T(8,128)(2,1)S(1)} %get-tuple-element.53), channel_id=1, source_target_pairs={{0,8},{4,12},{8,0},{12,4},{1,9},{5,13},{9,1},{13,5},{2,10},{6,14},... | collective-permute-start | bytes 245768 | tf_op jit(solution)/shard_map/ppermute | solution.py:126
  92.8 7.1 %collective-permute-start.25 = (bf16[40,1024]{1,0:T(8,128)(2,1)S(1)}, bf16[40,1024]{1,0:T(8,128)(2,1)S(1)}, u32[]{:S(2)}, u32[]{:S(2)}) collective-permute-start(bf16[40,1024]{1,0:T(8,128)(2,1)S(1)} %get-tuple-element.54), channel_id=1, source_target_pairs={{0,12},{4,8},{8,4},{12,0},{1,13},{5,9},{9,5},{13,1},{2,14},{6,10},... | collective-permute-start | bytes 245768 | tf_op jit(solution)/shard_map/ppermute | solution.py:126
  (6 other events, 53.3 us)

commit v6 on v5

--- a/solution.py
+++ b/solution.py
@@ -717,8 +717,12 @@
     own_queries = queries.reshape(slots, heads, lanes)
     query_blocks = swaps_of([own_queries] * count)
     keys, values = fetch(table, [(key_cache, None), (value_cache, None)], parts)
-    jobs = [(out_weight.reshape(-1, columns), (0, 1, 2, 3)), (down_weight, (0, 1))]
-    *blocks, project, down_near = attention(table, query_blocks, keys, values, jobs, parts)
+    jobs = [
+        (out_weight.reshape(-1, columns), (0, 1, 2, 3)),
+        (up_weight, (3,)),
+        (down_weight, (0, 1)),
+    ]
+    *blocks, project, up_corner, down_near = attention(table, query_blocks, keys, values, jobs, parts)
 
     blocks = swaps_of(blocks)
     padded = blocks[0].shape[0]
@@ -731,8 +735,7 @@
     (down_corner,) = fetch(table, [(down_weight, (3,))], parts)
     gain = norm_gain.reshape(1, columns)
     partial = projection([piece, beside, across, corner], project, slots, count)
-    jobs = [(gate_weight, (0, 1, 2, 3)), (up_weight, (3,))]
-    gate, up_corner = fetch(table, jobs, parts)
+    (gate,) = fetch(table, [(gate_weight, (0, 1, 2, 3))], parts)
     middle = residual(hidden_state, swaps_of(partial), False)
 
     rows = swaps_of([middle] * count)

time: 101 us -> 102 us (level)
  local copies, waits for them, and re-layouts: 0.97 us -> 3.3 us
  waiting for transfers between devices: 27.2 us -> 25.9 us
    unnamed x9 -> x13, local copies, waits for them, and re-layouts: 0.95 us -> 3.29 us
    ppermute x26, waiting for transfers between devices: 27.2 us -> 25.9 us  [pair_swap(): return lax.ppermute(value, axis, [(i, i ^ bit) for i in range(count)])]
    pallas_call x4, Pallas kernels: 19 us -> 17.9 us  [fetch(): pl.pallas_call(functools.partial(fetch_kernel, masks_of=masks_in(jobs), p...]
    pallas_call x1, Pallas kernels: 6.15 us -> 7.21 us  [attention(): pl.pallas_call(functools.partial(attention_kernel, slots=slots, count=cou...]
  transfers between devices with their start and end apart: 26 -> 26, of which waited for: 10 -> 9; matrix products, arithmetic and copies ran while one was open for 0% -> 0% of each run, Pallas kernels for 31% -> 30%
where the time goes in v6:
time: 102 us
  Pallas kernels  43.5 us (43%)
  starting transfers between devices  28.6 us (28%)
  waiting for transfers between devices  25.9 us (25%)
  local copies, waits for them, and re-layouts  3.3 us (3%)
    ppermute x26, starting transfers between devices, pair_swap(): return lax.ppermute(value, axis, [(i, i ^ bit) for i in range(count)])  28.6 us
    ppermute x26, waiting for transfers between devices, pair_swap(): return lax.ppermute(value, axis, [(i, i ^ bit) for i in range(count)])  25.9 us
    pallas_call x4, Pallas kernels, fetch(): pl.pallas_call(functools.partial(fetch_kernel, masks_of=masks_in(jobs), p...  17.9 us
    pallas_call x5, Pallas kernels, hidden_next(): pl.pallas_call(functools.partial(hidden_kernel, parts=tuple((part for _,...  8.32 us
    pallas_call x1, Pallas kernels, attention(): pl.pallas_call(functools.partial(attention_kernel, slots=slots, count=cou...  7.21 us
    unnamed x13, local copies, waits for them, and re-layouts  3.29 us
    pallas_call x3, Pallas kernels, down_part(): pl.pallas_call(functools.partial(down_kernel, parts=tuple((part for _, _,...  3.09 us
    pallas_call x1, Pallas kernels, selection(): pl.pallas_call(functools.partial(selection_kernel, slots=slots, count=cou...  2.59 us
  transfers between devices with their start and end apart: 26, of which 9 were waited for; matrix products, arithmetic and copies ran while one was open for 0% of the time, Pallas kernels for 30%

profile of v6, /device:TPU:0, one launch (start us, length us, event | category | flops | bytes accessed | tf_op | source)
XLA Modules:
  0.0 101.6 jit_solution(5747077269401398435)
XLA Ops:
  1.0 3.1 %collective-permute-start = (bf16[20,16,128]{2,1,0:T(8,128)(2,1)S(1)}, bf16[20,16,128]{2,1,0:T(8,128)(2,1)S(1)}, u32[]{:S(2)}, u32[]{:S(2)}) collective-permute-start(bf16[20,16,128]{2,1,0:T(8,128)(2,1)S(1)} %slice.refs_0_), channel_id=1, source_target_pairs={{0,4},{4,0},{8,12},{12,8},{1,5},{5,1},{9,13},{13,9},{2,6},{6,2},{1... | collective-permute-start | bytes 245768 | tf_op jit(solution)/shard_map/ppermute | solution.py:126
  4.1 2.6 %collective-permute-start.1 = (bf16[20,16,128]{2,1,0:T(8,128)(2,1)S(1)}, bf16[20,16,128]{2,1,0:T(8,128)(2,1)S(1)}, u32[]{:S(2)}, u32[]{:S(2)}) collective-permute-start(bf16[20,16,128]{2,1,0:T(8,128)(2,1)S(1)} %slice.refs_0_), channel_id=1, source_target_pairs={{0,8},{4,12},{8,0},{12,4},{1,9},{5,13},{9,1},{13,5},{2,10},{6,14},... | collective-permute-start | bytes 245768 | tf_op jit(solution)/shard_map/ppermute | solution.py:126
  6.7 4.8 %fetch.4 = (bf16[12800,256]{1,0:T(8,128)(2,1)S(1)}, bf16[12800,256]{1,0:T(8,128)(2,1)S(1)}) custom-call(bf16[12800,256]{1,0:T(8,128)(2,1)} %refs_0_.2, bf16[12800,256]{1,0:T(8,128)(2,1)} %refs_1_.4), custom_call_target="tpu_custom_call" | custom-call | bytes 26214400 | tf_op jit(solution)/shard_map/fetch/pallas_call | solution.py:212
  11.5 1.7 %collective-permute-done.1.refs_2_ = bf16[20,16,128]{2,1,0:T(8,128)(2,1)S(1)} collective-permute-done((bf16[20,16,128]{2,1,0:T(8,128)(2,1)S(1)}, bf16[20,16,128]{2,1,0:T(8,128)(2,1)S(1)}, u32[]{:S(2)}, u32[]{:S(2)}) %collective-permute-start.1) | collective-permute-done | bytes 81952 | tf_op jit(solution)/shard_map/ppermute | solution.py:126
  13.3 7.2 %attention.1 = (bf16[24,512]{1,0:T(8,128)(2,1)S(1)}, bf16[24,512]{1,0:T(8,128)(2,1)S(1)}, bf16[24,512]{1,0:T(8,128)(2,1)S(1)}, bf16[24,512]{1,0:T(8,128)(2,1)S(1...) custom-call(s32[102]{0:T(128)S(1)} %pad_add_fusion.table.refs_0_, ...), custom_call_target="tpu_custom_call" | custom-call | flops 104857600 | bytes 13107200 | tf_op jit(solution)/shard_map/attention/pallas_call | solution.py:364
  22.0 1.6 %collective-permute-start.4 = (bf16[24,512]{1,0:T(8,128)(2,1)S(1)}, bf16[24,512]{1,0:T(8,128)(2,1)S(1)}, u32[]{:S(2)}, u32[]{:S(2)}) collective-permute-start(bf16[24,512]{1,0:T(8,128)(2,1)S(1)} %get-tuple-element.34), channel_id=1, source_target_pairs={{0,8},{4,12},{8,0},{12,4},{1,9},{5,13},{9,1},{13,5},{2,10},{6,14},... | collective-permute-start | bytes 73736 | tf_op jit(solution)/shard_map/ppermute | solution.py:126
  24.9 2.6 %selection.1 = (bf16[1,896,2048]{2,1,0:T(8,128)(2,1)S(1)}, bf16[4,80,24]{2,1,0:T(8,128)(2,1)S(1)}) custom-call(s32[102]{0:T(128)S(1)} %pad_add_fusion.table.refs_0_, bf16[3584,2048]{1,0:T(8,128)(2,1)} %refs_1_.7), custom_call_target="tpu_custom_call" | custom-call | bytes 7340032 | tf_op jit(solution)/shard_map/selection/pallas_call | solution.py:429
  27.5 1.8 %copy-done = bf16[1,896,2048]{2,1,0:T(8,128)(2,1)} copy-done((bf16[1,896,2048]{2,1,0:T(8,128)(2,1)}, bf16[1,896,2048]{2,1,0:T(8,128)(2,1)S(1)}, u32[]{:S(2)}) %copy-start) | copy-done | bytes 3670040
  31.1 2.9 %collective-permute-done.7.refs_2_ = bf16[80,512]{1,0:T(8,128)(2,1)S(1)} collective-permute-done((bf16[80,512]{1,0:T(8,128)(2,1)S(1)}, bf16[80,512]{1,0:T(8,128)(2,1)S(1)}, u32[]{:S(2)}, u32[]{:S(2)}) %collective-permute-start.7) | collective-permute-done | bytes 81952 | tf_op jit(solution)/shard_map/ppermute | solution.py:126
  35.4 1.6 %projection.1 = (bf16[40,1024]{1,0:T(8,128)(2,1)S(1)}, bf16[40,1024]{1,0:T(8,128)(2,1)S(1)}, bf16[40,1024]{1,0:T(8,128)(2,1)S(1)}, bf16[40,1024]{1,0:T(8,128)(2,1)S(1)}) custom-call(bf16[80,512]{1,0:T(8,128)(2,1)S(1)} %ordered.1.refs_0_, bf16[80,512]{1,0:T(8,128)(2,1)S(1)} %collective-permute-done.6.refs_1_, ...), custom_call_target="tpu_custom_call" | custom-call | flops 671088640 | bytes 4194304 | tf_op jit(solution)/shard_map/projection/pallas_call | solution.py:475
  37.0 1.6 %collective-permute-start.10 = (bf16[40,1024]{1,0:T(8,128)(2,1)S(1)}, bf16[40,1024]{1,0:T(8,128)(2,1)S(1)}, u32[]{:S(2)}, u32[]{:S(2)}) collective-permute-start(bf16[40,1024]{1,0:T(8,128)(2,1)S(1)} %get-tuple-element.39), channel_id=1, source_target_pairs={{0,8},{4,12},{8,0},{12,4},{1,9},{5,13},{9,1},{13,5},{2,10},{6,14},... | collective-permute-start | bytes 245768 | tf_op jit(solution)/shard_map/ppermute | solution.py:126
  40.5 5.5 %collective-permute-done.10.refs_3_ = bf16[40,1024]{1,0:T(8,128)(2,1)S(1)} collective-permute-done((bf16[40,1024]{1,0:T(8,128)(2,1)S(1)}, bf16[40,1024]{1,0:T(8,128)(2,1)S(1)}, u32[]{:S(2)}, u32[]{:S(2)}) %collective-permute-start.10) | collective-permute-done | bytes 81952 | tf_op jit(solution)/shard_map/ppermute | solution.py:126
  48.4 1.9 %collective-permute-start.13 = (bf16[40,1024]{1,0:T(8,128)(2,1)S(1)}, bf16[40,1024]{1,0:T(8,128)(2,1)S(1)}, u32[]{:S(2)}, u32[]{:S(2)}) collective-permute-start(bf16[40,1024]{1,0:T(8,128)(2,1)S(1)} %residual.2.refs_0_), channel_id=1, source_target_pairs={{0,8},{4,12},{8,0},{12,4},{1,9},{5,13},{9,1},{13,5},{2,10},{6,14},... | collective-permute-start | bytes 245768 | tf_op jit(solution)/shard_map/ppermute | solution.py:126
  51.8 4.8 %fetch.6.refs_1_.refs_0_ = bf16[3,896,2048]{2,1,0:T(8,128)(2,1)S(1)} custom-call(s32[102]{0:T(128)S(1)} %pad_add_fusion.table.refs_0_, bf16[3584,2048]{1,0:T(8,128)(2,1)} %refs_1_.6), custom_call_target="tpu_custom_call" | custom-call | bytes 22020096 | tf_op jit(solution)/shard_map/fetch/pallas_call | solution.py:212
  56.6 5.8 %fetch.5.refs_5_.refs_0_ = bf16[4,896,2048]{2,1,0:T(8,128)(2,1)S(1)} custom-call(s32[102]{0:T(128)S(1)} %pad_add_fusion.table.refs_0_, bf16[3584,2048]{1,0:T(8,128)(2,1)} %refs_1_.5), custom_call_target="tpu_custom_call" | custom-call | bytes 29360128 | tf_op jit(solution)/shard_map/fetch/pallas_call | solution.py:212
  65.5 2.3 %hidden_next.6 = bf16[80,1792]{1,0:T(8,128)(2,1)S(1)} custom-call(bf16[80,2048]{1,0:T(8,128)(2,1)S(1)} %get-tuple-element.41.scaled, bf16[4,896,2048]{2,1,0:T(8,128)(2,1)S(1)} %fetch.5.refs_5_.refs_0_, bf16[3,896,2048]{2,1,0:T(8,128)(2,1)S(1)} %fetch.6.refs_1_.refs_0_), custom_call_target="tpu_custom_call" | custom-call | flops 587202560 | bytes 3670016 | tf_op jit(solution)/shard_map/hidden_next/pallas_call | solution.py:570
  69.4 1.6 %collective-permute-start.17 = (bf16[80,1024]{1,0:T(8,128)(2,1)S(1)}, bf16[80,1024]{1,0:T(8,128)(2,1)S(1)}, u32[]{:S(2)}, u32[]{:S(2)}) collective-permute-start(bf16[80,1024]{1,0:T(8,128)(2,1)S(1)} %get-tuple-element.44), channel_id=1, source_target_pairs={{0,2},{1,3},{2,0},{3,1},{4,6},{5,7},{6,4},{7,5},{8,10},{9,11},{10,... | collective-permute-start | bytes 491528 | tf_op jit(solution)/shard_map/ppermute | solution.py:126
  72.8 2.3 %hidden_next.5.near = f32[80,1792]{1,0:T(8,128)S(1)} custom-call(bf16[80,2048]{1,0:T(8,128)(2,1)S(1)} %get-tuple-element.41.scaled, bf16[4,896,2048]{2,1,0:T(8,128)(2,1)S(1)} %fetch.5.refs_5_.refs_0_, bf16[3,896,2048]{2,1,0:T(8,128)(2,1)S(1)} %fetch.6.refs_1_.refs_0_), custom_call_target="tpu_custom_call" | custom-call | flops 587202560 | bytes 3670016 | tf_op jit(solution)/shard_map/hidden_next/pallas_call | solution.py:570
  75.2 3.9 %collective-permute-done.19.far_up = bf16[80,896]{1,0:T(8,128)(2,1)S(1)} collective-permute-done((bf16[80,896]{1,0:T(8,128)(2,1)S(1)}, bf16[80,896]{1,0:T(8,128)(2,1)S(1)}, u32[]{:S(2)}, u32[]{:S(2)}) %collective-permute-start.19) | collective-permute-done | bytes 143392 | tf_op jit(solution)/shard_map/ppermute | solution.py:126
  80.9 3.7 %collective-permute-done.20.refs_0_ = bf16[80,896]{1,0:T(8,128)(2,1)S(1)} collective-permute-done((bf16[80,896]{1,0:T(8,128)(2,1)S(1)}, bf16[80,896]{1,0:T(8,128)(2,1)S(1)}, u32[]{:S(2)}, u32[]{:S(2)}) %collective-permute-start.20) | collective-permute-done | bytes 143392 | tf_op jit(solution)/shard_map/ppermute | solution.py:126
  84.7 2.6 %fetch.7.refs_1_ = bf16[1,896,2048]{2,1,0:T(8,128)(2,1)S(1)} custom-call(s32[102]{0:T(128)S(1)} %pad_add_fusion.table.refs_0_, bf16[3584,2048]{1,0:T(8,128)(2,1)} %refs_1_.7), custom_call_target="tpu_custom_call" | custom-call | bytes 7340032 | tf_op jit(solution)/shard_map/fetch/pallas_call | solution.py:212
  91.1 2.8 %collective-permute-start.24 = (bf16[40,1024]{1,0:T(8,128)(2,1)S(1)}, bf16[40,1024]{1,0:T(8,128)(2,1)S(1)}, u32[]{:S(2)}, u32[]{:S(2)}) collective-permute-start(bf16[40,1024]{1,0:T(8,128)(2,1)S(1)} %get-tuple-element.51), channel_id=1, source_target_pairs={{0,8},{4,12},{8,0},{12,4},{1,9},{5,13},{9,1},{13,5},{2,10},{6,14},... | collective-permute-start | bytes 245768 | tf_op jit(solution)/shard_map/ppermute | solution.py:126
  95.4 1.8 %collective-permute-done.23.refs_2_ = bf16[40,1024]{1,0:T(8,128)(2,1)S(1)} collective-permute-done((bf16[40,1024]{1,0:T(8,128)(2,1)S(1)}, bf16[40,1024]{1,0:T(8,128)(2,1)S(1)}, u32[]{:S(2)}, u32[]{:S(2)}) %collective-permute-start.23) | collective-permute-done | bytes 81952 | tf_op jit(solution)/shard_map/ppermute | solution.py:126
  97.2 3.7 %collective-permute-done.24.refs_3_ = bf16[40,1024]{1,0:T(8,128)(2,1)S(1)} collective-permute-done((bf16[40,1024]{1,0:T(8,128)(2,1)S(1)}, bf16[40,1024]{1,0:T(8,128)(2,1)S(1)}, u32[]{:S(2)}, u32[]{:S(2)}) %collective-permute-start.24) | collective-permute-done | bytes 81952 | tf_op jit(solution)/shard_map/ppermute | solution.py:126
  (66 shorter events, 27.1 us)
Async XLA Ops:
  1.0 10.6 %collective-permute-start = (bf16[20,16,128]{2,1,0:T(8,128)(2,1)S(1)}, bf16[20,16,128]{2,1,0:T(8,128)(2,1)S(1)}, u32[]{:S(2)}, u32[]{:S(2)}) collective-permute-start(bf16[20,16,128]{2,1,0:T(8,128)(2,1)S(1)} %slice.refs_0_), channel_id=1, source_target_pairs={{0,4},{4,0},{8,12},{12,8},{1,5},{5,1},{9,13},{13,9},{2,6},{6,2},{1... | collective-permute-start | bytes 245768 | tf_op jit(solution)/shard_map/ppermute | solution.py:126
  4.1 9.2 %collective-permute-start.1 = (bf16[20,16,128]{2,1,0:T(8,128)(2,1)S(1)}, bf16[20,16,128]{2,1,0:T(8,128)(2,1)S(1)}, u32[]{:S(2)}, u32[]{:S(2)}) collective-permute-start(bf16[20,16,128]{2,1,0:T(8,128)(2,1)S(1)} %slice.refs_0_), channel_id=1, source_target_pairs={{0,8},{4,12},{8,0},{12,4},{1,9},{5,13},{9,1},{13,5},{2,10},{6,14},... | collective-permute-start | bytes 245768 | tf_op jit(solution)/shard_map/ppermute | solution.py:126
  6.7 6.6 %collective-permute-start.2 = (bf16[20,16,128]{2,1,0:T(8,128)(2,1)S(1)}, bf16[20,16,128]{2,1,0:T(8,128)(2,1)S(1)}, u32[]{:S(2)}, u32[]{:S(2)}) collective-permute-start(bf16[20,16,128]{2,1,0:T(8,128)(2,1)S(1)} %slice.refs_0_), channel_id=1, source_target_pairs={{0,12},{4,8},{8,4},{12,0},{1,13},{5,9},{9,5},{13,1},{2,14},{6,10},... | collective-permute-start | bytes 245768 | tf_op jit(solution)/shard_map/ppermute | solution.py:126
  20.5 8.8 %collective-permute-start.3 = (bf16[24,512]{1,0:T(8,128)(2,1)S(1)}, bf16[24,512]{1,0:T(8,128)(2,1)S(1)}, u32[]{:S(2)}, u32[]{:S(2)}) collective-permute-start(bf16[24,512]{1,0:T(8,128)(2,1)S(1)} %get-tuple-element.33), channel_id=1, source_target_pairs={{0,4},{4,0},{8,12},{12,8},{1,5},{5,1},{9,13},{13,9},{2,6},{6,2},{1... | collective-permute-start | bytes 73736 | tf_op jit(solution)/shard_map/ppermute | solution.py:126
  22.0 7.3 %collective-permute-start.4 = (bf16[24,512]{1,0:T(8,128)(2,1)S(1)}, bf16[24,512]{1,0:T(8,128)(2,1)S(1)}, u32[]{:S(2)}, u32[]{:S(2)}) collective-permute-start(bf16[24,512]{1,0:T(8,128)(2,1)S(1)} %get-tuple-element.34), channel_id=1, source_target_pairs={{0,8},{4,12},{8,0},{12,4},{1,9},{5,13},{9,1},{13,5},{2,10},{6,14},... | collective-permute-start | bytes 73736 | tf_op jit(solution)/shard_map/ppermute | solution.py:126
  23.6 5.7 %collective-permute-start.5 = (bf16[24,512]{1,0:T(8,128)(2,1)S(1)}, bf16[24,512]{1,0:T(8,128)(2,1)S(1)}, u32[]{:S(2)}, u32[]{:S(2)}) collective-permute-start(bf16[24,512]{1,0:T(8,128)(2,1)S(1)} %get-tuple-element.35), channel_id=1, source_target_pairs={{0,12},{4,8},{8,4},{12,0},{1,13},{5,9},{9,5},{13,1},{2,14},{6,10},... | collective-permute-start | bytes 73736 | tf_op jit(solution)/shard_map/ppermute | solution.py:126
  29.6 4.5 %collective-permute-start.7 = (bf16[80,512]{1,0:T(8,128)(2,1)S(1)}, bf16[80,512]{1,0:T(8,128)(2,1)S(1)}, u32[]{:S(2)}, u32[]{:S(2)}) collective-permute-start(bf16[80,512]{1,0:T(8,128)(2,1)S(1)} %ordered.1.refs_0_), channel_id=1, source_target_pairs={{0,2},{1,3},{2,0},{3,1},{4,6},{5,7},{6,4},{7,5},{8,10},{9,11},{10,... | collective-permute-start | bytes 245768 | tf_op jit(solution)/shard_map/ppermute | solution.py:126
  37.0 9.1 %collective-permute-start.10 = (bf16[40,1024]{1,0:T(8,128)(2,1)S(1)}, bf16[40,1024]{1,0:T(8,128)(2,1)S(1)}, u32[]{:S(2)}, u32[]{:S(2)}) collective-permute-start(bf16[40,1024]{1,0:T(8,128)(2,1)S(1)} %get-tuple-element.39), channel_id=1, source_target_pairs={{0,8},{4,12},{8,0},{12,4},{1,9},{5,13},{9,1},{13,5},{2,10},{6,14},... | collective-permute-start | bytes 245768 | tf_op jit(solution)/shard_map/ppermute | solution.py:126
  38.6 7.5 %collective-permute-start.11 = (bf16[40,1024]{1,0:T(8,128)(2,1)S(1)}, bf16[40,1024]{1,0:T(8,128)(2,1)S(1)}, u32[]{:S(2)}, u32[]{:S(2)}) collective-permute-start(bf16[40,1024]{1,0:T(8,128)(2,1)S(1)} %get-tuple-element.40), channel_id=1, source_target_pairs={{0,12},{4,8},{8,4},{12,0},{1,13},{5,9},{9,5},{13,1},{2,14},{6,10},... | collective-permute-start | bytes 245768 | tf_op jit(solution)/shard_map/ppermute | solution.py:126
  39.9 7.4 %collective-permute-start.9 = (bf16[40,1024]{1,0:T(8,128)(2,1)S(1)}, bf16[40,1024]{1,0:T(8,128)(2,1)S(1)}, u32[]{:S(2)}, u32[]{:S(2)}) collective-permute-start(bf16[40,1024]{1,0:T(8,128)(2,1)S(1)} %get-tuple-element.38), channel_id=1, source_target_pairs={{0,4},{4,0},{8,12},{12,8},{1,5},{5,1},{9,13},{13,9},{2,6},{6,2},{1... | collective-permute-start | bytes 245768 | tf_op jit(solution)/shard_map/ppermute | solution.py:126
  47.4 15.1 %collective-permute-start.12 = (bf16[40,1024]{1,0:T(8,128)(2,1)S(1)}, bf16[40,1024]{1,0:T(8,128)(2,1)S(1)}, u32[]{:S(2)}, u32[]{:S(2)}) collective-permute-start(bf16[40,1024]{1,0:T(8,128)(2,1)S(1)} %residual.2.refs_0_), channel_id=1, source_target_pairs={{0,4},{4,0},{8,12},{12,8},{1,5},{5,1},{9,13},{13,9},{2,6},{6,2},{1... | collective-permute-start | bytes 245768 | tf_op jit(solution)/shard_map/ppermute | solution.py:126
  48.4 14.1 %collective-permute-start.13 = (bf16[40,1024]{1,0:T(8,128)(2,1)S(1)}, bf16[40,1024]{1,0:T(8,128)(2,1)S(1)}, u32[]{:S(2)}, u32[]{:S(2)}) collective-permute-start(bf16[40,1024]{1,0:T(8,128)(2,1)S(1)} %residual.2.refs_0_), channel_id=1, source_target_pairs={{0,8},{4,12},{8,0},{12,4},{1,9},{5,13},{9,1},{13,5},{2,10},{6,14},... | collective-permute-start | bytes 245768 | tf_op jit(solution)/shard_map/ppermute | solution.py:126
  50.3 12.2 %collective-permute-start.14 = (bf16[40,1024]{1,0:T(8,128)(2,1)S(1)}, bf16[40,1024]{1,0:T(8,128)(2,1)S(1)}, u32[]{:S(2)}, u32[]{:S(2)}) collective-permute-start(bf16[40,1024]{1,0:T(8,128)(2,1)S(1)} %residual.2.refs_0_), channel_id=1, source_target_pairs={{0,12},{4,8},{8,4},{12,0},{1,13},{5,9},{9,5},{13,1},{2,14},{6,10},... | collective-permute-start | bytes 245768 | tf_op jit(solution)/shard_map/ppermute | solution.py:126
  65.0 7.2 %collective-permute-start.18 = (bf16[80,896]{1,0:T(8,128)(2,1)S(1)}, bf16[80,896]{1,0:T(8,128)(2,1)S(1)}, u32[]{:S(2)}, u32[]{:S(2)}) collective-permute-start(bf16[80,896]{1,0:T(8,128)(2,1)S(1)} %hidden_next.9), channel_id=1, source_target_pairs={{0,1},{1,0},{2,3},{3,2},{4,5},{5,4},{6,7},{7,6},{8,9},{9,8},{10,11... | collective-permute-start | bytes 430088 | tf_op jit(solution)/shard_map/ppermute | solution.py:126
  65.0 4.2 %collective-permute-start.16 = (bf16[80,1024]{1,0:T(8,128)(2,1)S(1)}, bf16[80,1024]{1,0:T(8,128)(2,1)S(1)}, u32[]{:S(2)}, u32[]{:S(2)}) collective-permute-start(bf16[80,1024]{1,0:T(8,128)(2,1)S(1)} %get-tuple-element.43), channel_id=1, source_target_pairs={{0,1},{1,0},{2,3},{3,2},{4,5},{5,4},{6,7},{7,6},{8,9},{9,8},{10,11... | collective-permute-start | bytes 491528 | tf_op jit(solution)/shard_map/ppermute | solution.py:126
  67.9 11.2 %collective-permute-start.15 = (bf16[80,1792]{1,0:T(8,128)(2,1)S(1)}, bf16[80,1792]{1,0:T(8,128)(2,1)S(1)}, u32[]{:S(2)}, u32[]{:S(2)}) collective-permute-start(bf16[80,1792]{1,0:T(8,128)(2,1)S(1)} %hidden_next.6), channel_id=1, source_target_pairs={{0,1},{1,0},{2,3},{3,2},{4,5},{5,4},{6,7},{7,6},{8,9},{9,8},{10,11... | collective-permute-start | bytes 860168 | tf_op jit(solution)/shard_map/ppermute | solution.py:126
  69.4 9.7 %collective-permute-start.17 = (bf16[80,1024]{1,0:T(8,128)(2,1)S(1)}, bf16[80,1024]{1,0:T(8,128)(2,1)S(1)}, u32[]{:S(2)}, u32[]{:S(2)}) collective-permute-start(bf16[80,1024]{1,0:T(8,128)(2,1)S(1)} %get-tuple-element.44), channel_id=1, source_target_pairs={{0,2},{1,3},{2,0},{3,1},{4,6},{5,7},{6,4},{7,5},{8,10},{9,11},{10,... | collective-permute-start | bytes 491528 | tf_op jit(solution)/shard_map/ppermute | solution.py:126
  72.2 6.8 %collective-permute-start.19 = (bf16[80,896]{1,0:T(8,128)(2,1)S(1)}, bf16[80,896]{1,0:T(8,128)(2,1)S(1)}, u32[]{:S(2)}, u32[]{:S(2)}) collective-permute-start(bf16[80,896]{1,0:T(8,128)(2,1)S(1)} %chip_sum.1), channel_id=1, source_target_pairs={{0,2},{1,3},{2,0},{3,1},{4,6},{5,7},{6,4},{7,5},{8,10},{9,11},{10,... | collective-permute-start | bytes 430088 | tf_op jit(solution)/shard_map/ppermute | solution.py:126
  79.4 5.3 %collective-permute-start.20 = (bf16[80,896]{1,0:T(8,128)(2,1)S(1)}, bf16[80,896]{1,0:T(8,128)(2,1)S(1)}, u32[]{:S(2)}, u32[]{:S(2)}) collective-permute-start(bf16[80,896]{1,0:T(8,128)(2,1)S(1)} %active.1.refs_0_), channel_id=1, source_target_pairs={{0,2},{1,3},{2,0},{3,1},{4,6},{5,7},{6,4},{7,5},{8,10},{9,11},{10,... | collective-permute-start | bytes 430088 | tf_op jit(solution)/shard_map/ppermute | solution.py:126
  80.9 6.3 %collective-permute-start.22 = (bf16[80,896]{1,0:T(8,128)(2,1)S(1)}, bf16[80,896]{1,0:T(8,128)(2,1)S(1)}, u32[]{:S(2)}, u32[]{:S(2)}) collective-permute-start(bf16[80,896]{1,0:T(8,128)(2,1)S(1)} %active.1.refs_0_), channel_id=1, source_target_pairs={{0,1},{1,0},{2,3},{3,2},{4,5},{5,4},{6,7},{7,6},{8,9},{9,8},{10,11... | collective-permute-start | bytes 430088 | tf_op jit(solution)/shard_map/ppermute | solution.py:126
  84.7 5.5 %collective-permute-start.21 = (bf16[80,896]{1,0:T(8,128)(2,1)S(1)}, bf16[80,896]{1,0:T(8,128)(2,1)S(1)}, u32[]{:S(2)}, u32[]{:S(2)}) collective-permute-start(bf16[80,896]{1,0:T(8,128)(2,1)S(1)} %collective-permute-done.20.refs_0_), channel_id=1, source_target_pairs={{0,1},{1,0},{2,3},{3,2},{4,5},{5,4},{6,7},{7,6},{8,9},{9,8},{10,11... | collective-permute-start | bytes 430088 | tf_op jit(solution)/shard_map/ppermute | solution.py:126
  91.0 6.3 %collective-permute-start.23 = (bf16[40,1024]{1,0:T(8,128)(2,1)S(1)}, bf16[40,1024]{1,0:T(8,128)(2,1)S(1)}, u32[]{:S(2)}, u32[]{:S(2)}) collective-permute-start(bf16[40,1024]{1,0:T(8,128)(2,1)S(1)} %get-tuple-element.50), channel_id=1, source_target_pairs={{0,4},{4,0},{8,12},{12,8},{1,5},{5,1},{9,13},{13,9},{2,6},{6,2},{1... | collective-permute-start | bytes 245768 | tf_op jit(solution)/shard_map/ppermute | solution.py:126
  91.1 9.8 %collective-permute-start.24 = (bf16[40,1024]{1,0:T(8,128)(2,1)S(1)}, bf16[40,1024]{1,0:T(8,128)(2,1)S(1)}, u32[]{:S(2)}, u32[]{:S(2)}) collective-permute-start(bf16[40,1024]{1,0:T(8,128)(2,1)S(1)} %get-tuple-element.51), channel_id=1, source_target_pairs={{0,8},{4,12},{8,0},{12,4},{1,9},{5,13},{9,1},{13,5},{2,10},{6,14},... | collective-permute-start | bytes 245768 | tf_op jit(solution)/shard_map/ppermute | solution.py:126
  93.9 7.0 %collective-permute-start.25 = (bf16[40,1024]{1,0:T(8,128)(2,1)S(1)}, bf16[40,1024]{1,0:T(8,128)(2,1)S(1)}, u32[]{:S(2)}, u32[]{:S(2)}) collective-permute-start(bf16[40,1024]{1,0:T(8,128)(2,1)S(1)} %get-tuple-element.52), channel_id=1, source_target_pairs={{0,12},{4,8},{8,4},{12,0},{1,13},{5,9},{9,5},{13,1},{2,14},{6,10},... | collective-permute-start | bytes 245768 | tf_op jit(solution)/shard_map/ppermute | solution.py:126
  (8 other events, 54.7 us)

commit v7 on v5

--- a/solution.py
+++ b/solution.py
@@ -194,10 +194,9 @@
     return tuple(masks for _, masks in jobs)
 
 
-def fetch_kernel(*refs, masks_of, placed):
-    own = refs[0][1] if placed else None
-    refs = refs[1:] if placed else refs
+def fetch_kernel(*refs, masks_of):
     count = len(masks_of)
+    own = lax.axis_index("ffn")
     copies = job_copies(own, masks_of, refs[:count], refs[count:-1], refs[-1])
     for copy in copies:
         copy.start()
@@ -205,20 +204,19 @@
         copy.wait()
 
 
-def fetch(table, jobs, parts):
+def fetch(jobs, parts):
     shapes = job_shapes(jobs, parts)
-    placed = any(masks is not None for _, masks in jobs)
     moved = sum(2 * math.prod(shape.shape) for shape in shapes)
     return pl.pallas_call(
-        functools.partial(fetch_kernel, masks_of=masks_in(jobs), placed=placed),
-        in_specs=([smem] if placed else []) + [hbm] * len(jobs),
+        functools.partial(fetch_kernel, masks_of=masks_in(jobs)),
+        in_specs=[hbm] * len(jobs),
         out_specs=[vmem] * len(jobs),
         out_shape=shapes,
         scratch_shapes=[pltpu.SemaphoreType.DMA((job_count(jobs),))],
         compiler_params=params(1),
         cost_estimate=pl.CostEstimate(flops=0, bytes_accessed=2 * moved, transcendentals=0),
         name="fetch",
-    )(*([table] if placed else []), *[in_hbm(array) for array, _ in jobs])
+    )(*[in_hbm(array) for array, _ in jobs])
 
 
 def folded(combine, value):
@@ -401,11 +399,11 @@
     )
 
 
-def selection_kernel(table, source, target, choose, sems, *, slots, count, masks_of):
-    copies = job_copies(table[1], masks_of, [source], [target], sems)
+def selection_kernel(served, source, target, choose, sems, *, slots, count, masks_of):
+    copies = job_copies(lax.axis_index("ffn"), masks_of, [source], [target], sems)
     for copy in copies:
         copy.start()
-    own = table[0]
+    own = lax.axis_index("att")
     requests, padded = choose.shape[1:]
     row = lax.broadcasted_iota(I32, (requests, padded), 0)
     wanted = row
@@ -414,30 +412,29 @@
         wanted = jnp.where((row >= k * slots) & (row < (k + 1) * slots), moved, wanted)
     lane = lax.broadcasted_iota(I32, (1, padded), 1)
     for k in range(count):
-        served = jnp.full((1, padded), -1, I32)
-        for i in range(slots):
-            request = table[2 + slots + (own ^ k) * slots + i]
-            served = jnp.where(lane == i, request, served)
-        choose[k] = (wanted == served).astype(F32).astype(BF16)
+        turn = (count - (own ^ k)) * slots
+        first = pltpu.roll(served[...], lax.rem(turn + lanes - count * slots, lanes), 1)
+        request = jnp.where(lane < slots, first[:1, :padded], -1)
+        choose[k] = (wanted == request).astype(F32).astype(BF16)
     for copy in copies:
         copy.wait()
 
 
-def selection(table, jobs, parts, slots, padded, count):
+def selection(served, jobs, parts, slots, padded, count):
     shapes = job_shapes(jobs, parts)
     moved = sum(2 * math.prod(shape.shape) for shape in shapes)
     return pl.pallas_call(
         functools.partial(
             selection_kernel, slots=slots, count=count, masks_of=masks_in(jobs)
         ),
-        in_specs=[smem, hbm],
+        in_specs=[vmem, hbm],
         out_specs=[vmem] * 2,
         out_shape=shapes + [jax.ShapeDtypeStruct((count, slots * count, padded), BF16)],
         scratch_shapes=[pltpu.SemaphoreType.DMA((job_count(jobs),))],
         compiler_params=params(1),
         cost_estimate=pl.CostEstimate(flops=0, bytes_accessed=2 * moved, transcendentals=0),
         name="selection",
-    )(table, in_hbm(jobs[0][0]))
+    )(served, in_hbm(jobs[0][0]))
 
 
 def ordered_kernel(choose, *refs):
@@ -714,29 +711,31 @@
     heads = queries.shape[1] // lanes
     own = jnp.stack([lax.axis_index("att"), lax.axis_index("ffn")]).astype(I32)
     table = jnp.concatenate([own, lengths, assignment])
+    served = jnp.pad(assignment, (0, lanes - assignment.shape[0]))
+    served = lax.broadcast_in_dim(served, (8, lanes), (1,))
+
     own_queries = queries.reshape(slots, heads, lanes)
     query_blocks = swaps_of([own_queries] * count)
-    keys, values = fetch(table, [(key_cache, None), (value_cache, None)], parts)
+    keys, values = fetch([(key_cache, None), (value_cache, None)], parts)
     jobs = [(out_weight.reshape(-1, columns), (0, 1, 2, 3)), (down_weight, (0, 1))]
     *blocks, project, down_near = attention(table, query_blocks, keys, values, jobs, parts)
 
     blocks = swaps_of(blocks)
     padded = blocks[0].shape[0]
-    jobs = [(down_weight, (2,))]
-    down_across, choose = selection(table, jobs, parts, slots, padded, count)
+    jobs = [(up_weight, (3,))]
+    up_corner, choose = selection(served, jobs, parts, slots, padded, count)
     piece = ordered(choose, blocks)
     across = pair_swap(piece, "ffn", 2)
     beside = pair_swap(piece, "ffn", 1)
     corner = pair_swap(across, "ffn", 1)
-    (down_corner,) = fetch(table, [(down_weight, (3,))], parts)
+    (down_far,) = fetch([(down_weight, (2, 3))], parts)
     gain = norm_gain.reshape(1, columns)
     partial = projection([piece, beside, across, corner], project, slots, count)
-    jobs = [(gate_weight, (0, 1, 2, 3)), (up_weight, (3,))]
-    gate, up_corner = fetch(table, jobs, parts)
+    (gate,) = fetch([(gate_weight, (0, 1, 2, 3))], parts)
     middle = residual(hidden_state, swaps_of(partial), False)
 
     rows = swaps_of([middle] * count)
-    (up,) = fetch(table, [(up_weight, (0, 1, 2))], parts)
+    (up,) = fetch([(up_weight, (0, 1, 2))], parts)
     send, scaled, squares = hidden_first(rows, gain, gate, 3)
     arrived = pair_swap(send, "ffn", 1)
     keep = hidden_next(scaled, [(gate, 2)], F32)
@@ -756,8 +755,8 @@
     chosen = [(active, down_near, 0), (beside, down_near, 1)]
     (before,) = down_part(chosen, count, None, False)
     corner = pair_swap(across, "ffn", 1)
-    (before,) = down_part([(across, down_across, 0)], count, before, False)
-    partial = down_part([(corner, down_corner, 0)], count, before, True)
+    (before,) = down_part([(across, down_far, 0)], count, before, False)
+    partial = down_part([(corner, down_far, 1)], count, before, True)
     return residual(middle, swaps_of(partial), True)
 
 

time: 101 us -> 99.2 us (0.982)
  Pallas kernels: 43.4 us -> 41.4 us
    pallas_call x4, Pallas kernels: 19 us -> 17.4 us  [fetch(): pl.pallas_call(functools.partial(fetch_kernel, masks_of=masks_in(jobs)),...]
  transfers between devices with their start and end apart: 26 -> 26, of which waited for: 10 -> 10; matrix products, arithmetic and copies ran while one was open for 0% -> 0% of each run, Pallas kernels for 31% -> 29%
where the time goes in v7:
time: 99.2 us; the launch traced here: 99 us
  Pallas kernels  41.4 us (42%)
  starting transfers between devices  28.6 us (29%)
  waiting for transfers between devices  27.7 us (28%)
    ppermute x26, starting transfers between devices, pair_swap(): return lax.ppermute(value, axis, [(i, i ^ bit) for i in range(count)])  28.6 us
    ppermute x26, waiting for transfers between devices, pair_swap(): return lax.ppermute(value, axis, [(i, i ^ bit) for i in range(count)])  27.7 us
    pallas_call x4, Pallas kernels, fetch(): pl.pallas_call(functools.partial(fetch_kernel, masks_of=masks_in(jobs)),...  17.4 us
    pallas_call x5, Pallas kernels, hidden_next(): pl.pallas_call(functools.partial(hidden_kernel, parts=tuple((part for _,...  8.32 us
    pallas_call x1, Pallas kernels, attention(): pl.pallas_call(functools.partial(attention_kernel, slots=slots, count=cou...  6.15 us
    pallas_call x3, Pallas kernels, down_part(): pl.pallas_call(functools.partial(down_kernel, parts=tuple((part for _, _,...  3.08 us
    pallas_call x1, Pallas kernels, selection(): pl.pallas_call(functools.partial(selection_kernel, slots=slots, count=cou...  2.1 us
  transfers between devices with their start and end apart: 26, of which 10 were waited for; matrix products, arithmetic and copies ran while one was open for 0% of the time, Pallas kernels for 29%

profile of v7, /device:TPU:0, one launch (start us, length us, event | category | flops | bytes accessed | tf_op | source)
XLA Modules:
  0.0 99.0 jit_solution(17853701131629222320)
XLA Ops:
  1.0 3.1 %collective-permute-start = (bf16[20,16,128]{2,1,0:T(8,128)(2,1)S(1)}, bf16[20,16,128]{2,1,0:T(8,128)(2,1)S(1)}, u32[]{:S(2)}, u32[]{:S(2)}) collective-permute-start(bf16[20,16,128]{2,1,0:T(8,128)(2,1)S(1)} %slice.refs_0_), channel_id=1, source_target_pairs={{0,4},{4,0},{8,12},{12,8},{1,5},{5,1},{9,13},{13,9},{2,6},{6,2},{1... | collective-permute-start | bytes 245768 | tf_op jit(solution)/shard_map/ppermute | solution.py:126
  4.1 2.6 %collective-permute-start.1 = (bf16[20,16,128]{2,1,0:T(8,128)(2,1)S(1)}, bf16[20,16,128]{2,1,0:T(8,128)(2,1)S(1)}, u32[]{:S(2)}, u32[]{:S(2)}) collective-permute-start(bf16[20,16,128]{2,1,0:T(8,128)(2,1)S(1)} %slice.refs_0_), channel_id=1, source_target_pairs={{0,8},{4,12},{8,0},{12,4},{1,9},{5,13},{9,1},{13,5},{2,10},{6,14},... | collective-permute-start | bytes 245768 | tf_op jit(solution)/shard_map/ppermute | solution.py:126
  6.7 4.8 %fetch.4 = (bf16[12800,256]{1,0:T(8,128)(2,1)S(1)}, bf16[12800,256]{1,0:T(8,128)(2,1)S(1)}) custom-call(bf16[12800,256]{1,0:T(8,128)(2,1)} %refs_0_.5, bf16[12800,256]{1,0:T(8,128)(2,1)} %refs_1_.1), custom_call_target="tpu_custom_call" | custom-call | bytes 26214400 | tf_op jit(solution)/shard_map/fetch/pallas_call | solution.py:210
  11.5 1.7 %collective-permute-done.1.refs_2_ = bf16[20,16,128]{2,1,0:T(8,128)(2,1)S(1)} collective-permute-done((bf16[20,16,128]{2,1,0:T(8,128)(2,1)S(1)}, bf16[20,16,128]{2,1,0:T(8,128)(2,1)S(1)}, u32[]{:S(2)}, u32[]{:S(2)}) %collective-permute-start.1) | collective-permute-done | bytes 81952 | tf_op jit(solution)/shard_map/ppermute | solution.py:126
  13.3 6.2 %attention.1 = (bf16[24,512]{1,0:T(8,128)(2,1)S(1)}, bf16[24,512]{1,0:T(8,128)(2,1)S(1)}, bf16[24,512]{1,0:T(8,128)(2,1)S(1)}, bf16[24,512]{1,0:T(8,128)(2,1)S(1...) custom-call(s32[102]{0:T(128)S(1)} %pad_add_fusion.table, bf16[20,16,128]{2,1,0:T(8,128)(2,1)S(1)} %slice.refs_0_, ...), custom_call_target="tpu_custom_call" | custom-call | flops 104857600 | bytes 13107200 | tf_op jit(solution)/shard_map/attention/pallas_call | solution.py:362
  20.9 2.7 %collective-permute-start.4 = (bf16[24,512]{1,0:T(8,128)(2,1)S(1)}, bf16[24,512]{1,0:T(8,128)(2,1)S(1)}, u32[]{:S(2)}, u32[]{:S(2)}) collective-permute-start(bf16[24,512]{1,0:T(8,128)(2,1)S(1)} %get-tuple-element.33), channel_id=1, source_target_pairs={{0,8},{4,12},{8,0},{12,4},{1,9},{5,13},{9,1},{13,5},{2,10},{6,14},... | collective-permute-start | bytes 73736 | tf_op jit(solution)/shard_map/ppermute | solution.py:126
  23.9 2.1 %selection.1 = (bf16[1,896,2048]{2,1,0:T(8,128)(2,1)S(1)}, bf16[4,80,24]{2,1,0:T(8,128)(2,1)S(1)}) custom-call(s32[8,128]{1,0:T(8,128)S(1)} %broadcast_in_dim.3.served, bf16[3584,2048]{1,0:T(8,128)(2,1)} %refs_0_.8), custom_call_target="tpu_custom_call" | custom-call | bytes 7340032 | tf_op jit(solution)/shard_map/selection/pallas_call | solution.py:426
  26.0 3.2 %collective-permute-done.5.refs_3_ = bf16[24,512]{1,0:T(8,128)(2,1)S(1)} collective-permute-done((bf16[24,512]{1,0:T(8,128)(2,1)S(1)}, bf16[24,512]{1,0:T(8,128)(2,1)S(1)}, u32[]{:S(2)}, u32[]{:S(2)}) %collective-permute-start.5) | collective-permute-done | bytes 24608 | tf_op jit(solution)/shard_map/ppermute | solution.py:126
  31.0 2.9 %collective-permute-done.7.refs_2_ = bf16[80,512]{1,0:T(8,128)(2,1)S(1)} collective-permute-done((bf16[80,512]{1,0:T(8,128)(2,1)S(1)}, bf16[80,512]{1,0:T(8,128)(2,1)S(1)}, u32[]{:S(2)}, u32[]{:S(2)}) %collective-permute-start.7) | collective-permute-done | bytes 81952 | tf_op jit(solution)/shard_map/ppermute | solution.py:126
  37.8 2.5 %collective-permute-start.9 = (bf16[40,1024]{1,0:T(8,128)(2,1)S(1)}, bf16[40,1024]{1,0:T(8,128)(2,1)S(1)}, u32[]{:S(2)}, u32[]{:S(2)}) collective-permute-start(bf16[40,1024]{1,0:T(8,128)(2,1)S(1)} %get-tuple-element.37), channel_id=1, source_target_pairs={{0,4},{4,0},{8,12},{12,8},{1,5},{5,1},{9,13},{13,9},{2,6},{6,2},{1... | collective-permute-start | bytes 245768 | tf_op jit(solution)/shard_map/ppermute | solution.py:126
  40.4 4.5 %collective-permute-done.10.refs_3_ = bf16[40,1024]{1,0:T(8,128)(2,1)S(1)} collective-permute-done((bf16[40,1024]{1,0:T(8,128)(2,1)S(1)}, bf16[40,1024]{1,0:T(8,128)(2,1)S(1)}, u32[]{:S(2)}, u32[]{:S(2)}) %collective-permute-start.10) | collective-permute-done | bytes 81952 | tf_op jit(solution)/shard_map/ppermute | solution.py:126
  46.5 1.7 %collective-permute-start.13 = (bf16[40,1024]{1,0:T(8,128)(2,1)S(1)}, bf16[40,1024]{1,0:T(8,128)(2,1)S(1)}, u32[]{:S(2)}, u32[]{:S(2)}) collective-permute-start(bf16[40,1024]{1,0:T(8,128)(2,1)S(1)} %residual.2.refs_0_), channel_id=1, source_target_pairs={{0,8},{4,12},{8,0},{12,4},{1,9},{5,13},{9,1},{13,5},{2,10},{6,14},... | collective-permute-start | bytes 245768 | tf_op jit(solution)/shard_map/ppermute | solution.py:126
  48.2 2.1 %collective-permute-start.14 = (bf16[40,1024]{1,0:T(8,128)(2,1)S(1)}, bf16[40,1024]{1,0:T(8,128)(2,1)S(1)}, u32[]{:S(2)}, u32[]{:S(2)}) collective-permute-start(bf16[40,1024]{1,0:T(8,128)(2,1)S(1)} %residual.2.refs_0_), channel_id=1, source_target_pairs={{0,12},{4,8},{8,4},{12,0},{1,13},{5,9},{9,5},{13,1},{2,14},{6,10},... | collective-permute-start | bytes 245768 | tf_op jit(solution)/shard_map/ppermute | solution.py:126
  50.3 4.2 %fetch.6.refs_1_.refs_0_ = bf16[3,896,2048]{2,1,0:T(8,128)(2,1)S(1)} custom-call(bf16[3584,2048]{1,0:T(8,128)(2,1)} %refs_0_.8), custom_call_target="tpu_custom_call" | custom-call | bytes 22020096 | tf_op jit(solution)/shard_map/fetch/pallas_call | solution.py:210
  54.6 5.3 %fetch.5.refs_5_.refs_0_ = bf16[4,896,2048]{2,1,0:T(8,128)(2,1)S(1)} custom-call(bf16[3584,2048]{1,0:T(8,128)(2,1)} %refs_0_.7), custom_call_target="tpu_custom_call" | custom-call | bytes 29360128 | tf_op jit(solution)/shard_map/fetch/pallas_call | solution.py:210
  63.0 2.3 %hidden_next.6 = bf16[80,1792]{1,0:T(8,128)(2,1)S(1)} custom-call(bf16[80,2048]{1,0:T(8,128)(2,1)S(1)} %get-tuple-element.40.scaled, bf16[4,896,2048]{2,1,0:T(8,128)(2,1)S(1)} %fetch.5.refs_5_.refs_0_, bf16[3,896,2048]{2,1,0:T(8,128)(2,1)S(1)} %fetch.6.refs_1_.refs_0_), custom_call_target="tpu_custom_call" | custom-call | flops 587202560 | bytes 3670016 | tf_op jit(solution)/shard_map/hidden_next/pallas_call | solution.py:567
  70.3 2.3 %hidden_next.5.near = f32[80,1792]{1,0:T(8,128)S(1)} custom-call(bf16[80,2048]{1,0:T(8,128)(2,1)S(1)} %get-tuple-element.40.scaled, bf16[4,896,2048]{2,1,0:T(8,128)(2,1)S(1)} %fetch.5.refs_5_.refs_0_, bf16[3,896,2048]{2,1,0:T(8,128)(2,1)S(1)} %fetch.6.refs_1_.refs_0_), custom_call_target="tpu_custom_call" | custom-call | flops 587202560 | bytes 3670016 | tf_op jit(solution)/shard_map/hidden_next/pallas_call | solution.py:567
  72.6 3.9 %collective-permute-done.19.far_up = bf16[80,896]{1,0:T(8,128)(2,1)S(1)} collective-permute-done((bf16[80,896]{1,0:T(8,128)(2,1)S(1)}, bf16[80,896]{1,0:T(8,128)(2,1)S(1)}, u32[]{:S(2)}, u32[]{:S(2)}) %collective-permute-start.19) | collective-permute-done | bytes 143392 | tf_op jit(solution)/shard_map/ppermute | solution.py:126
  78.4 3.8 %collective-permute-done.20.refs_0_ = bf16[80,896]{1,0:T(8,128)(2,1)S(1)} collective-permute-done((bf16[80,896]{1,0:T(8,128)(2,1)S(1)}, bf16[80,896]{1,0:T(8,128)(2,1)S(1)}, u32[]{:S(2)}, u32[]{:S(2)}) %collective-permute-start.20) | collective-permute-done | bytes 143392 | tf_op jit(solution)/shard_map/ppermute | solution.py:126
  82.1 3.2 %fetch.7.refs_1_ = bf16[2,896,2048]{2,1,0:T(8,128)(2,1)S(1)} custom-call(bf16[3584,2048]{1,0:T(8,128)(2,1)} %refs_0_.9), custom_call_target="tpu_custom_call" | custom-call | bytes 14680064 | tf_op jit(solution)/shard_map/fetch/pallas_call | solution.py:210
  88.5 2.2 %collective-permute-start.24 = (bf16[40,1024]{1,0:T(8,128)(2,1)S(1)}, bf16[40,1024]{1,0:T(8,128)(2,1)S(1)}, u32[]{:S(2)}, u32[]{:S(2)}) collective-permute-start(bf16[40,1024]{1,0:T(8,128)(2,1)S(1)} %get-tuple-element.49), channel_id=1, source_target_pairs={{0,8},{4,12},{8,0},{12,4},{1,9},{5,13},{9,1},{13,5},{2,10},{6,14},... | collective-permute-start | bytes 245768 | tf_op jit(solution)/shard_map/ppermute | solution.py:126
  90.7 2.1 %collective-permute-start.25 = (bf16[40,1024]{1,0:T(8,128)(2,1)S(1)}, bf16[40,1024]{1,0:T(8,128)(2,1)S(1)}, u32[]{:S(2)}, u32[]{:S(2)}) collective-permute-start(bf16[40,1024]{1,0:T(8,128)(2,1)S(1)} %get-tuple-element.50), channel_id=1, source_target_pairs={{0,12},{4,8},{8,4},{12,0},{1,13},{5,9},{9,5},{13,1},{2,14},{6,10},... | collective-permute-start | bytes 245768 | tf_op jit(solution)/shard_map/ppermute | solution.py:126
  92.9 1.6 %collective-permute-done.23.refs_2_ = bf16[40,1024]{1,0:T(8,128)(2,1)S(1)} collective-permute-done((bf16[40,1024]{1,0:T(8,128)(2,1)S(1)}, bf16[40,1024]{1,0:T(8,128)(2,1)S(1)}, u32[]{:S(2)}, u32[]{:S(2)}) %collective-permute-start.23) | collective-permute-done | bytes 81952 | tf_op jit(solution)/shard_map/ppermute | solution.py:126
  94.5 3.8 %collective-permute-done.24.refs_3_ = bf16[40,1024]{1,0:T(8,128)(2,1)S(1)} collective-permute-done((bf16[40,1024]{1,0:T(8,128)(2,1)S(1)}, bf16[40,1024]{1,0:T(8,128)(2,1)S(1)}, u32[]{:S(2)}, u32[]{:S(2)}) %collective-permute-start.24) | collective-permute-done | bytes 81952 | tf_op jit(solution)/shard_map/ppermute | solution.py:126
  (64 shorter events, 23.8 us)
Async XLA Ops:
  1.0 10.6 %collective-permute-start = (bf16[20,16,128]{2,1,0:T(8,128)(2,1)S(1)}, bf16[20,16,128]{2,1,0:T(8,128)(2,1)S(1)}, u32[]{:S(2)}, u32[]{:S(2)}) collective-permute-start(bf16[20,16,128]{2,1,0:T(8,128)(2,1)S(1)} %slice.refs_0_), channel_id=1, source_target_pairs={{0,4},{4,0},{8,12},{12,8},{1,5},{5,1},{9,13},{13,9},{2,6},{6,2},{1... | collective-permute-start | bytes 245768 | tf_op jit(solution)/shard_map/ppermute | solution.py:126
  4.1 9.2 %collective-permute-start.1 = (bf16[20,16,128]{2,1,0:T(8,128)(2,1)S(1)}, bf16[20,16,128]{2,1,0:T(8,128)(2,1)S(1)}, u32[]{:S(2)}, u32[]{:S(2)}) collective-permute-start(bf16[20,16,128]{2,1,0:T(8,128)(2,1)S(1)} %slice.refs_0_), channel_id=1, source_target_pairs={{0,8},{4,12},{8,0},{12,4},{1,9},{5,13},{9,1},{13,5},{2,10},{6,14},... | collective-permute-start | bytes 245768 | tf_op jit(solution)/shard_map/ppermute | solution.py:126
  6.7 6.6 %collective-permute-start.2 = (bf16[20,16,128]{2,1,0:T(8,128)(2,1)S(1)}, bf16[20,16,128]{2,1,0:T(8,128)(2,1)S(1)}, u32[]{:S(2)}, u32[]{:S(2)}) collective-permute-start(bf16[20,16,128]{2,1,0:T(8,128)(2,1)S(1)} %slice.refs_0_), channel_id=1, source_target_pairs={{0,12},{4,8},{8,4},{12,0},{1,13},{5,9},{9,5},{13,1},{2,14},{6,10},... | collective-permute-start | bytes 245768 | tf_op jit(solution)/shard_map/ppermute | solution.py:126
  19.4 6.6 %collective-permute-start.3 = (bf16[24,512]{1,0:T(8,128)(2,1)S(1)}, bf16[24,512]{1,0:T(8,128)(2,1)S(1)}, u32[]{:S(2)}, u32[]{:S(2)}) collective-permute-start(bf16[24,512]{1,0:T(8,128)(2,1)S(1)} %get-tuple-element.32), channel_id=1, source_target_pairs={{0,4},{4,0},{8,12},{12,8},{1,5},{5,1},{9,13},{13,9},{2,6},{6,2},{1... | collective-permute-start | bytes 73736 | tf_op jit(solution)/shard_map/ppermute | solution.py:126
  20.9 5.1 %collective-permute-start.4 = (bf16[24,512]{1,0:T(8,128)(2,1)S(1)}, bf16[24,512]{1,0:T(8,128)(2,1)S(1)}, u32[]{:S(2)}, u32[]{:S(2)}) collective-permute-start(bf16[24,512]{1,0:T(8,128)(2,1)S(1)} %get-tuple-element.33), channel_id=1, source_target_pairs={{0,8},{4,12},{8,0},{12,4},{1,9},{5,13},{9,1},{13,5},{2,10},{6,14},... | collective-permute-start | bytes 73736 | tf_op jit(solution)/shard_map/ppermute | solution.py:126
  23.6 5.6 %collective-permute-start.5 = (bf16[24,512]{1,0:T(8,128)(2,1)S(1)}, bf16[24,512]{1,0:T(8,128)(2,1)S(1)}, u32[]{:S(2)}, u32[]{:S(2)}) collective-permute-start(bf16[24,512]{1,0:T(8,128)(2,1)S(1)} %get-tuple-element.34), channel_id=1, source_target_pairs={{0,12},{4,8},{8,4},{12,0},{1,13},{5,9},{9,5},{13,1},{2,14},{6,10},... | collective-permute-start | bytes 73736 | tf_op jit(solution)/shard_map/ppermute | solution.py:126
  29.4 4.5 %collective-permute-start.7 = (bf16[80,512]{1,0:T(8,128)(2,1)S(1)}, bf16[80,512]{1,0:T(8,128)(2,1)S(1)}, u32[]{:S(2)}, u32[]{:S(2)}) collective-permute-start(bf16[80,512]{1,0:T(8,128)(2,1)S(1)} %ordered.1.refs_0_), channel_id=1, source_target_pairs={{0,2},{1,3},{2,0},{3,1},{4,6},{5,7},{6,4},{7,5},{8,10},{9,11},{10,... | collective-permute-start | bytes 245768 | tf_op jit(solution)/shard_map/ppermute | solution.py:126
  36.8 8.0 %collective-permute-start.10 = (bf16[40,1024]{1,0:T(8,128)(2,1)S(1)}, bf16[40,1024]{1,0:T(8,128)(2,1)S(1)}, u32[]{:S(2)}, u32[]{:S(2)}) collective-permute-start(bf16[40,1024]{1,0:T(8,128)(2,1)S(1)} %get-tuple-element.38), channel_id=1, source_target_pairs={{0,8},{4,12},{8,0},{12,4},{1,9},{5,13},{9,1},{13,5},{2,10},{6,14},... | collective-permute-start | bytes 245768 | tf_op jit(solution)/shard_map/ppermute | solution.py:126
  36.9 8.0 %collective-permute-start.11 = (bf16[40,1024]{1,0:T(8,128)(2,1)S(1)}, bf16[40,1024]{1,0:T(8,128)(2,1)S(1)}, u32[]{:S(2)}, u32[]{:S(2)}) collective-permute-start(bf16[40,1024]{1,0:T(8,128)(2,1)S(1)} %get-tuple-element.39), channel_id=1, source_target_pairs={{0,12},{4,8},{8,4},{12,0},{1,13},{5,9},{9,5},{13,1},{2,14},{6,10},... | collective-permute-start | bytes 245768 | tf_op jit(solution)/shard_map/ppermute | solution.py:126
  37.8 8.0 %collective-permute-start.9 = (bf16[40,1024]{1,0:T(8,128)(2,1)S(1)}, bf16[40,1024]{1,0:T(8,128)(2,1)S(1)}, u32[]{:S(2)}, u32[]{:S(2)}) collective-permute-start(bf16[40,1024]{1,0:T(8,128)(2,1)S(1)} %get-tuple-element.37), channel_id=1, source_target_pairs={{0,4},{4,0},{8,12},{12,8},{1,5},{5,1},{9,13},{13,9},{2,6},{6,2},{1... | collective-permute-start | bytes 245768 | tf_op jit(solution)/shard_map/ppermute | solution.py:126
  45.9 14.0 %collective-permute-start.12 = (bf16[40,1024]{1,0:T(8,128)(2,1)S(1)}, bf16[40,1024]{1,0:T(8,128)(2,1)S(1)}, u32[]{:S(2)}, u32[]{:S(2)}) collective-permute-start(bf16[40,1024]{1,0:T(8,128)(2,1)S(1)} %residual.2.refs_0_), channel_id=1, source_target_pairs={{0,4},{4,0},{8,12},{12,8},{1,5},{5,1},{9,13},{13,9},{2,6},{6,2},{1... | collective-permute-start | bytes 245768 | tf_op jit(solution)/shard_map/ppermute | solution.py:126
  46.5 13.4 %collective-permute-start.13 = (bf16[40,1024]{1,0:T(8,128)(2,1)S(1)}, bf16[40,1024]{1,0:T(8,128)(2,1)S(1)}, u32[]{:S(2)}, u32[]{:S(2)}) collective-permute-start(bf16[40,1024]{1,0:T(8,128)(2,1)S(1)} %residual.2.refs_0_), channel_id=1, source_target_pairs={{0,8},{4,12},{8,0},{12,4},{1,9},{5,13},{9,1},{13,5},{2,10},{6,14},... | collective-permute-start | bytes 245768 | tf_op jit(solution)/shard_map/ppermute | solution.py:126
  48.2 11.7 %collective-permute-start.14 = (bf16[40,1024]{1,0:T(8,128)(2,1)S(1)}, bf16[40,1024]{1,0:T(8,128)(2,1)S(1)}, u32[]{:S(2)}, u32[]{:S(2)}) collective-permute-start(bf16[40,1024]{1,0:T(8,128)(2,1)S(1)} %residual.2.refs_0_), channel_id=1, source_target_pairs={{0,12},{4,8},{8,4},{12,0},{1,13},{5,9},{9,5},{13,1},{2,14},{6,10},... | collective-permute-start | bytes 245768 | tf_op jit(solution)/shard_map/ppermute | solution.py:126
  62.4 7.2 %collective-permute-start.18 = (bf16[80,896]{1,0:T(8,128)(2,1)S(1)}, bf16[80,896]{1,0:T(8,128)(2,1)S(1)}, u32[]{:S(2)}, u32[]{:S(2)}) collective-permute-start(bf16[80,896]{1,0:T(8,128)(2,1)S(1)} %hidden_next.9), channel_id=1, source_target_pairs={{0,1},{1,0},{2,3},{3,2},{4,5},{5,4},{6,7},{7,6},{8,9},{9,8},{10,11... | collective-permute-start | bytes 430088 | tf_op jit(solution)/shard_map/ppermute | solution.py:126
  62.5 4.2 %collective-permute-start.16 = (bf16[80,1024]{1,0:T(8,128)(2,1)S(1)}, bf16[80,1024]{1,0:T(8,128)(2,1)S(1)}, u32[]{:S(2)}, u32[]{:S(2)}) collective-permute-start(bf16[80,1024]{1,0:T(8,128)(2,1)S(1)} %get-tuple-element.42), channel_id=1, source_target_pairs={{0,1},{1,0},{2,3},{3,2},{4,5},{5,4},{6,7},{7,6},{8,9},{9,8},{10,11... | collective-permute-start | bytes 491528 | tf_op jit(solution)/shard_map/ppermute | solution.py:126
  65.3 11.2 %collective-permute-start.15 = (bf16[80,1792]{1,0:T(8,128)(2,1)S(1)}, bf16[80,1792]{1,0:T(8,128)(2,1)S(1)}, u32[]{:S(2)}, u32[]{:S(2)}) collective-permute-start(bf16[80,1792]{1,0:T(8,128)(2,1)S(1)} %hidden_next.6), channel_id=1, source_target_pairs={{0,1},{1,0},{2,3},{3,2},{4,5},{5,4},{6,7},{7,6},{8,9},{9,8},{10,11... | collective-permute-start | bytes 860168 | tf_op jit(solution)/shard_map/ppermute | solution.py:126
  66.8 9.7 %collective-permute-start.17 = (bf16[80,1024]{1,0:T(8,128)(2,1)S(1)}, bf16[80,1024]{1,0:T(8,128)(2,1)S(1)}, u32[]{:S(2)}, u32[]{:S(2)}) collective-permute-start(bf16[80,1024]{1,0:T(8,128)(2,1)S(1)} %get-tuple-element.43), channel_id=1, source_target_pairs={{0,2},{1,3},{2,0},{3,1},{4,6},{5,7},{6,4},{7,5},{8,10},{9,11},{10,... | collective-permute-start | bytes 491528 | tf_op jit(solution)/shard_map/ppermute | solution.py:126
  69.7 6.9 %collective-permute-start.19 = (bf16[80,896]{1,0:T(8,128)(2,1)S(1)}, bf16[80,896]{1,0:T(8,128)(2,1)S(1)}, u32[]{:S(2)}, u32[]{:S(2)}) collective-permute-start(bf16[80,896]{1,0:T(8,128)(2,1)S(1)} %chip_sum.1), channel_id=1, source_target_pairs={{0,2},{1,3},{2,0},{3,1},{4,6},{5,7},{6,4},{7,5},{8,10},{9,11},{10,... | collective-permute-start | bytes 430088 | tf_op jit(solution)/shard_map/ppermute | solution.py:126
  76.8 5.3 %collective-permute-start.20 = (bf16[80,896]{1,0:T(8,128)(2,1)S(1)}, bf16[80,896]{1,0:T(8,128)(2,1)S(1)}, u32[]{:S(2)}, u32[]{:S(2)}) collective-permute-start(bf16[80,896]{1,0:T(8,128)(2,1)S(1)} %active.1.refs_0_), channel_id=1, source_target_pairs={{0,2},{1,3},{2,0},{3,1},{4,6},{5,7},{6,4},{7,5},{8,10},{9,11},{10,... | collective-permute-start | bytes 430088 | tf_op jit(solution)/shard_map/ppermute | solution.py:126
  78.4 6.9 %collective-permute-start.22 = (bf16[80,896]{1,0:T(8,128)(2,1)S(1)}, bf16[80,896]{1,0:T(8,128)(2,1)S(1)}, u32[]{:S(2)}, u32[]{:S(2)}) collective-permute-start(bf16[80,896]{1,0:T(8,128)(2,1)S(1)} %active.1.refs_0_), channel_id=1, source_target_pairs={{0,1},{1,0},{2,3},{3,2},{4,5},{5,4},{6,7},{7,6},{8,9},{9,8},{10,11... | collective-permute-start | bytes 430088 | tf_op jit(solution)/shard_map/ppermute | solution.py:126
  82.1 5.5 %collective-permute-start.21 = (bf16[80,896]{1,0:T(8,128)(2,1)S(1)}, bf16[80,896]{1,0:T(8,128)(2,1)S(1)}, u32[]{:S(2)}, u32[]{:S(2)}) collective-permute-start(bf16[80,896]{1,0:T(8,128)(2,1)S(1)} %collective-permute-done.20.refs_0_), channel_id=1, source_target_pairs={{0,1},{1,0},{2,3},{3,2},{4,5},{5,4},{6,7},{7,6},{8,9},{9,8},{10,11... | collective-permute-start | bytes 430088 | tf_op jit(solution)/shard_map/ppermute | solution.py:126
  88.4 6.1 %collective-permute-start.23 = (bf16[40,1024]{1,0:T(8,128)(2,1)S(1)}, bf16[40,1024]{1,0:T(8,128)(2,1)S(1)}, u32[]{:S(2)}, u32[]{:S(2)}) collective-permute-start(bf16[40,1024]{1,0:T(8,128)(2,1)S(1)} %get-tuple-element.48), channel_id=1, source_target_pairs={{0,4},{4,0},{8,12},{12,8},{1,5},{5,1},{9,13},{13,9},{2,6},{6,2},{1... | collective-permute-start | bytes 245768 | tf_op jit(solution)/shard_map/ppermute | solution.py:126
  88.5 9.8 %collective-permute-start.24 = (bf16[40,1024]{1,0:T(8,128)(2,1)S(1)}, bf16[40,1024]{1,0:T(8,128)(2,1)S(1)}, u32[]{:S(2)}, u32[]{:S(2)}) collective-permute-start(bf16[40,1024]{1,0:T(8,128)(2,1)S(1)} %get-tuple-element.49), channel_id=1, source_target_pairs={{0,8},{4,12},{8,0},{12,4},{1,9},{5,13},{9,1},{13,5},{2,10},{6,14},... | collective-permute-start | bytes 245768 | tf_op jit(solution)/shard_map/ppermute | solution.py:126
  90.7 7.6 %collective-permute-start.25 = (bf16[40,1024]{1,0:T(8,128)(2,1)S(1)}, bf16[40,1024]{1,0:T(8,128)(2,1)S(1)}, u32[]{:S(2)}, u32[]{:S(2)}) collective-permute-start(bf16[40,1024]{1,0:T(8,128)(2,1)S(1)} %get-tuple-element.50), channel_id=1, source_target_pairs={{0,12},{4,8},{8,4},{12,0},{1,13},{5,9},{9,5},{13,1},{2,14},{6,10},... | collective-permute-start | bytes 245768 | tf_op jit(solution)/shard_map/ppermute | solution.py:126
  (6 other events, 54.3 us)

commit v8 on v7

--- a/solution.py
+++ b/solution.py
@@ -12,6 +12,8 @@
 masked_score = -1e30
 lanes = 128
 block_rows = 256
+max_context = 1279
+most_blocks = (max_context + block_rows - 2) // block_rows + 1
 slot_group = 2
 contract_minor = (((1,), (1,)), ((), ()))
 F32 = jnp.float32
@@ -275,12 +277,10 @@
         first = jnp.where(covered, first + 1, first)
         last = (end - 1) // block_rows
 
-        def item(block, made):
-            items[2 * made] = block
-            items[2 * made + 1] = s
-            return made + 1
-
-        made_now = lax.fori_loop(first, last + 1, item, made)
+        for j in range(most_blocks):
+            items[2 * (made + j)] = first + j
+            items[2 * (made + j) + 1] = s
+        made_now = made + jnp.maximum(last + 1 - first, 0)
         new = made_now > made
         return (
             end,
@@ -290,7 +290,8 @@
         )
 
     none = jnp.int32(-1)
-    _, made, _, _ = lax.fori_loop(0, slots, slot, (jnp.int32(0), jnp.int32(0), none, none))
+    start = (jnp.int32(0), jnp.int32(0), none, none)
+    _, made, _, _ = lax.fori_loop(0, slots, slot, start, unroll=True)
     for u in range(unroll):
         items[2 * (made + u)] = 0
         items[2 * (made + u) + 1] = slots
@@ -353,11 +354,11 @@
         copy.wait()
 
 
-def attention(table, query_blocks, keys, values, jobs, parts, unroll=8):
+def attention(table, query_blocks, keys, values, jobs, parts, unroll=14):
     count = len(query_blocks)
     slots, heads, _ = query_blocks[0].shape
     pool, width = keys.shape
-    most = pool // block_rows + slots + unroll
+    most = pool // block_rows + slots + max(unroll, most_blocks)
     rows = (slots + slot_group) * heads
     return pl.pallas_call(
         functools.partial(

time: 99.2 us -> 98.6 us (level)
  transfers between devices with their start and end apart: 26 -> 26, of which waited for: 10 -> 10; matrix products, arithmetic and copies ran while one was open for 0% -> 0% of each run, Pallas kernels for 29% -> 30%
where the time goes in v8:
time: 98.6 us; the launch traced here: 98.5 us
  Pallas kernels  41.4 us (42%)
  starting transfers between devices  28.6 us (29%)
  waiting for transfers between devices  27.2 us (28%)
    ppermute x26, starting transfers between devices, pair_swap(): return lax.ppermute(value, axis, [(i, i ^ bit) for i in range(count)])  28.6 us
    ppermute x26, waiting for transfers between devices, pair_swap(): return lax.ppermute(value, axis, [(i, i ^ bit) for i in range(count)])  27.2 us
    pallas_call x4, Pallas kernels, fetch(): pl.pallas_call(functools.partial(fetch_kernel, masks_of=masks_in(jobs)),...  17.4 us
    pallas_call x5, Pallas kernels, hidden_next(): pl.pallas_call(functools.partial(hidden_kernel, parts=tuple((part for _,...  8.32 us
    pallas_call x1, Pallas kernels, attention(): pl.pallas_call(functools.partial(attention_kernel, slots=slots, count=cou...  6.16 us
    pallas_call x3, Pallas kernels, down_part(): pl.pallas_call(functools.partial(down_kernel, parts=tuple((part for _, _,...  3.07 us
    pallas_call x1, Pallas kernels, selection(): pl.pallas_call(functools.partial(selection_kernel, slots=slots, count=cou...  2.1 us
  transfers between devices with their start and end apart: 26, of which 10 were waited for; matrix products, arithmetic and copies ran while one was open for 0% of the time, Pallas kernels for 30%

profile of v8, /device:TPU:0, one launch (start us, length us, event | category | flops | bytes accessed | tf_op | source)
XLA Modules:
  0.0 98.5 jit_solution(17085773098725196650)
XLA Ops:
  1.0 3.1 %collective-permute-start = (bf16[20,16,128]{2,1,0:T(8,128)(2,1)S(1)}, bf16[20,16,128]{2,1,0:T(8,128)(2,1)S(1)}, u32[]{:S(2)}, u32[]{:S(2)}) collective-permute-start(bf16[20,16,128]{2,1,0:T(8,128)(2,1)S(1)} %slice.refs_0_), channel_id=1, source_target_pairs={{0,4},{4,0},{8,12},{12,8},{1,5},{5,1},{9,13},{13,9},{2,6},{6,2},{1... | collective-permute-start | bytes 245768 | tf_op jit(solution)/shard_map/ppermute | solution.py:128
  4.1 2.6 %collective-permute-start.1 = (bf16[20,16,128]{2,1,0:T(8,128)(2,1)S(1)}, bf16[20,16,128]{2,1,0:T(8,128)(2,1)S(1)}, u32[]{:S(2)}, u32[]{:S(2)}) collective-permute-start(bf16[20,16,128]{2,1,0:T(8,128)(2,1)S(1)} %slice.refs_0_), channel_id=1, source_target_pairs={{0,8},{4,12},{8,0},{12,4},{1,9},{5,13},{9,1},{13,5},{2,10},{6,14},... | collective-permute-start | bytes 245768 | tf_op jit(solution)/shard_map/ppermute | solution.py:128
  6.7 4.8 %fetch.4 = (bf16[12800,256]{1,0:T(8,128)(2,1)S(1)}, bf16[12800,256]{1,0:T(8,128)(2,1)S(1)}) custom-call(bf16[12800,256]{1,0:T(8,128)(2,1)} %refs_0_.5, bf16[12800,256]{1,0:T(8,128)(2,1)} %refs_1_.1), custom_call_target="tpu_custom_call" | custom-call | bytes 26214400 | tf_op jit(solution)/shard_map/fetch/pallas_call | solution.py:212
  11.5 1.7 %collective-permute-done.1.refs_2_ = bf16[20,16,128]{2,1,0:T(8,128)(2,1)S(1)} collective-permute-done((bf16[20,16,128]{2,1,0:T(8,128)(2,1)S(1)}, bf16[20,16,128]{2,1,0:T(8,128)(2,1)S(1)}, u32[]{:S(2)}, u32[]{:S(2)}) %collective-permute-start.1) | collective-permute-done | bytes 81952 | tf_op jit(solution)/shard_map/ppermute | solution.py:128
  13.3 6.2 %attention.1 = (bf16[24,512]{1,0:T(8,128)(2,1)S(1)}, bf16[24,512]{1,0:T(8,128)(2,1)S(1)}, bf16[24,512]{1,0:T(8,128)(2,1)S(1)}, bf16[24,512]{1,0:T(8,128)(2,1)S(1...) custom-call(s32[102]{0:T(128)S(1)} %pad_add_fusion.table, bf16[20,16,128]{2,1,0:T(8,128)(2,1)S(1)} %slice.refs_0_, ...), custom_call_target="tpu_custom_call" | custom-call | flops 104857600 | bytes 13107200 | tf_op jit(solution)/shard_map/attention/pallas_call | solution.py:363
  23.9 2.1 %selection.1 = (bf16[1,896,2048]{2,1,0:T(8,128)(2,1)S(1)}, bf16[4,80,24]{2,1,0:T(8,128)(2,1)S(1)}) custom-call(s32[8,128]{1,0:T(8,128)S(1)} %broadcast_in_dim.3.served, bf16[3584,2048]{1,0:T(8,128)(2,1)} %refs_0_.8), custom_call_target="tpu_custom_call" | custom-call | bytes 7340032 | tf_op jit(solution)/shard_map/selection/pallas_call | solution.py:427
  26.0 2.1 %collective-permute-done.5.refs_3_ = bf16[24,512]{1,0:T(8,128)(2,1)S(1)} collective-permute-done((bf16[24,512]{1,0:T(8,128)(2,1)S(1)}, bf16[24,512]{1,0:T(8,128)(2,1)S(1)}, u32[]{:S(2)}, u32[]{:S(2)}) %collective-permute-start.5) | collective-permute-done | bytes 24608 | tf_op jit(solution)/shard_map/ppermute | solution.py:128
  29.9 2.9 %collective-permute-done.7.refs_2_ = bf16[80,512]{1,0:T(8,128)(2,1)S(1)} collective-permute-done((bf16[80,512]{1,0:T(8,128)(2,1)S(1)}, bf16[80,512]{1,0:T(8,128)(2,1)S(1)}, u32[]{:S(2)}, u32[]{:S(2)}) %collective-permute-start.7) | collective-permute-done | bytes 81952 | tf_op jit(solution)/shard_map/ppermute | solution.py:128
  34.2 1.6 %projection.1 = (bf16[40,1024]{1,0:T(8,128)(2,1)S(1)}, bf16[40,1024]{1,0:T(8,128)(2,1)S(1)}, bf16[40,1024]{1,0:T(8,128)(2,1)S(1)}, bf16[40,1024]{1,0:T(8,128)(2,1)S(1)}) custom-call(bf16[80,512]{1,0:T(8,128)(2,1)S(1)} %ordered.1.refs_0_, bf16[80,512]{1,0:T(8,128)(2,1)S(1)} %collective-permute-done.6.refs_1_, ...), custom_call_target="tpu_custom_call" | custom-call | flops 671088640 | bytes 4194304 | tf_op jit(solution)/shard_map/projection/pallas_call | solution.py:473
  35.9 2.0 %collective-permute-start.11 = (bf16[40,1024]{1,0:T(8,128)(2,1)S(1)}, bf16[40,1024]{1,0:T(8,128)(2,1)S(1)}, u32[]{:S(2)}, u32[]{:S(2)}) collective-permute-start(bf16[40,1024]{1,0:T(8,128)(2,1)S(1)} %get-tuple-element.39), channel_id=1, source_target_pairs={{0,12},{4,8},{8,4},{12,0},{1,13},{5,9},{9,5},{13,1},{2,14},{6,10},... | collective-permute-start | bytes 245768 | tf_op jit(solution)/shard_map/ppermute | solution.py:128
  39.3 4.6 %collective-permute-done.10.refs_3_ = bf16[40,1024]{1,0:T(8,128)(2,1)S(1)} collective-permute-done((bf16[40,1024]{1,0:T(8,128)(2,1)S(1)}, bf16[40,1024]{1,0:T(8,128)(2,1)S(1)}, u32[]{:S(2)}, u32[]{:S(2)}) %collective-permute-start.10) | collective-permute-done | bytes 81952 | tf_op jit(solution)/shard_map/ppermute | solution.py:128
  46.3 1.7 %collective-permute-start.13 = (bf16[40,1024]{1,0:T(8,128)(2,1)S(1)}, bf16[40,1024]{1,0:T(8,128)(2,1)S(1)}, u32[]{:S(2)}, u32[]{:S(2)}) collective-permute-start(bf16[40,1024]{1,0:T(8,128)(2,1)S(1)} %residual.2.refs_0_), channel_id=1, source_target_pairs={{0,8},{4,12},{8,0},{12,4},{1,9},{5,13},{9,1},{13,5},{2,10},{6,14},... | collective-permute-start | bytes 245768 | tf_op jit(solution)/shard_map/ppermute | solution.py:128
  48.1 1.7 %collective-permute-start.14 = (bf16[40,1024]{1,0:T(8,128)(2,1)S(1)}, bf16[40,1024]{1,0:T(8,128)(2,1)S(1)}, u32[]{:S(2)}, u32[]{:S(2)}) collective-permute-start(bf16[40,1024]{1,0:T(8,128)(2,1)S(1)} %residual.2.refs_0_), channel_id=1, source_target_pairs={{0,12},{4,8},{8,4},{12,0},{1,13},{5,9},{9,5},{13,1},{2,14},{6,10},... | collective-permute-start | bytes 245768 | tf_op jit(solution)/shard_map/ppermute | solution.py:128
  49.8 4.2 %fetch.6.refs_1_.refs_0_ = bf16[3,896,2048]{2,1,0:T(8,128)(2,1)S(1)} custom-call(bf16[3584,2048]{1,0:T(8,128)(2,1)} %refs_0_.8), custom_call_target="tpu_custom_call" | custom-call | bytes 22020096 | tf_op jit(solution)/shard_map/fetch/pallas_call | solution.py:212
  54.0 5.3 %fetch.5.refs_5_.refs_0_ = bf16[4,896,2048]{2,1,0:T(8,128)(2,1)S(1)} custom-call(bf16[3584,2048]{1,0:T(8,128)(2,1)} %refs_0_.7), custom_call_target="tpu_custom_call" | custom-call | bytes 29360128 | tf_op jit(solution)/shard_map/fetch/pallas_call | solution.py:212
  62.4 2.3 %hidden_next.6 = bf16[80,1792]{1,0:T(8,128)(2,1)S(1)} custom-call(bf16[80,2048]{1,0:T(8,128)(2,1)S(1)} %get-tuple-element.40.scaled, bf16[4,896,2048]{2,1,0:T(8,128)(2,1)S(1)} %fetch.5.refs_5_.refs_0_, bf16[3,896,2048]{2,1,0:T(8,128)(2,1)S(1)} %fetch.6.refs_1_.refs_0_), custom_call_target="tpu_custom_call" | custom-call | flops 587202560 | bytes 3670016 | tf_op jit(solution)/shard_map/hidden_next/pallas_call | solution.py:568
  69.7 2.3 %hidden_next.5.near = f32[80,1792]{1,0:T(8,128)S(1)} custom-call(bf16[80,2048]{1,0:T(8,128)(2,1)S(1)} %get-tuple-element.40.scaled, bf16[4,896,2048]{2,1,0:T(8,128)(2,1)S(1)} %fetch.5.refs_5_.refs_0_, bf16[3,896,2048]{2,1,0:T(8,128)(2,1)S(1)} %fetch.6.refs_1_.refs_0_), custom_call_target="tpu_custom_call" | custom-call | flops 587202560 | bytes 3670016 | tf_op jit(solution)/shard_map/hidden_next/pallas_call | solution.py:568
  72.0 3.9 %collective-permute-done.19.far_up = bf16[80,896]{1,0:T(8,128)(2,1)S(1)} collective-permute-done((bf16[80,896]{1,0:T(8,128)(2,1)S(1)}, bf16[80,896]{1,0:T(8,128)(2,1)S(1)}, u32[]{:S(2)}, u32[]{:S(2)}) %collective-permute-start.19) | collective-permute-done | bytes 143392 | tf_op jit(solution)/shard_map/ppermute | solution.py:128
  77.8 3.7 %collective-permute-done.20.refs_0_ = bf16[80,896]{1,0:T(8,128)(2,1)S(1)} collective-permute-done((bf16[80,896]{1,0:T(8,128)(2,1)S(1)}, bf16[80,896]{1,0:T(8,128)(2,1)S(1)}, u32[]{:S(2)}, u32[]{:S(2)}) %collective-permute-start.20) | collective-permute-done | bytes 143392 | tf_op jit(solution)/shard_map/ppermute | solution.py:128
  81.6 3.2 %fetch.7.refs_1_ = bf16[2,896,2048]{2,1,0:T(8,128)(2,1)S(1)} custom-call(bf16[3584,2048]{1,0:T(8,128)(2,1)} %refs_0_.9), custom_call_target="tpu_custom_call" | custom-call | bytes 14680064 | tf_op jit(solution)/shard_map/fetch/pallas_call | solution.py:212
  88.0 2.6 %collective-permute-start.24 = (bf16[40,1024]{1,0:T(8,128)(2,1)S(1)}, bf16[40,1024]{1,0:T(8,128)(2,1)S(1)}, u32[]{:S(2)}, u32[]{:S(2)}) collective-permute-start(bf16[40,1024]{1,0:T(8,128)(2,1)S(1)} %get-tuple-element.49), channel_id=1, source_target_pairs={{0,8},{4,12},{8,0},{12,4},{1,9},{5,13},{9,1},{13,5},{2,10},{6,14},... | collective-permute-start | bytes 245768 | tf_op jit(solution)/shard_map/ppermute | solution.py:128
  90.6 1.7 %collective-permute-start.25 = (bf16[40,1024]{1,0:T(8,128)(2,1)S(1)}, bf16[40,1024]{1,0:T(8,128)(2,1)S(1)}, u32[]{:S(2)}, u32[]{:S(2)}) collective-permute-start(bf16[40,1024]{1,0:T(8,128)(2,1)S(1)} %get-tuple-element.50), channel_id=1, source_target_pairs={{0,12},{4,8},{8,4},{12,0},{1,13},{5,9},{9,5},{13,1},{2,14},{6,10},... | collective-permute-start | bytes 245768 | tf_op jit(solution)/shard_map/ppermute | solution.py:128
  92.3 1.7 %collective-permute-done.23.refs_2_ = bf16[40,1024]{1,0:T(8,128)(2,1)S(1)} collective-permute-done((bf16[40,1024]{1,0:T(8,128)(2,1)S(1)}, bf16[40,1024]{1,0:T(8,128)(2,1)S(1)}, u32[]{:S(2)}, u32[]{:S(2)}) %collective-permute-start.23) | collective-permute-done | bytes 81952 | tf_op jit(solution)/shard_map/ppermute | solution.py:128
  94.0 3.8 %collective-permute-done.24.refs_3_ = bf16[40,1024]{1,0:T(8,128)(2,1)S(1)} collective-permute-done((bf16[40,1024]{1,0:T(8,128)(2,1)S(1)}, bf16[40,1024]{1,0:T(8,128)(2,1)S(1)}, u32[]{:S(2)}, u32[]{:S(2)}) %collective-permute-start.24) | collective-permute-done | bytes 81952 | tf_op jit(solution)/shard_map/ppermute | solution.py:128
  (64 shorter events, 26.2 us)
Async XLA Ops:
  1.0 10.6 %collective-permute-start = (bf16[20,16,128]{2,1,0:T(8,128)(2,1)S(1)}, bf16[20,16,128]{2,1,0:T(8,128)(2,1)S(1)}, u32[]{:S(2)}, u32[]{:S(2)}) collective-permute-start(bf16[20,16,128]{2,1,0:T(8,128)(2,1)S(1)} %slice.refs_0_), channel_id=1, source_target_pairs={{0,4},{4,0},{8,12},{12,8},{1,5},{5,1},{9,13},{13,9},{2,6},{6,2},{1... | collective-permute-start | bytes 245768 | tf_op jit(solution)/shard_map/ppermute | solution.py:128
  4.1 9.2 %collective-permute-start.1 = (bf16[20,16,128]{2,1,0:T(8,128)(2,1)S(1)}, bf16[20,16,128]{2,1,0:T(8,128)(2,1)S(1)}, u32[]{:S(2)}, u32[]{:S(2)}) collective-permute-start(bf16[20,16,128]{2,1,0:T(8,128)(2,1)S(1)} %slice.refs_0_), channel_id=1, source_target_pairs={{0,8},{4,12},{8,0},{12,4},{1,9},{5,13},{9,1},{13,5},{2,10},{6,14},... | collective-permute-start | bytes 245768 | tf_op jit(solution)/shard_map/ppermute | solution.py:128
  6.7 6.6 %collective-permute-start.2 = (bf16[20,16,128]{2,1,0:T(8,128)(2,1)S(1)}, bf16[20,16,128]{2,1,0:T(8,128)(2,1)S(1)}, u32[]{:S(2)}, u32[]{:S(2)}) collective-permute-start(bf16[20,16,128]{2,1,0:T(8,128)(2,1)S(1)} %slice.refs_0_), channel_id=1, source_target_pairs={{0,12},{4,8},{8,4},{12,0},{1,13},{5,9},{9,5},{13,1},{2,14},{6,10},... | collective-permute-start | bytes 245768 | tf_op jit(solution)/shard_map/ppermute | solution.py:128
  19.4 6.6 %collective-permute-start.3 = (bf16[24,512]{1,0:T(8,128)(2,1)S(1)}, bf16[24,512]{1,0:T(8,128)(2,1)S(1)}, u32[]{:S(2)}, u32[]{:S(2)}) collective-permute-start(bf16[24,512]{1,0:T(8,128)(2,1)S(1)} %get-tuple-element.32), channel_id=1, source_target_pairs={{0,4},{4,0},{8,12},{12,8},{1,5},{5,1},{9,13},{13,9},{2,6},{6,2},{1... | collective-permute-start | bytes 73736 | tf_op jit(solution)/shard_map/ppermute | solution.py:128
  20.9 5.1 %collective-permute-start.4 = (bf16[24,512]{1,0:T(8,128)(2,1)S(1)}, bf16[24,512]{1,0:T(8,128)(2,1)S(1)}, u32[]{:S(2)}, u32[]{:S(2)}) collective-permute-start(bf16[24,512]{1,0:T(8,128)(2,1)S(1)} %get-tuple-element.33), channel_id=1, source_target_pairs={{0,8},{4,12},{8,0},{12,4},{1,9},{5,13},{9,1},{13,5},{2,10},{6,14},... | collective-permute-start | bytes 73736 | tf_op jit(solution)/shard_map/ppermute | solution.py:128
  22.5 5.6 %collective-permute-start.5 = (bf16[24,512]{1,0:T(8,128)(2,1)S(1)}, bf16[24,512]{1,0:T(8,128)(2,1)S(1)}, u32[]{:S(2)}, u32[]{:S(2)}) collective-permute-start(bf16[24,512]{1,0:T(8,128)(2,1)S(1)} %get-tuple-element.34), channel_id=1, source_target_pairs={{0,12},{4,8},{8,4},{12,0},{1,13},{5,9},{9,5},{13,1},{2,14},{6,10},... | collective-permute-start | bytes 73736 | tf_op jit(solution)/shard_map/ppermute | solution.py:128
  28.4 4.5 %collective-permute-start.7 = (bf16[80,512]{1,0:T(8,128)(2,1)S(1)}, bf16[80,512]{1,0:T(8,128)(2,1)S(1)}, u32[]{:S(2)}, u32[]{:S(2)}) collective-permute-start(bf16[80,512]{1,0:T(8,128)(2,1)S(1)} %ordered.1.refs_0_), channel_id=1, source_target_pairs={{0,2},{1,3},{2,0},{3,1},{4,6},{5,7},{6,4},{7,5},{8,10},{9,11},{10,... | collective-permute-start | bytes 245768 | tf_op jit(solution)/shard_map/ppermute | solution.py:128
  35.8 8.2 %collective-permute-start.10 = (bf16[40,1024]{1,0:T(8,128)(2,1)S(1)}, bf16[40,1024]{1,0:T(8,128)(2,1)S(1)}, u32[]{:S(2)}, u32[]{:S(2)}) collective-permute-start(bf16[40,1024]{1,0:T(8,128)(2,1)S(1)} %get-tuple-element.38), channel_id=1, source_target_pairs={{0,8},{4,12},{8,0},{12,4},{1,9},{5,13},{9,1},{13,5},{2,10},{6,14},... | collective-permute-start | bytes 245768 | tf_op jit(solution)/shard_map/ppermute | solution.py:128
  35.9 8.1 %collective-permute-start.11 = (bf16[40,1024]{1,0:T(8,128)(2,1)S(1)}, bf16[40,1024]{1,0:T(8,128)(2,1)S(1)}, u32[]{:S(2)}, u32[]{:S(2)}) collective-permute-start(bf16[40,1024]{1,0:T(8,128)(2,1)S(1)} %get-tuple-element.39), channel_id=1, source_target_pairs={{0,12},{4,8},{8,4},{12,0},{1,13},{5,9},{9,5},{13,1},{2,14},{6,10},... | collective-permute-start | bytes 245768 | tf_op jit(solution)/shard_map/ppermute | solution.py:128
  37.9 7.4 %collective-permute-start.9 = (bf16[40,1024]{1,0:T(8,128)(2,1)S(1)}, bf16[40,1024]{1,0:T(8,128)(2,1)S(1)}, u32[]{:S(2)}, u32[]{:S(2)}) collective-permute-start(bf16[40,1024]{1,0:T(8,128)(2,1)S(1)} %get-tuple-element.37), channel_id=1, source_target_pairs={{0,4},{4,0},{8,12},{12,8},{1,5},{5,1},{9,13},{13,9},{2,6},{6,2},{1... | collective-permute-start | bytes 245768 | tf_op jit(solution)/shard_map/ppermute | solution.py:128
  45.3 14.0 %collective-permute-start.12 = (bf16[40,1024]{1,0:T(8,128)(2,1)S(1)}, bf16[40,1024]{1,0:T(8,128)(2,1)S(1)}, u32[]{:S(2)}, u32[]{:S(2)}) collective-permute-start(bf16[40,1024]{1,0:T(8,128)(2,1)S(1)} %residual.2.refs_0_), channel_id=1, source_target_pairs={{0,4},{4,0},{8,12},{12,8},{1,5},{5,1},{9,13},{13,9},{2,6},{6,2},{1... | collective-permute-start | bytes 245768 | tf_op jit(solution)/shard_map/ppermute | solution.py:128
  46.3 13.0 %collective-permute-start.13 = (bf16[40,1024]{1,0:T(8,128)(2,1)S(1)}, bf16[40,1024]{1,0:T(8,128)(2,1)S(1)}, u32[]{:S(2)}, u32[]{:S(2)}) collective-permute-start(bf16[40,1024]{1,0:T(8,128)(2,1)S(1)} %residual.2.refs_0_), channel_id=1, source_target_pairs={{0,8},{4,12},{8,0},{12,4},{1,9},{5,13},{9,1},{13,5},{2,10},{6,14},... | collective-permute-start | bytes 245768 | tf_op jit(solution)/shard_map/ppermute | solution.py:128
  48.1 11.3 %collective-permute-start.14 = (bf16[40,1024]{1,0:T(8,128)(2,1)S(1)}, bf16[40,1024]{1,0:T(8,128)(2,1)S(1)}, u32[]{:S(2)}, u32[]{:S(2)}) collective-permute-start(bf16[40,1024]{1,0:T(8,128)(2,1)S(1)} %residual.2.refs_0_), channel_id=1, source_target_pairs={{0,12},{4,8},{8,4},{12,0},{1,13},{5,9},{9,5},{13,1},{2,14},{6,10},... | collective-permute-start | bytes 245768 | tf_op jit(solution)/shard_map/ppermute | solution.py:128
  61.9 7.2 %collective-permute-start.18 = (bf16[80,896]{1,0:T(8,128)(2,1)S(1)}, bf16[80,896]{1,0:T(8,128)(2,1)S(1)}, u32[]{:S(2)}, u32[]{:S(2)}) collective-permute-start(bf16[80,896]{1,0:T(8,128)(2,1)S(1)} %hidden_next.9), channel_id=1, source_target_pairs={{0,1},{1,0},{2,3},{3,2},{4,5},{5,4},{6,7},{7,6},{8,9},{9,8},{10,11... | collective-permute-start | bytes 430088 | tf_op jit(solution)/shard_map/ppermute | solution.py:128
  61.9 4.2 %collective-permute-start.16 = (bf16[80,1024]{1,0:T(8,128)(2,1)S(1)}, bf16[80,1024]{1,0:T(8,128)(2,1)S(1)}, u32[]{:S(2)}, u32[]{:S(2)}) collective-permute-start(bf16[80,1024]{1,0:T(8,128)(2,1)S(1)} %get-tuple-element.42), channel_id=1, source_target_pairs={{0,1},{1,0},{2,3},{3,2},{4,5},{5,4},{6,7},{7,6},{8,9},{9,8},{10,11... | collective-permute-start | bytes 491528 | tf_op jit(solution)/shard_map/ppermute | solution.py:128
  64.8 11.2 %collective-permute-start.15 = (bf16[80,1792]{1,0:T(8,128)(2,1)S(1)}, bf16[80,1792]{1,0:T(8,128)(2,1)S(1)}, u32[]{:S(2)}, u32[]{:S(2)}) collective-permute-start(bf16[80,1792]{1,0:T(8,128)(2,1)S(1)} %hidden_next.6), channel_id=1, source_target_pairs={{0,1},{1,0},{2,3},{3,2},{4,5},{5,4},{6,7},{7,6},{8,9},{9,8},{10,11... | collective-permute-start | bytes 860168 | tf_op jit(solution)/shard_map/ppermute | solution.py:128
  66.3 9.7 %collective-permute-start.17 = (bf16[80,1024]{1,0:T(8,128)(2,1)S(1)}, bf16[80,1024]{1,0:T(8,128)(2,1)S(1)}, u32[]{:S(2)}, u32[]{:S(2)}) collective-permute-start(bf16[80,1024]{1,0:T(8,128)(2,1)S(1)} %get-tuple-element.43), channel_id=1, source_target_pairs={{0,2},{1,3},{2,0},{3,1},{4,6},{5,7},{6,4},{7,5},{8,10},{9,11},{10,... | collective-permute-start | bytes 491528 | tf_op jit(solution)/shard_map/ppermute | solution.py:128
  69.1 6.9 %collective-permute-start.19 = (bf16[80,896]{1,0:T(8,128)(2,1)S(1)}, bf16[80,896]{1,0:T(8,128)(2,1)S(1)}, u32[]{:S(2)}, u32[]{:S(2)}) collective-permute-start(bf16[80,896]{1,0:T(8,128)(2,1)S(1)} %chip_sum.1), channel_id=1, source_target_pairs={{0,2},{1,3},{2,0},{3,1},{4,6},{5,7},{6,4},{7,5},{8,10},{9,11},{10,... | collective-permute-start | bytes 430088 | tf_op jit(solution)/shard_map/ppermute | solution.py:128
  76.2 5.3 %collective-permute-start.20 = (bf16[80,896]{1,0:T(8,128)(2,1)S(1)}, bf16[80,896]{1,0:T(8,128)(2,1)S(1)}, u32[]{:S(2)}, u32[]{:S(2)}) collective-permute-start(bf16[80,896]{1,0:T(8,128)(2,1)S(1)} %active.1.refs_0_), channel_id=1, source_target_pairs={{0,2},{1,3},{2,0},{3,1},{4,6},{5,7},{6,4},{7,5},{8,10},{9,11},{10,... | collective-permute-start | bytes 430088 | tf_op jit(solution)/shard_map/ppermute | solution.py:128
  77.8 6.9 %collective-permute-start.22 = (bf16[80,896]{1,0:T(8,128)(2,1)S(1)}, bf16[80,896]{1,0:T(8,128)(2,1)S(1)}, u32[]{:S(2)}, u32[]{:S(2)}) collective-permute-start(bf16[80,896]{1,0:T(8,128)(2,1)S(1)} %active.1.refs_0_), channel_id=1, source_target_pairs={{0,1},{1,0},{2,3},{3,2},{4,5},{5,4},{6,7},{7,6},{8,9},{9,8},{10,11... | collective-permute-start | bytes 430088 | tf_op jit(solution)/shard_map/ppermute | solution.py:128
  81.6 5.5 %collective-permute-start.21 = (bf16[80,896]{1,0:T(8,128)(2,1)S(1)}, bf16[80,896]{1,0:T(8,128)(2,1)S(1)}, u32[]{:S(2)}, u32[]{:S(2)}) collective-permute-start(bf16[80,896]{1,0:T(8,128)(2,1)S(1)} %collective-permute-done.20.refs_0_), channel_id=1, source_target_pairs={{0,1},{1,0},{2,3},{3,2},{4,5},{5,4},{6,7},{7,6},{8,9},{9,8},{10,11... | collective-permute-start | bytes 430088 | tf_op jit(solution)/shard_map/ppermute | solution.py:128
  87.8 6.1 %collective-permute-start.23 = (bf16[40,1024]{1,0:T(8,128)(2,1)S(1)}, bf16[40,1024]{1,0:T(8,128)(2,1)S(1)}, u32[]{:S(2)}, u32[]{:S(2)}) collective-permute-start(bf16[40,1024]{1,0:T(8,128)(2,1)S(1)} %get-tuple-element.48), channel_id=1, source_target_pairs={{0,4},{4,0},{8,12},{12,8},{1,5},{5,1},{9,13},{13,9},{2,6},{6,2},{1... | collective-permute-start | bytes 245768 | tf_op jit(solution)/shard_map/ppermute | solution.py:128
  88.0 9.8 %collective-permute-start.24 = (bf16[40,1024]{1,0:T(8,128)(2,1)S(1)}, bf16[40,1024]{1,0:T(8,128)(2,1)S(1)}, u32[]{:S(2)}, u32[]{:S(2)}) collective-permute-start(bf16[40,1024]{1,0:T(8,128)(2,1)S(1)} %get-tuple-element.49), channel_id=1, source_target_pairs={{0,8},{4,12},{8,0},{12,4},{1,9},{5,13},{9,1},{13,5},{2,10},{6,14},... | collective-permute-start | bytes 245768 | tf_op jit(solution)/shard_map/ppermute | solution.py:128
  90.6 7.2 %collective-permute-start.25 = (bf16[40,1024]{1,0:T(8,128)(2,1)S(1)}, bf16[40,1024]{1,0:T(8,128)(2,1)S(1)}, u32[]{:S(2)}, u32[]{:S(2)}) collective-permute-start(bf16[40,1024]{1,0:T(8,128)(2,1)S(1)} %get-tuple-element.50), channel_id=1, source_target_pairs={{0,12},{4,8},{8,4},{12,0},{1,13},{5,9},{9,5},{13,1},{2,14},{6,10},... | collective-permute-start | bytes 245768 | tf_op jit(solution)/shard_map/ppermute | solution.py:128
  (6 other events, 53.8 us)

commit v9 on v8

--- a/solution.py
+++ b/solution.py
@@ -718,7 +718,7 @@
     own_queries = queries.reshape(slots, heads, lanes)
     query_blocks = swaps_of([own_queries] * count)
     keys, values = fetch([(key_cache, None), (value_cache, None)], parts)
-    jobs = [(out_weight.reshape(-1, columns), (0, 1, 2, 3)), (down_weight, (0, 1))]
+    jobs = [(out_weight.reshape(-1, columns), (0, 1, 2, 3)), (down_weight, (0,))]
     *blocks, project, down_near = attention(table, query_blocks, keys, values, jobs, parts)
 
     blocks = swaps_of(blocks)
@@ -732,7 +732,8 @@
     (down_far,) = fetch([(down_weight, (2, 3))], parts)
     gain = norm_gain.reshape(1, columns)
     partial = projection([piece, beside, across, corner], project, slots, count)
-    (gate,) = fetch([(gate_weight, (0, 1, 2, 3))], parts)
+    jobs = [(gate_weight, (0, 1, 2, 3)), (down_weight, (1,))]
+    gate, down_beside = fetch(jobs, parts)
     middle = residual(hidden_state, swaps_of(partial), False)
 
     rows = swaps_of([middle] * count)
@@ -753,7 +754,7 @@
 
     across = pair_swap(active, "ffn", 2)
     beside = pair_swap(active, "ffn", 1)
-    chosen = [(active, down_near, 0), (beside, down_near, 1)]
+    chosen = [(active, down_near, 0), (beside, down_beside, 0)]
     (before,) = down_part(chosen, count, None, False)
     corner = pair_swap(across, "ffn", 1)
     (before,) = down_part([(across, down_far, 0)], count, before, False)

time: 98.6 us -> 99.1 us (level)
    pallas_call x4, Pallas kernels: 17.4 us -> 18.5 us  [fetch(): pl.pallas_call(functools.partial(fetch_kernel, masks_of=masks_in(jobs)),...]
    pallas_call x1, Pallas kernels: 6.16 us -> 5.1 us  [attention(): pl.pallas_call(functools.partial(attention_kernel, slots=slots, count=cou...]
where the time goes in v9:
time: 99.1 us; the launch traced here: 98.9 us
  Pallas kernels  41.4 us (42%)
  starting transfers between devices  28.6 us (29%)
  waiting for transfers between devices  27.7 us (28%)
    ppermute x26, starting transfers between devices, pair_swap(): return lax.ppermute(value, axis, [(i, i ^ bit) for i in range(count)])  28.6 us
    ppermute x26, waiting for transfers between devices, pair_swap(): return lax.ppermute(value, axis, [(i, i ^ bit) for i in range(count)])  27.7 us
    pallas_call x4, Pallas kernels, fetch(): pl.pallas_call(functools.partial(fetch_kernel, masks_of=masks_in(jobs)),...  18.5 us
    pallas_call x5, Pallas kernels, hidden_next(): pl.pallas_call(functools.partial(hidden_kernel, parts=tuple((part for _,...  8.32 us
    pallas_call x1, Pallas kernels, attention(): pl.pallas_call(functools.partial(attention_kernel, slots=slots, count=cou...  5.1 us
    pallas_call x3, Pallas kernels, down_part(): pl.pallas_call(functools.partial(down_kernel, parts=tuple((part for _, _,...  3.08 us
    pallas_call x1, Pallas kernels, selection(): pl.pallas_call(functools.partial(selection_kernel, slots=slots, count=cou...  2.06 us
  transfers between devices with their start and end apart: 26, of which 10 were waited for; matrix products, arithmetic and copies ran while one was open for 0% of the time, Pallas kernels for 30%

profile of v9, /device:TPU:0, one launch (start us, length us, event | category | flops | bytes accessed | tf_op | source)
XLA Modules:
  0.0 98.9 jit_solution(11285586010701925143)
XLA Ops:
  1.0 3.1 %collective-permute-start = (bf16[20,16,128]{2,1,0:T(8,128)(2,1)S(1)}, bf16[20,16,128]{2,1,0:T(8,128)(2,1)S(1)}, u32[]{:S(2)}, u32[]{:S(2)}) collective-permute-start(bf16[20,16,128]{2,1,0:T(8,128)(2,1)S(1)} %slice.refs_0_), channel_id=1, source_target_pairs={{0,4},{4,0},{8,12},{12,8},{1,5},{5,1},{9,13},{13,9},{2,6},{6,2},{1... | collective-permute-start | bytes 245768 | tf_op jit(solution)/shard_map/ppermute | solution.py:128
  4.1 2.6 %collective-permute-start.1 = (bf16[20,16,128]{2,1,0:T(8,128)(2,1)S(1)}, bf16[20,16,128]{2,1,0:T(8,128)(2,1)S(1)}, u32[]{:S(2)}, u32[]{:S(2)}) collective-permute-start(bf16[20,16,128]{2,1,0:T(8,128)(2,1)S(1)} %slice.refs_0_), channel_id=1, source_target_pairs={{0,8},{4,12},{8,0},{12,4},{1,9},{5,13},{9,1},{13,5},{2,10},{6,14},... | collective-permute-start | bytes 245768 | tf_op jit(solution)/shard_map/ppermute | solution.py:128
  6.7 4.8 %fetch.4 = (bf16[12800,256]{1,0:T(8,128)(2,1)S(1)}, bf16[12800,256]{1,0:T(8,128)(2,1)S(1)}) custom-call(bf16[12800,256]{1,0:T(8,128)(2,1)} %refs_0_.5, bf16[12800,256]{1,0:T(8,128)(2,1)} %refs_1_.2), custom_call_target="tpu_custom_call" | custom-call | bytes 26214400 | tf_op jit(solution)/shard_map/fetch/pallas_call | solution.py:212
  11.5 1.7 %collective-permute-done.1.refs_2_ = bf16[20,16,128]{2,1,0:T(8,128)(2,1)S(1)} collective-permute-done((bf16[20,16,128]{2,1,0:T(8,128)(2,1)S(1)}, bf16[20,16,128]{2,1,0:T(8,128)(2,1)S(1)}, u32[]{:S(2)}, u32[]{:S(2)}) %collective-permute-start.1) | collective-permute-done | bytes 81952 | tf_op jit(solution)/shard_map/ppermute | solution.py:128
  13.3 5.1 %attention.1 = (bf16[24,512]{1,0:T(8,128)(2,1)S(1)}, bf16[24,512]{1,0:T(8,128)(2,1)S(1)}, bf16[24,512]{1,0:T(8,128)(2,1)S(1)}, bf16[24,512]{1,0:T(8,128)(2,1)S(1...) custom-call(s32[102]{0:T(128)S(1)} %pad_add_fusion.table, bf16[20,16,128]{2,1,0:T(8,128)(2,1)S(1)} %slice.refs_0_, ...), custom_call_target="tpu_custom_call" | custom-call | flops 104857600 | bytes 13107200 | tf_op jit(solution)/shard_map/attention/pallas_call | solution.py:363
  19.9 2.5 %collective-permute-start.4 = (bf16[24,512]{1,0:T(8,128)(2,1)S(1)}, bf16[24,512]{1,0:T(8,128)(2,1)S(1)}, u32[]{:S(2)}, u32[]{:S(2)}) collective-permute-start(bf16[24,512]{1,0:T(8,128)(2,1)S(1)} %get-tuple-element.35), channel_id=1, source_target_pairs={{0,8},{4,12},{8,0},{12,4},{1,9},{5,13},{9,1},{13,5},{2,10},{6,14},... | collective-permute-start | bytes 73736 | tf_op jit(solution)/shard_map/ppermute | solution.py:128
  22.8 2.1 %selection.1 = (bf16[1,896,2048]{2,1,0:T(8,128)(2,1)S(1)}, bf16[4,80,24]{2,1,0:T(8,128)(2,1)S(1)}) custom-call(s32[8,128]{1,0:T(8,128)S(1)} %broadcast_in_dim.3.served, bf16[3584,2048]{1,0:T(8,128)(2,1)} %refs_0_.8), custom_call_target="tpu_custom_call" | custom-call | bytes 7340032 | tf_op jit(solution)/shard_map/selection/pallas_call | solution.py:427
  24.9 3.1 %collective-permute-done.5.refs_3_ = bf16[24,512]{1,0:T(8,128)(2,1)S(1)} collective-permute-done((bf16[24,512]{1,0:T(8,128)(2,1)S(1)}, bf16[24,512]{1,0:T(8,128)(2,1)S(1)}, u32[]{:S(2)}, u32[]{:S(2)}) %collective-permute-start.5) | collective-permute-done | bytes 24608 | tf_op jit(solution)/shard_map/ppermute | solution.py:128
  29.8 3.0 %collective-permute-done.7.refs_2_ = bf16[80,512]{1,0:T(8,128)(2,1)S(1)} collective-permute-done((bf16[80,512]{1,0:T(8,128)(2,1)S(1)}, bf16[80,512]{1,0:T(8,128)(2,1)S(1)}, u32[]{:S(2)}, u32[]{:S(2)}) %collective-permute-start.7) | collective-permute-done | bytes 81952 | tf_op jit(solution)/shard_map/ppermute | solution.py:128
  36.8 2.4 %collective-permute-start.9 = (bf16[40,1024]{1,0:T(8,128)(2,1)S(1)}, bf16[40,1024]{1,0:T(8,128)(2,1)S(1)}, u32[]{:S(2)}, u32[]{:S(2)}) collective-permute-start(bf16[40,1024]{1,0:T(8,128)(2,1)S(1)} %get-tuple-element.39), channel_id=1, source_target_pairs={{0,4},{4,0},{8,12},{12,8},{1,5},{5,1},{9,13},{13,9},{2,6},{6,2},{1... | collective-permute-start | bytes 245768 | tf_op jit(solution)/shard_map/ppermute | solution.py:128
  39.2 4.5 %collective-permute-done.10.refs_3_ = bf16[40,1024]{1,0:T(8,128)(2,1)S(1)} collective-permute-done((bf16[40,1024]{1,0:T(8,128)(2,1)S(1)}, bf16[40,1024]{1,0:T(8,128)(2,1)S(1)}, u32[]{:S(2)}, u32[]{:S(2)}) %collective-permute-start.10) | collective-permute-done | bytes 81952 | tf_op jit(solution)/shard_map/ppermute | solution.py:128
  45.4 1.7 %collective-permute-start.13 = (bf16[40,1024]{1,0:T(8,128)(2,1)S(1)}, bf16[40,1024]{1,0:T(8,128)(2,1)S(1)}, u32[]{:S(2)}, u32[]{:S(2)}) collective-permute-start(bf16[40,1024]{1,0:T(8,128)(2,1)S(1)} %residual.2.refs_0_), channel_id=1, source_target_pairs={{0,8},{4,12},{8,0},{12,4},{1,9},{5,13},{9,1},{13,5},{2,10},{6,14},... | collective-permute-start | bytes 245768 | tf_op jit(solution)/shard_map/ppermute | solution.py:128
  47.1 2.1 %collective-permute-start.14 = (bf16[40,1024]{1,0:T(8,128)(2,1)S(1)}, bf16[40,1024]{1,0:T(8,128)(2,1)S(1)}, u32[]{:S(2)}, u32[]{:S(2)}) collective-permute-start(bf16[40,1024]{1,0:T(8,128)(2,1)S(1)} %residual.2.refs_0_), channel_id=1, source_target_pairs={{0,12},{4,8},{8,4},{12,0},{1,13},{5,9},{9,5},{13,1},{2,14},{6,10},... | collective-permute-start | bytes 245768 | tf_op jit(solution)/shard_map/ppermute | solution.py:128
  49.2 4.2 %fetch.6.refs_1_.refs_0_ = bf16[3,896,2048]{2,1,0:T(8,128)(2,1)S(1)} custom-call(bf16[3584,2048]{1,0:T(8,128)(2,1)} %refs_0_.8), custom_call_target="tpu_custom_call" | custom-call | bytes 22020096 | tf_op jit(solution)/shard_map/fetch/pallas_call | solution.py:212
  53.4 6.3 %fetch.5 = (bf16[4,896,2048]{2,1,0:T(8,128)(2,1)S(1)}, bf16[1,896,2048]{2,1,0:T(8,128)(2,1)S(1)}) custom-call(bf16[3584,2048]{1,0:T(8,128)(2,1)} %refs_0_.7, bf16[3584,2048]{1,0:T(8,128)(2,1)} %refs_0_.9), custom_call_target="tpu_custom_call" | custom-call | bytes 36700160 | tf_op jit(solution)/shard_map/fetch/pallas_call | solution.py:212
  62.9 2.3 %hidden_next.6 = bf16[80,1792]{1,0:T(8,128)(2,1)S(1)} custom-call(bf16[80,2048]{1,0:T(8,128)(2,1)S(1)} %get-tuple-element.43.scaled, bf16[4,896,2048]{2,1,0:T(8,128)(2,1)S(1)} %get-tuple-element.42.refs_5_.refs_0_, bf16[3,896,2048]{2,1,0:T(8,128)(2,1)S(1)} %fetch.6.refs_1_.refs_0_), custom_call_target="tpu_custom_call" | custom-call | flops 587202560 | bytes 3670016 | tf_op jit(solution)/shard_map/hidden_next/pallas_call | solution.py:568
  70.2 2.3 %hidden_next.5.near = f32[80,1792]{1,0:T(8,128)S(1)} custom-call(bf16[80,2048]{1,0:T(8,128)(2,1)S(1)} %get-tuple-element.43.scaled, bf16[4,896,2048]{2,1,0:T(8,128)(2,1)S(1)} %get-tuple-element.42.refs_5_.refs_0_, bf16[3,896,2048]{2,1,0:T(8,128)(2,1)S(1)} %fetch.6.refs_1_.refs_0_), custom_call_target="tpu_custom_call" | custom-call | flops 587202560 | bytes 3670016 | tf_op jit(solution)/shard_map/hidden_next/pallas_call | solution.py:568
  72.5 3.9 %collective-permute-done.19.far_up = bf16[80,896]{1,0:T(8,128)(2,1)S(1)} collective-permute-done((bf16[80,896]{1,0:T(8,128)(2,1)S(1)}, bf16[80,896]{1,0:T(8,128)(2,1)S(1)}, u32[]{:S(2)}, u32[]{:S(2)}) %collective-permute-start.19) | collective-permute-done | bytes 143392 | tf_op jit(solution)/shard_map/ppermute | solution.py:128
  78.2 3.8 %collective-permute-done.20.refs_0_ = bf16[80,896]{1,0:T(8,128)(2,1)S(1)} collective-permute-done((bf16[80,896]{1,0:T(8,128)(2,1)S(1)}, bf16[80,896]{1,0:T(8,128)(2,1)S(1)}, u32[]{:S(2)}, u32[]{:S(2)}) %collective-permute-start.20) | collective-permute-done | bytes 143392 | tf_op jit(solution)/shard_map/ppermute | solution.py:128
  82.0 3.2 %fetch.7.refs_1_ = bf16[2,896,2048]{2,1,0:T(8,128)(2,1)S(1)} custom-call(bf16[3584,2048]{1,0:T(8,128)(2,1)} %refs_0_.9), custom_call_target="tpu_custom_call" | custom-call | bytes 14680064 | tf_op jit(solution)/shard_map/fetch/pallas_call | solution.py:212
  88.4 2.3 %collective-permute-start.24 = (bf16[40,1024]{1,0:T(8,128)(2,1)S(1)}, bf16[40,1024]{1,0:T(8,128)(2,1)S(1)}, u32[]{:S(2)}, u32[]{:S(2)}) collective-permute-start(bf16[40,1024]{1,0:T(8,128)(2,1)S(1)} %get-tuple-element.53), channel_id=1, source_target_pairs={{0,8},{4,12},{8,0},{12,4},{1,9},{5,13},{9,1},{13,5},{2,10},{6,14},... | collective-permute-start | bytes 245768 | tf_op jit(solution)/shard_map/ppermute | solution.py:128
  90.7 2.1 %collective-permute-start.25 = (bf16[40,1024]{1,0:T(8,128)(2,1)S(1)}, bf16[40,1024]{1,0:T(8,128)(2,1)S(1)}, u32[]{:S(2)}, u32[]{:S(2)}) collective-permute-start(bf16[40,1024]{1,0:T(8,128)(2,1)S(1)} %get-tuple-element.54), channel_id=1, source_target_pairs={{0,12},{4,8},{8,4},{12,0},{1,13},{5,9},{9,5},{13,1},{2,14},{6,10},... | collective-permute-start | bytes 245768 | tf_op jit(solution)/shard_map/ppermute | solution.py:128
  92.8 1.6 %collective-permute-done.23.refs_2_ = bf16[40,1024]{1,0:T(8,128)(2,1)S(1)} collective-permute-done((bf16[40,1024]{1,0:T(8,128)(2,1)S(1)}, bf16[40,1024]{1,0:T(8,128)(2,1)S(1)}, u32[]{:S(2)}, u32[]{:S(2)}) %collective-permute-start.23) | collective-permute-done | bytes 81952 | tf_op jit(solution)/shard_map/ppermute | solution.py:128
  94.4 3.8 %collective-permute-done.24.refs_3_ = bf16[40,1024]{1,0:T(8,128)(2,1)S(1)} collective-permute-done((bf16[40,1024]{1,0:T(8,128)(2,1)S(1)}, bf16[40,1024]{1,0:T(8,128)(2,1)S(1)}, u32[]{:S(2)}, u32[]{:S(2)}) %collective-permute-start.24) | collective-permute-done | bytes 81952 | tf_op jit(solution)/shard_map/ppermute | solution.py:128
  (64 shorter events, 24.1 us)
Async XLA Ops:
  1.0 10.6 %collective-permute-start = (bf16[20,16,128]{2,1,0:T(8,128)(2,1)S(1)}, bf16[20,16,128]{2,1,0:T(8,128)(2,1)S(1)}, u32[]{:S(2)}, u32[]{:S(2)}) collective-permute-start(bf16[20,16,128]{2,1,0:T(8,128)(2,1)S(1)} %slice.refs_0_), channel_id=1, source_target_pairs={{0,4},{4,0},{8,12},{12,8},{1,5},{5,1},{9,13},{13,9},{2,6},{6,2},{1... | collective-permute-start | bytes 245768 | tf_op jit(solution)/shard_map/ppermute | solution.py:128
  4.1 9.2 %collective-permute-start.1 = (bf16[20,16,128]{2,1,0:T(8,128)(2,1)S(1)}, bf16[20,16,128]{2,1,0:T(8,128)(2,1)S(1)}, u32[]{:S(2)}, u32[]{:S(2)}) collective-permute-start(bf16[20,16,128]{2,1,0:T(8,128)(2,1)S(1)} %slice.refs_0_), channel_id=1, source_target_pairs={{0,8},{4,12},{8,0},{12,4},{1,9},{5,13},{9,1},{13,5},{2,10},{6,14},... | collective-permute-start | bytes 245768 | tf_op jit(solution)/shard_map/ppermute | solution.py:128
  6.7 6.6 %collective-permute-start.2 = (bf16[20,16,128]{2,1,0:T(8,128)(2,1)S(1)}, bf16[20,16,128]{2,1,0:T(8,128)(2,1)S(1)}, u32[]{:S(2)}, u32[]{:S(2)}) collective-permute-start(bf16[20,16,128]{2,1,0:T(8,128)(2,1)S(1)} %slice.refs_0_), channel_id=1, source_target_pairs={{0,12},{4,8},{8,4},{12,0},{1,13},{5,9},{9,5},{13,1},{2,14},{6,10},... | collective-permute-start | bytes 245768 | tf_op jit(solution)/shard_map/ppermute | solution.py:128
  18.4 6.5 %collective-permute-start.3 = (bf16[24,512]{1,0:T(8,128)(2,1)S(1)}, bf16[24,512]{1,0:T(8,128)(2,1)S(1)}, u32[]{:S(2)}, u32[]{:S(2)}) collective-permute-start(bf16[24,512]{1,0:T(8,128)(2,1)S(1)} %get-tuple-element.34), channel_id=1, source_target_pairs={{0,4},{4,0},{8,12},{12,8},{1,5},{5,1},{9,13},{13,9},{2,6},{6,2},{1... | collective-permute-start | bytes 73736 | tf_op jit(solution)/shard_map/ppermute | solution.py:128
  19.9 5.1 %collective-permute-start.4 = (bf16[24,512]{1,0:T(8,128)(2,1)S(1)}, bf16[24,512]{1,0:T(8,128)(2,1)S(1)}, u32[]{:S(2)}, u32[]{:S(2)}) collective-permute-start(bf16[24,512]{1,0:T(8,128)(2,1)S(1)} %get-tuple-element.35), channel_id=1, source_target_pairs={{0,8},{4,12},{8,0},{12,4},{1,9},{5,13},{9,1},{13,5},{2,10},{6,14},... | collective-permute-start | bytes 73736 | tf_op jit(solution)/shard_map/ppermute | solution.py:128
  22.4 5.6 %collective-permute-start.5 = (bf16[24,512]{1,0:T(8,128)(2,1)S(1)}, bf16[24,512]{1,0:T(8,128)(2,1)S(1)}, u32[]{:S(2)}, u32[]{:S(2)}) collective-permute-start(bf16[24,512]{1,0:T(8,128)(2,1)S(1)} %get-tuple-element.36), channel_id=1, source_target_pairs={{0,12},{4,8},{8,4},{12,0},{1,13},{5,9},{9,5},{13,1},{2,14},{6,10},... | collective-permute-start | bytes 73736 | tf_op jit(solution)/shard_map/ppermute | solution.py:128
  28.3 4.5 %collective-permute-start.7 = (bf16[80,512]{1,0:T(8,128)(2,1)S(1)}, bf16[80,512]{1,0:T(8,128)(2,1)S(1)}, u32[]{:S(2)}, u32[]{:S(2)}) collective-permute-start(bf16[80,512]{1,0:T(8,128)(2,1)S(1)} %ordered.1.refs_0_), channel_id=1, source_target_pairs={{0,2},{1,3},{2,0},{3,1},{4,6},{5,7},{6,4},{7,5},{8,10},{9,11},{10,... | collective-permute-start | bytes 245768 | tf_op jit(solution)/shard_map/ppermute | solution.py:128
  35.7 8.0 %collective-permute-start.10 = (bf16[40,1024]{1,0:T(8,128)(2,1)S(1)}, bf16[40,1024]{1,0:T(8,128)(2,1)S(1)}, u32[]{:S(2)}, u32[]{:S(2)}) collective-permute-start(bf16[40,1024]{1,0:T(8,128)(2,1)S(1)} %get-tuple-element.40), channel_id=1, source_target_pairs={{0,8},{4,12},{8,0},{12,4},{1,9},{5,13},{9,1},{13,5},{2,10},{6,14},... | collective-permute-start | bytes 245768 | tf_op jit(solution)/shard_map/ppermute | solution.py:128
  35.7 8.0 %collective-permute-start.11 = (bf16[40,1024]{1,0:T(8,128)(2,1)S(1)}, bf16[40,1024]{1,0:T(8,128)(2,1)S(1)}, u32[]{:S(2)}, u32[]{:S(2)}) collective-permute-start(bf16[40,1024]{1,0:T(8,128)(2,1)S(1)} %get-tuple-element.41), channel_id=1, source_target_pairs={{0,12},{4,8},{8,4},{12,0},{1,13},{5,9},{9,5},{13,1},{2,14},{6,10},... | collective-permute-start | bytes 245768 | tf_op jit(solution)/shard_map/ppermute | solution.py:128
  36.8 7.8 %collective-permute-start.9 = (bf16[40,1024]{1,0:T(8,128)(2,1)S(1)}, bf16[40,1024]{1,0:T(8,128)(2,1)S(1)}, u32[]{:S(2)}, u32[]{:S(2)}) collective-permute-start(bf16[40,1024]{1,0:T(8,128)(2,1)S(1)} %get-tuple-element.39), channel_id=1, source_target_pairs={{0,4},{4,0},{8,12},{12,8},{1,5},{5,1},{9,13},{13,9},{2,6},{6,2},{1... | collective-permute-start | bytes 245768 | tf_op jit(solution)/shard_map/ppermute | solution.py:128
  44.7 15.1 %collective-permute-start.12 = (bf16[40,1024]{1,0:T(8,128)(2,1)S(1)}, bf16[40,1024]{1,0:T(8,128)(2,1)S(1)}, u32[]{:S(2)}, u32[]{:S(2)}) collective-permute-start(bf16[40,1024]{1,0:T(8,128)(2,1)S(1)} %residual.2.refs_0_), channel_id=1, source_target_pairs={{0,4},{4,0},{8,12},{12,8},{1,5},{5,1},{9,13},{13,9},{2,6},{6,2},{1... | collective-permute-start | bytes 245768 | tf_op jit(solution)/shard_map/ppermute | solution.py:128
  45.4 14.5 %collective-permute-start.13 = (bf16[40,1024]{1,0:T(8,128)(2,1)S(1)}, bf16[40,1024]{1,0:T(8,128)(2,1)S(1)}, u32[]{:S(2)}, u32[]{:S(2)}) collective-permute-start(bf16[40,1024]{1,0:T(8,128)(2,1)S(1)} %residual.2.refs_0_), channel_id=1, source_target_pairs={{0,8},{4,12},{8,0},{12,4},{1,9},{5,13},{9,1},{13,5},{2,10},{6,14},... | collective-permute-start | bytes 245768 | tf_op jit(solution)/shard_map/ppermute | solution.py:128
  47.1 12.7 %collective-permute-start.14 = (bf16[40,1024]{1,0:T(8,128)(2,1)S(1)}, bf16[40,1024]{1,0:T(8,128)(2,1)S(1)}, u32[]{:S(2)}, u32[]{:S(2)}) collective-permute-start(bf16[40,1024]{1,0:T(8,128)(2,1)S(1)} %residual.2.refs_0_), channel_id=1, source_target_pairs={{0,12},{4,8},{8,4},{12,0},{1,13},{5,9},{9,5},{13,1},{2,14},{6,10},... | collective-permute-start | bytes 245768 | tf_op jit(solution)/shard_map/ppermute | solution.py:128
  62.3 7.2 %collective-permute-start.18 = (bf16[80,896]{1,0:T(8,128)(2,1)S(1)}, bf16[80,896]{1,0:T(8,128)(2,1)S(1)}, u32[]{:S(2)}, u32[]{:S(2)}) collective-permute-start(bf16[80,896]{1,0:T(8,128)(2,1)S(1)} %hidden_next.9), channel_id=1, source_target_pairs={{0,1},{1,0},{2,3},{3,2},{4,5},{5,4},{6,7},{7,6},{8,9},{9,8},{10,11... | collective-permute-start | bytes 430088 | tf_op jit(solution)/shard_map/ppermute | solution.py:128
  62.4 4.2 %collective-permute-start.16 = (bf16[80,1024]{1,0:T(8,128)(2,1)S(1)}, bf16[80,1024]{1,0:T(8,128)(2,1)S(1)}, u32[]{:S(2)}, u32[]{:S(2)}) collective-permute-start(bf16[80,1024]{1,0:T(8,128)(2,1)S(1)} %get-tuple-element.45), channel_id=1, source_target_pairs={{0,1},{1,0},{2,3},{3,2},{4,5},{5,4},{6,7},{7,6},{8,9},{9,8},{10,11... | collective-permute-start | bytes 491528 | tf_op jit(solution)/shard_map/ppermute | solution.py:128
  65.2 11.2 %collective-permute-start.15 = (bf16[80,1792]{1,0:T(8,128)(2,1)S(1)}, bf16[80,1792]{1,0:T(8,128)(2,1)S(1)}, u32[]{:S(2)}, u32[]{:S(2)}) collective-permute-start(bf16[80,1792]{1,0:T(8,128)(2,1)S(1)} %hidden_next.6), channel_id=1, source_target_pairs={{0,1},{1,0},{2,3},{3,2},{4,5},{5,4},{6,7},{7,6},{8,9},{9,8},{10,11... | collective-permute-start | bytes 860168 | tf_op jit(solution)/shard_map/ppermute | solution.py:128
  66.7 9.7 %collective-permute-start.17 = (bf16[80,1024]{1,0:T(8,128)(2,1)S(1)}, bf16[80,1024]{1,0:T(8,128)(2,1)S(1)}, u32[]{:S(2)}, u32[]{:S(2)}) collective-permute-start(bf16[80,1024]{1,0:T(8,128)(2,1)S(1)} %get-tuple-element.46), channel_id=1, source_target_pairs={{0,2},{1,3},{2,0},{3,1},{4,6},{5,7},{6,4},{7,5},{8,10},{9,11},{10,... | collective-permute-start | bytes 491528 | tf_op jit(solution)/shard_map/ppermute | solution.py:128
  69.6 6.9 %collective-permute-start.19 = (bf16[80,896]{1,0:T(8,128)(2,1)S(1)}, bf16[80,896]{1,0:T(8,128)(2,1)S(1)}, u32[]{:S(2)}, u32[]{:S(2)}) collective-permute-start(bf16[80,896]{1,0:T(8,128)(2,1)S(1)} %chip_sum.1), channel_id=1, source_target_pairs={{0,2},{1,3},{2,0},{3,1},{4,6},{5,7},{6,4},{7,5},{8,10},{9,11},{10,... | collective-permute-start | bytes 430088 | tf_op jit(solution)/shard_map/ppermute | solution.py:128
  76.7 5.3 %collective-permute-start.20 = (bf16[80,896]{1,0:T(8,128)(2,1)S(1)}, bf16[80,896]{1,0:T(8,128)(2,1)S(1)}, u32[]{:S(2)}, u32[]{:S(2)}) collective-permute-start(bf16[80,896]{1,0:T(8,128)(2,1)S(1)} %active.1.refs_0_), channel_id=1, source_target_pairs={{0,2},{1,3},{2,0},{3,1},{4,6},{5,7},{6,4},{7,5},{8,10},{9,11},{10,... | collective-permute-start | bytes 430088 | tf_op jit(solution)/shard_map/ppermute | solution.py:128
  78.2 6.9 %collective-permute-start.22 = (bf16[80,896]{1,0:T(8,128)(2,1)S(1)}, bf16[80,896]{1,0:T(8,128)(2,1)S(1)}, u32[]{:S(2)}, u32[]{:S(2)}) collective-permute-start(bf16[80,896]{1,0:T(8,128)(2,1)S(1)} %active.1.refs_0_), channel_id=1, source_target_pairs={{0,1},{1,0},{2,3},{3,2},{4,5},{5,4},{6,7},{7,6},{8,9},{9,8},{10,11... | collective-permute-start | bytes 430088 | tf_op jit(solution)/shard_map/ppermute | solution.py:128
  82.0 5.5 %collective-permute-start.21 = (bf16[80,896]{1,0:T(8,128)(2,1)S(1)}, bf16[80,896]{1,0:T(8,128)(2,1)S(1)}, u32[]{:S(2)}, u32[]{:S(2)}) collective-permute-start(bf16[80,896]{1,0:T(8,128)(2,1)S(1)} %collective-permute-done.20.refs_0_), channel_id=1, source_target_pairs={{0,1},{1,0},{2,3},{3,2},{4,5},{5,4},{6,7},{7,6},{8,9},{9,8},{10,11... | collective-permute-start | bytes 430088 | tf_op jit(solution)/shard_map/ppermute | solution.py:128
  88.3 6.1 %collective-permute-start.23 = (bf16[40,1024]{1,0:T(8,128)(2,1)S(1)}, bf16[40,1024]{1,0:T(8,128)(2,1)S(1)}, u32[]{:S(2)}, u32[]{:S(2)}) collective-permute-start(bf16[40,1024]{1,0:T(8,128)(2,1)S(1)} %get-tuple-element.52), channel_id=1, source_target_pairs={{0,4},{4,0},{8,12},{12,8},{1,5},{5,1},{9,13},{13,9},{2,6},{6,2},{1... | collective-permute-start | bytes 245768 | tf_op jit(solution)/shard_map/ppermute | solution.py:128
  88.4 9.8 %collective-permute-start.24 = (bf16[40,1024]{1,0:T(8,128)(2,1)S(1)}, bf16[40,1024]{1,0:T(8,128)(2,1)S(1)}, u32[]{:S(2)}, u32[]{:S(2)}) collective-permute-start(bf16[40,1024]{1,0:T(8,128)(2,1)S(1)} %get-tuple-element.53), channel_id=1, source_target_pairs={{0,8},{4,12},{8,0},{12,4},{1,9},{5,13},{9,1},{13,5},{2,10},{6,14},... | collective-permute-start | bytes 245768 | tf_op jit(solution)/shard_map/ppermute | solution.py:128
  90.7 7.6 %collective-permute-start.25 = (bf16[40,1024]{1,0:T(8,128)(2,1)S(1)}, bf16[40,1024]{1,0:T(8,128)(2,1)S(1)}, u32[]{:S(2)}, u32[]{:S(2)}) collective-permute-start(bf16[40,1024]{1,0:T(8,128)(2,1)S(1)} %get-tuple-element.54), channel_id=1, source_target_pairs={{0,12},{4,8},{8,4},{12,0},{1,13},{5,9},{9,5},{13,1},{2,14},{6,10},... | collective-permute-start | bytes 245768 | tf_op jit(solution)/shard_map/ppermute | solution.py:128
  (6 other events, 53.2 us)

commit v10 on v9

--- a/solution.py
+++ b/solution.py
@@ -729,7 +729,7 @@
     across = pair_swap(piece, "ffn", 2)
     beside = pair_swap(piece, "ffn", 1)
     corner = pair_swap(across, "ffn", 1)
-    (down_far,) = fetch([(down_weight, (2, 3))], parts)
+    (down_across,) = fetch([(down_weight, (2,))], parts)
     gain = norm_gain.reshape(1, columns)
     partial = projection([piece, beside, across, corner], project, slots, count)
     jobs = [(gate_weight, (0, 1, 2, 3)), (down_weight, (1,))]
@@ -737,7 +737,8 @@
     middle = residual(hidden_state, swaps_of(partial), False)
 
     rows = swaps_of([middle] * count)
-    (up,) = fetch([(up_weight, (0, 1, 2))], parts)
+    jobs = [(up_weight, (0, 1, 2)), (down_weight, (3,))]
+    up, down_corner = fetch(jobs, parts)
     send, scaled, squares = hidden_first(rows, gain, gate, 3)
     arrived = pair_swap(send, "ffn", 1)
     keep = hidden_next(scaled, [(gate, 2)], F32)
@@ -757,8 +758,8 @@
     chosen = [(active, down_near, 0), (beside, down_beside, 0)]
     (before,) = down_part(chosen, count, None, False)
     corner = pair_swap(across, "ffn", 1)
-    (before,) = down_part([(across, down_far, 0)], count, before, False)
-    partial = down_part([(corner, down_far, 1)], count, before, True)
+    (before,) = down_part([(across, down_across, 0)], count, before, False)
+    partial = down_part([(corner, down_corner, 0)], count, before, True)
     return residual(middle, swaps_of(partial), True)
 
 

time: 99.1 us -> 99 us (level)
  no operation moved by 1% of the time
where the time goes in v10:
time: 99 us; the launch traced here: 98.8 us
  Pallas kernels  41.3 us (42%)
  starting transfers between devices  28.6 us (29%)
  waiting for transfers between devices  27.6 us (28%)
    ppermute x26, starting transfers between devices, pair_swap(): return lax.ppermute(value, axis, [(i, i ^ bit) for i in range(count)])  28.6 us
    ppermute x26, waiting for transfers between devices, pair_swap(): return lax.ppermute(value, axis, [(i, i ^ bit) for i in range(count)])  27.6 us
    pallas_call x4, Pallas kernels, fetch(): pl.pallas_call(functools.partial(fetch_kernel, masks_of=masks_in(jobs)),...  18.5 us
    pallas_call x5, Pallas kernels, hidden_next(): pl.pallas_call(functools.partial(hidden_kernel, parts=tuple((part for _,...  8.32 us
    pallas_call x1, Pallas kernels, attention(): pl.pallas_call(functools.partial(attention_kernel, slots=slots, count=cou...  5.1 us
    pallas_call x3, Pallas kernels, down_part(): pl.pallas_call(functools.partial(down_kernel, parts=tuple((part for _, _,...  3.1 us
    pallas_call x1, Pallas kernels, selection(): pl.pallas_call(functools.partial(selection_kernel, slots=slots, count=cou...  2.06 us
  transfers between devices with their start and end apart: 26, of which 10 were waited for; matrix products, arithmetic and copies ran while one was open for 0% of the time, Pallas kernels for 30%

profile of v10, /device:TPU:0, one launch (start us, length us, event | category | flops | bytes accessed | tf_op | source)
XLA Modules:
  0.0 98.8 jit_solution(5060921325140213362)
XLA Ops:
  0.9 3.1 %collective-permute-start = (bf16[20,16,128]{2,1,0:T(8,128)(2,1)S(1)}, bf16[20,16,128]{2,1,0:T(8,128)(2,1)S(1)}, u32[]{:S(2)}, u32[]{:S(2)}) collective-permute-start(bf16[20,16,128]{2,1,0:T(8,128)(2,1)S(1)} %slice.refs_0_), channel_id=1, source_target_pairs={{0,4},{4,0},{8,12},{12,8},{1,5},{5,1},{9,13},{13,9},{2,6},{6,2},{1... | collective-permute-start | bytes 245768 | tf_op jit(solution)/shard_map/ppermute | solution.py:128
  4.0 2.6 %collective-permute-start.1 = (bf16[20,16,128]{2,1,0:T(8,128)(2,1)S(1)}, bf16[20,16,128]{2,1,0:T(8,128)(2,1)S(1)}, u32[]{:S(2)}, u32[]{:S(2)}) collective-permute-start(bf16[20,16,128]{2,1,0:T(8,128)(2,1)S(1)} %slice.refs_0_), channel_id=1, source_target_pairs={{0,8},{4,12},{8,0},{12,4},{1,9},{5,13},{9,1},{13,5},{2,10},{6,14},... | collective-permute-start | bytes 245768 | tf_op jit(solution)/shard_map/ppermute | solution.py:128
  6.6 4.8 %fetch.4 = (bf16[12800,256]{1,0:T(8,128)(2,1)S(1)}, bf16[12800,256]{1,0:T(8,128)(2,1)S(1)}) custom-call(bf16[12800,256]{1,0:T(8,128)(2,1)} %refs_0_.5, bf16[12800,256]{1,0:T(8,128)(2,1)} %refs_1_.3), custom_call_target="tpu_custom_call" | custom-call | bytes 26214400 | tf_op jit(solution)/shard_map/fetch/pallas_call | solution.py:212
  11.5 1.7 %collective-permute-done.1.refs_2_ = bf16[20,16,128]{2,1,0:T(8,128)(2,1)S(1)} collective-permute-done((bf16[20,16,128]{2,1,0:T(8,128)(2,1)S(1)}, bf16[20,16,128]{2,1,0:T(8,128)(2,1)S(1)}, u32[]{:S(2)}, u32[]{:S(2)}) %collective-permute-start.1) | collective-permute-done | bytes 81952 | tf_op jit(solution)/shard_map/ppermute | solution.py:128
  13.2 5.1 %attention.1 = (bf16[24,512]{1,0:T(8,128)(2,1)S(1)}, bf16[24,512]{1,0:T(8,128)(2,1)S(1)}, bf16[24,512]{1,0:T(8,128)(2,1)S(1)}, bf16[24,512]{1,0:T(8,128)(2,1)S(1...) custom-call(s32[102]{0:T(128)S(1)} %pad_add_fusion.table, bf16[20,16,128]{2,1,0:T(8,128)(2,1)S(1)} %slice.refs_0_, ...), custom_call_target="tpu_custom_call" | custom-call | flops 104857600 | bytes 13107200 | tf_op jit(solution)/shard_map/attention/pallas_call | solution.py:363
  19.9 2.5 %collective-permute-start.4 = (bf16[24,512]{1,0:T(8,128)(2,1)S(1)}, bf16[24,512]{1,0:T(8,128)(2,1)S(1)}, u32[]{:S(2)}, u32[]{:S(2)}) collective-permute-start(bf16[24,512]{1,0:T(8,128)(2,1)S(1)} %get-tuple-element.37), channel_id=1, source_target_pairs={{0,8},{4,12},{8,0},{12,4},{1,9},{5,13},{9,1},{13,5},{2,10},{6,14},... | collective-permute-start | bytes 73736 | tf_op jit(solution)/shard_map/ppermute | solution.py:128
  22.8 2.1 %selection.1 = (bf16[1,896,2048]{2,1,0:T(8,128)(2,1)S(1)}, bf16[4,80,24]{2,1,0:T(8,128)(2,1)S(1)}) custom-call(s32[8,128]{1,0:T(8,128)S(1)} %broadcast_in_dim.3.served, bf16[3584,2048]{1,0:T(8,128)(2,1)} %refs_0_.8), custom_call_target="tpu_custom_call" | custom-call | bytes 7340032 | tf_op jit(solution)/shard_map/selection/pallas_call | solution.py:427
  24.9 3.1 %collective-permute-done.5.refs_3_ = bf16[24,512]{1,0:T(8,128)(2,1)S(1)} collective-permute-done((bf16[24,512]{1,0:T(8,128)(2,1)S(1)}, bf16[24,512]{1,0:T(8,128)(2,1)S(1)}, u32[]{:S(2)}, u32[]{:S(2)}) %collective-permute-start.5) | collective-permute-done | bytes 24608 | tf_op jit(solution)/shard_map/ppermute | solution.py:128
  29.8 2.9 %collective-permute-done.7.refs_2_ = bf16[80,512]{1,0:T(8,128)(2,1)S(1)} collective-permute-done((bf16[80,512]{1,0:T(8,128)(2,1)S(1)}, bf16[80,512]{1,0:T(8,128)(2,1)S(1)}, u32[]{:S(2)}, u32[]{:S(2)}) %collective-permute-start.7) | collective-permute-done | bytes 81952 | tf_op jit(solution)/shard_map/ppermute | solution.py:128
  36.8 2.4 %collective-permute-start.9 = (bf16[40,1024]{1,0:T(8,128)(2,1)S(1)}, bf16[40,1024]{1,0:T(8,128)(2,1)S(1)}, u32[]{:S(2)}, u32[]{:S(2)}) collective-permute-start(bf16[40,1024]{1,0:T(8,128)(2,1)S(1)} %get-tuple-element.41), channel_id=1, source_target_pairs={{0,4},{4,0},{8,12},{12,8},{1,5},{5,1},{9,13},{13,9},{2,6},{6,2},{1... | collective-permute-start | bytes 245768 | tf_op jit(solution)/shard_map/ppermute | solution.py:128
  39.2 4.5 %collective-permute-done.10.refs_3_ = bf16[40,1024]{1,0:T(8,128)(2,1)S(1)} collective-permute-done((bf16[40,1024]{1,0:T(8,128)(2,1)S(1)}, bf16[40,1024]{1,0:T(8,128)(2,1)S(1)}, u32[]{:S(2)}, u32[]{:S(2)}) %collective-permute-start.10) | collective-permute-done | bytes 81952 | tf_op jit(solution)/shard_map/ppermute | solution.py:128
  45.3 1.7 %collective-permute-start.13 = (bf16[40,1024]{1,0:T(8,128)(2,1)S(1)}, bf16[40,1024]{1,0:T(8,128)(2,1)S(1)}, u32[]{:S(2)}, u32[]{:S(2)}) collective-permute-start(bf16[40,1024]{1,0:T(8,128)(2,1)S(1)} %residual.2.refs_0_), channel_id=1, source_target_pairs={{0,8},{4,12},{8,0},{12,4},{1,9},{5,13},{9,1},{13,5},{2,10},{6,14},... | collective-permute-start | bytes 245768 | tf_op jit(solution)/shard_map/ppermute | solution.py:128
  47.0 2.1 %collective-permute-start.14 = (bf16[40,1024]{1,0:T(8,128)(2,1)S(1)}, bf16[40,1024]{1,0:T(8,128)(2,1)S(1)}, u32[]{:S(2)}, u32[]{:S(2)}) collective-permute-start(bf16[40,1024]{1,0:T(8,128)(2,1)S(1)} %residual.2.refs_0_), channel_id=1, source_target_pairs={{0,12},{4,8},{8,4},{12,0},{1,13},{5,9},{9,5},{13,1},{2,14},{6,10},... | collective-permute-start | bytes 245768 | tf_op jit(solution)/shard_map/ppermute | solution.py:128
  49.1 5.3 %fetch.6 = (bf16[3,896,2048]{2,1,0:T(8,128)(2,1)S(1)}, bf16[1,896,2048]{2,1,0:T(8,128)(2,1)S(1)}) custom-call(bf16[3584,2048]{1,0:T(8,128)(2,1)} %refs_0_.8, bf16[3584,2048]{1,0:T(8,128)(2,1)} %refs_0_.9), custom_call_target="tpu_custom_call" | custom-call | bytes 29360128 | tf_op jit(solution)/shard_map/fetch/pallas_call | solution.py:212
  54.4 6.3 %fetch.5 = (bf16[4,896,2048]{2,1,0:T(8,128)(2,1)S(1)}, bf16[1,896,2048]{2,1,0:T(8,128)(2,1)S(1)}) custom-call(bf16[3584,2048]{1,0:T(8,128)(2,1)} %refs_0_.7, bf16[3584,2048]{1,0:T(8,128)(2,1)} %refs_0_.9), custom_call_target="tpu_custom_call" | custom-call | bytes 36700160 | tf_op jit(solution)/shard_map/fetch/pallas_call | solution.py:212
  63.9 2.3 %hidden_next.6 = bf16[80,1792]{1,0:T(8,128)(2,1)S(1)} custom-call(bf16[80,2048]{1,0:T(8,128)(2,1)S(1)} %get-tuple-element.45.scaled, bf16[4,896,2048]{2,1,0:T(8,128)(2,1)S(1)} %get-tuple-element.44.refs_5_.refs_0_, bf16[3,896,2048]{2,1,0:T(8,128)(2,1)S(1)} %get-tuple-element.46.refs_1_.refs_0_), custom_call_target="tpu_custom_call" | custom-call | flops 587202560 | bytes 3670016 | tf_op jit(solution)/shard_map/hidden_next/pallas_call | solution.py:568
  71.2 2.3 %hidden_next.5.near = f32[80,1792]{1,0:T(8,128)S(1)} custom-call(bf16[80,2048]{1,0:T(8,128)(2,1)S(1)} %get-tuple-element.45.scaled, bf16[4,896,2048]{2,1,0:T(8,128)(2,1)S(1)} %get-tuple-element.44.refs_5_.refs_0_, bf16[3,896,2048]{2,1,0:T(8,128)(2,1)S(1)} %get-tuple-element.46.refs_1_.refs_0_), custom_call_target="tpu_custom_call" | custom-call | flops 587202560 | bytes 3670016 | tf_op jit(solution)/shard_map/hidden_next/pallas_call | solution.py:568
  73.5 3.9 %collective-permute-done.19.far_up = bf16[80,896]{1,0:T(8,128)(2,1)S(1)} collective-permute-done((bf16[80,896]{1,0:T(8,128)(2,1)S(1)}, bf16[80,896]{1,0:T(8,128)(2,1)S(1)}, u32[]{:S(2)}, u32[]{:S(2)}) %collective-permute-start.19) | collective-permute-done | bytes 143392 | tf_op jit(solution)/shard_map/ppermute | solution.py:128
  79.3 3.7 %collective-permute-done.20.refs_0_ = bf16[80,896]{1,0:T(8,128)(2,1)S(1)} collective-permute-done((bf16[80,896]{1,0:T(8,128)(2,1)S(1)}, bf16[80,896]{1,0:T(8,128)(2,1)S(1)}, u32[]{:S(2)}, u32[]{:S(2)}) %collective-permute-start.20) | collective-permute-done | bytes 143392 | tf_op jit(solution)/shard_map/ppermute | solution.py:128
  83.0 2.0 %fetch.7.refs_1_ = bf16[1,896,2048]{2,1,0:T(8,128)(2,1)S(1)} custom-call(bf16[3584,2048]{1,0:T(8,128)(2,1)} %refs_0_.9), custom_call_target="tpu_custom_call" | custom-call | bytes 7340032 | tf_op jit(solution)/shard_map/fetch/pallas_call | solution.py:212
  88.3 2.3 %collective-permute-start.24 = (bf16[40,1024]{1,0:T(8,128)(2,1)S(1)}, bf16[40,1024]{1,0:T(8,128)(2,1)S(1)}, u32[]{:S(2)}, u32[]{:S(2)}) collective-permute-start(bf16[40,1024]{1,0:T(8,128)(2,1)S(1)} %get-tuple-element.57), channel_id=1, source_target_pairs={{0,8},{4,12},{8,0},{12,4},{1,9},{5,13},{9,1},{13,5},{2,10},{6,14},... | collective-permute-start | bytes 245768 | tf_op jit(solution)/shard_map/ppermute | solution.py:128
  90.6 2.1 %collective-permute-start.25 = (bf16[40,1024]{1,0:T(8,128)(2,1)S(1)}, bf16[40,1024]{1,0:T(8,128)(2,1)S(1)}, u32[]{:S(2)}, u32[]{:S(2)}) collective-permute-start(bf16[40,1024]{1,0:T(8,128)(2,1)S(1)} %get-tuple-element.58), channel_id=1, source_target_pairs={{0,12},{4,8},{8,4},{12,0},{1,13},{5,9},{9,5},{13,1},{2,14},{6,10},... | collective-permute-start | bytes 245768 | tf_op jit(solution)/shard_map/ppermute | solution.py:128
  92.6 1.6 %collective-permute-done.23.refs_2_ = bf16[40,1024]{1,0:T(8,128)(2,1)S(1)} collective-permute-done((bf16[40,1024]{1,0:T(8,128)(2,1)S(1)}, bf16[40,1024]{1,0:T(8,128)(2,1)S(1)}, u32[]{:S(2)}, u32[]{:S(2)}) %collective-permute-start.23) | collective-permute-done | bytes 81952 | tf_op jit(solution)/shard_map/ppermute | solution.py:128
  94.3 3.8 %collective-permute-done.24.refs_3_ = bf16[40,1024]{1,0:T(8,128)(2,1)S(1)} collective-permute-done((bf16[40,1024]{1,0:T(8,128)(2,1)S(1)}, bf16[40,1024]{1,0:T(8,128)(2,1)S(1)}, u32[]{:S(2)}, u32[]{:S(2)}) %collective-permute-start.24) | collective-permute-done | bytes 81952 | tf_op jit(solution)/shard_map/ppermute | solution.py:128
  (64 shorter events, 24.1 us)
Async XLA Ops:
  0.9 10.6 %collective-permute-start = (bf16[20,16,128]{2,1,0:T(8,128)(2,1)S(1)}, bf16[20,16,128]{2,1,0:T(8,128)(2,1)S(1)}, u32[]{:S(2)}, u32[]{:S(2)}) collective-permute-start(bf16[20,16,128]{2,1,0:T(8,128)(2,1)S(1)} %slice.refs_0_), channel_id=1, source_target_pairs={{0,4},{4,0},{8,12},{12,8},{1,5},{5,1},{9,13},{13,9},{2,6},{6,2},{1... | collective-permute-start | bytes 245768 | tf_op jit(solution)/shard_map/ppermute | solution.py:128
  4.0 9.2 %collective-permute-start.1 = (bf16[20,16,128]{2,1,0:T(8,128)(2,1)S(1)}, bf16[20,16,128]{2,1,0:T(8,128)(2,1)S(1)}, u32[]{:S(2)}, u32[]{:S(2)}) collective-permute-start(bf16[20,16,128]{2,1,0:T(8,128)(2,1)S(1)} %slice.refs_0_), channel_id=1, source_target_pairs={{0,8},{4,12},{8,0},{12,4},{1,9},{5,13},{9,1},{13,5},{2,10},{6,14},... | collective-permute-start | bytes 245768 | tf_op jit(solution)/shard_map/ppermute | solution.py:128
  6.6 6.6 %collective-permute-start.2 = (bf16[20,16,128]{2,1,0:T(8,128)(2,1)S(1)}, bf16[20,16,128]{2,1,0:T(8,128)(2,1)S(1)}, u32[]{:S(2)}, u32[]{:S(2)}) collective-permute-start(bf16[20,16,128]{2,1,0:T(8,128)(2,1)S(1)} %slice.refs_0_), channel_id=1, source_target_pairs={{0,12},{4,8},{8,4},{12,0},{1,13},{5,9},{9,5},{13,1},{2,14},{6,10},... | collective-permute-start | bytes 245768 | tf_op jit(solution)/shard_map/ppermute | solution.py:128
  18.3 6.5 %collective-permute-start.3 = (bf16[24,512]{1,0:T(8,128)(2,1)S(1)}, bf16[24,512]{1,0:T(8,128)(2,1)S(1)}, u32[]{:S(2)}, u32[]{:S(2)}) collective-permute-start(bf16[24,512]{1,0:T(8,128)(2,1)S(1)} %get-tuple-element.36), channel_id=1, source_target_pairs={{0,4},{4,0},{8,12},{12,8},{1,5},{5,1},{9,13},{13,9},{2,6},{6,2},{1... | collective-permute-start | bytes 73736 | tf_op jit(solution)/shard_map/ppermute | solution.py:128
  19.9 5.1 %collective-permute-start.4 = (bf16[24,512]{1,0:T(8,128)(2,1)S(1)}, bf16[24,512]{1,0:T(8,128)(2,1)S(1)}, u32[]{:S(2)}, u32[]{:S(2)}) collective-permute-start(bf16[24,512]{1,0:T(8,128)(2,1)S(1)} %get-tuple-element.37), channel_id=1, source_target_pairs={{0,8},{4,12},{8,0},{12,4},{1,9},{5,13},{9,1},{13,5},{2,10},{6,14},... | collective-permute-start | bytes 73736 | tf_op jit(solution)/shard_map/ppermute | solution.py:128
  22.4 5.6 %collective-permute-start.5 = (bf16[24,512]{1,0:T(8,128)(2,1)S(1)}, bf16[24,512]{1,0:T(8,128)(2,1)S(1)}, u32[]{:S(2)}, u32[]{:S(2)}) collective-permute-start(bf16[24,512]{1,0:T(8,128)(2,1)S(1)} %get-tuple-element.38), channel_id=1, source_target_pairs={{0,12},{4,8},{8,4},{12,0},{1,13},{5,9},{9,5},{13,1},{2,14},{6,10},... | collective-permute-start | bytes 73736 | tf_op jit(solution)/shard_map/ppermute | solution.py:128
  28.2 4.5 %collective-permute-start.7 = (bf16[80,512]{1,0:T(8,128)(2,1)S(1)}, bf16[80,512]{1,0:T(8,128)(2,1)S(1)}, u32[]{:S(2)}, u32[]{:S(2)}) collective-permute-start(bf16[80,512]{1,0:T(8,128)(2,1)S(1)} %ordered.1.refs_0_), channel_id=1, source_target_pairs={{0,2},{1,3},{2,0},{3,1},{4,6},{5,7},{6,4},{7,5},{8,10},{9,11},{10,... | collective-permute-start | bytes 245768 | tf_op jit(solution)/shard_map/ppermute | solution.py:128
  35.6 8.0 %collective-permute-start.10 = (bf16[40,1024]{1,0:T(8,128)(2,1)S(1)}, bf16[40,1024]{1,0:T(8,128)(2,1)S(1)}, u32[]{:S(2)}, u32[]{:S(2)}) collective-permute-start(bf16[40,1024]{1,0:T(8,128)(2,1)S(1)} %get-tuple-element.42), channel_id=1, source_target_pairs={{0,8},{4,12},{8,0},{12,4},{1,9},{5,13},{9,1},{13,5},{2,10},{6,14},... | collective-permute-start | bytes 245768 | tf_op jit(solution)/shard_map/ppermute | solution.py:128
  35.7 8.0 %collective-permute-start.11 = (bf16[40,1024]{1,0:T(8,128)(2,1)S(1)}, bf16[40,1024]{1,0:T(8,128)(2,1)S(1)}, u32[]{:S(2)}, u32[]{:S(2)}) collective-permute-start(bf16[40,1024]{1,0:T(8,128)(2,1)S(1)} %get-tuple-element.43), channel_id=1, source_target_pairs={{0,12},{4,8},{8,4},{12,0},{1,13},{5,9},{9,5},{13,1},{2,14},{6,10},... | collective-permute-start | bytes 245768 | tf_op jit(solution)/shard_map/ppermute | solution.py:128
  36.8 7.8 %collective-permute-start.9 = (bf16[40,1024]{1,0:T(8,128)(2,1)S(1)}, bf16[40,1024]{1,0:T(8,128)(2,1)S(1)}, u32[]{:S(2)}, u32[]{:S(2)}) collective-permute-start(bf16[40,1024]{1,0:T(8,128)(2,1)S(1)} %get-tuple-element.41), channel_id=1, source_target_pairs={{0,4},{4,0},{8,12},{12,8},{1,5},{5,1},{9,13},{13,9},{2,6},{6,2},{1... | collective-permute-start | bytes 245768 | tf_op jit(solution)/shard_map/ppermute | solution.py:128
  44.7 16.1 %collective-permute-start.12 = (bf16[40,1024]{1,0:T(8,128)(2,1)S(1)}, bf16[40,1024]{1,0:T(8,128)(2,1)S(1)}, u32[]{:S(2)}, u32[]{:S(2)}) collective-permute-start(bf16[40,1024]{1,0:T(8,128)(2,1)S(1)} %residual.2.refs_0_), channel_id=1, source_target_pairs={{0,4},{4,0},{8,12},{12,8},{1,5},{5,1},{9,13},{13,9},{2,6},{6,2},{1... | collective-permute-start | bytes 245768 | tf_op jit(solution)/shard_map/ppermute | solution.py:128
  45.3 15.5 %collective-permute-start.13 = (bf16[40,1024]{1,0:T(8,128)(2,1)S(1)}, bf16[40,1024]{1,0:T(8,128)(2,1)S(1)}, u32[]{:S(2)}, u32[]{:S(2)}) collective-permute-start(bf16[40,1024]{1,0:T(8,128)(2,1)S(1)} %residual.2.refs_0_), channel_id=1, source_target_pairs={{0,8},{4,12},{8,0},{12,4},{1,9},{5,13},{9,1},{13,5},{2,10},{6,14},... | collective-permute-start | bytes 245768 | tf_op jit(solution)/shard_map/ppermute | solution.py:128
  47.0 13.8 %collective-permute-start.14 = (bf16[40,1024]{1,0:T(8,128)(2,1)S(1)}, bf16[40,1024]{1,0:T(8,128)(2,1)S(1)}, u32[]{:S(2)}, u32[]{:S(2)}) collective-permute-start(bf16[40,1024]{1,0:T(8,128)(2,1)S(1)} %residual.2.refs_0_), channel_id=1, source_target_pairs={{0,12},{4,8},{8,4},{12,0},{1,13},{5,9},{9,5},{13,1},{2,14},{6,10},... | collective-permute-start | bytes 245768 | tf_op jit(solution)/shard_map/ppermute | solution.py:128
  63.3 7.2 %collective-permute-start.18 = (bf16[80,896]{1,0:T(8,128)(2,1)S(1)}, bf16[80,896]{1,0:T(8,128)(2,1)S(1)}, u32[]{:S(2)}, u32[]{:S(2)}) collective-permute-start(bf16[80,896]{1,0:T(8,128)(2,1)S(1)} %hidden_next.9), channel_id=1, source_target_pairs={{0,1},{1,0},{2,3},{3,2},{4,5},{5,4},{6,7},{7,6},{8,9},{9,8},{10,11... | collective-permute-start | bytes 430088 | tf_op jit(solution)/shard_map/ppermute | solution.py:128
  63.4 4.2 %collective-permute-start.16 = (bf16[80,1024]{1,0:T(8,128)(2,1)S(1)}, bf16[80,1024]{1,0:T(8,128)(2,1)S(1)}, u32[]{:S(2)}, u32[]{:S(2)}) collective-permute-start(bf16[80,1024]{1,0:T(8,128)(2,1)S(1)} %get-tuple-element.48), channel_id=1, source_target_pairs={{0,1},{1,0},{2,3},{3,2},{4,5},{5,4},{6,7},{7,6},{8,9},{9,8},{10,11... | collective-permute-start | bytes 491528 | tf_op jit(solution)/shard_map/ppermute | solution.py:128
  66.2 11.2 %collective-permute-start.15 = (bf16[80,1792]{1,0:T(8,128)(2,1)S(1)}, bf16[80,1792]{1,0:T(8,128)(2,1)S(1)}, u32[]{:S(2)}, u32[]{:S(2)}) collective-permute-start(bf16[80,1792]{1,0:T(8,128)(2,1)S(1)} %hidden_next.6), channel_id=1, source_target_pairs={{0,1},{1,0},{2,3},{3,2},{4,5},{5,4},{6,7},{7,6},{8,9},{9,8},{10,11... | collective-permute-start | bytes 860168 | tf_op jit(solution)/shard_map/ppermute | solution.py:128
  67.8 9.7 %collective-permute-start.17 = (bf16[80,1024]{1,0:T(8,128)(2,1)S(1)}, bf16[80,1024]{1,0:T(8,128)(2,1)S(1)}, u32[]{:S(2)}, u32[]{:S(2)}) collective-permute-start(bf16[80,1024]{1,0:T(8,128)(2,1)S(1)} %get-tuple-element.49), channel_id=1, source_target_pairs={{0,2},{1,3},{2,0},{3,1},{4,6},{5,7},{6,4},{7,5},{8,10},{9,11},{10,... | collective-permute-start | bytes 491528 | tf_op jit(solution)/shard_map/ppermute | solution.py:128
  70.6 6.8 %collective-permute-start.19 = (bf16[80,896]{1,0:T(8,128)(2,1)S(1)}, bf16[80,896]{1,0:T(8,128)(2,1)S(1)}, u32[]{:S(2)}, u32[]{:S(2)}) collective-permute-start(bf16[80,896]{1,0:T(8,128)(2,1)S(1)} %chip_sum.1), channel_id=1, source_target_pairs={{0,2},{1,3},{2,0},{3,1},{4,6},{5,7},{6,4},{7,5},{8,10},{9,11},{10,... | collective-permute-start | bytes 430088 | tf_op jit(solution)/shard_map/ppermute | solution.py:128
  77.7 5.3 %collective-permute-start.20 = (bf16[80,896]{1,0:T(8,128)(2,1)S(1)}, bf16[80,896]{1,0:T(8,128)(2,1)S(1)}, u32[]{:S(2)}, u32[]{:S(2)}) collective-permute-start(bf16[80,896]{1,0:T(8,128)(2,1)S(1)} %active.1.refs_0_), channel_id=1, source_target_pairs={{0,2},{1,3},{2,0},{3,1},{4,6},{5,7},{6,4},{7,5},{8,10},{9,11},{10,... | collective-permute-start | bytes 430088 | tf_op jit(solution)/shard_map/ppermute | solution.py:128
  79.3 5.8 %collective-permute-start.22 = (bf16[80,896]{1,0:T(8,128)(2,1)S(1)}, bf16[80,896]{1,0:T(8,128)(2,1)S(1)}, u32[]{:S(2)}, u32[]{:S(2)}) collective-permute-start(bf16[80,896]{1,0:T(8,128)(2,1)S(1)} %active.1.refs_0_), channel_id=1, source_target_pairs={{0,1},{1,0},{2,3},{3,2},{4,5},{5,4},{6,7},{7,6},{8,9},{9,8},{10,11... | collective-permute-start | bytes 430088 | tf_op jit(solution)/shard_map/ppermute | solution.py:128
  83.0 4.4 %collective-permute-start.21 = (bf16[80,896]{1,0:T(8,128)(2,1)S(1)}, bf16[80,896]{1,0:T(8,128)(2,1)S(1)}, u32[]{:S(2)}, u32[]{:S(2)}) collective-permute-start(bf16[80,896]{1,0:T(8,128)(2,1)S(1)} %collective-permute-done.20.refs_0_), channel_id=1, source_target_pairs={{0,1},{1,0},{2,3},{3,2},{4,5},{5,4},{6,7},{7,6},{8,9},{9,8},{10,11... | collective-permute-start | bytes 430088 | tf_op jit(solution)/shard_map/ppermute | solution.py:128
  88.2 6.1 %collective-permute-start.23 = (bf16[40,1024]{1,0:T(8,128)(2,1)S(1)}, bf16[40,1024]{1,0:T(8,128)(2,1)S(1)}, u32[]{:S(2)}, u32[]{:S(2)}) collective-permute-start(bf16[40,1024]{1,0:T(8,128)(2,1)S(1)} %get-tuple-element.56), channel_id=1, source_target_pairs={{0,4},{4,0},{8,12},{12,8},{1,5},{5,1},{9,13},{13,9},{2,6},{6,2},{1... | collective-permute-start | bytes 245768 | tf_op jit(solution)/shard_map/ppermute | solution.py:128
  88.3 9.8 %collective-permute-start.24 = (bf16[40,1024]{1,0:T(8,128)(2,1)S(1)}, bf16[40,1024]{1,0:T(8,128)(2,1)S(1)}, u32[]{:S(2)}, u32[]{:S(2)}) collective-permute-start(bf16[40,1024]{1,0:T(8,128)(2,1)S(1)} %get-tuple-element.57), channel_id=1, source_target_pairs={{0,8},{4,12},{8,0},{12,4},{1,9},{5,13},{9,1},{13,5},{2,10},{6,14},... | collective-permute-start | bytes 245768 | tf_op jit(solution)/shard_map/ppermute | solution.py:128
  90.6 7.5 %collective-permute-start.25 = (bf16[40,1024]{1,0:T(8,128)(2,1)S(1)}, bf16[40,1024]{1,0:T(8,128)(2,1)S(1)}, u32[]{:S(2)}, u32[]{:S(2)}) collective-permute-start(bf16[40,1024]{1,0:T(8,128)(2,1)S(1)} %get-tuple-element.58), channel_id=1, source_target_pairs={{0,12},{4,8},{8,4},{12,0},{1,13},{5,9},{9,5},{13,1},{2,14},{6,10},... | collective-permute-start | bytes 245768 | tf_op jit(solution)/shard_map/ppermute | solution.py:128
  (6 other events, 39.9 us)
